TPU v7x, 32 devices: a whole 2x2x4 slice. The times are simulated.
32 devices in a mesh: rows: 4 (over y, core), chan: 8 (over z, x).
Axes of the slice: x: 2, y: 2, z: 4, core: 2. Of those that a mesh axis runs over, the one named last changes fastest.
Arguments:
- hidden_in: bfloat16 [4, 1024, 512], P('rows', 'chan'), may hold values from -6 to 6
- segments: int32 [4, 1024], P('rows'), may hold values from 0 to 3, never falling along the last dimension, each value on 1 to 512 neighbouring positions
- filters: bfloat16 [24, 1024], replicated, may hold values from -0.1875 to 0.1875
- gain_one: float32 [512], replicated, may hold values from 0.1 to 1.9
- mixing: bfloat16 [51, 512, 512], P(None, 'chan'), may hold values from -0.0390625 to 0.0390625
- gain_two: float32 [512], replicated, may hold values from 0.1 to 1.9
- w_gate: bfloat16 [512, 2048], replicated, may hold values from -0.25 to 0.25
- w_up: bfloat16 [512, 2048], replicated, may hold values from -0.25 to 0.25
- w_down: bfloat16 [2048, 512], replicated, may hold values from -0.125 to 0.125
- out_grad: bfloat16 [4, 1024, 512], P('rows', 'chan'), may hold values from -6 to 6
Outputs:
- output: bfloat16 [4, 1024, 512], P('rows', 'chan')
- input_grad: float32 [4, 1024, 512], P('rows', 'chan')
- mixing_grad: float32 [51, 512, 512], P(None, 'chan')
- gate_grad: float32 [512, 2048], P(None, 'chan')
- up_grad: float32 [512, 2048], P(None, 'chan')
- down_grad: float32 [2048, 512], P('chan')
- gain_one_grad: float32 [512], P('chan')
- gain_two_grad: float32 [512], P('chan')
Inputs may be any that keep to these rules, and one draw needn't show every extreme that they name: `segments`: along each row the numbers never fall; each of the 4 numbers covers 1 to 512 consecutive positions, and one covers exactly 512.
All inputs are finite; a program needn't handle non-finite values.
Results may differ from a plain program's by a relative error of at most 0.025.
Values may be sent and summed in bfloat16 or wider, within the bound.
No kernel may reach another device: no remote copies, remote signals or barrier semaphores. Data moves between devices by JAX's collectives and lax.ppermute only.
A program may use at most 320 MiB of HBM per device.

v0:
```python
import jax
import jax.numpy as jnp
from jax import lax
from jax.sharding import PartitionSpec as P

K = 24
AR = 3


eps_norm = 1e-05
block_limit = 512


def rms_scale(values, scales):
    return values * lax.rsqrt(jnp.mean(values * values, axis=-1, keepdims=True) + eps_norm) * scales


def gelu_product(gate_value, upper_value):
    return jax.nn.gelu(gate_value, approximate=True) * upper_value


def contract_first(left, right):
    return lax.dot_general(
        left, right, (((0,), (0,)), ((), ())), preferred_element_type=jnp.float32
    )


def contract_last(left, right):
    return lax.dot_general(
        left, right, (((1,), (1,)), ((), ())), preferred_element_type=jnp.float32
    )


def toeplitz_block(padded_filters, segment_ids, out_block, in_block, block_rows):
    filter_count = padded_filters.shape[0]
    start = (out_block - in_block) * block_rows + 1
    window = lax.dynamic_slice_in_dim(padded_filters, start, 2 * block_rows - 1, 1)
    flipped = window[:, ::-1]
    skewed = jnp.concatenate(
        [
            flipped[:, block_rows - 1 :],
            jnp.zeros((filter_count, 1), flipped.dtype),
            flipped[:, : block_rows - 1],
        ],
        axis=1,
    )
    tiled = jnp.tile(skewed, (1, block_rows))[:, : block_rows * (2 * block_rows - 1)]
    values = tiled.reshape(filter_count, block_rows, 2 * block_rows - 1)[:, :, :block_rows]
    positions = lax.iota(jnp.int32, block_rows)
    offsets = (out_block * block_rows + positions)[:, None] - (in_block * block_rows + positions)[
        None, :
    ]
    target_ids = lax.dynamic_slice_in_dim(segment_ids, out_block * block_rows, block_rows)
    source_ids = lax.dynamic_slice_in_dim(segment_ids, in_block * block_rows, block_rows)
    keep_mask = (offsets >= 0) & (target_ids[:, None] == source_ids[None, :])
    return jnp.where(keep_mask[None], values, jnp.zeros_like(values))


def spectral_maps(doubled_t, padded_filters, segment_ids):
    columns, length = doubled_t.shape
    filter_count = padded_filters.shape[0]
    block_rows = min(block_limit, length)
    block_count = length // block_rows

    def per_target(out_block, result):

        def add_source(in_block, partial_value):
            toeplitz = toeplitz_block(padded_filters, segment_ids, out_block, in_block, block_rows)
            source = lax.dynamic_slice_in_dim(doubled_t, in_block * block_rows, block_rows, 1)
            return partial_value + jnp.einsum(
                "cs,kts->ckt", source, toeplitz, preferred_element_type=jnp.float32
            )

        start_value = jnp.zeros((columns, filter_count, block_rows), jnp.float32)
        partial_value = lax.fori_loop(0, out_block + 1, add_source, start_value)
        return lax.dynamic_update_slice_in_dim(result, partial_value, out_block * block_rows, 2)

    empty = jnp.zeros((columns, filter_count, length), jnp.float32)
    return lax.fori_loop(0, block_count, per_target, empty)


def spectral_back(grads_t, padded_filters, segment_ids):
    columns, filter_count, length = grads_t.shape
    block_rows = min(block_limit, length)
    block_count = length // block_rows

    def per_source(in_block, result):

        def add_target(out_block, partial_value):
            toeplitz = toeplitz_block(padded_filters, segment_ids, out_block, in_block, block_rows)
            target = lax.dynamic_slice_in_dim(grads_t, out_block * block_rows, block_rows, 2)
            return partial_value + jnp.einsum(
                "ckt,kts->cs", target, toeplitz, preferred_element_type=jnp.float32
            )

        partial_value = lax.fori_loop(
            in_block, block_count, add_target, jnp.zeros((columns, block_rows), jnp.float32)
        )
        return lax.dynamic_update_slice_in_dim(result, partial_value, in_block * block_rows, 1)

    return lax.fori_loop(0, block_count, per_source, jnp.zeros((columns, length), jnp.float32))


def same_mask(segment_ids, offset):
    length = segment_ids.shape[0]
    before = jnp.concatenate([jnp.full((offset,), -1, jnp.int32), segment_ids[: length - offset]])
    return before == segment_ids


def build_maps(inputs, segment_ids, padded_filters):
    length, channels = inputs.shape
    parity = (1 - 2 * (lax.iota(jnp.int32, length) % 2)).astype(jnp.bfloat16)
    doubled_t = jnp.concatenate([inputs.T, (parity[:, None] * inputs).T], axis=0)
    filtered = spectral_maps(doubled_t, padded_filters, segment_ids)
    plus_maps = filtered[:channels]
    minus_maps = parity.astype(jnp.float32)[None, None, :] * filtered[channels:]
    spectral = jnp.concatenate([plus_maps, minus_maps], axis=1).astype(jnp.bfloat16)
    spectral = jnp.transpose(spectral, (2, 1, 0)).reshape(length, -1)
    pieces = [spectral]
    for offset in range(AR):
        shifted = jnp.concatenate(
            [jnp.zeros((offset, channels), jnp.bfloat16), inputs[: length - offset]], axis=0
        )
        pieces.append(shifted * same_mask(segment_ids, offset)[:, None].astype(jnp.bfloat16))
    return jnp.concatenate(pieces, axis=1)


def shards(
    hidden_in, segments, filters, gain_one, mixing, gain_two, w_gate, w_up, w_down, out_grad
):
    tokens = hidden_in[0].astype(jnp.float32)
    normed_one = rms_scale(tokens, gain_one).astype(jnp.bfloat16)
    inputs = lax.all_to_all(normed_one, "chan", split_axis=1, concat_axis=0, tiled=True)
    segment_ids = segments[0]
    length, channels = inputs.shape
    block_rows = min(block_limit, length)
    padded_filters = jnp.concatenate(
        [jnp.zeros((filters.shape[0], block_rows), filters.dtype), filters], axis=1
    )
    model_width = mixing.shape[2]
    flat_mixing = mixing.reshape(-1, model_width)
    filtered = build_maps(inputs, segment_ids, padded_filters)
    mixed = lax.psum_scatter(
        jnp.dot(filtered, flat_mixing, preferred_element_type=jnp.float32).astype(jnp.bfloat16),
        "chan",
        scatter_dimension=0,
        tiled=True,
    ).astype(jnp.float32)
    resid = tokens + mixed
    normed_two = rms_scale(resid, gain_two).astype(jnp.bfloat16)
    gate_value = jnp.dot(normed_two, w_gate, preferred_element_type=jnp.float32)
    upper_value = jnp.dot(normed_two, w_up, preferred_element_type=jnp.float32)
    hidden = gelu_product(gate_value, upper_value).astype(jnp.bfloat16)
    output = (resid + jnp.dot(hidden, w_down, preferred_element_type=jnp.float32)).astype(
        jnp.bfloat16
    )
    cotangent = out_grad[0]
    hidden_grad = contract_last(cotangent, w_down)
    _, gelu_pull = jax.vjp(gelu_product, gate_value, upper_value)
    gate_float, upper_float = gelu_pull(hidden_grad)
    gate_back = gate_float.astype(jnp.bfloat16)
    upper_back = upper_float.astype(jnp.bfloat16)
    normed_grad = contract_last(gate_back, w_gate) + contract_last(upper_back, w_up)
    _, second_pull = jax.vjp(rms_scale, resid, gain_two)
    resid_part, second_local = second_pull(normed_grad)
    resid_grad = cotangent.astype(jnp.float32) + resid_part
    full_grad = lax.all_gather(resid_grad.astype(jnp.bfloat16), "chan", axis=0, tiled=True)
    inputs_again, full_grad = lax.optimization_barrier((inputs, full_grad))
    used_maps = build_maps(inputs_again, segment_ids, padded_filters)
    mixing_local = contract_first(used_maps, full_grad).reshape(mixing.shape)
    maps_grad = contract_last(full_grad, flat_mixing)
    spectral_width = 2 * K * channels
    spectral_grad = (
        maps_grad[:, :spectral_width].astype(jnp.bfloat16).reshape(length, 2 * K, channels)
    )
    parity = (1 - 2 * (lax.iota(jnp.int32, length) % 2)).astype(jnp.bfloat16)
    plus_t = jnp.transpose(spectral_grad[:, :K], (2, 1, 0))
    minus_t = jnp.transpose(parity[:, None, None] * spectral_grad[:, K:], (2, 1, 0))
    grads_t = jnp.concatenate([plus_t, minus_t], axis=0)
    doubled_back = spectral_back(grads_t, padded_filters, segment_ids)
    input_back = (
        doubled_back[:channels].T + parity.astype(jnp.float32)[:, None] * doubled_back[channels:].T
    )
    lag_grad = maps_grad[:, spectral_width:]
    for offset in range(AR):
        lag_term = lag_grad[:, offset * channels : (offset + 1) * channels]
        lag_term = lag_term * same_mask(segment_ids, offset)[:, None].astype(jnp.float32)
        input_back = input_back + jnp.concatenate(
            [lag_term[offset:], jnp.zeros((offset, channels), jnp.float32)], axis=0
        )
    token_grad = lax.all_to_all(
        input_back.astype(jnp.bfloat16), "chan", split_axis=0, concat_axis=1, tiled=True
    )
    _, first_pull = jax.vjp(rms_scale, tokens, gain_one)
    tokens_part, first_local = first_pull(token_grad.astype(jnp.float32))
    input_total = resid_grad + tokens_part
    down_local = contract_first(hidden, cotangent)
    gate_local = contract_first(normed_two, gate_back)
    up_local = contract_first(normed_two, upper_back)
    mixing_sum, gate_sum, up_sum, down_sum, first_sum, second_sum = (
        lax.psum(mixing_local.astype(jnp.bfloat16), "rows").astype(jnp.float32),
        lax.psum(gate_local.astype(jnp.bfloat16), "rows").astype(jnp.float32),
        lax.psum(up_local.astype(jnp.bfloat16), "rows").astype(jnp.float32),
        lax.psum(down_local.astype(jnp.bfloat16), "rows").astype(jnp.float32),
        lax.psum(first_local.astype(jnp.bfloat16), "rows").astype(jnp.float32),
        lax.psum(second_local.astype(jnp.bfloat16), "rows").astype(jnp.float32),
    )
    gate_share, up_share, down_share, first_share, second_share = (
        lax.psum_scatter(
            gate_sum.astype(jnp.bfloat16), "chan", scatter_dimension=1, tiled=True
        ).astype(jnp.float32),
        lax.psum_scatter(
            up_sum.astype(jnp.bfloat16), "chan", scatter_dimension=1, tiled=True
        ).astype(jnp.float32),
        lax.psum_scatter(
            down_sum.astype(jnp.bfloat16), "chan", scatter_dimension=0, tiled=True
        ).astype(jnp.float32),
        lax.psum_scatter(
            first_sum.astype(jnp.bfloat16), "chan", scatter_dimension=0, tiled=True
        ).astype(jnp.float32),
        lax.psum_scatter(
            second_sum.astype(jnp.bfloat16), "chan", scatter_dimension=0, tiled=True
        ).astype(jnp.float32),
    )
    return (
        output[None],
        input_total[None],
        mixing_sum,
        gate_share,
        up_share,
        down_share,
        first_share,
        second_share,
    )


def solution(mesh):
    in_specs = (
        P("rows", "chan", None),
        P("rows", None),
        P(),
        P(),
        P(None, "chan", None),
        P(),
        P(),
        P(),
        P(),
        P("rows", "chan", None),
    )
    out_specs = (
        P("rows", "chan", None),
        P("rows", "chan", None),
        P(None, "chan", None),
        P(None, "chan"),
        P(None, "chan"),
        P("chan", None),
        P("chan"),
        P("chan"),
    )
    return jax.shard_map(shards, mesh=mesh, in_specs=in_specs, out_specs=out_specs, check_vma=False)
```

profile of v0, /device:TPU:0, one launch (start us, length us, event | category | flops | bytes accessed | tf_op | source)
XLA Modules:
  0.0 1693.7 jit_solution(7181150705269363369)
XLA Ops:
  34.7 478.4 %while.139 = (s32[]{:T(128)}, f32[128,24,1024]{2,0,1:T(8,128)}, s32[1024]{0:T(1024)S(1)}, bf16[128,1024]{1,0:T(8,128)(2,1)}, bf16[24,1536]{1,0:T(8,128)(2,1)S(1)...) while((s32[]{:T(128)}, f32[128,24,1024]{2,0,1:T(8,128)}, ...), condition=%wide.region_4.5_spmd, body=%wide.region_1.4_spmd.sunk | while | flops 1619674112 | bytes 221192720 | solution.py:79
  38.3 152.6 %while.144 = (s32[]{:T(128)}, f32[128,24,512]{2,0,1:T(8,128)}, s32[]{:T(128)}, bf16[128,1024]{1,0:T(8,128)(2,1)}, s32[]{:T(128)}, /*index=5*/s32[512]{0:T(512)S(...) while((s32[]{:T(128)}, f32[128,24,512]{2,0,1:T(8,128)}, ...), condition=%wide.region_3.3_spmd, body=%wide.region_2.2_spmd.sunk | while | flops 1619674112 | bytes 202313856 | solution.py:75
  42.6 46.0 %copy.50 = bf16[3,8,512,1024]{3,1,2,0:T(8,128)(2,1)} copy(bf16[3,8,512,1024]{3,2,1,0:T(8,128)(2,1)S(1)} %bitcast.178) | data formatting | bytes 50331648 | tf_op jit(solution)/shard_map/while/body/eval_jaxpr/while
  88.7 20.4 %slice.280 = bf16[24,523776]{1,0:T(8,128)(2,1)} slice(bf16[24,524288]{1,0:T(8,128)(2,1)} %bitcast.181), slice={[0:24], [0:523776]} | slice | bytes 50282496 | tf_op jit(solution)/shard_map/while/body/eval_jaxpr/while/body/slice | solution.py:47
  109.1 68.2 %reshape.424 = bf16[24,512,1023]{2,1,0:T(8,128)(2,1)} reshape(bf16[24,523776]{1,0:T(8,128)(2,1)} %slice.280) | data formatting | bytes 50282496 | tf_op jit(solution)/shard_map/while/body/eval_jaxpr/while/body/reshape | solution.py:48
  177.6 13.3 fusion.137
  201.0 305.3 %while.144 = (s32[]{:T(128)}, f32[128,24,512]{2,0,1:T(8,128)}, s32[]{:T(128)}, bf16[128,1024]{1,0:T(8,128)(2,1)}, s32[]{:T(128)}, /*index=5*/s32[512]{0:T(512)S(...) while((s32[]{:T(128)}, f32[128,24,512]{2,0,1:T(8,128)}, ...), condition=%wide.region_3.3_spmd, body=%wide.region_2.2_spmd.sunk | while | flops 1619674112 | bytes 202313856 | solution.py:75
  205.4 46.0 %copy.50 = bf16[3,8,512,1024]{3,1,2,0:T(8,128)(2,1)} copy(bf16[3,8,512,1024]{3,2,1,0:T(8,128)(2,1)S(1)} %bitcast.178) | data formatting | bytes 50331648 | tf_op jit(solution)/shard_map/while/body/eval_jaxpr/while
  251.4 20.4 %slice.280 = bf16[24,523776]{1,0:T(8,128)(2,1)} slice(bf16[24,524288]{1,0:T(8,128)(2,1)} %bitcast.181), slice={[0:24], [0:523776]} | slice | bytes 50282496 | tf_op jit(solution)/shard_map/while/body/eval_jaxpr/while/body/slice | solution.py:47
  271.8 68.2 %reshape.424 = bf16[24,512,1023]{2,1,0:T(8,128)(2,1)} reshape(bf16[24,523776]{1,0:T(8,128)(2,1)} %slice.280) | data formatting | bytes 50282496 | tf_op jit(solution)/shard_map/while/body/eval_jaxpr/while/body/reshape | solution.py:48
  340.4 13.3 fusion.137
  358.0 46.0 %copy.50 = bf16[3,8,512,1024]{3,1,2,0:T(8,128)(2,1)} copy(bf16[3,8,512,1024]{3,2,1,0:T(8,128)(2,1)S(1)} %bitcast.178) | data formatting | bytes 50331648 | tf_op jit(solution)/shard_map/while/body/eval_jaxpr/while
  404.0 20.4 %slice.280 = bf16[24,523776]{1,0:T(8,128)(2,1)} slice(bf16[24,524288]{1,0:T(8,128)(2,1)} %bitcast.181), slice={[0:24], [0:523776]} | slice | bytes 50282496 | tf_op jit(solution)/shard_map/while/body/eval_jaxpr/while/body/slice | solution.py:47
  424.4 68.2 %reshape.424 = bf16[24,512,1023]{2,1,0:T(8,128)(2,1)} reshape(bf16[24,523776]{1,0:T(8,128)(2,1)} %slice.280) | data formatting | bytes 50282496 | tf_op jit(solution)/shard_map/while/body/eval_jaxpr/while/body/reshape | solution.py:48
  493.0 13.3 fusion.137
  530.4 61.7 %reduce-scatter.5.cloned.1.call-done = bf16[128,512]{1,0:T(8,128)(2,1)} async-done(((bf16[1024,512]{1,0:T(8,128)(2,1)}), bf16[128,512]{1,0:T(8,128)(2,1)}) %reduce-scatter.5.cloned.1.call-update) | async-done | bytes 131088 | tf_op jit(solution)/shard_map/reduce_scatter | solution.py:143
  618.4 25.6 %all-gather.2.cloned.1.call-done = bf16[1024,512]{1,0:T(8,128)(2,1)} async-done(((bf16[128,512]{1,0:T(8,128)(2,1)}), bf16[1024,512]{1,0:T(8,128)(2,1)}) %all-gather.2.cloned.1.call-update) | async-done | bytes 1048592 | tf_op jit(solution)/shard_map/all_gather | solution.py:167
  651.0 482.6 %while.143 = (s32[]{:T(128)}, f32[128,24,1024]{2,0,1:T(8,128)}, s32[1024]{0:T(1024)}, bf16[128,1024]{1,0:T(8,128)(2,1)}, bf16[24,1536]{1,0:T(8,128)(2,1)S(1)}, /...) while((s32[]{:T(128)}, f32[128,24,1024]{2,0,1:T(8,128)}, ...), condition=%wide.region_16.17_spmd, body=%wide.region_13.0_spmd.sunk | while | flops 1619674112 | bytes 221176272 | solution.py:79
  655.4 153.5 %while.146 = (s32[]{:T(128)}, f32[128,24,512]{2,0,1:T(8,128)}, s32[]{:T(128)}, bf16[128,1024]{1,0:T(8,128)(2,1)}, s32[]{:T(128)}, /*index=5*/s32[512]{0:T(512)S(...) while((s32[]{:T(128)}, f32[128,24,512]{2,0,1:T(8,128)}, ...), condition=%wide.region_15.15_spmd, body=%wide.region_14.14_spmd.sunk | while | flops 1619674112 | bytes 202297424 | solution.py:75
  659.8 46.0 %copy.48 = bf16[3,8,512,1024]{3,1,2,0:T(8,128)(2,1)} copy(bf16[3,8,512,1024]{3,2,1,0:T(8,128)(2,1)S(1)} %bitcast.179) | data formatting | bytes 50331648 | tf_op jit(solution)/shard_map/while/body/eval_jaxpr/while
  705.8 20.5 %slice.272 = bf16[24,523776]{1,0:T(8,128)(2,1)} slice(bf16[24,524288]{1,0:T(8,128)(2,1)} %bitcast.182), slice={[0:24], [0:523776]} | slice | bytes 50282496 | tf_op jit(solution)/shard_map/while/body/eval_jaxpr/while/body/slice | solution.py:47
  726.3 68.3 %reshape.422 = bf16[24,512,1023]{2,1,0:T(8,128)(2,1)} reshape(bf16[24,523776]{1,0:T(8,128)(2,1)} %slice.272) | data formatting | bytes 50282496 | tf_op jit(solution)/shard_map/while/body/eval_jaxpr/while/body/reshape | solution.py:48
  795.6 13.3 fusion.131
  820.0 306.6 %while.146 = (s32[]{:T(128)}, f32[128,24,512]{2,0,1:T(8,128)}, s32[]{:T(128)}, bf16[128,1024]{1,0:T(8,128)(2,1)}, s32[]{:T(128)}, /*index=5*/s32[512]{0:T(512)S(...) while((s32[]{:T(128)}, f32[128,24,512]{2,0,1:T(8,128)}, ...), condition=%wide.region_15.15_spmd, body=%wide.region_14.14_spmd.sunk | while | flops 1619674112 | bytes 202297424 | solution.py:75
  824.3 46.0 %copy.48 = bf16[3,8,512,1024]{3,1,2,0:T(8,128)(2,1)} copy(bf16[3,8,512,1024]{3,2,1,0:T(8,128)(2,1)S(1)} %bitcast.179) | data formatting | bytes 50331648 | tf_op jit(solution)/shard_map/while/body/eval_jaxpr/while
  870.4 20.4 %slice.272 = bf16[24,523776]{1,0:T(8,128)(2,1)} slice(bf16[24,524288]{1,0:T(8,128)(2,1)} %bitcast.182), slice={[0:24], [0:523776]} | slice | bytes 50282496 | tf_op jit(solution)/shard_map/while/body/eval_jaxpr/while/body/slice | solution.py:47
  890.8 68.2 %reshape.422 = bf16[24,512,1023]{2,1,0:T(8,128)(2,1)} reshape(bf16[24,523776]{1,0:T(8,128)(2,1)} %slice.272) | data formatting | bytes 50282496 | tf_op jit(solution)/shard_map/while/body/eval_jaxpr/while/body/reshape | solution.py:48
  960.0 13.3 fusion.131
  977.6 46.0 %copy.48 = bf16[3,8,512,1024]{3,1,2,0:T(8,128)(2,1)} copy(bf16[3,8,512,1024]{3,2,1,0:T(8,128)(2,1)S(1)} %bitcast.179) | data formatting | bytes 50331648 | tf_op jit(solution)/shard_map/while/body/eval_jaxpr/while
  1023.7 20.4 %slice.272 = bf16[24,523776]{1,0:T(8,128)(2,1)} slice(bf16[24,524288]{1,0:T(8,128)(2,1)} %bitcast.182), slice={[0:24], [0:523776]} | slice | bytes 50282496 | tf_op jit(solution)/shard_map/while/body/eval_jaxpr/while/body/slice | solution.py:47
  1044.1 68.2 %reshape.422 = bf16[24,512,1023]{2,1,0:T(8,128)(2,1)} reshape(bf16[24,523776]{1,0:T(8,128)(2,1)} %slice.272) | data formatting | bytes 50282496 | tf_op jit(solution)/shard_map/while/body/eval_jaxpr/while/body/reshape | solution.py:48
  1113.3 13.3 fusion.131
  1141.6 8.3 slice.249
  1166.2 13.7 fusion.47
  1180.7 451.1 %while.141 = (s32[]{:T(128)}, f32[128,1024]{1,0:T(8,128)}, s32[1024]{0:T(1024)}, bf16[128,24,1024]{2,0,1:T(8,128)(2,1)}, bf16[24,1536]{1,0:T(8,128)(2,1)S(1)}, /...) while((s32[]{:T(128)}, f32[128,1024]{1,0:T(8,128)}, ...), condition=%wide.region_11.12_spmd, body=%wide.region_8.11_spmd.sunk | while | flops 1618166784 | bytes 194044368 | solution.py:101
  1182.4 296.4 %while.145 = (s32[]{:T(128)}, f32[128,512]{1,0:T(8,128)}, bf16[128,24,1024]{2,0,1:T(8,128)(2,1)}, s32[]{:T(128)}, s32[1024]{0:T(1024)}, /*index=5*/s32[512]{0:T(...) while((s32[]{:T(128)}, f32[128,512]{1,0:T(8,128)}, ...), condition=%wide.region_10.10_spmd, body=%wide.region_9.9_spmd.sunk | while | flops 1618166784 | bytes 193253472 | solution.py:96
  1186.7 46.0 %copy.49 = bf16[3,8,512,1024]{3,1,2,0:T(8,128)(2,1)} copy(bf16[3,8,512,1024]{3,2,1,0:T(8,128)(2,1)S(1)} %bitcast.180) | data formatting | bytes 50331648 | tf_op jit(solution)/shard_map/while/body/eval_jaxpr/while
  1232.7 20.5 %slice.276 = bf16[24,523776]{1,0:T(8,128)(2,1)} slice(bf16[24,524288]{1,0:T(8,128)(2,1)} %bitcast.183), slice={[0:24], [0:523776]} | slice | bytes 50282496 | tf_op jit(solution)/shard_map/while/body/eval_jaxpr/while/body/slice | solution.py:47
  1253.2 68.2 %reshape.423 = bf16[24,512,1023]{2,1,0:T(8,128)(2,1)} reshape(bf16[24,523776]{1,0:T(8,128)(2,1)} %slice.276) | data formatting | bytes 50282496 | tf_op jit(solution)/shard_map/while/body/eval_jaxpr/while/body/reshape | solution.py:48
  1334.9 46.0 %copy.49 = bf16[3,8,512,1024]{3,1,2,0:T(8,128)(2,1)} copy(bf16[3,8,512,1024]{3,2,1,0:T(8,128)(2,1)S(1)} %bitcast.180) | data formatting | bytes 50331648 | tf_op jit(solution)/shard_map/while/body/eval_jaxpr/while
  1381.0 20.4 %slice.276 = bf16[24,523776]{1,0:T(8,128)(2,1)} slice(bf16[24,524288]{1,0:T(8,128)(2,1)} %bitcast.183), slice={[0:24], [0:523776]} | slice | bytes 50282496 | tf_op jit(solution)/shard_map/while/body/eval_jaxpr/while/body/slice | solution.py:47
  1401.4 68.2 %reshape.423 = bf16[24,512,1023]{2,1,0:T(8,128)(2,1)} reshape(bf16[24,523776]{1,0:T(8,128)(2,1)} %slice.276) | data formatting | bytes 50282496 | tf_op jit(solution)/shard_map/while/body/eval_jaxpr/while/body/reshape | solution.py:48
  1470.6 8.2 fusion.134
  1482.0 148.2 %while.145 = (s32[]{:T(128)}, f32[128,512]{1,0:T(8,128)}, bf16[128,24,1024]{2,0,1:T(8,128)(2,1)}, s32[]{:T(128)}, s32[1024]{0:T(1024)}, /*index=5*/s32[512]{0:T(...) while((s32[]{:T(128)}, f32[128,512]{1,0:T(8,128)}, ...), condition=%wide.region_10.10_spmd, body=%wide.region_9.9_spmd.sunk | while | flops 1618166784 | bytes 193253472 | solution.py:96
  1486.3 46.0 %copy.49 = bf16[3,8,512,1024]{3,1,2,0:T(8,128)(2,1)} copy(bf16[3,8,512,1024]{3,2,1,0:T(8,128)(2,1)S(1)} %bitcast.180) | data formatting | bytes 50331648 | tf_op jit(solution)/shard_map/while/body/eval_jaxpr/while
  1532.3 20.4 %slice.276 = bf16[24,523776]{1,0:T(8,128)(2,1)} slice(bf16[24,524288]{1,0:T(8,128)(2,1)} %bitcast.183), slice={[0:24], [0:523776]} | slice | bytes 50282496 | tf_op jit(solution)/shard_map/while/body/eval_jaxpr/while/body/slice | solution.py:47
  1552.7 68.2 %reshape.423 = bf16[24,512,1023]{2,1,0:T(8,128)(2,1)} reshape(bf16[24,523776]{1,0:T(8,128)(2,1)} %slice.276) | data formatting | bytes 50282496 | tf_op jit(solution)/shard_map/while/body/eval_jaxpr/while/body/reshape | solution.py:48
  1651.1 18.2 %all-reduce.10 = (bf16[512]{0:T(512)(128)(2,1)S(1)}, bf16[512]{0:T(512)(128)(2,1)S(1)}) all-reduce(bf16[512]{0:T(512)(128)(2,1)S(1)} %get-tuple-element.765, bf16[512]{0:T(512)(128)(2,1)S(1)} %copy-done.43), channel_id=6, replica_groups=mesh['rows'=4,'chan'=8] {'chan'}, use_global_device_ids=true, to_apply=%region_26.27.clone | all-reduce | flops 1024 | bytes 4096
  (308 shorter events, 249.4 us)
Async XLA Ops:
  7.2 516.5 %copy-start = (bf16[51,64,512]{2,1,0:T(8,128)(2,1)S(1)}, bf16[51,64,512]{2,1,0:T(8,128)(2,1)}, u32[]{:S(2)}) copy-start(bf16[51,64,512]{2,1,0:T(8,128)(2,1)} %param.26) | copy-start | bytes 10027012
  10.1 11.9 copy-start.41
  12.6 14.6 all-to-all-start
  19.8 572.3 %reduce-scatter.5.cloned.1.call-start = ((), (), s32[]{:S(2)}) async-start(), calls=%async_computation.6 | async-start | bytes 1179648 | tf_op jit(solution)/shard_map/reduce_scatter | solution.py:143
  23.4 11.4 copy-start.28
  28.6 6.1 copy-start.4
  109.1 68.2 %copy-start.5 = (s32[1,1024]{1,0:T(1,128)S(1)}, s32[1,1024]{1,0:T(1,128)}, u32[]{:S(2)}) copy-start(s32[1,1024]{1,0:T(1,128)} %get-tuple-element.1573) | copy-start | bytes 12292 | tf_op jit(solution)/shard_map/while/body/eval_jaxpr/while
  271.8 68.2 %copy-start.5 = (s32[1,1024]{1,0:T(1,128)S(1)}, s32[1,1024]{1,0:T(1,128)}, u32[]{:S(2)}) copy-start(s32[1,1024]{1,0:T(1,128)} %get-tuple-element.1573) | copy-start | bytes 12292 | tf_op jit(solution)/shard_map/while/body/eval_jaxpr/while
  424.4 68.2 %copy-start.5 = (s32[1,1024]{1,0:T(1,128)S(1)}, s32[1,1024]{1,0:T(1,128)}, u32[]{:S(2)}) copy-start(s32[1,1024]{1,0:T(1,128)} %get-tuple-element.1573) | copy-start | bytes 12292 | tf_op jit(solution)/shard_map/while/body/eval_jaxpr/while
  513.2 3.3 copy-start.23
  520.2 3.3 copy-start.8
  520.2 3.3 copy-start.32
  523.7 68.5 %copy-start.2 = (bf16[1,128,512]{2,1,0:T(8,128)(2,1)S(1)}, bf16[1,128,512]{2,1,0:T(8,128)(2,1)}, u32[]{:S(2)}) copy-start(bf16[1,128,512]{2,1,0:T(8,128)(2,1)} %param.22) | copy-start | bytes 393220
  523.7 69.7 %copy-start.26 = (f32[512]{0:T(512)S(1)}, f32[512]{0:T(512)}, u32[]{:S(2)}) copy-start(f32[512]{0:T(512)} %param.27) | copy-start | bytes 6148
  530.4 113.7 %all-gather.2.cloned.1.call-start = ((), (), s32[]{:S(2)}) async-start(), calls=%async_computation.7 | async-start | bytes 1179648 | tf_op jit(solution)/shard_map/all_gather | solution.py:167
  592.2 6.5 copy-start.14
  592.2 6.5 copy-start.17
  593.4 9.8 copy-start.39
  596.5 4.3 copy-start.6
  601.7 11.0 copy-start.38
  604.7 575.2 %reduce-scatter.7.cloned.1.call-start = ((), (), s32[]{:S(2)}) async-start(), calls=%async_computation.8 | async-start | bytes 2359296 | tf_op jit(solution)/shard_map/reduce_scatter | solution.py:209
  607.9 36.2 %copy-start.9 = (bf16[1024,64]{0,1:T(8,128)(2,1)S(1)}, bf16[1024,64]{0,1:T(8,128)(2,1)}, u32[]{:S(2)}) copy-start(bf16[1024,64]{0,1:T(8,128)(2,1)} %get-tuple-element.761) | copy-start | bytes 393220
  607.9 36.2 %copy-start.29 = (bf16[1024]{0:T(1024)(128)(2,1)S(1)}, bf16[1024]{0:T(1024)(128)(2,1)}, u32[]{:S(2)}) copy-start(bf16[1024]{0:T(1024)(128)(2,1)} %copy-done.28) | copy-start | bytes 6148
  607.9 571.9 %reduce-scatter.9.cloned.1.call-start = ((), (), s32[]{:S(2)}) async-start(), calls=%async_computation.9 | async-start | bytes 2359296 | tf_op jit(solution)/shard_map/reduce_scatter | solution.py:212
  611.3 568.5 %reduce-scatter.11.cloned.1.call-start = ((), (), s32[]{:S(2)}) async-start(), calls=%async_computation.10 | async-start | bytes 2359296 | tf_op jit(solution)/shard_map/reduce_scatter | solution.py:215
  618.4 1059.8 %all-reduce.15.cloned.1.call-start = ((), (), s32[]{:S(2)}) async-start(), calls=%async_computation.11 | async-start | bytes 8257536 | tf_op jit(solution)/shard_map/psum | solution.py:201
  1141.6 11.8 copy-start.10
  1141.6 11.8 copy-start.35
  1149.9 4.2 copy-start.33
  1150.0 5.0 copy-start.1
  1150.0 5.0 copy-start.30
  1155.4 3.8 copy-start.24
  1162.9 3.3 copy-start.21
  1180.7 452.3 %copy-start.37 = (f32[1023]{0:T(1024)S(1)}, f32[1023]{0:T(1024)}, u32[]{:S(2)}) copy-start(f32[1023]{0:T(1024)} %slice.201) | copy-start | bytes 12280
  1180.7 452.4 %copy-start.36 = (f32[1022]{0:T(1024)S(1)}, f32[1022]{0:T(1024)}, u32[]{:S(2)}) copy-start(f32[1022]{0:T(1024)} %slice.204) | copy-start | bytes 12268
  1180.7 452.6 %copy-start.25 = (f32[1024]{0:T(1024)S(1)}, f32[1024]{0:T(1024)}, u32[]{:S(2)}) copy-start(f32[1024]{0:T(1024)} %fusion.83) | copy-start | bytes 12292
  1631.8 18.2 %copy-start.3 = (bf16[1,128,512]{2,1,0:T(8,128)(2,1)S(1)}, bf16[1,128,512]{2,1,0:T(8,128)(2,1)}, u32[]{:S(2)}) copy-start(bf16[1,128,512]{2,1,0:T(8,128)(2,1)} %param.22) | copy-start | bytes 393220
  1631.8 18.2 %copy-start.31 = (f32[512]{0:T(512)S(1)}, f32[512]{0:T(512)}, u32[]{:S(2)}) copy-start(f32[512]{0:T(512)} %param.25) | copy-start | bytes 6148
  1631.8 18.2 %copy-start.42 = (f32[128]{0:T(128)S(1)}, f32[128]{0:T(128)}, u32[]{:S(2)}) copy-start(f32[128]{0:T(128)} %copy-done.41) | copy-start | bytes 1540
  1631.8 19.3 %copy-start.43 = (bf16[512]{0:T(512)(128)(2,1)S(1)}, bf16[512]{0:T(512)(128)(2,1)}, u32[]{:S(2)}) copy-start(bf16[512]{0:T(512)(128)(2,1)} %get-tuple-element.763) | copy-start | bytes 3076
  1631.8 44.3 %copy-start.47 = (f32[128]{0:T(128)S(1)}, f32[128]{0:T(128)}, u32[]{:S(2)}) copy-start(f32[128]{0:T(128)} %copy-done.46) | copy-start | bytes 1540
  1631.8 44.3 %copy-start.27 = (f32[512]{0:T(512)S(1)}, f32[512]{0:T(512)}, u32[]{:S(2)}) copy-start(f32[512]{0:T(512)} %param.27) | copy-start | bytes 6148
  1631.8 44.3 %copy-start.40 = (f32[128]{0:T(128)S(1)}, f32[128]{0:T(128)}, u32[]{:S(2)}) copy-start(f32[128]{0:T(128)} %copy-done.39) | copy-start | bytes 1540
  1631.8 44.3 %copy-start.45 = (f32[128]{0:T(128)S(1)}, f32[128]{0:T(128)}, u32[]{:S(2)}) copy-start(f32[128]{0:T(128)} %copy-done.44) | copy-start | bytes 1540
  1635.1 11.4 all-to-all-start.1
  1678.2 5.8 copy-start.20
  1678.2 6.6 copy-start.19
  1678.2 7.4 copy-start.18
  (11 other events, 25.5 us)
Sparse Core Ops, SparseCore 0:
  530.5 61.6 reduce-scatter.4
  604.8 39.2 all-gather.1
  648.0 66.8 reduce-scatter.6
  718.7 67.1 reduce-scatter.8
  789.7 66.8 reduce-scatter.10
  1180.0 84.2 all-reduce.14
where the time goes:
time: 1710 us; the launch traced here: 1690 us
  local copies, waits for them, and re-layouts  1340 us (78%)
  matrix products  154 us (9%)
  waiting for transfers between devices  95.3 us (6%)
  other arithmetic  50.1 us (3%)
  blocking collectives  23.9 us (1%)
    reshape x9, local copies, waits for them, and re-layouts, toeplitz_block(): tiled.reshape(filter_count, block_rows, 2 * block_rows - 1)  614 us
    while x33, local copies, waits for them, and re-layouts  418 us
    slice x9, local copies, waits for them, and re-layouts, toeplitz_block(): jnp.tile(skewed, (1, block_rows))[:, :block_rows * (2 * block_rows - 1)]  184 us
    dot_general x6, matrix products, add_source(): jnp.einsum('cs,kts->ckt', source, toeplitz, preferred_element_type=jnp.fl...  79.8 us
    reduce_scatter x1, waiting for transfers between devices, shards(): lax.psum_scatter(jnp.dot(filtered, flat_mixing, preferred_element_type=jn...  61.7 us
  transfers between devices with their start and end apart: 8, of which 4 were waited for; matrix products, arithmetic and copies ran while one was open for 60% of the time, Pallas kernels for 0%

commit v1 on v0

v1 whole, which is shorter than its diff:
```python
import functools

import jax
import jax.numpy as jnp
from jax import lax
from jax.experimental import pallas as pl
from jax.experimental.pallas import tpu as pltpu
from jax.sharding import PartitionSpec as P

K = 24
AR = 3
TILE = 256
HALF = 128
PER_STEP = 4

eps_norm = 1e-05


def rms_scale(values, scales):
    return values * lax.rsqrt(jnp.mean(values * values, axis=-1, keepdims=True) + eps_norm) * scales


def gelu_product(gate_value, upper_value):
    return jax.nn.gelu(gate_value, approximate=True) * upper_value


def contract_first(left, right):
    return lax.dot_general(
        left, right, (((0,), (0,)), ((), ())), preferred_element_type=jnp.float32
    )


def contract_last(left, right):
    return lax.dot_general(
        left, right, (((1,), (1,)), ((), ())), preferred_element_type=jnp.float32
    )


def tile_pairs(length):
    blocks, reach = length // TILE, length // 2 // TILE
    return [(tb, sb) for tb in range(blocks) for sb in range(max(0, tb - reach), tb + 1)]


def parity_lanes(rows, lanes, dtype=jnp.float32):
    lane = lax.broadcasted_iota(jnp.int32, (rows, lanes), 1)
    return (1 - 2 * (lane % 2)).astype(dtype)


def build_masks(seg_row, seg_col, masks, length):
    for index, (tb, sb) in enumerate(tile_pairs(length)):
        targets = seg_row[:, tb * TILE : (tb + 1) * TILE]
        sources = seg_col[sb * TILE : (sb + 1) * TILE, :]
        same = sources == targets
        if tb == sb:
            row = lax.broadcasted_iota(jnp.int32, (TILE, TILE), 0)
            col = lax.broadcasted_iota(jnp.int32, (TILE, TILE), 1)
            same = same & (col >= row)
        masks[index] = jnp.where(same, 1.0, 0.0).astype(jnp.bfloat16)


def build_slab(filter_row, slab, width):
    wide = jnp.broadcast_to(filter_row.astype(jnp.float32), (HALF, width))
    rolled = pltpu.roll(wide, 0, 1, stride=1, stride_axis=0).astype(jnp.bfloat16)
    slab[:HALF, :] = rolled
    slab[HALF:, HALF:] = rolled[:, : width - HALF]
    slab[HALF:, :HALF] = rolled[:, :HALF]


def spectral_kernel(length, width, filters, doubled, seg_row, seg_col, maps, slabs, masks):
    channels = maps.shape[2]
    pairs = tile_pairs(length)

    @pl.when(pl.program_id(0) == 0)
    def _():
        build_masks(seg_row, seg_col, masks, length)

    parity = parity_lanes(channels, TILE)
    for k in range(PER_STEP):
        slab = slabs.at[k]
        build_slab(filters[k], slab, width)
        for tb in range(length // TILE):
            chosen = [(i, sb) for i, (t, sb) in enumerate(pairs) if t == tb]
            tiles = [
                slab[:, (tb - sb) * TILE : (tb - sb + 1) * TILE] * masks[i] for i, sb in chosen
            ]
            first = chosen[0][1]
            both = jnp.dot(
                doubled[:, first * TILE : (tb + 1) * TILE],
                jnp.concatenate(tiles, axis=0),
                preferred_element_type=jnp.float32,
            )
            maps[0, k, :, tb * TILE : (tb + 1) * TILE] = both[:channels].astype(jnp.bfloat16)
            maps[1, k, :, tb * TILE : (tb + 1) * TILE] = (both[channels:] * parity).astype(
                jnp.bfloat16
            )


def spectral_back_kernel(length, width, filters, grads, seg_row, seg_col, out, slabs, masks, acc):
    channels = grads.shape[2]
    pairs = tile_pairs(length)

    @pl.when(pl.program_id(0) == 0)
    def _():
        build_masks(seg_row, seg_col, masks, length)
        acc[...] = jnp.zeros_like(acc)

    parity = parity_lanes(channels, length, jnp.bfloat16)
    for k in range(PER_STEP):
        slab = slabs.at[k]
        build_slab(filters[k], slab, width)
        both = jnp.concatenate([grads[0, k], grads[1, k] * parity], axis=0)
        for sb in range(length // TILE):
            chosen = [(i, tb) for i, (tb, s) in enumerate(pairs) if s == sb]
            tiles = [
                slab[:, (tb - sb) * TILE : (tb - sb + 1) * TILE] * masks[i] for i, tb in chosen
            ]
            last = chosen[-1][1]
            acc[:, sb * TILE : (sb + 1) * TILE] += contract_last(
                both[:, sb * TILE : (last + 1) * TILE], jnp.concatenate(tiles, axis=1)
            )

    @pl.when(pl.program_id(0) == pl.num_programs(0) - 1)
    def _():
        out[...] = acc[:channels] + parity.astype(jnp.float32) * acc[channels:]


def slab_width(length):
    return length // 2 + TILE


def common_specs(filters, segment_ids):
    length = filters.shape[1]
    width = slab_width(length)
    specs = [
        pl.BlockSpec((PER_STEP, 1, width), lambda k: (k, 0, 0)),
    ]
    masks = pltpu.VMEM((len(tile_pairs(length)), TILE, TILE), jnp.bfloat16)
    slabs = pltpu.VMEM((PER_STEP, TILE, width), jnp.bfloat16)
    segs = [
        pl.BlockSpec((1, length), lambda k: (0, 0)),
        pl.BlockSpec((length, 1), lambda k: (0, 0)),
    ]
    return length, width, specs, segs, slabs, masks


def spectral_maps(doubled, filters, segment_ids):
    length, width, specs, segs, slabs, masks = common_specs(filters, segment_ids)
    channels = doubled.shape[0] // 2
    count = filters.shape[0]
    return pl.pallas_call(
        functools.partial(spectral_kernel, length, width),
        grid=(count // PER_STEP,),
        in_specs=[*specs, pl.BlockSpec((2 * channels, length), lambda k: (0, 0)), *segs],
        out_specs=pl.BlockSpec((2, PER_STEP, channels, length), lambda k: (0, k, 0, 0)),
        out_shape=jax.ShapeDtypeStruct((2, count, channels, length), jnp.bfloat16),
        scratch_shapes=[slabs, masks],
        compiler_params=pltpu.CompilerParams(vmem_limit_bytes=40 << 20),
        name="spectral_maps",
    )(filters[:, None, :], doubled, segment_ids[None, :], segment_ids[:, None])


def spectral_back(grads, filters, segment_ids):
    length, width, specs, segs, slabs, masks = common_specs(filters, segment_ids)
    channels = grads.shape[2]
    count = filters.shape[0]
    return pl.pallas_call(
        functools.partial(spectral_back_kernel, length, width),
        grid=(count // PER_STEP,),
        in_specs=[
            *specs,
            pl.BlockSpec((2, PER_STEP, channels, length), lambda k: (0, k, 0, 0)),
            *segs,
        ],
        out_specs=pl.BlockSpec((channels, length), lambda k: (0, 0)),
        out_shape=jax.ShapeDtypeStruct((channels, length), jnp.float32),
        scratch_shapes=[slabs, masks, pltpu.VMEM((2 * channels, length), jnp.float32)],
        compiler_params=pltpu.CompilerParams(vmem_limit_bytes=40 << 20),
        name="spectral_back",
    )(filters[:, None, :], grads, segment_ids[None, :], segment_ids[:, None])


def same_mask(segment_ids, offset):
    length = segment_ids.shape[0]
    before = jnp.concatenate([jnp.full((offset,), -1, jnp.int32), segment_ids[: length - offset]])
    return before == segment_ids


def swap(values, axis, mask):
    count = lax.axis_size(axis)
    return lax.ppermute(values, axis, [(i, i ^ mask) for i in range(count)])


def bits_of(axis):
    return [1 << b for b in range(lax.axis_size(axis).bit_length() - 1)]


def join(mine, other, high, dim):
    return jnp.where(
        high, jnp.concatenate([other, mine], dim), jnp.concatenate([mine, other], dim)
    )


def doubled_gather(values, order):
    me = lax.axis_index("chan")
    held = values[None]
    sizes = []
    for mask in order:
        held = join(held[None], swap(held, "chan", mask)[None], (me & mask) != 0, 0)
        held = held.reshape(-1, *values.shape)
        sizes.insert(0, mask)
    bits = len(order)
    split = held.reshape(*([2] * bits), *values.shape)
    place = [sizes.index(m) for m in sorted(order, reverse=True)]
    split = jnp.transpose(split, place + list(range(bits, split.ndim)))
    return split.reshape(-1, *values.shape)


def gather_tokens(values):
    masks = bits_of("chan")
    half = values.shape[0] // 2
    first = doubled_gather(values[:half], masks[::-1])
    second = doubled_gather(values[half:], masks[:1] + masks[:0:-1])
    return jnp.concatenate([first, second], axis=1).reshape(-1, values.shape[1])


def halved_sum(values, order):
    me = lax.axis_index("chan")
    masks = bits_of("chan")[::-1]
    held = values.reshape(*([2] * len(masks)), *values.shape[1:])
    for mask in order:
        dim, bit = masks.index(mask), (me & mask) // mask
        keep = lax.dynamic_slice_in_dim(held, bit, 1, dim)
        give = lax.dynamic_slice_in_dim(held, 1 - bit, 1, dim)
        got = swap(give, "chan", mask)
        held = keep.astype(jnp.float32) + got.astype(jnp.float32)
        if mask != order[-1]:
            held = held.astype(jnp.bfloat16)
    return held.reshape(values.shape[1:])


def scatter_tokens(values):
    count = lax.axis_size("chan")
    masks = bits_of("chan")
    pieces = values.reshape(count, -1, values.shape[1])
    half = values.shape[1] // 2
    return jnp.concatenate(
        [
            halved_sum(pieces[..., :half], masks[:1] + masks[1:]),
            halved_sum(pieces[..., half:], masks[1:] + masks[:1]),
        ],
        axis=1,
    )


def sum_rows(values):
    me = lax.axis_index("rows")
    masks = bits_of("rows")
    half = values.shape[0] // 2
    high = (me & 1) != 0
    keep = lax.dynamic_slice_in_dim(values, (me & 1) * half, half, 0)
    give = lax.dynamic_slice_in_dim(values, (1 - (me & 1)) * half, half, 0)
    held = keep.astype(jnp.float32) + swap(give, "rows", 1).astype(jnp.float32)
    for mask in masks[1:]:
        held = held.astype(jnp.bfloat16)
        held = held.astype(jnp.float32) + swap(held, "rows", mask).astype(jnp.float32)
    held = held.astype(jnp.bfloat16)
    return join(held, swap(held, "rows", 1), high, 0)


def sum_rows_small(values):
    for mask in bits_of("rows"):
        values = values + swap(values, "rows", mask)
    return values


def shards(
    hidden_in, segments, filters, gain_one, mixing, gain_two, w_gate, w_up, w_down, out_grad
):
    chans = lax.axis_size("chan")
    me = lax.axis_index("chan")
    tokens = hidden_in[0].astype(jnp.float32)
    cotangent = out_grad[0]
    normed_one = rms_scale(tokens, gain_one).astype(jnp.bfloat16)
    share, width = normed_one.shape
    inputs = lax.all_to_all(
        normed_one.T.reshape(chans, width // chans, share), "chan", split_axis=0, concat_axis=0
    )
    inputs = jnp.swapaxes(inputs, 0, 1).reshape(width // chans, -1)
    segment_ids = segments[0]
    channels, length = inputs.shape
    model_width = mixing.shape[2]
    flat_mixing = mixing.reshape(-1, model_width)
    spectral_rows = 2 * K * channels
    parity = (1 - 2 * (lax.iota(jnp.int32, length) % 2)).astype(jnp.bfloat16)
    doubled = jnp.concatenate([inputs, inputs * parity], axis=0)
    maps = spectral_maps(doubled, filters, segment_ids).reshape(spectral_rows, length)
    lags = jnp.concatenate(
        [
            jnp.concatenate(
                [jnp.zeros((channels, j), jnp.bfloat16), inputs[:, : length - j]], axis=1
            )
            * same_mask(segment_ids, j).astype(jnp.bfloat16)
            for j in range(AR)
        ],
        axis=0,
    )
    mixed = contract_first(maps, flat_mixing[:spectral_rows]) + contract_first(
        lags, flat_mixing[spectral_rows:]
    )
    mixed = scatter_tokens(mixed.astype(jnp.bfloat16))
    resid = tokens + mixed
    normed_two = rms_scale(resid, gain_two).astype(jnp.bfloat16)
    gate_value = jnp.dot(normed_two, w_gate, preferred_element_type=jnp.float32)
    upper_value = jnp.dot(normed_two, w_up, preferred_element_type=jnp.float32)
    hidden = gelu_product(gate_value, upper_value).astype(jnp.bfloat16)
    output = (resid + jnp.dot(hidden, w_down, preferred_element_type=jnp.float32)).astype(
        jnp.bfloat16
    )
    hidden_grad = contract_last(cotangent, w_down)
    _, gelu_pull = jax.vjp(gelu_product, gate_value, upper_value)
    gate_float, upper_float = gelu_pull(hidden_grad)
    normed_grad = contract_last(gate_float.astype(jnp.bfloat16), w_gate) + contract_last(
        upper_float.astype(jnp.bfloat16), w_up
    )
    _, second_pull = jax.vjp(rms_scale, resid, gain_two)
    resid_part, second_local = second_pull(normed_grad)
    resid_grad = cotangent.astype(jnp.float32) + resid_part
    full_grad = gather_tokens(resid_grad.astype(jnp.bfloat16))
    all_normed = gather_tokens(normed_two)
    all_cotangent = gather_tokens(cotangent)
    units = w_gate.shape[1] // chans
    gate_part = lax.dynamic_slice_in_dim(w_gate, me * units, units, 1)
    up_part = lax.dynamic_slice_in_dim(w_up, me * units, units, 1)
    down_part = lax.dynamic_slice_in_dim(w_down, me * units, units, 0)
    gate_units = jnp.dot(all_normed, gate_part, preferred_element_type=jnp.float32)
    upper_units = jnp.dot(all_normed, up_part, preferred_element_type=jnp.float32)
    product, unit_pull = jax.vjp(gelu_product, gate_units, upper_units)
    gate_back, upper_back = unit_pull(contract_last(all_cotangent, down_part))
    gate_local = contract_first(all_normed, gate_back.astype(jnp.bfloat16))
    up_local = contract_first(all_normed, upper_back.astype(jnp.bfloat16))
    down_local = contract_first(product.astype(jnp.bfloat16), all_cotangent)
    ff_sum = sum_rows(
        jnp.concatenate(
            [gate_local.astype(jnp.bfloat16), up_local.astype(jnp.bfloat16)], axis=1
        )
    ).astype(jnp.float32)
    down_sum = sum_rows(down_local.astype(jnp.bfloat16)).astype(jnp.float32)

    spectral_grad = contract_last(flat_mixing[:spectral_rows], full_grad).astype(jnp.bfloat16)
    lag_grad = contract_last(flat_mixing[spectral_rows:], full_grad)
    input_back = spectral_back(
        spectral_grad.reshape(2, K, channels, length), filters, segment_ids
    )
    for j in range(AR):
        lag_term = lag_grad[j * channels : (j + 1) * channels]
        lag_term = lag_term * same_mask(segment_ids, j).astype(jnp.float32)
        input_back = input_back + jnp.concatenate(
            [lag_term[:, j:], jnp.zeros((channels, j), jnp.float32)], axis=1
        )
    back = input_back.astype(jnp.bfloat16)
    token_grad = lax.all_to_all(
        jnp.swapaxes(back.reshape(channels, chans, share), 0, 1),
        "chan",
        split_axis=0,
        concat_axis=0,
    ).reshape(width, share).T
    mixing_local = jnp.concatenate(
        [
            jnp.dot(maps, full_grad, preferred_element_type=jnp.float32).astype(jnp.bfloat16),
            jnp.dot(lags, full_grad, preferred_element_type=jnp.float32).astype(jnp.bfloat16),
        ],
        axis=0,
    )
    mixing_sum = sum_rows(mixing_local).astype(jnp.float32).reshape(mixing.shape)
    first_local = jnp.sum(back.astype(jnp.float32) * inputs.astype(jnp.float32), axis=1)
    first_local = first_local / lax.dynamic_slice_in_dim(gain_one, me * channels, channels, 0)
    second_pieces = lax.all_to_all(
        second_local.reshape(chans, 1, channels), "chan", split_axis=0, concat_axis=0
    )
    gains = sum_rows_small(jnp.stack([first_local, jnp.sum(second_pieces, axis=(0, 1))]))
    _, first_pull = jax.vjp(rms_scale, tokens, gain_one)
    tokens_part, _ = first_pull(token_grad.astype(jnp.float32))
    input_total = resid_grad + tokens_part
    return (
        output[None],
        input_total[None],
        mixing_sum,
        ff_sum[:, :units],
        ff_sum[:, units:],
        down_sum,
        gains[0],
        gains[1],
    )


def solution(mesh):
    in_specs = (
        P("rows", "chan", None),
        P("rows", None),
        P(),
        P(),
        P(None, "chan", None),
        P(),
        P(),
        P(),
        P(),
        P("rows", "chan", None),
    )
    out_specs = (
        P("rows", "chan", None),
        P("rows", "chan", None),
        P(None, "chan", None),
        P(None, "chan"),
        P(None, "chan"),
        P("chan", None),
        P("chan"),
        P("chan"),
    )
    return jax.shard_map(shards, mesh=mesh, in_specs=in_specs, out_specs=out_specs, check_vma=False)
```

time: 1710 us -> 235 us (0.14)
  local copies, waits for them, and re-layouts: 1340 us -> 33.1 us
  matrix products: 154 us -> 28.1 us
  starting transfers between devices: 11.5 us -> 54.4 us
  waiting for transfers between devices: 95.3 us -> 56.4 us
  blocking collectives: 23.9 us -> 0 us
  Pallas kernels: 0 us -> 18.7 us
    reshape x9 -> x2, local copies, waits for them, and re-layouts: 614 us -> 0.69 us  [the longest x1 0.67 us: shards(): second_local.reshape(chans, 1, channels)]
    while x33 -> x0, local copies, waits for them, and re-layouts: 418 us -> none
    slice x42 -> x8, local copies, waits for them, and re-layouts: 207 us -> 6.78 us  [the longest x1 3.97 us: shards(): flat_mixing[:spectral_rows]]
    dot_general x10 -> x4, matrix products: 111 us -> 6.28 us  [the longest x1 3.61 us: shards(): jnp.dot(maps, full_grad, preferred_element_type=jnp.float32)]
    reduce_scatter x4 -> x0, waiting for transfers between devices: 61.8 us -> none  [the longest x1 61.7 us: shards(): lax.psum_scatter(jnp.dot(filtered, flat_mixing, preferred_element_type=jn...]
    another operation x17 -> x1, local copies, waits for them, and re-layouts: 57.3 us -> 0.22 us  [spectral_maps(): segment_ids[:, None]]
    ppermute x0 -> x35, waiting for transfers between devices: none -> 55.6 us  [swap(): return lax.ppermute(values, axis, [(i, i ^ mask) for i in range(count)])]
    ppermute x0 -> x35, starting transfers between devices: none -> 37.7 us  [swap(): return lax.ppermute(values, axis, [(i, i ^ mask) for i in range(count)])]
  transfers between devices with their start and end apart: 8 -> 38, of which waited for: 4 -> 13; matrix products, arithmetic and copies ran while one was open for 60% -> 29% of each run, Pallas kernels for 0% -> 8%
where the time goes in v1:
time: 235 us; the launch traced here: 233 us
  waiting for transfers between devices  56.4 us (24%)
  starting transfers between devices  54.4 us (23%)
  other arithmetic  40.6 us (17%)
  local copies, waits for them, and re-layouts  33.1 us (14%)
  matrix products  28.1 us (12%)
  Pallas kernels  18.7 us (8%)
    ppermute x35, waiting for transfers between devices, swap(): return lax.ppermute(values, axis, [(i, i ^ mask) for i in range(count)])  55.6 us
    ppermute x35, starting transfers between devices, swap(): return lax.ppermute(values, axis, [(i, i ^ mask) for i in range(count)])  37.7 us
    dot_general x6, matrix products, contract_last(): lax.dot_general(left, right, (((1,), (1,)), ((), ())), preferred_element_...  13.4 us
    unnamed x126, local copies, waits for them, and re-layouts  12.8 us
    select_n x25, other arithmetic, join(): jnp.where(high, jnp.concatenate([other, mine], dim), jnp.concatenate([min...  12.1 us
    pallas_call x1, Pallas kernels, spectral_back(): pl.pallas_call(functools.partial(spectral_back_kernel, length, width), gr...  11.8 us
    convert_element_type x6, other arithmetic, sum_rows(): held = held.astype(jnp.bfloat16)  9.03 us
    convert_element_type x1, local copies, waits for them, and re-layouts, shards(): contract_last(flat_mixing[:spectral_rows], full_grad).astype(jnp.bfloat16)  8.62 us
  transfers between devices with their start and end apart: 38, of which 13 were waited for; matrix products, arithmetic and copies ran while one was open for 29% of the time, Pallas kernels for 8%

profile of v1, /device:TPU:0, one launch (start us, length us, event | category | flops | bytes accessed | tf_op | source)
XLA Modules:
  0.0 233.3 jit_solution(2273547341644256728)
XLA Ops:
  0.6 1.2 fusion.31
  4.6 7.3 %all-to-all-start = ((bf16[8,64,128]{2,1,0:T(8,128)(2,1)}), bf16[8,64,128]{2,1,0:T(8,128)(2,1)S(1)}, u32[]{:S(2)}, u32[]{:S(2)}) async-start(bf16[8,64,128]{2,1,0:T(8,128)(2,1)} %bitcast.4), calls=%async_computation | async-start | bytes 262144 | tf_op jit(solution)/shard_map/all_to_all | solution.py:285
  11.9 1.5 fusion.100
  13.4 2.9 %collective-permute-start.21 = (bf16[1,64,512]{2,1,0:T(8,128)(2,1)S(1)}, bf16[1,64,512]{2,1,0:T(8,128)(2,1)S(1)}, u32[]{:S(2)}, u32[]{:S(2)}) collective-permute-start(bf16[1,64,512]{2,1,0:T(8,128)(2,1)S(1)} %get-tuple-element.56), channel_id=1, source_target_pairs={{0,4},{1,5},{2,6},{3,7},{4,0},{5,1},{6,2},{7,3},{8,12},{9,13},{10,... | collective-permute-start | bytes 196616 | tf_op jit(solution)/shard_map/ppermute | solution.py:190
  16.3 1.5 collective-permute-start.24
  18.8 4.0 %slice.85 = bf16[48,64,512]{2,1,0:T(8,128)(2,1)} slice(bf16[51,64,512]{2,1,0:T(8,128)(2,1)} %param.14), slice={[0:48], [0:64], [0:512]} | slice | bytes 6291456 | tf_op jit(solution)/shard_map/slice | solution.py:307
  23.4 3.4 %fusion.48 = f32[128,2048]{1,0:T(8,128)} fusion(bf16[2048,512]{1,0:T(8,128)(2,1)} %param.18, bf16[1,128,512]{2,1,0:T(8,128)(2,1)S(1)} %copy-done.22), kind=kOutput, calls=%fused_computation.141 | convolution fusion | flops 268435456 | bytes 3276800 | tf_op jit(solution)/shard_map/dot_general | solution.py:34
  28.5 1.5 collective-permute-start.22
  30.0 4.9 %collective-permute-done.22 = bf16[2,64,512]{2,1,0:T(8,128)(2,1)S(1)} collective-permute-done((bf16[2,64,512]{2,1,0:T(8,128)(2,1)S(1)}, bf16[2,64,512]{2,1,0:T(8,128)(2,1)S(1)}, u32[]{:S(2)}, u32[]{:S(2)}) %collective-permute-start.22) | collective-permute-done | bytes 131104 | tf_op jit(solution)/shard_map/ppermute | solution.py:190
  38.8 6.9 %spectral_maps.1 = bf16[2,24,64,1024]{3,2,1,0:T(8,128)(2,1)S(1)} custom-call(bf16[24,1,1024]{2,1,0:T(2,128)(2,1)S(1)} %copy.59.filters, bf16[128,1024]{1,0:T(8,128)(2,1)S(1)} %pad_maximum_fusion.4.doubled, s32[1,1024]{1,0:T(1,128)S(1)} %copy-done.4, s32[1024,1]{1,0:T(8,128)S(1)} %copy.60.seg_col), custom_call_target="tpu_custom_call" | custom-call | tf_op jit(solution)/shard_map/spectral_maps/pallas_call | solution.py:150
  45.8 3.4 %fusion.101 = f32[1024,512]{1,0:T(8,128)S(1)} fusion(bf16[3072,1024]{1,0:T(8,128)(2,1)S(1)} %bitcast.194, bf16[3072,512]{1,0:T(8,128)(2,1)S(1)} %bitcast.216), kind=kOutput, calls=%fused_computation.228 | convolution fusion | flops 3221225472 | bytes 11534336 | tf_op jit(solution)/shard_map/dot_general | solution.py:28
  50.2 1.6 collective-permute-start
  51.9 1.7 collective-permute-start.3
  54.8 1.3 fusion.23
  56.5 1.5 fusion.45
  58.5 2.6 %collective-permute-done.3 = bf16[2,1,2,128,256]{4,3,2,1,0:T(8,128)(2,1)S(1)} collective-permute-done((bf16[2,1,2,128,256]{4,3,2,1,0:T(8,128)(2,1)S(1)}, bf16[2,1,2,128,256]{4,3,2,1,0:T(8,128)(2,1)S(1)}, u32[]{:S(2)}, u32[]{:S(2)}) %collective-permute-start.3) | collective-permute-done | bytes 262176 | tf_op jit(solution)/shard_map/ppermute | solution.py:190
  61.2 2.0 collective-permute-start.4
  63.3 3.6 %collective-permute-start.2 = (bf16[1,1,1,128,256]{4,3,2,1,0:T(8,128)(2,1)S(1)}, bf16[1,1,1,128,256]{4,3,2,1,0:T(8,128)(2,1)S(1)}, u32[]{:S(2)}, u32[]{:S(2)}) collective-permute-start(bf16[1,1,1,128,256]{4,3,2,1,0:T(8,128)(2,1)S(1)} %constant_dynamic-slice_fusion.4), channel_id=1, source_target_pairs={{0,4},{1,5},{2,6},{3,7},{4,0},{5,1},{6,2},{7,3},{8,12},{9,13},{10,... | collective-permute-start | bytes 196616 | tf_op jit(solution)/shard_map/ppermute | solution.py:190
  67.0 1.7 collective-permute-done.4
  69.4 3.7 %collective-permute-done.5 = bf16[1,1,1,128,256]{4,3,2,1,0:T(8,128)(2,1)S(1)} collective-permute-done((bf16[1,1,1,128,256]{4,3,2,1,0:T(8,128)(2,1)S(1)}, bf16[1,1,1,128,256]{4,3,2,1,0:T(8,128)(2,1)S(1)}, u32[]{:S(2)}, u32[]{:S(2)}) %collective-permute-start.5) | collective-permute-done | bytes 65568 | tf_op jit(solution)/shard_map/ppermute | solution.py:190
  76.2 1.3 fusion.3
  78.7 1.6 multiply_reduce_fusion
  81.0 4.8 %all-to-all-start.2 = ((f32[8,1,64]{2,1,0:T(1,128)}), f32[8,1,64]{2,1,0:T(1,128)S(1)}, u32[]{:S(2)}, u32[]{:S(2)}) async-start(f32[8,1,64]{2,1,0:T(1,128)} %reshape.1046), calls=%async_computation.2 | async-start | bytes 8192 | tf_op jit(solution)/shard_map/all_to_all | solution.py:377
  86.9 3.0 %collective-permute-start.6 = (bf16[1,64,512]{2,1,0:T(8,128)(2,1)S(1)}, bf16[1,64,512]{2,1,0:T(8,128)(2,1)S(1)}, u32[]{:S(2)}, u32[]{:S(2)}) collective-permute-start(bf16[1,64,512]{2,1,0:T(8,128)(2,1)S(1)} %get-tuple-element.64), channel_id=1, source_target_pairs={{0,4},{1,5},{2,6},{3,7},{4,0},{5,1},{6,2},{7,3},{8,12},{9,13},{10,... | collective-permute-start | bytes 196616 | tf_op jit(solution)/shard_map/ppermute | solution.py:190
  89.9 1.5 collective-permute-start.9
  99.1 2.3 collective-permute-start.16
  104.1 1.5 collective-permute-start.7
  105.6 1.2 collective-permute-done.16
  108.8 2.5 %collective-permute-done.7 = bf16[2,64,512]{2,1,0:T(8,128)(2,1)S(1)} collective-permute-done((bf16[2,64,512]{2,1,0:T(8,128)(2,1)S(1)}, bf16[2,64,512]{2,1,0:T(8,128)(2,1)S(1)}, u32[]{:S(2)}, u32[]{:S(2)}) %collective-permute-start.7) | collective-permute-done | bytes 131104 | tf_op jit(solution)/shard_map/ppermute | solution.py:190
  112.1 1.6 collective-permute-start.11
  115.3 1.8 fusion.41
  119.6 3.6 %convolution_convert_fusion = bf16[3072,512]{1,0:T(8,128)(2,1)S(1)} fusion(bf16[3072,1024]{1,0:T(8,128)(2,1)S(1)} %bitcast.197, bf16[1024,512]{1,0:T(8,128)(2,1)S(1)} %bitcast.210), kind=kOutput, calls=%fused_computation.3 | convolution fusion | flops 3222798336 | bytes 10485760 | tf_op jit(solution)/shard_map/dot_general | solution.py:369
  124.2 2.2 copy-done.16
  126.4 5.3 %convert_bitcast_fusion = bf16[3072,1024]{0,1:T(8,128)(2,1)} fusion(bf16[1024,512]{1,0:T(8,128)(2,1)S(1)} %bitcast.213, bf16[3072,512]{1,0:T(8,128)(2,1)S(1)} %bitcast.217), kind=kOutput, calls=%fused_computation | convolution fusion | flops 3224371200 | bytes 10485760 | tf_op jit(solution)/shard_map/dot_general | solution.py:34
  133.1 2.9 %fusion = bf16[1632,512]{1,0:T(8,128)(2,1)} fusion(s32[]{:T(128)S(6)} %select_n.409, bf16[3072,512]{1,0:T(8,128)(2,1)S(1)} %convolution_convert_fusion, bf16[192,512]{1,0:T(8,128)(2,1)S(1)} %convolution_convert_fusion.4), kind=kLoop, calls=%fused_computation.10 | loop fusion | flops 3342336 | bytes 5013508 | tf_op jit(solution)/shard_map/concatenate | solution.py:367
  136.5 8.6 %copy.63 = bf16[3072,1024]{1,0:T(8,128)(2,1)} copy(bf16[3072,1024]{0,1:T(8,128)(2,1)} %convert_bitcast_fusion) | data formatting | bytes 12582912 | tf_op jit(solution)/shard_map/convert_element_type | solution.py:349
  145.2 2.8 %copy-done.2 = bf16[3072,1024]{1,0:T(8,128)(2,1)S(1)} copy-done((bf16[3072,1024]{1,0:T(8,128)(2,1)S(1)}, bf16[3072,1024]{1,0:T(8,128)(2,1)}, u32[]{:S(2)}) %copy-start.2) | copy-done | bytes 6291480
  148.0 11.8 %spectral_back.1 = f32[64,1024]{1,0:T(8,128)S(1)} custom-call(bf16[24,1,1024]{2,1,0:T(2,128)(2,1)S(1)} %copy.59.filters, bf16[2,24,64,1024]{3,2,1,0:T(8,128)(2,1)S(1)} %bitcast.193, s32[1,1024]{1,0:T(1,128)S(1)} %copy-done.4, s32[1024,1]{1,0:T(8,128)S(1)} %copy.60.seg_col), custom_call_target="tpu_custom_call" | custom-call | tf_op jit(solution)/shard_map/spectral_back/pallas_call | solution.py:166
  164.6 3.3 %add_convert_fusion.1 = bf16[1632,512]{1,0:T(8,128)(2,1)S(1)} fusion(bf16[1632,512]{1,0:T(8,128)(2,1)} %collective-permute-done.12, s32[]{:T(128)S(6)} %select_n.408, bf16[3072,512]{1,0:T(8,128)(2,1)S(1)} %copy-done.6, bf16[192,512]{1,0:T(8,128)(2,1)S(1)} %copy-done.41), kind=kLoop, calls=%fused_computation.6 | loop fusion | flops 5849088 | bytes 6684676 | tf_op jit(solution)/shard_map/convert_element_type | solution.py:264
  167.9 1.6 collective-permute-start.13
  172.1 4.7 %all-to-all-start.1 = ((bf16[8,64,128]{2,1,0:T(8,128)(2,1)}), bf16[8,64,128]{2,1,0:T(8,128)(2,1)S(1)}, u32[]{:S(2)}, u32[]{:S(2)}) async-start(bf16[8,64,128]{2,1,0:T(8,128)(2,1)} %bitcast_bitcast_fusion), calls=%async_computation.1 | async-start | bytes 262144 | tf_op jit(solution)/shard_map/all_to_all | solution.py:361
  176.7 29.8 %collective-permute-done.34 = f32[2,64]{1,0:T(2,128)S(1)} collective-permute-done((f32[2,64]{1,0:T(2,128)S(1)}, f32[2,64]{1,0:T(2,128)S(1)}, u32[]{:S(2)}, u32[]{:S(2)}) %collective-permute-start.34) | collective-permute-done | bytes 544 | tf_op jit(solution)/shard_map/ppermute | solution.py:190
  207.0 1.6 add_convert_fusion.8
  208.6 1.5 collective-permute-start.31
  211.0 2.0 add_convert_fusion
  216.1 6.9 %collective-permute-done.28 = bf16[256,512]{0,1:T(8,128)(2,1)S(1)} collective-permute-done((bf16[256,512]{0,1:T(8,128)(2,1)S(1)}, bf16[256,512]{0,1:T(8,128)(2,1)S(1)}, u32[]{:S(2)}, u32[]{:S(2)}) %collective-permute-start.28) | collective-permute-done | bytes 262176 | tf_op jit(solution)/shard_map/ppermute | solution.py:190
  227.2 2.4 %maximum_select_fusion = bf16[3264,512]{1,0:T(8,128)(2,1)S(1)} fusion(bf16[1632,512]{1,0:T(8,128)(2,1)S(1)} %add_convert_fusion, bf16[1632,512]{1,0:T(8,128)(2,1)} %collective-permute-done.14, pred[]{:T(512)S(6)} %ne.75), kind=kLoop, calls=%fused_computation.4 | loop fusion | flops 15040512 | bytes 6684673 | tf_op jit(solution)/shard_map/jit(_where)/select_n | solution.py:198
  229.5 3.8 %convert.7 = f32[51,64,512]{2,1,0:T(8,128)} convert(bf16[51,64,512]{2,1,0:T(8,128)(2,1)S(1)} %bitcast.202) | non-fusion elementwise | flops 1671168 | bytes 10027008 | tf_op jit(solution)/shard_map/convert_element_type | solution.py:374
  (292 shorter events, 55.6 us)
Async XLA Ops:
  0.6 75.1 %copy-start = (bf16[512,2048]{1,0:T(8,128)(2,1)S(1)}, bf16[512,2048]{1,0:T(8,128)(2,1)}, u32[]{:S(2)}) copy-start(bf16[512,2048]{1,0:T(8,128)(2,1)} %param.17) | copy-start | bytes 6291460
  4.6 34.1 %all-to-all-start = ((bf16[8,64,128]{2,1,0:T(8,128)(2,1)}), bf16[8,64,128]{2,1,0:T(8,128)(2,1)S(1)}, u32[]{:S(2)}, u32[]{:S(2)}) async-start(bf16[8,64,128]{2,1,0:T(8,128)(2,1)} %bitcast.4), calls=%async_computation | async-start | bytes 262144 | tf_op jit(solution)/shard_map/all_to_all | solution.py:285
  13.4 15.0 %collective-permute-start.21 = (bf16[1,64,512]{2,1,0:T(8,128)(2,1)S(1)}, bf16[1,64,512]{2,1,0:T(8,128)(2,1)S(1)}, u32[]{:S(2)}, u32[]{:S(2)}) collective-permute-start(bf16[1,64,512]{2,1,0:T(8,128)(2,1)S(1)} %get-tuple-element.56), channel_id=1, source_target_pairs={{0,4},{1,5},{2,6},{3,7},{4,0},{5,1},{6,2},{7,3},{8,12},{9,13},{10,... | collective-permute-start | bytes 196616 | tf_op jit(solution)/shard_map/ppermute | solution.py:190
  16.3 10.5 %collective-permute-start.24 = (bf16[1,64,512]{2,1,0:T(8,128)(2,1)}, bf16[1,64,512]{2,1,0:T(8,128)(2,1)S(1)}, u32[]{:S(2)}, u32[]{:S(2)}) collective-permute-start(bf16[1,64,512]{2,1,0:T(8,128)(2,1)} %get-tuple-element.59), channel_id=1, source_target_pairs={{0,1},{1,0},{2,3},{3,2},{4,5},{5,4},{6,7},{7,6},{8,9},{9,8},{10,11... | collective-permute-start | bytes 196616 | tf_op jit(solution)/shard_map/ppermute | solution.py:190
  18.7 30.7 %copy-start.27 = (bf16[3,64,512]{2,1,0:T(8,128)(2,1)}, bf16[3,64,512]{2,1,0:T(8,128)(2,1)S(1)}, u32[]{:S(2)}) copy-start(bf16[3,64,512]{2,1,0:T(8,128)(2,1)S(1)} %slice.92) | copy-start | bytes 589828
  27.8 8.1 %collective-permute-start.25 = (bf16[2,64,512]{2,1,0:T(8,128)(2,1)S(1)}, bf16[2,64,512]{2,1,0:T(8,128)(2,1)S(1)}, u32[]{:S(2)}, u32[]{:S(2)}) collective-permute-start(bf16[2,64,512]{2,1,0:T(8,128)(2,1)S(1)} %maximum_select_fusion.31), channel_id=1, source_target_pairs={{0,4},{1,5},{2,6},{3,7},{4,0},{5,1},{6,2},{7,3},{8,12},{9,13},{10,... | collective-permute-start | bytes 393224 | tf_op jit(solution)/shard_map/ppermute | solution.py:190
  28.5 6.5 %collective-permute-start.22 = (bf16[2,64,512]{2,1,0:T(8,128)(2,1)S(1)}, bf16[2,64,512]{2,1,0:T(8,128)(2,1)S(1)}, u32[]{:S(2)}, u32[]{:S(2)}) collective-permute-start(bf16[2,64,512]{2,1,0:T(8,128)(2,1)S(1)} %maximum_select_fusion.29), channel_id=1, source_target_pairs={{0,2},{1,3},{2,0},{3,1},{4,6},{5,7},{6,4},{7,5},{8,10},{9,11},{10,... | collective-permute-start | bytes 393224 | tf_op jit(solution)/shard_map/ppermute | solution.py:190
  35.7 17.9 %collective-permute-start.23 = (bf16[4,64,512]{2,1,0:T(8,128)(2,1)}, bf16[4,64,512]{2,1,0:T(8,128)(2,1)}, u32[]{:S(2)}, u32[]{:S(2)}) collective-permute-start(bf16[4,64,512]{2,1,0:T(8,128)(2,1)} %bitcast.73), channel_id=1, source_target_pairs={{0,1},{1,0},{2,3},{3,2},{4,5},{5,4},{6,7},{7,6},{8,9},{9,8},{10,11... | collective-permute-start | bytes 786440 | tf_op jit(solution)/shard_map/ppermute | solution.py:190
  36.6 18.2 %collective-permute-start.26 = (bf16[4,64,512]{2,1,0:T(8,128)(2,1)}, bf16[4,64,512]{2,1,0:T(8,128)(2,1)}, u32[]{:S(2)}, u32[]{:S(2)}) collective-permute-start(bf16[4,64,512]{2,1,0:T(8,128)(2,1)} %bitcast.82), channel_id=1, source_target_pairs={{0,2},{1,3},{2,0},{3,1},{4,6},{5,7},{6,4},{7,5},{8,10},{9,11},{10,... | collective-permute-start | bytes 786440 | tf_op jit(solution)/shard_map/ppermute | solution.py:190
  50.2 7.7 %collective-permute-start = (bf16[2,2,1,128,256]{4,3,2,1,0:T(8,128)(2,1)S(1)}, bf16[2,2,1,128,256]{4,3,2,1,0:T(8,128)(2,1)S(1)}, u32[]{:S(2)}, u32[]{:S(2)}) collective-permute-start(bf16[2,2,1,128,256]{4,3,2,1,0:T(8,128)(2,1)S(1)} %constant_dynamic-slice_fusion.6), channel_id=1, source_target_pairs={{0,1},{1,0},{2,3},{3,2},{4,5},{5,4},{6,7},{7,6},{8,9},{9,8},{10,11... | collective-permute-start | bytes 786440 | tf_op jit(solution)/shard_map/ppermute | solution.py:190
  51.9 9.2 %collective-permute-start.3 = (bf16[2,1,2,128,256]{4,3,2,1,0:T(8,128)(2,1)S(1)}, bf16[2,1,2,128,256]{4,3,2,1,0:T(8,128)(2,1)S(1)}, u32[]{:S(2)}, u32[]{:S(2)}) collective-permute-start(bf16[2,1,2,128,256]{4,3,2,1,0:T(8,128)(2,1)S(1)} %constant_dynamic-slice_fusion.3), channel_id=1, source_target_pairs={{0,2},{1,3},{2,0},{3,1},{4,6},{5,7},{6,4},{7,5},{8,10},{9,11},{10,... | collective-permute-start | bytes 786440 | tf_op jit(solution)/shard_map/ppermute | solution.py:190
  58.0 15.1 %copy-start.14 = (bf16[1,128,512]{2,1,0:T(8,128)(2,1)S(1)}, bf16[1,128,512]{2,1,0:T(8,128)(2,1)}, u32[]{:S(2)}) copy-start(bf16[1,128,512]{2,1,0:T(8,128)(2,1)} %param.10) | copy-start | bytes 393220
  58.0 15.3 %copy-start.51 = (f32[512]{0:T(512)S(1)}, f32[512]{0:T(512)}, u32[]{:S(2)}) copy-start(f32[512]{0:T(512)} %param.15) | copy-start | bytes 6148
  58.1 17.2 %copy-start.18 = (bf16[512,2048]{1,0:T(8,128)(2,1)S(1)}, bf16[512,2048]{1,0:T(8,128)(2,1)}, u32[]{:S(2)}) copy-start(bf16[512,2048]{1,0:T(8,128)(2,1)} %param.16) | copy-start | bytes 6291460
  58.1 5.1 %collective-permute-start.1 = (bf16[2,1,1,128,256]{4,3,2,1,0:T(8,128)(2,1)S(1)}, bf16[2,1,1,128,256]{4,3,2,1,0:T(8,128)(2,1)S(1)}, u32[]{:S(2)}, u32[]{:S(2)}) collective-permute-start(bf16[2,1,1,128,256]{4,3,2,1,0:T(8,128)(2,1)S(1)} %constant_dynamic-slice_fusion.5), channel_id=1, source_target_pairs={{0,2},{1,3},{2,0},{3,1},{4,6},{5,7},{6,4},{7,5},{8,10},{9,11},{10,... | collective-permute-start | bytes 393224 | tf_op jit(solution)/shard_map/ppermute | solution.py:190
  61.2 7.5 %collective-permute-start.4 = (bf16[1,1,2,128,256]{4,3,2,1,0:T(8,128)(2,1)S(1)}, bf16[1,1,2,128,256]{4,3,2,1,0:T(8,128)(2,1)S(1)}, u32[]{:S(2)}, u32[]{:S(2)}) collective-permute-start(bf16[1,1,2,128,256]{4,3,2,1,0:T(8,128)(2,1)S(1)} %constant_dynamic-slice_fusion.2), channel_id=1, source_target_pairs={{0,4},{1,5},{2,6},{3,7},{4,0},{5,1},{6,2},{7,3},{8,12},{9,13},{10,... | collective-permute-start | bytes 393224 | tf_op jit(solution)/shard_map/ppermute | solution.py:190
  63.3 6.1 %collective-permute-start.2 = (bf16[1,1,1,128,256]{4,3,2,1,0:T(8,128)(2,1)S(1)}, bf16[1,1,1,128,256]{4,3,2,1,0:T(8,128)(2,1)S(1)}, u32[]{:S(2)}, u32[]{:S(2)}) collective-permute-start(bf16[1,1,1,128,256]{4,3,2,1,0:T(8,128)(2,1)S(1)} %constant_dynamic-slice_fusion.4), channel_id=1, source_target_pairs={{0,4},{1,5},{2,6},{3,7},{4,0},{5,1},{6,2},{7,3},{8,12},{9,13},{10,... | collective-permute-start | bytes 196616 | tf_op jit(solution)/shard_map/ppermute | solution.py:190
  68.8 4.3 %collective-permute-start.5 = (bf16[1,1,1,128,256]{4,3,2,1,0:T(8,128)(2,1)S(1)}, bf16[1,1,1,128,256]{4,3,2,1,0:T(8,128)(2,1)S(1)}, u32[]{:S(2)}, u32[]{:S(2)}) collective-permute-start(bf16[1,1,1,128,256]{4,3,2,1,0:T(8,128)(2,1)S(1)} %constant_dynamic-slice_fusion.1), channel_id=1, source_target_pairs={{0,1},{1,0},{2,3},{3,2},{4,5},{5,4},{6,7},{7,6},{8,9},{9,8},{10,11... | collective-permute-start | bytes 196616 | tf_op jit(solution)/shard_map/ppermute | solution.py:190
  74.1 20.5 %collective-permute-start.15 = (bf16[1,64,512]{2,1,0:T(8,128)(2,1)}, bf16[1,64,512]{2,1,0:T(8,128)(2,1)S(1)}, u32[]{:S(2)}, u32[]{:S(2)}) collective-permute-start(bf16[1,64,512]{2,1,0:T(8,128)(2,1)} %get-tuple-element.60), channel_id=1, source_target_pairs={{0,4},{1,5},{2,6},{3,7},{4,0},{5,1},{6,2},{7,3},{8,12},{9,13},{10,... | collective-permute-start | bytes 196616 | tf_op jit(solution)/shard_map/ppermute | solution.py:190
  75.0 17.7 %collective-permute-start.18 = (bf16[1,64,512]{2,1,0:T(8,128)(2,1)}, bf16[1,64,512]{2,1,0:T(8,128)(2,1)S(1)}, u32[]{:S(2)}, u32[]{:S(2)}) collective-permute-start(bf16[1,64,512]{2,1,0:T(8,128)(2,1)} %get-tuple-element.63), channel_id=1, source_target_pairs={{0,1},{1,0},{2,3},{3,2},{4,5},{5,4},{6,7},{7,6},{8,9},{9,8},{10,11... | collective-permute-start | bytes 196616 | tf_op jit(solution)/shard_map/ppermute | solution.py:190
  80.3 23.8 %copy-start.56 = (f32[128]{0:T(128)}, f32[128]{0:T(128)S(1)}, u32[]{:S(2)}) copy-start(f32[128]{0:T(128)S(1)} %multiply_multiply_fusion.11) | copy-start | bytes 1540
  81.0 11.2 %all-to-all-start.2 = ((f32[8,1,64]{2,1,0:T(1,128)}), f32[8,1,64]{2,1,0:T(1,128)S(1)}, u32[]{:S(2)}, u32[]{:S(2)}) async-start(f32[8,1,64]{2,1,0:T(1,128)} %reshape.1046), calls=%async_computation.2 | async-start | bytes 8192 | tf_op jit(solution)/shard_map/all_to_all | solution.py:377
  86.9 9.7 %collective-permute-start.6 = (bf16[1,64,512]{2,1,0:T(8,128)(2,1)S(1)}, bf16[1,64,512]{2,1,0:T(8,128)(2,1)S(1)}, u32[]{:S(2)}, u32[]{:S(2)}) collective-permute-start(bf16[1,64,512]{2,1,0:T(8,128)(2,1)S(1)} %get-tuple-element.64), channel_id=1, source_target_pairs={{0,4},{1,5},{2,6},{3,7},{4,0},{5,1},{6,2},{7,3},{8,12},{9,13},{10,... | collective-permute-start | bytes 196616 | tf_op jit(solution)/shard_map/ppermute | solution.py:190
  89.9 6.6 %collective-permute-start.9 = (bf16[1,64,512]{2,1,0:T(8,128)(2,1)S(1)}, bf16[1,64,512]{2,1,0:T(8,128)(2,1)S(1)}, u32[]{:S(2)}, u32[]{:S(2)}) collective-permute-start(bf16[1,64,512]{2,1,0:T(8,128)(2,1)S(1)} %get-tuple-element.67), channel_id=1, source_target_pairs={{0,1},{1,0},{2,3},{3,2},{4,5},{5,4},{6,7},{7,6},{8,9},{9,8},{10,11... | collective-permute-start | bytes 196616 | tf_op jit(solution)/shard_map/ppermute | solution.py:190
  97.5 10.1 %collective-permute-start.19 = (bf16[2,64,512]{2,1,0:T(8,128)(2,1)S(1)}, bf16[2,64,512]{2,1,0:T(8,128)(2,1)S(1)}, u32[]{:S(2)}, u32[]{:S(2)}) collective-permute-start(bf16[2,64,512]{2,1,0:T(8,128)(2,1)S(1)} %maximum_select_fusion.27), channel_id=1, source_target_pairs={{0,4},{1,5},{2,6},{3,7},{4,0},{5,1},{6,2},{7,3},{8,12},{9,13},{10,... | collective-permute-start | bytes 393224 | tf_op jit(solution)/shard_map/ppermute | solution.py:190
  99.1 7.6 %collective-permute-start.16 = (bf16[2,64,512]{2,1,0:T(8,128)(2,1)S(1)}, bf16[2,64,512]{2,1,0:T(8,128)(2,1)S(1)}, u32[]{:S(2)}, u32[]{:S(2)}) collective-permute-start(bf16[2,64,512]{2,1,0:T(8,128)(2,1)S(1)} %maximum_select_fusion.25), channel_id=1, source_target_pairs={{0,2},{1,3},{2,0},{3,1},{4,6},{5,7},{6,4},{7,5},{8,10},{9,11},{10,... | collective-permute-start | bytes 393224 | tf_op jit(solution)/shard_map/ppermute | solution.py:190
  102.3 9.8 %collective-permute-start.10 = (bf16[2,64,512]{2,1,0:T(8,128)(2,1)S(1)}, bf16[2,64,512]{2,1,0:T(8,128)(2,1)S(1)}, u32[]{:S(2)}, u32[]{:S(2)}) collective-permute-start(bf16[2,64,512]{2,1,0:T(8,128)(2,1)S(1)} %maximum_select_fusion.23), channel_id=1, source_target_pairs={{0,4},{1,5},{2,6},{3,7},{4,0},{5,1},{6,2},{7,3},{8,12},{9,13},{10,... | collective-permute-start | bytes 393224 | tf_op jit(solution)/shard_map/ppermute | solution.py:190
  104.1 7.2 %collective-permute-start.7 = (bf16[2,64,512]{2,1,0:T(8,128)(2,1)S(1)}, bf16[2,64,512]{2,1,0:T(8,128)(2,1)S(1)}, u32[]{:S(2)}, u32[]{:S(2)}) collective-permute-start(bf16[2,64,512]{2,1,0:T(8,128)(2,1)S(1)} %maximum_select_fusion.21), channel_id=1, source_target_pairs={{0,2},{1,3},{2,0},{3,1},{4,6},{5,7},{6,4},{7,5},{8,10},{9,11},{10,... | collective-permute-start | bytes 393224 | tf_op jit(solution)/shard_map/ppermute | solution.py:190
  106.8 7.1 %collective-permute-start.17 = (bf16[4,64,512]{2,1,0:T(8,128)(2,1)S(1)}, bf16[4,64,512]{2,1,0:T(8,128)(2,1)S(1)}, u32[]{:S(2)}, u32[]{:S(2)}) collective-permute-start(bf16[4,64,512]{2,1,0:T(8,128)(2,1)S(1)} %bitcast.256), channel_id=1, source_target_pairs={{0,1},{1,0},{2,3},{3,2},{4,5},{5,4},{6,7},{7,6},{8,9},{9,8},{10,11... | collective-permute-start | bytes 786440 | tf_op jit(solution)/shard_map/ppermute | solution.py:190
  107.7 7.4 %collective-permute-start.20 = (bf16[4,64,512]{2,1,0:T(8,128)(2,1)S(1)}, bf16[4,64,512]{2,1,0:T(8,128)(2,1)S(1)}, u32[]{:S(2)}, u32[]{:S(2)}) collective-permute-start(bf16[4,64,512]{2,1,0:T(8,128)(2,1)S(1)} %bitcast.257), channel_id=1, source_target_pairs={{0,2},{1,3},{2,0},{3,1},{4,6},{5,7},{6,4},{7,5},{8,10},{9,11},{10,... | collective-permute-start | bytes 786440 | tf_op jit(solution)/shard_map/ppermute | solution.py:190
  111.3 6.4 %collective-permute-start.8 = (bf16[4,64,512]{2,1,0:T(8,128)(2,1)S(1)}, bf16[4,64,512]{2,1,0:T(8,128)(2,1)S(1)}, u32[]{:S(2)}, u32[]{:S(2)}) collective-permute-start(bf16[4,64,512]{2,1,0:T(8,128)(2,1)S(1)} %bitcast.255), channel_id=1, source_target_pairs={{0,1},{1,0},{2,3},{3,2},{4,5},{5,4},{6,7},{7,6},{8,9},{9,8},{10,11... | collective-permute-start | bytes 786440 | tf_op jit(solution)/shard_map/ppermute | solution.py:190
  112.1 6.4 %collective-permute-start.11 = (bf16[4,64,512]{2,1,0:T(8,128)(2,1)S(1)}, bf16[4,64,512]{2,1,0:T(8,128)(2,1)S(1)}, u32[]{:S(2)}, u32[]{:S(2)}) collective-permute-start(bf16[4,64,512]{2,1,0:T(8,128)(2,1)S(1)} %bitcast.254), channel_id=1, source_target_pairs={{0,2},{1,3},{2,0},{3,1},{4,6},{5,7},{6,4},{7,5},{8,10},{9,11},{10,... | collective-permute-start | bytes 786440 | tf_op jit(solution)/shard_map/ppermute | solution.py:190
  117.1 14.6 %copy-start.30 = (f32[1024,256]{1,0:T(8,128)}, f32[1024,256]{1,0:T(8,128)S(1)}, u32[]{:S(2)}) copy-start(f32[1024,256]{1,0:T(8,128)S(1)} %fusion.41) | copy-start | bytes 3145732
  118.3 13.4 %copy-start.32 = (f32[1024,256]{1,0:T(8,128)}, f32[1024,256]{1,0:T(8,128)S(1)}, u32[]{:S(2)}) copy-start(f32[1024,256]{1,0:T(8,128)S(1)} %fusion.43) | copy-start | bytes 3145732
  133.1 73.9 %collective-permute-start.30 = (bf16[128,512]{1,0:T(8,128)(2,1)}, bf16[128,512]{1,0:T(8,128)(2,1)}, u32[]{:S(2)}, u32[]{:S(2)}) collective-permute-start(bf16[128,512]{1,0:T(8,128)(2,1)} %constant_dynamic-slice_fusion), channel_id=1, source_target_pairs={{0,8},{8,0},{16,24},{24,16},{1,9},{9,1},{17,25},{25,17},{2,10},{10... | collective-permute-start | bytes 393224 | tf_op jit(solution)/shard_map/ppermute | solution.py:190
  136.0 27.5 %collective-permute-start.12 = (bf16[1632,512]{1,0:T(8,128)(2,1)}, bf16[1632,512]{1,0:T(8,128)(2,1)}, u32[]{:S(2)}, u32[]{:S(2)}) collective-permute-start(bf16[1632,512]{1,0:T(8,128)(2,1)} %fusion), channel_id=1, source_target_pairs={{0,8},{8,0},{16,24},{24,16},{1,9},{9,1},{17,25},{25,17},{2,10},{10... | collective-permute-start | bytes 5013512 | tf_op jit(solution)/shard_map/ppermute | solution.py:190
  148.0 12.5 %copy-start.31 = (f32[1024,256]{1,0:T(8,128)S(1)}, f32[1024,256]{1,0:T(8,128)}, u32[]{:S(2)}) copy-start(f32[1024,256]{1,0:T(8,128)} %copy-done.30) | copy-start | bytes 3145732
  163.5 43.5 %copy-start.47 = (bf16[256,512]{1,0:T(8,128)(2,1)S(1)}, bf16[256,512]{1,0:T(8,128)(2,1)}, u32[]{:S(2)}) copy-start(bf16[256,512]{1,0:T(8,128)(2,1)} %copy-done.46) | copy-start | bytes 786436
  167.9 43.1 %collective-permute-start.13 = (bf16[1632,512]{1,0:T(8,128)(2,1)S(1)}, bf16[1632,512]{1,0:T(8,128)(2,1)}, u32[]{:S(2)}, u32[]{:S(2)}) collective-permute-start(bf16[1632,512]{1,0:T(8,128)(2,1)S(1)} %add_convert_fusion.1), channel_id=1, source_target_pairs={{0,16},{8,24},{16,0},{24,8},{1,17},{9,25},{17,1},{25,9},{2,18},{10... | collective-permute-start | bytes 5013512 | tf_op jit(solution)/shard_map/ppermute | solution.py:190
  169.5 1.3 collective-permute-start.33
  170.3 42.8 %collective-permute-start.27 = (bf16[256,512]{0,1:T(8,128)(2,1)}, bf16[256,512]{0,1:T(8,128)(2,1)}, u32[]{:S(2)}, u32[]{:S(2)}) collective-permute-start(bf16[256,512]{0,1:T(8,128)(2,1)} %fusion.35), channel_id=1, source_target_pairs={{0,8},{8,0},{16,24},{24,16},{1,9},{9,1},{17,25},{25,17},{2,10},{10... | collective-permute-start | bytes 786440 | tf_op jit(solution)/shard_map/ppermute | solution.py:190
  170.8 35.7 %collective-permute-start.34 = (f32[2,64]{1,0:T(2,128)S(1)}, f32[2,64]{1,0:T(2,128)S(1)}, u32[]{:S(2)}, u32[]{:S(2)}) collective-permute-start(f32[2,64]{1,0:T(2,128)S(1)} %fusion.92), channel_id=1, source_target_pairs={{0,16},{8,24},{16,0},{24,8},{1,17},{9,25},{17,1},{25,9},{2,18},{10... | collective-permute-start | bytes 1544 | tf_op jit(solution)/shard_map/ppermute | solution.py:190
  172.1 38.1 %all-to-all-start.1 = ((bf16[8,64,128]{2,1,0:T(8,128)(2,1)}), bf16[8,64,128]{2,1,0:T(8,128)(2,1)S(1)}, u32[]{:S(2)}, u32[]{:S(2)}) async-start(bf16[8,64,128]{2,1,0:T(8,128)(2,1)} %bitcast_bitcast_fusion), calls=%async_computation.1 | async-start | bytes 262144 | tf_op jit(solution)/shard_map/all_to_all | solution.py:361
  208.6 6.3 %collective-permute-start.31 = (bf16[128,512]{1,0:T(8,128)(2,1)}, bf16[128,512]{1,0:T(8,128)(2,1)}, u32[]{:S(2)}, u32[]{:S(2)}) collective-permute-start(bf16[128,512]{1,0:T(8,128)(2,1)} %add_convert_fusion.8), channel_id=1, source_target_pairs={{0,16},{8,24},{16,0},{24,8},{1,17},{9,25},{17,1},{25,9},{2,18},{10... | collective-permute-start | bytes 393224 | tf_op jit(solution)/shard_map/ppermute | solution.py:190
  213.1 14.1 %collective-permute-start.14 = (bf16[1632,512]{1,0:T(8,128)(2,1)S(1)}, bf16[1632,512]{1,0:T(8,128)(2,1)}, u32[]{:S(2)}, u32[]{:S(2)}) collective-permute-start(bf16[1632,512]{1,0:T(8,128)(2,1)S(1)} %add_convert_fusion), channel_id=1, source_target_pairs={{0,8},{8,0},{16,24},{24,16},{1,9},{9,1},{17,25},{25,17},{2,10},{10... | collective-permute-start | bytes 5013512 | tf_op jit(solution)/shard_map/ppermute | solution.py:190
  214.3 8.7 %collective-permute-start.28 = (bf16[256,512]{0,1:T(8,128)(2,1)S(1)}, bf16[256,512]{0,1:T(8,128)(2,1)S(1)}, u32[]{:S(2)}, u32[]{:S(2)}) collective-permute-start(bf16[256,512]{0,1:T(8,128)(2,1)S(1)} %add_convert_fusion.4), channel_id=1, source_target_pairs={{0,16},{8,24},{16,0},{24,8},{1,17},{9,25},{17,1},{25,9},{2,18},{10... | collective-permute-start | bytes 786440 | tf_op jit(solution)/shard_map/ppermute | solution.py:190
  215.9 8.1 %collective-permute-start.32 = (bf16[128,512]{1,0:T(8,128)(2,1)S(1)}, bf16[128,512]{1,0:T(8,128)(2,1)S(1)}, u32[]{:S(2)}, u32[]{:S(2)}) collective-permute-start(bf16[128,512]{1,0:T(8,128)(2,1)S(1)} %add_convert_fusion.7), channel_id=1, source_target_pairs={{0,8},{8,0},{16,24},{24,16},{1,9},{9,1},{17,25},{25,17},{2,10},{10... | collective-permute-start | bytes 393224 | tf_op jit(solution)/shard_map/ppermute | solution.py:190
  223.0 1.9 collective-permute-start.29
  (52 other events, 258.3 us)

commit v2 on v0

v2 whole, which is shorter than its diff:
```python
import functools
import math

import jax
import jax.numpy as jnp
from jax import lax
from jax.experimental import pallas as pl
from jax.experimental.pallas import tpu as pltpu
from jax.sharding import PartitionSpec as P

K = 24
AR = 3
TILE = 256
HALF = 128
PER_STEP = 4

eps_norm = 1e-05


def rms_scale(values, scales):
    return values * lax.rsqrt(jnp.mean(values * values, axis=-1, keepdims=True) + eps_norm) * scales


def contract_first(left, right):
    return lax.dot_general(
        left, right, (((0,), (0,)), ((), ())), preferred_element_type=jnp.float32
    )


def contract_last(left, right):
    return lax.dot_general(
        left, right, (((1,), (1,)), ((), ())), preferred_element_type=jnp.float32
    )


def product(left, right):
    return jnp.dot(left, right, preferred_element_type=jnp.float32)


def in_hbm(value):
    return pltpu.with_memory_space_constraint(value, pltpu.HBM)


def whole(shape):
    return pl.BlockSpec(shape, lambda *_: (0,) * len(shape))


def vmem(mebibytes):
    return pltpu.CompilerParams(vmem_limit_bytes=mebibytes << 20)


def first_norm_kernel(me, hidden, gain, segments, pieces):
    count, rows, share = pieces.shape
    channels = hidden.shape[2] // count
    normed = rms_scale(hidden[0].astype(jnp.float32), gain[...])
    normed = normed.T.astype(jnp.bfloat16)
    ids = segments[:, pl.ds(pl.multiple_of(me[0] * share, share), share)]
    ids = jnp.broadcast_to(ids.astype(jnp.float32), (rows - channels, share)).astype(jnp.bfloat16)
    for i in range(count):
        pieces[i, :channels, :] = normed[i * channels : (i + 1) * channels]
        pieces[i, channels:, :] = ids


def first_norm(me, hidden_in, gain, segments, count):
    _, share, width = hidden_in.shape
    shape = (count, width // count + 16, share)
    return pl.pallas_call(
        first_norm_kernel,
        grid_spec=pltpu.PrefetchScalarGridSpec(
            num_scalar_prefetch=1,
            grid=(1,),
            in_specs=[whole(hidden_in.shape), whole((1, width)), whole(segments.shape)],
            out_specs=whole(shape),
        ),
        out_shape=jax.ShapeDtypeStruct(shape, jnp.bfloat16),
        name="first_norm",
    )(me, hidden_in, gain[None, :], segments)


def first_norm_back_kernel(came, hidden, gain, grad, out):
    count, channels, share = came.shape
    normed_grad = came[...].astype(jnp.float32).reshape(count * channels, share).T
    tokens = hidden[0].astype(jnp.float32)
    scale = lax.rsqrt(jnp.mean(tokens * tokens, axis=-1, keepdims=True) + eps_norm)
    weighed = normed_grad * gain[...]
    along = jnp.mean(weighed * tokens, axis=-1, keepdims=True)
    out[0] = grad[...] + scale * (weighed - tokens * (scale * scale * along))


def first_norm_back(came, hidden_in, gain, grad):
    return pl.pallas_call(
        first_norm_back_kernel,
        out_shape=jax.ShapeDtypeStruct(hidden_in.shape, jnp.float32),
        name="first_norm_back",
    )(came, hidden_in, gain[None, :], grad)


def tile_pairs(length):
    blocks, reach = length // TILE, length // 2 // TILE
    return [(tb, sb) for tb in range(blocks) for sb in range(max(0, tb - reach), tb + 1)]


def slab_width(length):
    return length // 2 + TILE


def parity_lanes(rows, lanes, dtype=jnp.float32):
    lane = lax.broadcasted_iota(jnp.int32, (rows, lanes), 1)
    return (1 - 2 * (lane % 2)).astype(dtype)


def block(index):
    return slice(index * TILE, (index + 1) * TILE)


def segment_row(pieces):
    row = pieces.shape[1] - 8
    return jnp.concatenate(
        [pieces[i, row:, :].astype(jnp.float32) for i in range(pieces.shape[0])], axis=1
    )


def build_masks(ids, masks, length, targets_in_rows):
    row = lax.broadcasted_iota(jnp.int32, (TILE, TILE), 0)
    col = lax.broadcasted_iota(jnp.int32, (TILE, TILE), 1)
    in_lanes = [jnp.broadcast_to(ids[:1, block(b)], (TILE, TILE)) for b in range(length // TILE)]
    in_rows = [value.T for value in in_lanes]
    for index, (tb, sb) in enumerate(tile_pairs(length)):
        rows_of, lanes_of = (tb, sb) if targets_in_rows else (sb, tb)
        same = in_rows[rows_of] == in_lanes[lanes_of]
        if tb == sb:
            same = same & ((row >= col) if targets_in_rows else (col >= row))
        masks[index] = jnp.where(same, 1.0, 0.0).astype(jnp.bfloat16)


def lag_keep(ids, lag):
    lane = lax.broadcasted_iota(jnp.int32, ids.shape, 1)
    same = (pltpu.roll(ids, lag, 1) == ids) & (lane >= lag)
    return jnp.where(same, 1.0, 0.0)[:1]


def build_slab(taps, slab, width):
    rolled = pltpu.roll(jnp.broadcast_to(taps, (HALF, width)), 0, 1, stride=1, stride_axis=0)
    rolled = rolled.astype(jnp.bfloat16)
    slab[:HALF, :] = rolled
    slab[HALF:, HALF:] = rolled[:, : width - HALF]
    slab[HALF:, :HALF] = rolled[:, :HALF]


def start_maps(filters, pieces, lags, taps, masks, doubled):
    count, _, share = pieces.shape
    channels, length = lags.shape[1:]
    ids = segment_row(pieces)
    build_masks(ids, masks, length, False)
    taps[...] = filters[:, : taps.shape[1]].astype(jnp.float32)
    sign = parity_lanes(channels, share, jnp.bfloat16)
    for i in range(count):
        part = pieces[i, :channels, :]
        doubled[:channels, i * share : (i + 1) * share] = part
        doubled[channels:, i * share : (i + 1) * share] = part * sign
    inputs = doubled[:channels, :]
    lags[0] = inputs
    inputs = inputs.astype(jnp.float32)
    for j in range(1, AR):
        lags[j] = (pltpu.roll(inputs, j, 1) * lag_keep(ids, j)).astype(jnp.bfloat16)


def step_maps(first, maps, taps, slabs, masks, doubled):
    channels, length = maps.shape[2:]
    width = taps.shape[1]
    pairs = tile_pairs(length)
    parity = parity_lanes(channels, TILE)
    for k in range(PER_STEP):
        slab = slabs.at[k]
        build_slab(taps[pl.ds(first + k, 1), :], slab, width)
        for tb in range(length // TILE):
            chosen = [(i, sb) for i, (t, sb) in enumerate(pairs) if t == tb]
            tiles = [slab[:, block(tb - sb)] * masks[i] for i, sb in chosen]
            low = chosen[0][1]
            both = product(
                doubled[:, low * TILE : (tb + 1) * TILE], jnp.concatenate(tiles, axis=0)
            )
            maps[0, k, :, block(tb)] = both[:channels].astype(jnp.bfloat16)
            maps[1, k, :, block(tb)] = (both[channels:] * parity).astype(jnp.bfloat16)


def maps_kernel(start, filters, pieces, *refs):
    maps, lags, taps, slabs, masks, doubled = refs[-6:]
    step = pl.program_id(0)

    @pl.when(step == 0)
    def _():
        start_maps(filters, pieces, lags, taps, masks, doubled)

    step_maps(start + step * PER_STEP, maps, taps, slabs, masks, doubled)


def mixed_kernel(
    me,
    filters,
    pieces,
    plus_mixing,
    minus_mixing,
    lag_mixing,
    maps,
    lags,
    keep0,
    give0,
    keep1,
    give1,
    taps,
    slabs,
    masks,
    doubled,
    acc,
):
    _, channels, model_width = plus_mixing.shape
    count, _, share = pieces.shape
    length = lags.shape[2]
    step = pl.program_id(0)

    @pl.when(step == 0)
    def _():
        start_maps(filters, pieces, lags, taps, masks, doubled)
        acc[...] = jnp.zeros_like(acc)

    step_maps(step * PER_STEP, maps, taps, slabs, masks, doubled)
    rows = PER_STEP * channels

    def part(weights, values):
        return contract_first(weights.reshape(-1, model_width), values.reshape(-1, length))

    total = part(plus_mixing[...], maps[0]) + part(minus_mixing[...], maps[1])
    for i in range(count):
        acc[i] += total[:, i * share : (i + 1) * share]

    @pl.when(step == pl.num_programs(0) - 1)
    def _():
        last = part(lag_mixing[...], lags[...])
        for i in range(count):
            acc[i] += last[:, i * share : (i + 1) * share]
        half = model_width // 2
        low, near = me[0] & 1, (me[0] >> 1) & 1
        for r in range(count // 4):
            for a in range(2):
                for other, (out0, out1) in enumerate(((keep0, keep1), (give0, give1))):
                    out0[r, a] = acc[r * 4 + a * 2 + (low ^ other), :half].astype(jnp.bfloat16)
                    out1[r, a] = acc[r * 4 + (near ^ other) * 2 + a, half:].astype(jnp.bfloat16)


def place_tokens(me, parts, out):
    rows = parts[0].shape[2]
    for half, pair in enumerate((parts[:2], parts[2:])):
        for other, part in enumerate(pair):
            low, near = me & 1, (me >> 1) & 1
            for a in range(2):
                for r in range(part.shape[1]):
                    if half == 0:
                        owner = r * 4 + a * 2 + (low ^ other)
                    else:
                        owner = r * 4 + (near ^ other) * 2 + a
                    start = pl.multiple_of((owner * 2 + half) * rows, rows)
                    out[pl.ds(start, rows), :] = part[a, r, :rows, :]


def place_kernel(me, part0, part1, part2, part3, out):
    place_tokens(me[0], (part0, part1, part2, part3), out)


def place(me, parts):
    count = 2 * sum(math.prod(part.shape[:-1]) for part in parts[:2])
    shape = (count, parts[0].shape[-1])
    return pl.pallas_call(
        place_kernel,
        grid_spec=pltpu.PrefetchScalarGridSpec(
            num_scalar_prefetch=1,
            grid=(1,),
            in_specs=[whole(part.shape) for part in parts],
            out_specs=whole(shape),
        ),
        out_shape=pltpu.VMEM(shape, jnp.bfloat16),
        name="place",
    )(me, *parts)


def spectral_back_kernel(
    filters, plus_mixing, minus_mixing, pieces, grads, acc, taps, slabs, masks, both
):
    _, channels, model_width = plus_mixing.shape
    length, width = acc.shape[1], taps.shape[1]
    reach = length // 2
    pairs = tile_pairs(length)
    rows = PER_STEP * channels
    step = pl.program_id(0)

    @pl.when(step == 0)
    def _():
        build_masks(segment_row(pieces), masks, length, True)
        acc[...] = jnp.zeros_like(acc)
        source = lax.broadcasted_iota(jnp.int32, (width, width), 0)
        target = lax.broadcasted_iota(jnp.int32, (width, width), 1)
        flip = jnp.where(source + target == reach, 1.0, 0.0).astype(jnp.bfloat16)
        taps[...] = product(filters[:, :width], flip)

    sign = parity_lanes(rows, length, jnp.bfloat16)
    plus = contract_last(plus_mixing[...].reshape(rows, model_width), grads[...])
    both[:, :channels, :] = plus.astype(jnp.bfloat16).reshape(PER_STEP, channels, length)
    minus = contract_last(minus_mixing[...].reshape(rows, model_width), grads[...])
    both[:, channels:, :] = (minus.astype(jnp.bfloat16) * sign).reshape(
        PER_STEP, channels, length
    )
    for k in range(PER_STEP):
        build_slab(taps[pl.ds(step * PER_STEP + k, 1), :], slabs.at[k], width)
    for sb in range(length // TILE):
        chosen = [(i, tb) for i, (tb, s) in enumerate(pairs) if s == sb]
        last = chosen[-1][1]
        total = acc[:, block(sb)]
        for k in range(PER_STEP):
            tiles = []
            for i, tb in chosen:
                start = reach - (tb - sb) * TILE
                tiles.append(slabs[k, :, start : start + TILE] * masks[i])
            total = total + product(
                both[k, :, sb * TILE : (last + 1) * TILE], jnp.concatenate(tiles, axis=0)
            )
        acc[:, block(sb)] = total


def lag_back_kernel(acc, lag_mixing, grads, inputs, pieces, out, gain):
    _, channels, model_width = lag_mixing.shape
    length = acc.shape[1]
    count, _, share = out.shape
    ids = segment_row(pieces)
    lag_grad = contract_last(lag_mixing[...].reshape(AR * channels, model_width), grads[...])
    total = acc[:channels] + parity_lanes(channels, length) * acc[channels:]
    for j in range(AR):
        term = lag_grad[j * channels : (j + 1) * channels]
        if j:
            term = pltpu.roll(term * lag_keep(ids, j), length - j, 1)
        total = total + term
    back = total.astype(jnp.bfloat16)
    for i in range(count):
        out[i] = back[:, i * share : (i + 1) * share]
    weighed = back.astype(jnp.float32) * inputs[0].astype(jnp.float32)
    by_lane = jnp.broadcast_to(jnp.sum(weighed, axis=1, keepdims=True), (channels, 128))
    row = lax.broadcasted_iota(jnp.int32, by_lane.shape, 0)
    lane = lax.broadcasted_iota(jnp.int32, by_lane.shape, 1)
    total = jnp.sum(jnp.where(row == lane, by_lane, 0.0), axis=0, keepdims=True)
    gain[...] = jnp.broadcast_to(total, gain.shape)


def toeplitz_scratch(length, count):
    width = slab_width(length)
    return [
        pltpu.VMEM((count, width), jnp.float32),
        pltpu.VMEM((PER_STEP, TILE, width), jnp.bfloat16),
        pltpu.VMEM((len(tile_pairs(length)), TILE, TILE), jnp.bfloat16),
    ]


def maps_scratch(channels, length, count):
    return [
        *toeplitz_scratch(length, count),
        pltpu.VMEM((2 * channels, length), jnp.bfloat16),
    ]


def spectral_maps(pieces, filters, channels, start, count, into=None):
    length = filters.shape[1]
    first = start // PER_STEP
    given = [] if into is None else [in_hbm(into)]
    return pl.pallas_call(
        functools.partial(maps_kernel, start),
        grid=(count // PER_STEP,),
        in_specs=[
            whole(filters.shape),
            whole(pieces.shape),
            *[pl.BlockSpec(memory_space=pltpu.HBM) for _ in given],
        ],
        out_specs=[
            pl.BlockSpec((2, PER_STEP, channels, length), lambda k: (0, k + first, 0, 0)),
            whole((AR, channels, length)),
        ],
        out_shape=[
            pltpu.HBM((2, K, channels, length), jnp.bfloat16),
            jax.ShapeDtypeStruct((AR, channels, length), jnp.bfloat16),
        ],
        scratch_shapes=maps_scratch(channels, length, filters.shape[0]),
        input_output_aliases={2: 0} if given else {},
        compiler_params=vmem(16),
        cost_estimate=pl.CostEstimate(
            flops=6 * channels * count * length * length, transcendentals=0, bytes_accessed=4 << 20
        ),
        name="spectral_maps",
    )(filters, pieces, *given)


def spectral_mixed(me, pieces, filters, mixing):
    owners, _, share = pieces.shape
    channels, model_width = mixing.shape[1:]
    count, length = filters.shape
    steps = count // PER_STEP
    cut = (owners // 4, 2, model_width // 2, share)
    mix_block = (PER_STEP, channels, model_width)
    return pl.pallas_call(
        mixed_kernel,
        grid_spec=pltpu.PrefetchScalarGridSpec(
            num_scalar_prefetch=1,
            grid=(steps,),
            in_specs=[
                whole(filters.shape),
                whole(pieces.shape),
                pl.BlockSpec(mix_block, lambda k, _: (k, 0, 0)),
                pl.BlockSpec(mix_block, lambda k, _: (k + steps, 0, 0)),
                pl.BlockSpec((AR, channels, model_width), lambda k, _: (2 * count // AR, 0, 0)),
            ],
            out_specs=[
                pl.BlockSpec((2, PER_STEP, channels, length), lambda k, _: (0, k, 0, 0)),
                whole((AR, channels, length)),
                *[whole(cut)] * 4,
            ],
            scratch_shapes=[
                *maps_scratch(channels, length, count),
                pltpu.VMEM((owners, model_width, share), jnp.float32),
            ],
        ),
        out_shape=[
            pltpu.HBM((2, count, channels, length), jnp.bfloat16),
            jax.ShapeDtypeStruct((AR, channels, length), jnp.bfloat16),
            *[jax.ShapeDtypeStruct(cut, jnp.bfloat16)] * 4,
        ],
        compiler_params=vmem(24),
        name="spectral_mixed",
    )(me, filters, pieces, *[in_hbm(mixing)] * 3)


def spectral_back(grads, mixing, filters, pieces):
    channels, model_width = mixing.shape[1:]
    count, length = filters.shape
    steps = count // PER_STEP
    mix_block = (PER_STEP, channels, model_width)
    return pl.pallas_call(
        spectral_back_kernel,
        grid=(steps,),
        in_specs=[
            whole(filters.shape),
            pl.BlockSpec(mix_block, lambda k: (k, 0, 0)),
            pl.BlockSpec(mix_block, lambda k: (k + steps, 0, 0)),
            whole(pieces.shape),
            whole(grads.shape),
        ],
        out_specs=whole((2 * channels, length)),
        scratch_shapes=[
            *toeplitz_scratch(length, count),
            pltpu.VMEM((PER_STEP, 2 * channels, length), jnp.bfloat16),
        ],
        out_shape=jax.ShapeDtypeStruct((2 * channels, length), jnp.float32),
        compiler_params=vmem(24),
        name="spectral_back",
    )(filters, *[in_hbm(mixing)] * 2, pieces, grads)


def lag_back(acc, mixing, grads, lags, pieces):
    channels, model_width = mixing.shape[1:]
    owners, _, share = pieces.shape
    sent = (owners, channels, share)
    return pl.pallas_call(
        lag_back_kernel,
        grid=(1,),
        in_specs=[
            whole(acc.shape),
            pl.BlockSpec((AR, channels, model_width), lambda k: (2 * K // AR, 0, 0)),
            whole(grads.shape),
            pl.BlockSpec((1, *lags.shape[1:]), lambda k: (0, 0, 0)),
            whole(pieces.shape),
        ],
        out_specs=[whole(sent), whole((8, 128))],
        out_shape=[
            jax.ShapeDtypeStruct(sent, jnp.bfloat16),
            jax.ShapeDtypeStruct((8, 128), jnp.float32),
        ],
        compiler_params=vmem(16),
        name="lag_back",
    )(acc, in_hbm(mixing), grads, in_hbm(lags), pieces)


def gelu_parts(gate_value, upper_value, hidden_grad):
    slope = math.sqrt(2 / math.pi)
    square = gate_value * gate_value
    tanh = jnp.tanh(slope * gate_value * (1.0 + 0.044715 * square))
    rise = 0.5 * (1.0 + tanh)
    gelu = gate_value * rise
    bend = 0.5 * slope * (1.0 - tanh * tanh) * (1.0 + 3 * 0.044715 * square)
    return (
        gelu * upper_value,
        hidden_grad * upper_value * (rise + gate_value * bend),
        hidden_grad * gelu,
    )


def feed_forward_kernel(
    bit,
    held,
    got,
    hidden_in,
    gain,
    cotangent,
    gate,
    up,
    down,
    output,
    normed_out,
    grad,
    grad_low,
    normed,
    resid,
    acc,
    normed_grad,
):
    step = pl.program_id(0)
    share = resid.shape[0]

    @pl.when(step == 0)
    def _():
        mixed = held[bit[0]].astype(jnp.float32) + got[...].astype(jnp.float32)
        resid[...] = hidden_in[0].astype(jnp.float32) + mixed.T
        normed[...] = rms_scale(resid[...], gain[...]).astype(jnp.bfloat16)
        acc[...] = jnp.zeros_like(acc)
        normed_grad[...] = jnp.zeros_like(normed_grad)

    gate_value = product(normed[...], gate[...])
    upper_value = product(normed[...], up[...])
    hidden_grad = contract_last(cotangent[0], down[...])
    hidden, gate_back, upper_back = gelu_parts(gate_value, upper_value, hidden_grad)
    acc[...] += product(hidden.astype(jnp.bfloat16), down[...])
    normed_grad[...] += contract_last(gate_back.astype(jnp.bfloat16), gate[...]) + contract_last(
        upper_back.astype(jnp.bfloat16), up[...]
    )

    @pl.when(step == pl.num_programs(0) - 1)
    def _():
        value, back = resid[...], normed_grad[...]
        output[0] = (value + acc[...]).astype(jnp.bfloat16)
        scale = lax.rsqrt(jnp.mean(value * value, axis=-1, keepdims=True) + eps_norm)
        weighed = back * gain[...]
        along = jnp.mean(weighed * value, axis=-1, keepdims=True)
        total = cotangent[0].astype(jnp.float32) + scale * (
            weighed - value * (scale * scale * along)
        )
        grad[...] = total
        grad_low[...] = total.astype(jnp.bfloat16)
        gains = jnp.sum(back * value * scale, axis=0, keepdims=True)
        high = jnp.broadcast_to(gains, (16, gains.shape[1])).astype(jnp.bfloat16)
        low = (gains - high.astype(jnp.float32)).astype(jnp.bfloat16)
        row = lax.broadcasted_iota(jnp.int32, low.shape, 0)
        normed_out[:share, :] = normed[...]
        normed_out[share:, :] = jnp.where(row < 8, high, low)


def feed_forward(bit, held, got, hidden_in, gain, cotangent, w_gate, w_up, w_down):
    _, share, width = hidden_in.shape
    steps = 4
    units = w_gate.shape[1] // steps
    tokens = (share, width)
    return pl.pallas_call(
        feed_forward_kernel,
        grid_spec=pltpu.PrefetchScalarGridSpec(
            num_scalar_prefetch=1,
            grid=(steps,),
            in_specs=[
                whole(held.shape),
                whole(got.shape),
                whole(hidden_in.shape),
                whole((1, width)),
                whole(cotangent.shape),
                pl.BlockSpec((width, units), lambda k, _: (0, k)),
                pl.BlockSpec((width, units), lambda k, _: (0, k)),
                pl.BlockSpec((units, width), lambda k, _: (k, 0)),
            ],
            out_specs=[
                whole(hidden_in.shape),
                whole((share + 16, width)),
                whole(tokens),
                whole(tokens),
            ],
            scratch_shapes=[
                pltpu.VMEM(tokens, jnp.bfloat16),
                *[pltpu.VMEM(tokens, jnp.float32)] * 3,
            ],
        ),
        out_shape=[
            jax.ShapeDtypeStruct(hidden_in.shape, jnp.bfloat16),
            jax.ShapeDtypeStruct((share + 16, width), jnp.bfloat16),
            jax.ShapeDtypeStruct(tokens, jnp.float32),
            jax.ShapeDtypeStruct(tokens, jnp.bfloat16),
        ],
        compiler_params=vmem(16),
        name="feed_forward",
    )(bit, held, got, hidden_in, gain[None, :], cotangent, *map(in_hbm, (w_gate, w_up, w_down)))


def own_mixing_grad_kernel(maps, lags, grads, out, lag_out):
    maps = maps[...].reshape(-1, maps.shape[-1])
    out[...] = product(maps, grads[...]).astype(out.dtype).reshape(out.shape)

    @pl.when(pl.program_id(0) == pl.num_programs(0) - 1)
    def _():
        values = lags[...].reshape(-1, lags.shape[-1])
        lag_out[...] = product(values, grads[...]).astype(out.dtype).reshape(lag_out.shape)


def own_mixing_grad(maps, lags, grads):
    _, count, channels, length = maps.shape
    width = grads.shape[1]
    steps, rows = 4, count // 4
    return pl.pallas_call(
        own_mixing_grad_kernel,
        grid=(steps,),
        in_specs=[
            pl.BlockSpec((2, rows, channels, length), lambda k: (0, k, 0, 0)),
            whole(lags.shape),
            whole(grads.shape),
        ],
        out_specs=[
            pl.BlockSpec((2, rows, channels, width), lambda k: (0, k, 0, 0)),
            whole((AR, channels, width)),
        ],
        out_shape=[
            pltpu.HBM((2, count, channels, width), jnp.bfloat16),
            pltpu.HBM((AR, channels, width), jnp.bfloat16),
        ],
        compiler_params=vmem(24),
        name="own_mixing_grad",
    )(in_hbm(maps), in_hbm(lags), grads)


def mixing_grad_kernel(with_lags, maps, lags, grads, own, own_lags, out):
    step, size = pl.program_id(0), maps.shape[0] * maps.shape[1]

    def total(left, mine):
        values = product(left[...].reshape(-1, left.shape[-1]), grads[...])
        return (values + mine[...].reshape(values.shape).astype(jnp.float32)).astype(out.dtype)

    out[pl.ds(pl.multiple_of(step * size, size), size), :] = total(maps, own)

    if with_lags:

        @pl.when(step == pl.num_programs(0) - 1)
        def _():
            out[size * pl.num_programs(0) :, :] = total(lags, own_lags)


def mixing_grad(which, maps, lags, grads, own, own_lags):
    _, count, channels, length = maps.shape
    width = grads.shape[1]
    steps, rows = 3, count // 3
    total = (count + which * AR) * channels
    return pl.pallas_call(
        functools.partial(mixing_grad_kernel, bool(which)),
        grid=(steps,),
        in_specs=[
            pl.BlockSpec((None, rows, channels, length), lambda k: (which, k, 0, 0)),
            whole(lags.shape),
            whole(grads.shape),
            pl.BlockSpec((None, rows, channels, width), lambda k: (which, k, 0, 0)),
            whole(own_lags.shape),
        ],
        out_specs=whole((total, width)),
        out_shape=jax.ShapeDtypeStruct((total, width), jnp.bfloat16),
        compiler_params=vmem(24),
        name="mixing_grad",
    )(in_hbm(maps), in_hbm(lags), in_hbm(grads), in_hbm(own), in_hbm(own_lags))


def unit_grads_kernel(me, *refs):
    *parts, gate, up, down, first_gain, out, normed, cotangent = refs
    place_tokens(me[0], parts[:4], normed)
    place_tokens(me[0], parts[4:], cotangent)
    width, units = gate.shape
    hidden_grad = contract_last(cotangent[...], down[...])
    gate_value = product(normed[...], gate[...])
    upper_value = product(normed[...], up[...])
    hidden, gate_back, upper_back = gelu_parts(gate_value, upper_value, hidden_grad)
    gate_part = contract_first(normed[...], gate_back.astype(jnp.bfloat16))
    up_part = contract_first(normed[...], upper_back.astype(jnp.bfloat16))
    down_part = contract_first(hidden.astype(jnp.bfloat16), cotangent[...])
    out[:width] = gate_part.astype(jnp.bfloat16)
    out[width : 2 * width] = up_part.astype(jnp.bfloat16)
    for i in range(width // units):
        start = 2 * width + i * units
        out[start : start + units] = down_part[:, i * units : (i + 1) * units].astype(
            jnp.bfloat16
        )
    share_rows = parts[0].shape[2]
    second_gain = jnp.zeros((16, width), jnp.float32)
    for part in parts[2:4]:
        for a in range(2):
            for r in range(part.shape[1]):
                second_gain = second_gain + part[a, r, share_rows:, :].astype(jnp.float32)
    second_gain = (second_gain[:8] + second_gain[8:]).astype(jnp.bfloat16)
    start = 3 * width
    for i in range(width // units):
        out[start + 16 * i : start + 16 * i + 8] = second_gain[:, i * units : (i + 1) * units]
    start += 16 * (width // units)
    out[start : start + 8, : first_gain.shape[1]] = first_gain[...].astype(jnp.bfloat16)


def unit_grads(me, normed_parts, cotangent_parts, w_gate, w_up, w_down, first_gain):
    width, hidden = w_gate.shape
    chans = lax.axis_size("chan")
    units = hidden // chans
    rows = 3 * width + 16 * (width // units) + 16
    parts = [*normed_parts, *cotangent_parts]
    tokens = 2 * sum(math.prod(part.shape[:-1]) for part in normed_parts[:2])
    return pl.pallas_call(
        unit_grads_kernel,
        grid_spec=pltpu.PrefetchScalarGridSpec(
            num_scalar_prefetch=1,
            grid=(1,),
            in_specs=[
                *[whole(part.shape) for part in parts],
                pl.BlockSpec((width, units), lambda k, me: (0, me[0])),
                pl.BlockSpec((width, units), lambda k, me: (0, me[0])),
                pl.BlockSpec((units, width), lambda k, me: (me[0], 0)),
                whole(first_gain.shape),
            ],
            out_specs=whole((rows, units)),
            scratch_shapes=[pltpu.VMEM((tokens, width), jnp.bfloat16)] * 2,
        ),
        out_shape=jax.ShapeDtypeStruct((rows, units), jnp.bfloat16),
        compiler_params=vmem(24),
        name="unit_grads",
    )(me, *parts, in_hbm(w_gate), in_hbm(w_up), in_hbm(w_down), first_gain)


def swap(values, axis, mask):
    count = lax.axis_size(axis)
    return lax.ppermute(values, axis, [(i, i ^ mask) for i in range(count)])


def bits_of(axis):
    return [1 << b for b in range(lax.axis_size(axis).bit_length() - 1)]


def join(mine, other, high, dim):
    return jnp.where(
        high, jnp.concatenate([other, mine], dim), jnp.concatenate([mine, other], dim)
    )


def tie(*values):
    return lax.optimization_barrier(values)


def gather_round(held, mask):
    me = lax.axis_index("chan")
    return join(held[None], swap(held, "chan", mask)[None], (me & mask) != 0, 0)


class Gather:
    def __init__(self, values, half):
        masks = bits_of("chan")
        self.half = half
        self.shape = values.shape
        self.common = masks[2:]
        self.orders = [(masks[1], masks[0]), (masks[0], masks[1])]
        self.held = values[None]

    def first(self):
        for mask in self.common:
            self.held = gather_round(self.held, mask).reshape(-1, *self.shape)
        return self.held

    def second(self):
        self.halves = [self.held[:, : self.half], self.held[:, self.half :]]
        self.halves = [
            gather_round(h, order[0]) for h, order in zip(self.halves, self.orders, strict=True)
        ]
        return self.halves

    def third(self):
        self.others = [
            swap(h, "chan", order[1]) for h, order in zip(self.halves, self.orders, strict=True)
        ]
        return self.others

    def parts(self):
        return (self.halves[0], self.others[0], self.halves[1], self.others[1])


def add(left, right):
    return left.astype(jnp.float32) + right.astype(jnp.float32)


def own_entry(values, mask, dim):
    return add(*exchange(values, mask, dim)).squeeze(dim)


def exchange(values, mask, dim):
    bit = (lax.axis_index("chan") & mask) // mask
    keep = lax.dynamic_slice_in_dim(values, bit, 1, dim)
    give = lax.dynamic_slice_in_dim(values, 1 - bit, 1, dim)
    return keep, swap(give, "chan", mask)


def scatter_tokens(keep0, give0, keep1, give1, beside):
    masks = bits_of("chan")
    got0, got1 = swap(give0, "chan", masks[0]), swap(give1, "chan", masks[1])
    half0 = add(keep0, got0).astype(jnp.bfloat16)
    half1 = add(keep1, got1).astype(jnp.bfloat16)
    half0, half1, *beside = tie(half0, half1, *beside)
    half0 = own_entry(half0, masks[1], 1)
    half1 = own_entry(half1, masks[0], 1)
    held = jnp.concatenate([half0, half1], axis=1)
    for mask in masks[:2:-1]:
        held = held.astype(jnp.bfloat16).reshape(2, -1, *held.shape[1:])
        held = own_entry(held, mask, 0)
    held = held.astype(jnp.bfloat16)
    return held, exchange(held, masks[2], 0)[1][0], beside


def core_halves(values):
    core = lax.axis_index("rows") & 1
    half = values.shape[0] // 2
    return [lax.dynamic_slice_in_dim(values, which * half, half, 0) for which in (core, 1 - core)]


def both_halves(held, dim):
    other = swap(held, "rows", 1).astype(jnp.float32)
    return join(held.astype(jnp.float32), other, (lax.axis_index("rows") & 1) != 0, dim)


def shards(
    hidden_in, segments, filters, gain_one, mixing, gain_two, w_gate, w_up, w_down, out_grad
):
    chans = lax.axis_size("chan")
    me = lax.axis_index("chan").astype(jnp.int32)
    at = me.reshape(1)
    _, share, width = hidden_in.shape
    channels = width // chans
    cotangent_gather = Gather(out_grad[0], share // 2)
    cotangent_gather.first()
    pieces = lax.all_to_all(
        first_norm(at, hidden_in, gain_one, segments, chans),
        "chan",
        split_axis=0,
        concat_axis=0,
    )
    peer_pieces = swap(pieces, "rows", 2)
    maps, lags, *cut = spectral_mixed(at, pieces, filters, mixing)
    peer_pieces, lags = tie(peer_pieces, lags)
    peer_maps, peer_lags = spectral_maps(peer_pieces, filters, channels, 0, K // 2)
    cotangent_gather.second()
    beside = (peer_maps, *cotangent_gather.third())
    held, got, (peer_maps, *cotangent_gather.others) = scatter_tokens(*cut, beside)
    last_bit = ((me >> 2) & 1).reshape(1)
    output, normed_two, resid_grad, resid_low = feed_forward(
        last_bit, held, got, hidden_in, gain_two, out_grad, w_gate, w_up, w_down
    )
    grad_gather = Gather(resid_low, share // 2)
    first = grad_gather.first()
    peer_pieces, resid_grad = tie(peer_pieces, resid_grad)
    peer_maps, _ = spectral_maps(peer_pieces, filters, channels, K // 2, K // 2, peer_maps)
    normed_two, grad_gather.held, peer_maps = tie(normed_two, first, peer_maps)
    normed_gather = Gather(normed_two, share // 2)
    normed_gather.first()
    grad_gather.second()
    normed_gather.second()
    grad_gather.third()
    normed_gather.third()
    full_grad = place(at, grad_gather.parts())
    peer_grad = swap(full_grad, "rows", 2)
    acc = spectral_back(full_grad, mixing, filters, pieces)
    back, first_local = lag_back(acc, mixing, full_grad, lags, pieces)
    came = lax.all_to_all(back, "chan", split_axis=0, concat_axis=0)
    first_local, *normed_parts = tie(first_local, *normed_gather.parts())
    unit_parts = unit_grads(
        at, normed_parts, cotangent_gather.parts(), w_gate, w_up, w_down, first_local
    )
    unit_parts, full_grad = tie(unit_parts, full_grad)
    keep, give = core_halves(unit_parts)
    unit_given = swap(give, "rows", 1)
    own, own_lags = own_mixing_grad(maps, lags, full_grad)
    own_lags, unit_given = tie(own_lags, unit_given)
    unit_half = add(keep, unit_given).astype(jnp.bfloat16)
    unit_half, peer_grad = tie(unit_half, peer_grad)
    unit_other = swap(unit_half, "rows", 2)
    first_part = mixing_grad(0, peer_maps, peer_lags, peer_grad, own, own_lags)
    first_part, peer_grad = tie(first_part, peer_grad)
    second_part = mixing_grad(1, peer_maps, peer_lags, peer_grad, own, own_lags)
    second_part, came, unit_other = tie(second_part, came, unit_other)
    sums = []
    for part in (first_part, second_part):
        for mask in [1, *bits_of("rows")[2:]]:
            part = add(part, swap(part, "rows", mask)).astype(jnp.bfloat16)
        sums.append(part.astype(jnp.float32))
    mixing_sum = jnp.concatenate(sums, axis=0).reshape(mixing.shape)
    input_total = first_norm_back(came, hidden_in, gain_one, resid_grad)
    unit_half = add(unit_half, unit_other).astype(jnp.bfloat16)
    for mask in bits_of("rows")[2:]:
        unit_half = add(unit_half, swap(unit_half, "rows", mask)).astype(jnp.bfloat16)
    unit_sum = both_halves(unit_half, 0)
    units = w_gate.shape[1] // chans
    columns = range(0, width, units)
    down_sum = jnp.concatenate([unit_sum[2 * width + i : 2 * width + i + units] for i in columns], 1)
    gains = [unit_sum[3 * width + 16 * i] for i in range(len(columns))]
    second_gain = lax.dynamic_slice_in_dim(jnp.concatenate(gains), me * channels, channels)
    first_gain = unit_sum[3 * width + 16 * len(columns), :channels] / (
        lax.dynamic_slice_in_dim(gain_one, me * channels, channels)
    )
    return (
        output,
        input_total,
        mixing_sum,
        unit_sum[:width],
        unit_sum[width : 2 * width],
        down_sum,
        first_gain,
        second_gain,
    )


def solution(mesh):
    in_specs = (
        P("rows", "chan", None),
        P("rows", None),
        P(),
        P(),
        P(None, "chan", None),
        P(),
        P(),
        P(),
        P(),
        P("rows", "chan", None),
    )
    out_specs = (
        P("rows", "chan", None),
        P("rows", "chan", None),
        P(None, "chan", None),
        P(None, "chan"),
        P(None, "chan"),
        P("chan", None),
        P("chan"),
        P("chan"),
    )
    return jax.shard_map(shards, mesh=mesh, in_specs=in_specs, out_specs=out_specs, check_vma=False)
```

time: 1710 us -> 158 us (0.09)
  local copies, waits for them, and re-layouts: 1340 us -> 5.72 us
  matrix products: 154 us -> 0 us
  waiting for transfers between devices: 95.3 us -> 15.4 us
  Pallas kernels: 0 us -> 67.1 us
  starting transfers between devices: 11.5 us -> 51.1 us
  other arithmetic: 50.1 us -> 16.8 us
  blocking collectives: 23.9 us -> 0 us
    reshape x9 -> x0, local copies, waits for them, and re-layouts: 614 us -> none  [toeplitz_block(): tiled.reshape(filter_count, block_rows, 2 * block_rows - 1)]
    while x33 -> x0, local copies, waits for them, and re-layouts: 418 us -> none
    slice x42 -> x7, local copies, waits for them, and re-layouts: 207 us -> 1.84 us  [the longest x1 1.03 us: shards(): unit_sum[width:2 * width]]
    dot_general x21 -> x0, matrix products: 154 us -> none  [the longest x6 79.8 us: add_source(): jnp.einsum('cs,kts->ckt', source, toeplitz, preferred_element_type=jnp.fl...]
    pallas_call x0 -> x13, Pallas kernels: none -> 67.1 us  [the longest x1 12.8 us: spectral_mixed(): pl.pallas_call(mixed_kernel, grid_spec=pltpu.PrefetchScalarGridSpec(num_s...]
    reduce_scatter x4 -> x0, waiting for transfers between devices: 61.8 us -> none  [the longest x1 61.7 us: shards(): lax.psum_scatter(jnp.dot(filtered, flat_mixing, preferred_element_type=jn...]
    another operation x17 -> x0, local copies, waits for them, and re-layouts: 57.3 us -> none  [the longest x9 29.5 us: toeplitz_block(): jnp.tile(skewed, (1, block_rows))[:, :block_rows * (2 * block_rows - 1)]]
    ppermute x0 -> x27, starting transfers between devices: none -> 39.3 us  [swap(): return lax.ppermute(values, axis, [(i, i ^ mask) for i in range(count)])]
  transfers between devices with their start and end apart: 8 -> 29, of which waited for: 4 -> 8; matrix products, arithmetic and copies ran while one was open for 60% -> 7% of each run, Pallas kernels for 0% -> 38%
where the time goes in v2:
time: 158 us; the launch traced here: 157 us
  Pallas kernels  67.1 us (42%)
  starting transfers between devices  51.1 us (32%)
  other arithmetic  16.8 us (11%)
  waiting for transfers between devices  15.4 us (10%)
  local copies, waits for them, and re-layouts  5.72 us (4%)
    ppermute x27, starting transfers between devices, swap(): return lax.ppermute(values, axis, [(i, i ^ mask) for i in range(count)])  39.3 us
    pallas_call x1, Pallas kernels, spectral_mixed(): pl.pallas_call(mixed_kernel, grid_spec=pltpu.PrefetchScalarGridSpec(num_s...  12.8 us
    ppermute x27, waiting for transfers between devices, swap(): return lax.ppermute(values, axis, [(i, i ^ mask) for i in range(count)])  12.2 us
    pallas_call x1, Pallas kernels, spectral_back(): pl.pallas_call(spectral_back_kernel, grid=(steps,), in_specs=[whole(filte...  10.1 us
    pallas_call x2, Pallas kernels, mixing_grad(): pl.pallas_call(functools.partial(mixing_grad_kernel, bool(which)), grid=(...  9.73 us
    pallas_call x2, Pallas kernels, spectral_maps(): pl.pallas_call(functools.partial(maps_kernel, start), grid=(count // PER_...  9.03 us
    all_to_all x1, starting transfers between devices, shards(): came = lax.all_to_all(back, 'chan', split_axis=0, concat_axis=0)  8.01 us
    pallas_call x1, Pallas kernels, own_mixing_grad(): pl.pallas_call(own_mixing_grad_kernel, grid=(steps,), in_specs=[pl.BlockS...  7.58 us
  transfers between devices with their start and end apart: 29, of which 8 were waited for; matrix products, arithmetic and copies ran while one was open for 7% of the time, Pallas kernels for 38%

profile of v2, /device:TPU:0, one launch (start us, length us, event | category | flops | bytes accessed | tf_op | source)
XLA Modules:
  0.0 157.1 jit_solution(11886858335521630407)
XLA Ops:
  0.6 4.1 %collective-permute-start.3 = (bf16[1,128,512]{2,1,0:T(8,128)(2,1)}, bf16[1,128,512]{2,1,0:T(8,128)(2,1)S(1)}, u32[]{:S(2)}, u32[]{:S(2)}) collective-permute-start(bf16[1,128,512]{2,1,0:T(8,128)(2,1)} %cotangent.1), channel_id=1, source_target_pairs={{0,4},{1,5},{2,6},{3,7},{4,0},{5,1},{6,2},{7,3},{8,12},{9,13},{10,... | collective-permute-start | bytes 393224 | tf_op jit(solution)/shard_map/ppermute | solution.py:738
  4.7 1.8 %first_norm.1 = bf16[8,80,128]{2,1,0:T(8,128)(2,1)} custom-call(s32[1]{0:T(128)} %bitcast.1.me, bf16[1,128,512]{2,1,0:T(8,128)(2,1)} %hidden.3, f32[1,512]{1,0:T(1,128)} %bitcast.49, s32[1,1024]{1,0:T(1,128)} %segments.1), custom_call_target="tpu_custom_call" | custom-call | tf_op jit(solution)/shard_map/first_norm/pallas_call | solution.py:67
  6.5 3.8 %all-to-all-start = ((bf16[8,80,128]{2,1,0:T(8,128)(2,1)}), bf16[8,80,128]{2,1,0:T(8,128)(2,1)S(1)}, u32[]{:S(2)}, u32[]{:S(2)}) async-start(bf16[8,80,128]{2,1,0:T(8,128)(2,1)} %first_norm.1), calls=%async_computation | async-start | bytes 327680 | tf_op jit(solution)/shard_map/all_to_all | solution.py:843
  10.3 1.0 collective-permute-done.3
  11.3 1.0 maximum_select_fusion.3
  12.3 1.6 %collective-permute-start.6 = (bf16[2,64,512]{2,1,0:T(8,128)(2,1)S(1)}, bf16[2,64,512]{2,1,0:T(8,128)(2,1)S(1)}, u32[]{:S(2)}, u32[]{:S(2)}) collective-permute-start(bf16[2,64,512]{2,1,0:T(8,128)(2,1)S(1)} %get-tuple-element.114), channel_id=1, source_target_pairs={{0,1},{1,0},{2,3},{3,2},{4,5},{5,4},{6,7},{7,6},{8,9},{9,8},{10,11... | collective-permute-start | bytes 393224 | tf_op jit(solution)/shard_map/ppermute | solution.py:738
  13.9 1.0 collective-permute-start.4
  14.9 3.1 %all-to-all-done.pieces = bf16[8,80,128]{2,1,0:T(8,128)(2,1)S(1)} async-done(((bf16[8,80,128]{2,1,0:T(8,128)(2,1)}), bf16[8,80,128]{2,1,0:T(8,128)(2,1)S(1)}, u32[]{:S(2)}, u32[]{:S(2)}) %all-to-all-start) | async-done | bytes 163872 | tf_op jit(solution)/shard_map/all_to_all | solution.py:843
  18.1 1.5 collective-permute-start.2
  19.7 1.2 collective-permute-start.5
  20.9 12.8 %spectral_mixed.1 = (bf16[2,24,64,1024]{3,2,1,0:T(8,128)(2,1)}, bf16[3,64,1024]{2,1,0:T(8,128)(2,1)S(1)}, bf16[2,2,256,128]{3,2,1,0:T(8,128)(2,1)S(1)}, bf16[2,2...) custom-call(s32[1]{0:T(128)} %bitcast.1.me, ...), custom_call_target="tpu_custom_call" | custom-call | tf_op jit(solution)/shard_map/spectral_mixed/pallas_call | solution.py:405
  33.8 1.2 collective-permute-start.1
  35.0 1.9 %collective-permute-start = (bf16[2,2,256,128]{3,2,0,1:T(8,128)(2,1)S(1)}, bf16[2,2,256,128]{3,2,0,1:T(8,128)(2,1)S(1)}, u32[]{:S(2)}, u32[]{:S(2)}) collective-permute-start(bf16[2,2,256,128]{3,2,0,1:T(8,128)(2,1)S(1)} %copy.20), channel_id=1, source_target_pairs={{0,1},{1,0},{2,3},{3,2},{4,5},{5,4},{6,7},{7,6},{8,9},{9,8},{10,11... | collective-permute-start | bytes 786440 | tf_op jit(solution)/shard_map/ppermute | solution.py:738
  36.8 4.5 %spectral_maps.2 = (bf16[2,24,64,1024]{3,2,1,0:T(8,128)(2,1)}, bf16[3,64,1024]{2,1,0:T(8,128)(2,1)S(1)}) custom-call(bf16[24,1024]{1,0:T(8,128)(2,1)S(1)} %copy-done.11, bf16[8,80,128]{2,1,0:T(8,128)(2,1)S(1)} %collective-permute-done.2.pieces), custom_call_target="tpu_custom_call" | custom-call | flops 4831838208 | bytes 4194304 | tf_op jit(solution)/shard_map/spectral_maps/pallas_call | solution.py:372
  42.5 1.1 collective-permute-start.9
  43.6 3.7 %collective-permute-done.8 = bf16[2,1,256,128]{3,2,0,1:T(8,128)(2,1)S(1)} collective-permute-done((bf16[2,1,256,128]{3,2,0,1:T(8,128)(2,1)S(1)}, bf16[2,1,256,128]{3,2,0,1:T(8,128)(2,1)S(1)}, u32[]{:S(2)}, u32[]{:S(2)}) %collective-permute-start.8) | collective-permute-done | bytes 131104 | tf_op jit(solution)/shard_map/ppermute | solution.py:738
  47.6 2.7 %collective-permute-start.10 = (bf16[1,512,128]{2,1,0:T(8,128)(2,1)S(1)}, bf16[1,512,128]{2,1,0:T(8,128)(2,1)S(1)}, u32[]{:S(2)}, u32[]{:S(2)}) collective-permute-start(bf16[1,512,128]{2,1,0:T(8,128)(2,1)S(1)} %fusion.2), channel_id=1, source_target_pairs={{0,4},{1,5},{2,6},{3,7},{4,0},{5,1},{6,2},{7,3},{8,12},{9,13},{10,... | collective-permute-start | bytes 393224 | tf_op jit(solution)/shard_map/ppermute | solution.py:738
  50.4 3.2 %collective-permute-done.10 = bf16[1,512,128]{2,1,0:T(8,128)(2,1)S(1)} collective-permute-done((bf16[1,512,128]{2,1,0:T(8,128)(2,1)S(1)}, bf16[1,512,128]{2,1,0:T(8,128)(2,1)S(1)}, u32[]{:S(2)}, u32[]{:S(2)}) %collective-permute-start.10) | collective-permute-done | bytes 131104 | tf_op jit(solution)/shard_map/ppermute | solution.py:738
  53.6 6.8 %feed_forward.1 = (bf16[1,128,512]{2,1,0:T(8,128)(2,1)}, bf16[144,512]{1,0:T(8,128)(2,1)S(1)}, f32[128,512]{1,0:T(8,128)S(1)}, bf16[128,512]{1,0:T(8,128)(2,1)S(1)}) custom-call(s32[1]{0:T(128)} %bitcast.bit, bf16[2,512,128]{2,1,0:T(8,128)(2,1)S(1)} %pad_maximum_fusion.2.held, bf16[512,128]{1,0:T(8,128)(2,1)S(1)} %bitcast.41, ...), custom_call_target="tpu_custom_call" | custom-call | tf_op jit(solution)/shard_map/feed_forward/pallas_call | solution.py:565
  60.4 2.8 %collective-permute-start.11 = (bf16[1,128,512]{2,1,0:T(8,128)(2,1)S(1)}, bf16[1,128,512]{2,1,0:T(8,128)(2,1)S(1)}, u32[]{:S(2)}, u32[]{:S(2)}) collective-permute-start(bf16[1,128,512]{2,1,0:T(8,128)(2,1)S(1)} %bitcast.39), channel_id=1, source_target_pairs={{0,4},{1,5},{2,6},{3,7},{4,0},{5,1},{6,2},{7,3},{8,12},{9,13},{10,... | collective-permute-start | bytes 393224 | tf_op jit(solution)/shard_map/ppermute | solution.py:738
  63.3 4.6 %spectral_maps.3 = (bf16[2,24,64,1024]{3,2,1,0:T(8,128)(2,1)}, bf16[3,64,1024]{2,1,0:T(8,128)(2,1)}) custom-call(bf16[24,1024]{1,0:T(8,128)(2,1)S(1)} %copy-done.11, bf16[8,80,128]{2,1,0:T(8,128)(2,1)S(1)} %collective-permute-done.2.pieces, bf16[2,24,64,1024]{3,2,1,0:T(8,128)(2,1)} %get-tuple-element.67.refs_0_), custom_call_target="tpu_custom_call", output_to_operand_aliasing={{0}: (2, {})} | custom-call | flops 4831838208 | bytes 4194304 | tf_op jit(solution)/shard_map/spectral_maps/pallas_call | solution.py:372
  67.9 1.1 collective-permute-start.14
  69.0 3.8 %collective-permute-start.12 = (bf16[2,64,512]{2,1,0:T(8,128)(2,1)S(1)}, bf16[2,64,512]{2,1,0:T(8,128)(2,1)S(1)}, u32[]{:S(2)}, u32[]{:S(2)}) collective-permute-start(bf16[2,64,512]{2,1,0:T(8,128)(2,1)S(1)} %get-tuple-element.113), channel_id=1, source_target_pairs={{0,2},{1,3},{2,0},{3,1},{4,6},{5,7},{6,4},{7,5},{8,10},{9,11},{10,... | collective-permute-start | bytes 393224 | tf_op jit(solution)/shard_map/ppermute | solution.py:738
  72.8 3.4 %collective-permute-start.16 = (bf16[1,144,512]{2,1,0:T(8,128)(2,1)S(1)}, bf16[1,144,512]{2,1,0:T(8,128)(2,1)S(1)}, u32[]{:S(2)}, u32[]{:S(2)}) collective-permute-start(bf16[1,144,512]{2,1,0:T(8,128)(2,1)S(1)} %bitcast.37), channel_id=1, source_target_pairs={{0,4},{1,5},{2,6},{3,7},{4,0},{5,1},{6,2},{7,3},{8,12},{9,13},{10,... | collective-permute-start | bytes 442376 | tf_op jit(solution)/shard_map/ppermute | solution.py:738
  76.3 1.9 %collective-permute-start.15 = (bf16[2,2,64,512]{3,2,1,0:T(8,128)(2,1)S(1)}, bf16[2,2,64,512]{3,2,1,0:T(8,128)(2,1)S(1)}, u32[]{:S(2)}, u32[]{:S(2)}) collective-permute-start(bf16[2,2,64,512]{3,2,1,0:T(8,128)(2,1)S(1)} %maximum_select_fusion.8.part2), channel_id=1, source_target_pairs={{0,2},{1,3},{2,0},{3,1},{4,6},{5,7},{6,4},{7,5},{8,10},{9,11},{10,... | collective-permute-start | bytes 786440 | tf_op jit(solution)/shard_map/ppermute | solution.py:738
  78.3 1.1 collective-permute-start.13
  79.6 1.0 collective-permute-start.19
  81.2 2.8 %collective-permute-start.17 = (bf16[2,64,512]{2,1,0:T(8,128)(2,1)}, bf16[2,64,512]{2,1,0:T(8,128)(2,1)}, u32[]{:S(2)}, u32[]{:S(2)}) collective-permute-start(bf16[2,64,512]{2,1,0:T(8,128)(2,1)} %get-tuple-element.108), channel_id=1, source_target_pairs={{0,2},{1,3},{2,0},{3,1},{4,6},{5,7},{6,4},{7,5},{8,10},{9,11},{10,... | collective-permute-start | bytes 393224 | tf_op jit(solution)/shard_map/ppermute | solution.py:738
  84.0 3.9 %collective-permute-done.19 = bf16[2,80,512]{2,1,0:T(8,128)(2,1)S(1)} collective-permute-done((bf16[2,80,512]{2,1,0:T(8,128)(2,1)S(1)}, bf16[2,80,512]{2,1,0:T(8,128)(2,1)S(1)}, u32[]{:S(2)}, u32[]{:S(2)}) %collective-permute-start.19) | collective-permute-done | bytes 163872 | tf_op jit(solution)/shard_map/ppermute | solution.py:738
  87.9 1.8 %collective-permute-start.20 = (bf16[2,2,80,512]{3,2,1,0:T(8,128)(2,1)S(1)}, bf16[2,2,80,512]{3,2,1,0:T(8,128)(2,1)S(1)}, u32[]{:S(2)}, u32[]{:S(2)}) collective-permute-start(bf16[2,2,80,512]{3,2,1,0:T(8,128)(2,1)S(1)} %maximum_select_fusion.1.refs_2_), channel_id=1, source_target_pairs={{0,2},{1,3},{2,0},{3,1},{4,6},{5,7},{6,4},{7,5},{8,10},{9,11},{10,... | collective-permute-start | bytes 983048 | tf_op jit(solution)/shard_map/ppermute | solution.py:738
  90.4 1.3 place.1.grads
  91.7 1.7 %collective-permute-start.22 = (bf16[1024,512]{1,0:T(8,128)(2,1)S(1)}, bf16[1024,512]{1,0:T(8,128)(2,1)}, u32[]{:S(2)}, u32[]{:S(2)}) collective-permute-start(bf16[1024,512]{1,0:T(8,128)(2,1)S(1)} %place.1.grads), channel_id=1, source_target_pairs={{0,16},{8,24},{16,0},{24,8},{1,17},{9,25},{17,1},{25,9},{2,18},{10... | collective-permute-start | bytes 3145736 | tf_op jit(solution)/shard_map/ppermute | solution.py:738
  93.4 1.0 maximum_select_fusion.9.refs_0_
  95.2 10.1 %spectral_back.1.acc = f32[128,1024]{1,0:T(8,128)S(1)} custom-call(bf16[24,1024]{1,0:T(8,128)(2,1)S(1)} %copy-done.11, bf16[51,64,512]{2,1,0:T(8,128)(2,1)} %lag_mixing.3, bf16[51,64,512]{2,1,0:T(8,128)(2,1)} %lag_mixing.3, bf16[8,80,128]{2,1,0:T(8,128)(2,1)S(1)} %all-to-all-done.pieces, bf16[1024,512]{1,0:T(8,128)(2,1)S(1)} %place.1.grads), custom_call_target="tpu_custom_call" | custom-call | tf_op jit(solution)/shard_map/spectral_back/pallas_call | solution.py:442
  105.3 2.3 %lag_back.1 = (bf16[8,64,128]{2,1,0:T(8,128)(2,1)}, f32[8,128]{1,0:T(8,128)S(1)}) custom-call(f32[128,1024]{1,0:T(8,128)S(1)} %spectral_back.1.acc, bf16[51,64,512]{2,1,0:T(8,128)(2,1)} %lag_mixing.3, bf16[1024,512]{1,0:T(8,128)(2,1)S(1)} %place.1.grads, bf16[3,64,1024]{2,1,0:T(8,128)(2,1)} %copy-done.1, bf16[8,80,128]{2,1,0:T(8,128)(2,1)S(1)} %all-to-all-done.pieces), custom_call_target="tpu_custom_call" | custom-call | tf_op jit(solution)/shard_map/lag_back/pallas_call | solution.py:467
  109.3 3.6 %unit_grads.1 = bf16[1584,256]{1,0:T(8,128)(2,1)S(1)} custom-call(s32[1]{0:T(128)} %bitcast.1.me, bf16[2,2,64,512]{3,2,1,0:T(8,128)(2,1)S(1)} %maximum_select_fusion.9.refs_0_, bf16[2,2,64,512]{3,2,1,0:T(8,128)(2,1)S(1)} %copy-done.10, bf16[2,2,80,512]{3,2,1,0:T(8,128)(2,1)S(1)} %maximum_select_fusion.1.refs_2_, ...), custom_call_target="tpu_custom_call" | custom-call | tf_op jit(solution)/shard_map/unit_grads/pallas_call | solution.py:715
  113.1 7.6 %own_mixing_grad.1 = (bf16[2,24,64,512]{3,2,1,0:T(8,128)(2,1)}, bf16[3,64,512]{2,1,0:T(8,128)(2,1)}) custom-call(bf16[2,24,64,1024]{3,2,1,0:T(8,128)(2,1)} %get-tuple-element.83.maps, bf16[3,64,1024]{2,1,0:T(8,128)(2,1)} %copy-done.1, bf16[1024,512]{1,0:T(8,128)(2,1)S(1)} %place.1.grads), custom_call_target="tpu_custom_call" | custom-call | tf_op jit(solution)/shard_map/own_mixing_grad/pallas_call | solution.py:616
  121.5 8.0 %all-to-all-start.1 = ((bf16[8,64,128]{2,1,0:T(8,128)(2,1)}), bf16[8,64,128]{2,1,0:T(8,128)(2,1)S(1)}, u32[]{:S(2)}, u32[]{:S(2)}) async-start(bf16[8,64,128]{2,1,0:T(8,128)(2,1)} %get-tuple-element.91), calls=%async_computation.1 | async-start | bytes 262144 | tf_op jit(solution)/shard_map/all_to_all | solution.py:875
  129.5 4.7 %mixing_grad.2 = bf16[1536,512]{1,0:T(8,128)(2,1)S(1)} custom-call(bf16[2,24,64,1024]{3,2,1,0:T(8,128)(2,1)} %get-tuple-element.69.maps, bf16[3,64,1024]{2,1,0:T(8,128)(2,1)} %copy-done, bf16[1024,512]{1,0:T(8,128)(2,1)} %collective-permute-done.22.grads, bf16[2,24,64,512]{3,2,1,0:T(8,128)(2,1)} %get-tuple-element.88.own, ...), custom_call_target="tpu_custom_call" | custom-call | tf_op jit(solution)/shard_map/mixing_grad/pallas_call | solution.py:658
  134.2 5.1 %mixing_grad.3 = bf16[1728,512]{1,0:T(8,128)(2,1)S(1)} custom-call(bf16[2,24,64,1024]{3,2,1,0:T(8,128)(2,1)} %get-tuple-element.69.maps, bf16[3,64,1024]{2,1,0:T(8,128)(2,1)} %copy-done, bf16[1024,512]{1,0:T(8,128)(2,1)} %collective-permute-done.22.grads, bf16[2,24,64,512]{3,2,1,0:T(8,128)(2,1)} %get-tuple-element.88.own, ...), custom_call_target="tpu_custom_call" | custom-call | tf_op jit(solution)/shard_map/mixing_grad/pallas_call | solution.py:658
  139.3 2.3 %fusion.4 = (f32[792,256]{1,0:T(8,128)}, bf16[792,256]{1,0:T(8,128)(2,1)}) fusion(bf16[792,256]{1,0:T(8,128)(2,1)} %collective-permute-done.23, bf16[792,256]{1,0:T(8,128)(2,1)} %add_convert_fusion.3), kind=kLoop, calls=%fused_computation.38 | loop fusion | flops 1013760 | bytes 2027520 | tf_op jit(solution)/shard_map/convert_element_type | solution.py:830
  142.1 2.0 %first_norm_back.1 = f32[1,128,512]{2,1,0:T(8,128)} custom-call(bf16[8,64,128]{2,1,0:T(8,128)(2,1)} %copy-done.16, bf16[1,128,512]{2,1,0:T(8,128)(2,1)} %hidden.3, f32[1,512]{1,0:T(1,128)} %bitcast.50, f32[128,512]{1,0:T(8,128)} %copy-done.8), custom_call_target="tpu_custom_call" | custom-call | tf_op jit(solution)/shard_map/first_norm_back/pallas_call | solution.py:91
  144.2 1.1 convert_element_type.97
  147.0 1.3 fusion.3
  148.3 1.0 fusion.7
  149.3 1.8 %add_convert_fusion.1 = bf16[1536,512]{1,0:T(8,128)(2,1)S(1)} fusion(bf16[1536,512]{1,0:T(8,128)(2,1)} %collective-permute-done.24, bf16[1536,512]{1,0:T(8,128)(2,1)S(1)} %mixing_grad.2), kind=kLoop, calls=%fused_computation.2 | loop fusion | flops 3145728 | bytes 4718592 | tf_op jit(solution)/shard_map/convert_element_type | solution.py:895
  151.2 2.0 %add_convert_fusion = bf16[1728,512]{1,0:T(8,128)(2,1)S(1)} fusion(bf16[1728,512]{1,0:T(8,128)(2,1)} %collective-permute-done.25, bf16[1728,512]{1,0:T(8,128)(2,1)S(1)} %mixing_grad.3), kind=kLoop, calls=%fused_computation | loop fusion | flops 3538944 | bytes 5308416 | tf_op jit(solution)/shard_map/convert_element_type | solution.py:895
  153.4 3.8 %convert.12 = f32[51,64,512]{2,1,0:T(8,128)} convert(bf16[51,64,512]{2,1,0:T(8,128)(2,1)S(1)} %bitcast.43) | non-fusion elementwise | flops 1671168 | bytes 10027008 | tf_op jit(solution)/shard_map/reshape | solution.py:897
  (98 shorter events, 9.3 us)
Async XLA Ops:
  0.6 20.3 %copy-start.11 = (bf16[24,1024]{1,0:T(8,128)(2,1)S(1)}, bf16[24,1024]{1,0:T(8,128)(2,1)}, u32[]{:S(2)}) copy-start(bf16[24,1024]{1,0:T(8,128)(2,1)} %filters.7) | copy-start | bytes 147460
  0.6 10.6 %collective-permute-start.3 = (bf16[1,128,512]{2,1,0:T(8,128)(2,1)}, bf16[1,128,512]{2,1,0:T(8,128)(2,1)S(1)}, u32[]{:S(2)}, u32[]{:S(2)}) collective-permute-start(bf16[1,128,512]{2,1,0:T(8,128)(2,1)} %cotangent.1), channel_id=1, source_target_pairs={{0,4},{1,5},{2,6},{3,7},{4,0},{5,1},{6,2},{7,3},{8,12},{9,13},{10,... | collective-permute-start | bytes 393224 | tf_op jit(solution)/shard_map/ppermute | solution.py:738
  6.5 11.5 %all-to-all-start = ((bf16[8,80,128]{2,1,0:T(8,128)(2,1)}), bf16[8,80,128]{2,1,0:T(8,128)(2,1)S(1)}, u32[]{:S(2)}, u32[]{:S(2)}) async-start(bf16[8,80,128]{2,1,0:T(8,128)(2,1)} %first_norm.1), calls=%async_computation | async-start | bytes 327680 | tf_op jit(solution)/shard_map/all_to_all | solution.py:843
  12.3 7.3 %collective-permute-start.6 = (bf16[2,64,512]{2,1,0:T(8,128)(2,1)S(1)}, bf16[2,64,512]{2,1,0:T(8,128)(2,1)S(1)}, u32[]{:S(2)}, u32[]{:S(2)}) collective-permute-start(bf16[2,64,512]{2,1,0:T(8,128)(2,1)S(1)} %get-tuple-element.114), channel_id=1, source_target_pairs={{0,1},{1,0},{2,3},{3,2},{4,5},{5,4},{6,7},{7,6},{8,9},{9,8},{10,11... | collective-permute-start | bytes 393224 | tf_op jit(solution)/shard_map/ppermute | solution.py:738
  13.9 5.8 %collective-permute-start.4 = (bf16[2,64,512]{2,1,0:T(8,128)(2,1)S(1)}, bf16[2,64,512]{2,1,0:T(8,128)(2,1)S(1)}, u32[]{:S(2)}, u32[]{:S(2)}) collective-permute-start(bf16[2,64,512]{2,1,0:T(8,128)(2,1)S(1)} %get-tuple-element.117), channel_id=1, source_target_pairs={{0,2},{1,3},{2,0},{3,1},{4,6},{5,7},{6,4},{7,5},{8,10},{9,11},{10,... | collective-permute-start | bytes 393224 | tf_op jit(solution)/shard_map/ppermute | solution.py:738
  18.1 18.8 %collective-permute-start.2 = (bf16[8,80,128]{2,1,0:T(8,128)(2,1)S(1)}, bf16[8,80,128]{2,1,0:T(8,128)(2,1)S(1)}, u32[]{:S(2)}, u32[]{:S(2)}) collective-permute-start(bf16[8,80,128]{2,1,0:T(8,128)(2,1)S(1)} %all-to-all-done.pieces), channel_id=1, source_target_pairs={{0,16},{8,24},{16,0},{24,8},{1,17},{9,25},{17,1},{25,9},{2,18},{10... | collective-permute-start | bytes 491528 | tf_op jit(solution)/shard_map/ppermute | solution.py:738
  19.6 22.6 %collective-permute-start.7 = (bf16[2,2,64,512]{3,2,1,0:T(8,128)(2,1)S(1)}, bf16[2,2,64,512]{3,2,1,0:T(8,128)(2,1)S(1)}, u32[]{:S(2)}, u32[]{:S(2)}) collective-permute-start(bf16[2,2,64,512]{3,2,1,0:T(8,128)(2,1)S(1)} %maximum_select_fusion.5.refs_6_), channel_id=1, source_target_pairs={{0,2},{1,3},{2,0},{3,1},{4,6},{5,7},{6,4},{7,5},{8,10},{9,11},{10,... | collective-permute-start | bytes 786440 | tf_op jit(solution)/shard_map/ppermute | solution.py:738
  19.7 22.5 %collective-permute-start.5 = (bf16[2,2,64,512]{3,2,1,0:T(8,128)(2,1)S(1)}, bf16[2,2,64,512]{3,2,1,0:T(8,128)(2,1)S(1)}, u32[]{:S(2)}, u32[]{:S(2)}) collective-permute-start(bf16[2,2,64,512]{3,2,1,0:T(8,128)(2,1)S(1)} %maximum_select_fusion.4.refs_4_), channel_id=1, source_target_pairs={{0,1},{1,0},{2,3},{3,2},{4,5},{5,4},{6,7},{7,6},{8,9},{9,8},{10,11... | collective-permute-start | bytes 786440 | tf_op jit(solution)/shard_map/ppermute | solution.py:738
  33.7 7.6 %copy-start.1 = (bf16[3,64,1024]{2,1,0:T(8,128)(2,1)}, bf16[3,64,1024]{2,1,0:T(8,128)(2,1)S(1)}, u32[]{:S(2)}) copy-start(bf16[3,64,1024]{2,1,0:T(8,128)(2,1)S(1)} %get-tuple-element.72.inputs.lags) | copy-start | bytes 1179652
  33.8 8.3 %collective-permute-start.1 = (bf16[2,2,256,128]{3,2,0,1:T(8,128)(2,1)S(1)}, bf16[2,2,256,128]{3,2,0,1:T(8,128)(2,1)S(1)}, u32[]{:S(2)}, u32[]{:S(2)}) collective-permute-start(bf16[2,2,256,128]{3,2,0,1:T(8,128)(2,1)S(1)} %copy.22), channel_id=1, source_target_pairs={{0,2},{1,3},{2,0},{3,1},{4,6},{5,7},{6,4},{7,5},{8,10},{9,11},{10,... | collective-permute-start | bytes 786440 | tf_op jit(solution)/shard_map/ppermute | solution.py:738
  35.0 7.2 %collective-permute-start = (bf16[2,2,256,128]{3,2,0,1:T(8,128)(2,1)S(1)}, bf16[2,2,256,128]{3,2,0,1:T(8,128)(2,1)S(1)}, u32[]{:S(2)}, u32[]{:S(2)}) collective-permute-start(bf16[2,2,256,128]{3,2,0,1:T(8,128)(2,1)S(1)} %copy.20), channel_id=1, source_target_pairs={{0,1},{1,0},{2,3},{3,2},{4,5},{5,4},{6,7},{7,6},{8,9},{9,8},{10,11... | collective-permute-start | bytes 786440 | tf_op jit(solution)/shard_map/ppermute | solution.py:738
  41.3 0.7 copy-start
  42.1 11.5 %copy-start.2 = (bf16[1,128,512]{2,1,0:T(8,128)(2,1)S(1)}, bf16[1,128,512]{2,1,0:T(8,128)(2,1)}, u32[]{:S(2)}) copy-start(bf16[1,128,512]{2,1,0:T(8,128)(2,1)} %hidden.3) | copy-start | bytes 393220
  42.1 11.5 %copy-start.3 = (bf16[1,128,512]{2,1,0:T(8,128)(2,1)S(1)}, bf16[1,128,512]{2,1,0:T(8,128)(2,1)}, u32[]{:S(2)}) copy-start(bf16[1,128,512]{2,1,0:T(8,128)(2,1)} %cotangent.1) | copy-start | bytes 393220
  42.1 11.5 %copy-start.12 = (f32[512]{0:T(512)S(1)}, f32[512]{0:T(512)}, u32[]{:S(2)}) copy-start(f32[512]{0:T(512)} %param.15) | copy-start | bytes 6148
  42.2 18.2 %copy-start.4 = (bf16[2,2,64,512]{3,2,1,0:T(8,128)(2,1)}, bf16[2,2,64,512]{3,2,1,0:T(8,128)(2,1)S(1)}, u32[]{:S(2)}) copy-start(bf16[2,2,64,512]{3,2,1,0:T(8,128)(2,1)S(1)} %collective-permute-done.7.refs_7_) | copy-start | bytes 786436
  42.3 18.2 %copy-start.6 = (bf16[2,2,64,512]{3,2,1,0:T(8,128)(2,1)}, bf16[2,2,64,512]{3,2,1,0:T(8,128)(2,1)S(1)}, u32[]{:S(2)}) copy-start(bf16[2,2,64,512]{3,2,1,0:T(8,128)(2,1)S(1)} %collective-permute-done.5.refs_5_) | copy-start | bytes 786436
  42.3 5.0 %collective-permute-start.8 = (bf16[2,1,256,128]{3,2,0,1:T(8,128)(2,1)S(1)}, bf16[2,1,256,128]{3,2,0,1:T(8,128)(2,1)S(1)}, u32[]{:S(2)}, u32[]{:S(2)}) collective-permute-start(bf16[2,1,256,128]{3,2,0,1:T(8,128)(2,1)S(1)} %constant_dynamic-slice_fusion.2), channel_id=1, source_target_pairs={{0,2},{1,3},{2,0},{3,1},{4,6},{5,7},{6,4},{7,5},{8,10},{9,11},{10,... | collective-permute-start | bytes 393224 | tf_op jit(solution)/shard_map/ppermute | solution.py:738
  42.5 5.0 %collective-permute-start.9 = (bf16[2,1,256,128]{3,2,0,1:T(8,128)(2,1)S(1)}, bf16[2,1,256,128]{3,2,0,1:T(8,128)(2,1)S(1)}, u32[]{:S(2)}, u32[]{:S(2)}) collective-permute-start(bf16[2,1,256,128]{3,2,0,1:T(8,128)(2,1)S(1)} %constant_dynamic-slice_fusion.1), channel_id=1, source_target_pairs={{0,1},{1,0},{2,3},{3,2},{4,5},{5,4},{6,7},{7,6},{8,9},{9,8},{10,11... | collective-permute-start | bytes 393224 | tf_op jit(solution)/shard_map/ppermute | solution.py:738
  47.6 5.9 %collective-permute-start.10 = (bf16[1,512,128]{2,1,0:T(8,128)(2,1)S(1)}, bf16[1,512,128]{2,1,0:T(8,128)(2,1)S(1)}, u32[]{:S(2)}, u32[]{:S(2)}) collective-permute-start(bf16[1,512,128]{2,1,0:T(8,128)(2,1)S(1)} %fusion.2), channel_id=1, source_target_pairs={{0,4},{1,5},{2,6},{3,7},{4,0},{5,1},{6,2},{7,3},{8,12},{9,13},{10,... | collective-permute-start | bytes 393224 | tf_op jit(solution)/shard_map/ppermute | solution.py:738
  60.4 7.4 %copy-start.8 = (f32[128,512]{1,0:T(8,128)}, f32[128,512]{1,0:T(8,128)S(1)}, u32[]{:S(2)}) copy-start(f32[128,512]{1,0:T(8,128)S(1)} %get-tuple-element.94.grad) | copy-start | bytes 786436
  60.4 7.4 %collective-permute-start.11 = (bf16[1,128,512]{2,1,0:T(8,128)(2,1)S(1)}, bf16[1,128,512]{2,1,0:T(8,128)(2,1)S(1)}, u32[]{:S(2)}, u32[]{:S(2)}) collective-permute-start(bf16[1,128,512]{2,1,0:T(8,128)(2,1)S(1)} %bitcast.39), channel_id=1, source_target_pairs={{0,4},{1,5},{2,6},{3,7},{4,0},{5,1},{6,2},{7,3},{8,12},{9,13},{10,... | collective-permute-start | bytes 393224 | tf_op jit(solution)/shard_map/ppermute | solution.py:738
  67.9 8.3 %collective-permute-start.14 = (bf16[2,64,512]{2,1,0:T(8,128)(2,1)S(1)}, bf16[2,64,512]{2,1,0:T(8,128)(2,1)S(1)}, u32[]{:S(2)}, u32[]{:S(2)}) collective-permute-start(bf16[2,64,512]{2,1,0:T(8,128)(2,1)S(1)} %get-tuple-element.110), channel_id=1, source_target_pairs={{0,1},{1,0},{2,3},{3,2},{4,5},{5,4},{6,7},{7,6},{8,9},{9,8},{10,11... | collective-permute-start | bytes 393224 | tf_op jit(solution)/shard_map/ppermute | solution.py:738
  69.0 9.2 %collective-permute-start.12 = (bf16[2,64,512]{2,1,0:T(8,128)(2,1)S(1)}, bf16[2,64,512]{2,1,0:T(8,128)(2,1)S(1)}, u32[]{:S(2)}, u32[]{:S(2)}) collective-permute-start(bf16[2,64,512]{2,1,0:T(8,128)(2,1)S(1)} %get-tuple-element.113), channel_id=1, source_target_pairs={{0,2},{1,3},{2,0},{3,1},{4,6},{5,7},{6,4},{7,5},{8,10},{9,11},{10,... | collective-permute-start | bytes 393224 | tf_op jit(solution)/shard_map/ppermute | solution.py:738
  72.8 6.7 %collective-permute-start.16 = (bf16[1,144,512]{2,1,0:T(8,128)(2,1)S(1)}, bf16[1,144,512]{2,1,0:T(8,128)(2,1)S(1)}, u32[]{:S(2)}, u32[]{:S(2)}) collective-permute-start(bf16[1,144,512]{2,1,0:T(8,128)(2,1)S(1)} %bitcast.37), channel_id=1, source_target_pairs={{0,4},{1,5},{2,6},{3,7},{4,0},{5,1},{6,2},{7,3},{8,12},{9,13},{10,... | collective-permute-start | bytes 442376 | tf_op jit(solution)/shard_map/ppermute | solution.py:738
  76.3 14.2 %copy-start.14 = (bf16[2,2,64,512]{3,2,1,0:T(8,128)(2,1)}, bf16[2,2,64,512]{3,2,1,0:T(8,128)(2,1)S(1)}, u32[]{:S(2)}) copy-start(bf16[2,2,64,512]{3,2,1,0:T(8,128)(2,1)S(1)} %maximum_select_fusion.8.part2) | copy-start | bytes 786436
  76.3 13.4 %collective-permute-start.15 = (bf16[2,2,64,512]{3,2,1,0:T(8,128)(2,1)S(1)}, bf16[2,2,64,512]{3,2,1,0:T(8,128)(2,1)S(1)}, u32[]{:S(2)}, u32[]{:S(2)}) collective-permute-start(bf16[2,2,64,512]{3,2,1,0:T(8,128)(2,1)S(1)} %maximum_select_fusion.8.part2), channel_id=1, source_target_pairs={{0,2},{1,3},{2,0},{3,1},{4,6},{5,7},{6,4},{7,5},{8,10},{9,11},{10,... | collective-permute-start | bytes 786440 | tf_op jit(solution)/shard_map/ppermute | solution.py:738
  78.3 12.2 %copy-start.15 = (bf16[2,2,64,512]{3,2,1,0:T(8,128)(2,1)}, bf16[2,2,64,512]{3,2,1,0:T(8,128)(2,1)S(1)}, u32[]{:S(2)}) copy-start(bf16[2,2,64,512]{3,2,1,0:T(8,128)(2,1)S(1)} %maximum_select_fusion.7.part0) | copy-start | bytes 786436
  78.3 12.2 %collective-permute-start.13 = (bf16[2,2,64,512]{3,2,1,0:T(8,128)(2,1)S(1)}, bf16[2,2,64,512]{3,2,1,0:T(8,128)(2,1)}, u32[]{:S(2)}, u32[]{:S(2)}) collective-permute-start(bf16[2,2,64,512]{3,2,1,0:T(8,128)(2,1)S(1)} %maximum_select_fusion.7.part0), channel_id=1, source_target_pairs={{0,1},{1,0},{2,3},{3,2},{4,5},{5,4},{6,7},{7,6},{8,9},{9,8},{10,11... | collective-permute-start | bytes 786440 | tf_op jit(solution)/shard_map/ppermute | solution.py:738
  79.6 8.3 %collective-permute-start.19 = (bf16[2,80,512]{2,1,0:T(8,128)(2,1)S(1)}, bf16[2,80,512]{2,1,0:T(8,128)(2,1)S(1)}, u32[]{:S(2)}, u32[]{:S(2)}) collective-permute-start(bf16[2,80,512]{2,1,0:T(8,128)(2,1)S(1)} %get-tuple-element.106), channel_id=1, source_target_pairs={{0,1},{1,0},{2,3},{3,2},{4,5},{5,4},{6,7},{7,6},{8,9},{9,8},{10,11... | collective-permute-start | bytes 491528 | tf_op jit(solution)/shard_map/ppermute | solution.py:738
  81.2 12.2 %collective-permute-start.17 = (bf16[2,64,512]{2,1,0:T(8,128)(2,1)}, bf16[2,64,512]{2,1,0:T(8,128)(2,1)}, u32[]{:S(2)}, u32[]{:S(2)}) collective-permute-start(bf16[2,64,512]{2,1,0:T(8,128)(2,1)} %get-tuple-element.108), channel_id=1, source_target_pairs={{0,2},{1,3},{2,0},{3,1},{4,6},{5,7},{6,4},{7,5},{8,10},{9,11},{10,... | collective-permute-start | bytes 393224 | tf_op jit(solution)/shard_map/ppermute | solution.py:738
  87.9 20.4 %collective-permute-start.20 = (bf16[2,2,80,512]{3,2,1,0:T(8,128)(2,1)S(1)}, bf16[2,2,80,512]{3,2,1,0:T(8,128)(2,1)S(1)}, u32[]{:S(2)}, u32[]{:S(2)}) collective-permute-start(bf16[2,2,80,512]{3,2,1,0:T(8,128)(2,1)S(1)} %maximum_select_fusion.1.refs_2_), channel_id=1, source_target_pairs={{0,2},{1,3},{2,0},{3,1},{4,6},{5,7},{6,4},{7,5},{8,10},{9,11},{10,... | collective-permute-start | bytes 983048 | tf_op jit(solution)/shard_map/ppermute | solution.py:738
  89.7 0.7 copy-start.17
  91.7 29.8 %collective-permute-start.22 = (bf16[1024,512]{1,0:T(8,128)(2,1)S(1)}, bf16[1024,512]{1,0:T(8,128)(2,1)}, u32[]{:S(2)}, u32[]{:S(2)}) collective-permute-start(bf16[1024,512]{1,0:T(8,128)(2,1)S(1)} %place.1.grads), channel_id=1, source_target_pairs={{0,16},{8,24},{16,0},{24,8},{1,17},{9,25},{17,1},{25,9},{2,18},{10... | collective-permute-start | bytes 3145736 | tf_op jit(solution)/shard_map/ppermute | solution.py:738
  94.4 13.3 %collective-permute-start.18 = (bf16[2,2,64,512]{3,2,1,0:T(8,128)(2,1)S(1)}, bf16[2,2,64,512]{3,2,1,0:T(8,128)(2,1)S(1)}, u32[]{:S(2)}, u32[]{:S(2)}) collective-permute-start(bf16[2,2,64,512]{3,2,1,0:T(8,128)(2,1)S(1)} %maximum_select_fusion.9.refs_0_), channel_id=1, source_target_pairs={{0,1},{1,0},{2,3},{3,2},{4,5},{5,4},{6,7},{7,6},{8,9},{9,8},{10,11... | collective-permute-start | bytes 786440 | tf_op jit(solution)/shard_map/ppermute | solution.py:738
  105.3 3.1 %copy-start.5 = (bf16[2,2,64,512]{3,2,1,0:T(8,128)(2,1)S(1)}, bf16[2,2,64,512]{3,2,1,0:T(8,128)(2,1)}, u32[]{:S(2)}) copy-start(bf16[2,2,64,512]{3,2,1,0:T(8,128)(2,1)} %copy-done.4) | copy-start | bytes 786436
  105.3 3.0 %copy-start.7 = (bf16[2,2,64,512]{3,2,1,0:T(8,128)(2,1)S(1)}, bf16[2,2,64,512]{3,2,1,0:T(8,128)(2,1)}, u32[]{:S(2)}) copy-start(bf16[2,2,64,512]{3,2,1,0:T(8,128)(2,1)} %copy-done.6) | copy-start | bytes 786436
  107.7 0.7 copy-start.9
  108.4 1.0 copy-start.10
  113.0 7.7 %collective-permute-start.21 = (bf16[792,256]{1,0:T(8,128)(2,1)S(1)}, bf16[792,256]{1,0:T(8,128)(2,1)S(1)}, u32[]{:S(2)}, u32[]{:S(2)}) collective-permute-start(bf16[792,256]{1,0:T(8,128)(2,1)S(1)} %constant_dynamic-slice_fusion), channel_id=1, source_target_pairs={{0,8},{8,0},{16,24},{24,16},{1,9},{9,1},{17,25},{25,17},{2,10},{10... | collective-permute-start | bytes 1216520 | tf_op jit(solution)/shard_map/ppermute | solution.py:738
  121.5 17.8 %collective-permute-start.23 = (bf16[792,256]{1,0:T(8,128)(2,1)}, bf16[792,256]{1,0:T(8,128)(2,1)}, u32[]{:S(2)}, u32[]{:S(2)}) collective-permute-start(bf16[792,256]{1,0:T(8,128)(2,1)} %add_convert_fusion.3), channel_id=1, source_target_pairs={{0,16},{8,24},{16,0},{24,8},{1,17},{9,25},{17,1},{25,9},{2,18},{10... | collective-permute-start | bytes 1216520 | tf_op jit(solution)/shard_map/ppermute | solution.py:738
  121.5 17.8 %all-to-all-start.1 = ((bf16[8,64,128]{2,1,0:T(8,128)(2,1)}), bf16[8,64,128]{2,1,0:T(8,128)(2,1)S(1)}, u32[]{:S(2)}, u32[]{:S(2)}) async-start(bf16[8,64,128]{2,1,0:T(8,128)(2,1)} %get-tuple-element.91), calls=%async_computation.1 | async-start | bytes 262144 | tf_op jit(solution)/shard_map/all_to_all | solution.py:875
  139.3 2.8 %copy-start.16 = (bf16[8,64,128]{2,1,0:T(8,128)(2,1)}, bf16[8,64,128]{2,1,0:T(8,128)(2,1)S(1)}, u32[]{:S(2)}) copy-start(bf16[8,64,128]{2,1,0:T(8,128)(2,1)S(1)} %all-to-all-done.1.came) | copy-start | bytes 393220
  141.6 2.6 %collective-permute-start.26 = (bf16[792,256]{1,0:T(8,128)(2,1)}, bf16[792,256]{1,0:T(8,128)(2,1)}, u32[]{:S(2)}, u32[]{:S(2)}) collective-permute-start(bf16[792,256]{1,0:T(8,128)(2,1)} %get-tuple-element.99), channel_id=1, source_target_pairs={{0,8},{8,0},{16,24},{24,16},{1,9},{9,1},{17,25},{25,17},{2,10},{10... | collective-permute-start | bytes 1216520 | tf_op jit(solution)/shard_map/ppermute | solution.py:738
  141.6 7.7 %collective-permute-start.24 = (bf16[1536,512]{1,0:T(8,128)(2,1)S(1)}, bf16[1536,512]{1,0:T(8,128)(2,1)}, u32[]{:S(2)}, u32[]{:S(2)}) collective-permute-start(bf16[1536,512]{1,0:T(8,128)(2,1)S(1)} %mixing_grad.2), channel_id=1, source_target_pairs={{0,8},{8,0},{16,24},{24,16},{1,9},{9,1},{17,25},{25,17},{2,10},{10... | collective-permute-start | bytes 4718600 | tf_op jit(solution)/shard_map/ppermute | solution.py:738
  142.1 9.1 %collective-permute-start.25 = (bf16[1728,512]{1,0:T(8,128)(2,1)S(1)}, bf16[1728,512]{1,0:T(8,128)(2,1)}, u32[]{:S(2)}, u32[]{:S(2)}) collective-permute-start(bf16[1728,512]{1,0:T(8,128)(2,1)S(1)} %mixing_grad.3), channel_id=1, source_target_pairs={{0,8},{8,0},{16,24},{24,16},{1,9},{9,1},{17,25},{25,17},{2,10},{10... | collective-permute-start | bytes 5308424 | tf_op jit(solution)/shard_map/ppermute | solution.py:738
  144.1 1.3 copy-start.13

commit v3 on v2

--- a/solution.py
+++ b/solution.py
@@ -39,6 +39,10 @@
 
 def in_hbm(value):
     return pltpu.with_memory_space_constraint(value, pltpu.HBM)
+
+
+def in_vmem():
+    return pl.BlockSpec(memory_space=pltpu.VMEM)
 
 
 def whole(shape):
@@ -73,13 +77,19 @@
             out_specs=whole(shape),
         ),
         out_shape=jax.ShapeDtypeStruct(shape, jnp.bfloat16),
+        compiler_params=vmem(8),
         name="first_norm",
-    )(me, hidden_in, gain[None, :], segments)
-
-
-def first_norm_back_kernel(came, hidden, gain, grad, out):
-    count, channels, share = came.shape
-    normed_grad = came[...].astype(jnp.float32).reshape(count * channels, share).T
+    )(me, in_hbm(hidden_in), in_hbm(gain[None, :]), in_hbm(segments))
+
+
+def first_norm_back_kernel(me, kept, came, hidden, gain, grad, out):
+    half, channels, share = kept.shape
+    parts = []
+    for i in range(2 * half):
+        other = i ^ me[0]
+        pick = jnp.where(other < half, kept[other % half], came[other % half])
+        parts.append(pick.astype(jnp.float32))
+    normed_grad = jnp.concatenate(parts, axis=0).T
     tokens = hidden[0].astype(jnp.float32)
     scale = lax.rsqrt(jnp.mean(tokens * tokens, axis=-1, keepdims=True) + eps_norm)
     weighed = normed_grad * gain[...]
@@ -87,12 +97,26 @@
     out[0] = grad[...] + scale * (weighed - tokens * (scale * scale * along))
 
 
-def first_norm_back(came, hidden_in, gain, grad):
+def first_norm_back(me, kept, came, hidden_in, gain, grad):
+    _, share, width = hidden_in.shape
     return pl.pallas_call(
         first_norm_back_kernel,
+        grid_spec=pltpu.PrefetchScalarGridSpec(
+            num_scalar_prefetch=1,
+            grid=(1,),
+            in_specs=[
+                whole(kept.shape),
+                whole(came.shape),
+                whole(hidden_in.shape),
+                whole((1, width)),
+                whole(grad.shape),
+            ],
+            out_specs=whole(hidden_in.shape),
+        ),
         out_shape=jax.ShapeDtypeStruct(hidden_in.shape, jnp.float32),
+        compiler_params=vmem(8),
         name="first_norm_back",
-    )(came, hidden_in, gain[None, :], grad)
+    )(me, kept, came, hidden_in, gain[None, :], grad)
 
 
 def tile_pairs(length):
@@ -180,8 +204,8 @@
             both = product(
                 doubled[:, low * TILE : (tb + 1) * TILE], jnp.concatenate(tiles, axis=0)
             )
-            maps[0, k, :, block(tb)] = both[:channels].astype(jnp.bfloat16)
-            maps[1, k, :, block(tb)] = (both[channels:] * parity).astype(jnp.bfloat16)
+            maps[0, first + k, :, block(tb)] = both[:channels].astype(jnp.bfloat16)
+            maps[1, first + k, :, block(tb)] = (both[channels:] * parity).astype(jnp.bfloat16)
 
 
 def maps_kernel(start, filters, pieces, *refs):
@@ -225,12 +249,11 @@
         acc[...] = jnp.zeros_like(acc)
 
     step_maps(step * PER_STEP, maps, taps, slabs, masks, doubled)
-    rows = PER_STEP * channels
-
     def part(weights, values):
         return contract_first(weights.reshape(-1, model_width), values.reshape(-1, length))
 
-    total = part(plus_mixing[...], maps[0]) + part(minus_mixing[...], maps[1])
+    own = pl.ds(step * PER_STEP, PER_STEP)
+    total = part(plus_mixing[...], maps[0, own]) + part(minus_mixing[...], maps[1, own])
     for i in range(count):
         acc[i] += total[:, i * share : (i + 1) * share]
 
@@ -279,6 +302,7 @@
             out_specs=whole(shape),
         ),
         out_shape=pltpu.VMEM(shape, jnp.bfloat16),
+        compiler_params=vmem(8),
         name="place",
     )(me, *parts)
 
@@ -326,10 +350,10 @@
         acc[:, block(sb)] = total
 
 
-def lag_back_kernel(acc, lag_mixing, grads, inputs, pieces, out, gain):
+def lag_back_kernel(me, acc, lag_mixing, grads, inputs, pieces, scales, kept, given, gain):
     _, channels, model_width = lag_mixing.shape
     length = acc.shape[1]
-    count, _, share = out.shape
+    half, _, share = kept.shape
     ids = segment_row(pieces)
     lag_grad = contract_last(lag_mixing[...].reshape(AR * channels, model_width), grads[...])
     total = acc[:channels] + parity_lanes(channels, length) * acc[channels:]
@@ -339,14 +363,25 @@
             term = pltpu.roll(term * lag_keep(ids, j), length - j, 1)
         total = total + term
     back = total.astype(jnp.bfloat16)
-    for i in range(count):
-        out[i] = back[:, i * share : (i + 1) * share]
+    for i in range(2 * half):
+        part = back[:, i * share : (i + 1) * share]
+        other = i ^ me[0]
+        place = other >> 1
+
+        @pl.when((other & 1) == 0)
+        def _(part=part, place=place):
+            kept[place] = part
+
+        @pl.when((other & 1) == 1)
+        def _(part=part, place=place):
+            given[place] = part
+
     weighed = back.astype(jnp.float32) * inputs[0].astype(jnp.float32)
     by_lane = jnp.broadcast_to(jnp.sum(weighed, axis=1, keepdims=True), (channels, 128))
     row = lax.broadcasted_iota(jnp.int32, by_lane.shape, 0)
     lane = lax.broadcasted_iota(jnp.int32, by_lane.shape, 1)
     total = jnp.sum(jnp.where(row == lane, by_lane, 0.0), axis=0, keepdims=True)
-    gain[...] = jnp.broadcast_to(total, gain.shape)
+    gain[...] = jnp.broadcast_to(total / scales[...], gain.shape)
 
 
 def toeplitz_scratch(length, count):
@@ -367,22 +402,18 @@
 
 def spectral_maps(pieces, filters, channels, start, count, into=None):
     length = filters.shape[1]
-    first = start // PER_STEP
-    given = [] if into is None else [in_hbm(into)]
+    given = [] if into is None else [into]
     return pl.pallas_call(
         functools.partial(maps_kernel, start),
         grid=(count // PER_STEP,),
         in_specs=[
             whole(filters.shape),
             whole(pieces.shape),
-            *[pl.BlockSpec(memory_space=pltpu.HBM) for _ in given],
+            *[in_vmem() for _ in given],
         ],
-        out_specs=[
-            pl.BlockSpec((2, PER_STEP, channels, length), lambda k: (0, k + first, 0, 0)),
-            whole((AR, channels, length)),
-        ],
+        out_specs=[in_vmem(), whole((AR, channels, length))],
         out_shape=[
-            pltpu.HBM((2, K, channels, length), jnp.bfloat16),
+            pltpu.VMEM((2, K, channels, length), jnp.bfloat16),
             jax.ShapeDtypeStruct((AR, channels, length), jnp.bfloat16),
         ],
         scratch_shapes=maps_scratch(channels, length, filters.shape[0]),
@@ -414,18 +445,14 @@
                 pl.BlockSpec(mix_block, lambda k, _: (k + steps, 0, 0)),
                 pl.BlockSpec((AR, channels, model_width), lambda k, _: (2 * count // AR, 0, 0)),
             ],
-            out_specs=[
-                pl.BlockSpec((2, PER_STEP, channels, length), lambda k, _: (0, k, 0, 0)),
-                whole((AR, channels, length)),
-                *[whole(cut)] * 4,
-            ],
+            out_specs=[in_vmem(), whole((AR, channels, length)), *[whole(cut)] * 4],
             scratch_shapes=[
                 *maps_scratch(channels, length, count),
                 pltpu.VMEM((owners, model_width, share), jnp.float32),
             ],
         ),
         out_shape=[
-            pltpu.HBM((2, count, channels, length), jnp.bfloat16),
+            pltpu.VMEM((2, count, channels, length), jnp.bfloat16),
             jax.ShapeDtypeStruct((AR, channels, length), jnp.bfloat16),
             *[jax.ShapeDtypeStruct(cut, jnp.bfloat16)] * 4,
         ],
@@ -460,28 +487,33 @@
     )(filters, *[in_hbm(mixing)] * 2, pieces, grads)
 
 
-def lag_back(acc, mixing, grads, lags, pieces):
+def lag_back(me, acc, mixing, grads, lags, pieces, scales):
     channels, model_width = mixing.shape[1:]
     owners, _, share = pieces.shape
-    sent = (owners, channels, share)
+    sent = (owners // 2, channels, share)
     return pl.pallas_call(
         lag_back_kernel,
-        grid=(1,),
-        in_specs=[
-            whole(acc.shape),
-            pl.BlockSpec((AR, channels, model_width), lambda k: (2 * K // AR, 0, 0)),
-            whole(grads.shape),
-            pl.BlockSpec((1, *lags.shape[1:]), lambda k: (0, 0, 0)),
-            whole(pieces.shape),
-        ],
-        out_specs=[whole(sent), whole((8, 128))],
+        grid_spec=pltpu.PrefetchScalarGridSpec(
+            num_scalar_prefetch=1,
+            grid=(1,),
+            in_specs=[
+                whole(acc.shape),
+                pl.BlockSpec((AR, channels, model_width), lambda k, _: (2 * K // AR, 0, 0)),
+                whole(grads.shape),
+                pl.BlockSpec((1, *lags.shape[1:]), lambda k, _: (0, 0, 0)),
+                whole(pieces.shape),
+                whole(scales.shape),
+            ],
+            out_specs=[whole(sent), whole(sent), whole((8, 128))],
+        ),
         out_shape=[
+            jax.ShapeDtypeStruct(sent, jnp.bfloat16),
             jax.ShapeDtypeStruct(sent, jnp.bfloat16),
             jax.ShapeDtypeStruct((8, 128), jnp.float32),
         ],
         compiler_params=vmem(16),
         name="lag_back",
-    )(acc, in_hbm(mixing), grads, in_hbm(lags), pieces)
+    )(me, acc, in_hbm(mixing), grads, lags, pieces, scales)
 
 
 def gelu_parts(gate_value, upper_value, hidden_grad):
@@ -596,83 +628,106 @@
         ],
         compiler_params=vmem(16),
         name="feed_forward",
-    )(bit, held, got, hidden_in, gain[None, :], cotangent, *map(in_hbm, (w_gate, w_up, w_down)))
+    )(bit, held, got, hidden_in, gain[None, :], cotangent, w_gate, w_up, w_down)
+
+
+CHUNK = 6
 
 
 def own_mixing_grad_kernel(maps, lags, grads, out, lag_out):
-    maps = maps[...].reshape(-1, maps.shape[-1])
-    out[...] = product(maps, grads[...]).astype(out.dtype).reshape(out.shape)
-
-    @pl.when(pl.program_id(0) == pl.num_programs(0) - 1)
-    def _():
-        values = lags[...].reshape(-1, lags.shape[-1])
-        lag_out[...] = product(values, grads[...]).astype(out.dtype).reshape(lag_out.shape)
+    def chunk(index, _):
+        own = pl.ds(index * CHUNK, CHUNK)
+        for which in range(2):
+            values = maps[which, own]
+            total = product(values.reshape(-1, values.shape[-1]), grads[...])
+            out[which, own] = total.astype(out.dtype).reshape(CHUNK, *out.shape[2:])
+
+    lax.fori_loop(0, maps.shape[1] // CHUNK, chunk, None)
+    values = lags[...].reshape(-1, lags.shape[-1])
+    lag_out[...] = product(values, grads[...]).astype(out.dtype).reshape(lag_out.shape)
 
 
 def own_mixing_grad(maps, lags, grads):
-    _, count, channels, length = maps.shape
+    _, count, channels, _ = maps.shape
     width = grads.shape[1]
-    steps, rows = 4, count // 4
     return pl.pallas_call(
         own_mixing_grad_kernel,
+        in_specs=[in_vmem()] * 3,
+        out_specs=[in_vmem()] * 2,
+        out_shape=[
+            pltpu.VMEM((2, count, channels, width), jnp.bfloat16),
+            pltpu.VMEM((AR, channels, width), jnp.bfloat16),
+        ],
+        compiler_params=vmem(16),
+        name="own_mixing_grad",
+    )(maps, lags, grads)
+
+
+def mixing_grad_kernel(which, maps, lags, grads, own, own_lags, out):
+    def total(values, mine):
+        values = product(values.reshape(-1, values.shape[-1]), grads[...])
+        return (values + mine.reshape(values.shape).astype(jnp.float32)).astype(out.dtype)
+
+    count, channels = maps.shape[1:3]
+
+    def chunk(index, _):
+        part = pl.ds(index * CHUNK, CHUNK)
+        start = pl.multiple_of(index * CHUNK * channels, CHUNK * channels)
+        out[pl.ds(start, CHUNK * channels), :] = total(maps[which, part], own[which, part])
+
+    lax.fori_loop(0, count // CHUNK, chunk, None)
+    if which:
+        out[count * channels :, :] = total(lags[...], own_lags[...])
+
+
+def mixing_grad(which, maps, lags, grads, own, own_lags):
+    _, count, channels, _ = maps.shape
+    shape = ((count + which * AR) * channels, grads.shape[1])
+    return pl.pallas_call(
+        functools.partial(mixing_grad_kernel, which),
+        in_specs=[in_vmem()] * 5,
+        out_specs=in_vmem(),
+        out_shape=pltpu.VMEM(shape, jnp.bfloat16),
+        compiler_params=vmem(16),
+        name="mixing_grad",
+    )(maps, lags, grads, own, own_lags)
+
+
+def finish_mixing_kernel(part, got, *refs):
+    out = refs[-1]
+    out[...] = (part[...].astype(jnp.float32) + got[...].astype(jnp.float32)).reshape(out.shape)
+
+
+def finish_mixing(part, got, first, total, into=None):
+    channels = total[1]
+    count = part.shape[0] // channels
+    steps = 3
+    size = count // steps
+    given = [] if into is None else [into]
+    return pl.pallas_call(
+        finish_mixing_kernel,
         grid=(steps,),
         in_specs=[
-            pl.BlockSpec((2, rows, channels, length), lambda k: (0, k, 0, 0)),
-            whole(lags.shape),
-            whole(grads.shape),
+            pl.BlockSpec((size * channels, total[2]), lambda k: (k, 0)),
+            pl.BlockSpec((size * channels, total[2]), lambda k: (k, 0)),
+            *[pl.BlockSpec(memory_space=pl.ANY) for _ in given],
         ],
-        out_specs=[
-            pl.BlockSpec((2, rows, channels, width), lambda k: (0, k, 0, 0)),
-            whole((AR, channels, width)),
-        ],
-        out_shape=[
-            pltpu.HBM((2, count, channels, width), jnp.bfloat16),
-            pltpu.HBM((AR, channels, width), jnp.bfloat16),
-        ],
-        compiler_params=vmem(24),
-        name="own_mixing_grad",
-    )(in_hbm(maps), in_hbm(lags), grads)
-
-
-def mixing_grad_kernel(with_lags, maps, lags, grads, own, own_lags, out):
-    step, size = pl.program_id(0), maps.shape[0] * maps.shape[1]
-
-    def total(left, mine):
-        values = product(left[...].reshape(-1, left.shape[-1]), grads[...])
-        return (values + mine[...].reshape(values.shape).astype(jnp.float32)).astype(out.dtype)
-
-    out[pl.ds(pl.multiple_of(step * size, size), size), :] = total(maps, own)
-
-    if with_lags:
-
-        @pl.when(step == pl.num_programs(0) - 1)
-        def _():
-            out[size * pl.num_programs(0) :, :] = total(lags, own_lags)
-
-
-def mixing_grad(which, maps, lags, grads, own, own_lags):
-    _, count, channels, length = maps.shape
-    width = grads.shape[1]
-    steps, rows = 3, count // 3
-    total = (count + which * AR) * channels
-    return pl.pallas_call(
-        functools.partial(mixing_grad_kernel, bool(which)),
-        grid=(steps,),
-        in_specs=[
-            pl.BlockSpec((None, rows, channels, length), lambda k: (which, k, 0, 0)),
-            whole(lags.shape),
-            whole(grads.shape),
-            pl.BlockSpec((None, rows, channels, width), lambda k: (which, k, 0, 0)),
-            whole(own_lags.shape),
-        ],
-        out_specs=whole((total, width)),
-        out_shape=jax.ShapeDtypeStruct((total, width), jnp.bfloat16),
-        compiler_params=vmem(24),
-        name="mixing_grad",
-    )(in_hbm(maps), in_hbm(lags), in_hbm(grads), in_hbm(own), in_hbm(own_lags))
-
-
-def unit_grads_kernel(me, *refs):
+        out_specs=pl.BlockSpec(
+            tuple(map(pl.Element, (size, *total[1:]))), lambda k: (first + k * size, 0, 0)
+        ),
+        out_shape=jax.ShapeDtypeStruct(total, jnp.float32),
+        input_output_aliases={2: 0} if given else {},
+        compiler_params=vmem(16),
+        name="finish_mixing",
+    )(part, got, *given)
+
+
+def unit_rows(width, units):
+    blocks = width // units // 2
+    return [width + units * i for i in range(blocks)], width + units * blocks + 16
+
+
+def unit_grads_kernel(channels, me, *refs):
     *parts, gate, up, down, first_gain, out, normed, cotangent = refs
     place_tokens(me[0], parts[:4], normed)
     place_tokens(me[0], parts[4:], cotangent)
@@ -683,37 +738,37 @@
     hidden, gate_back, upper_back = gelu_parts(gate_value, upper_value, hidden_grad)
     gate_part = contract_first(normed[...], gate_back.astype(jnp.bfloat16))
     up_part = contract_first(normed[...], upper_back.astype(jnp.bfloat16))
-    down_part = contract_first(hidden.astype(jnp.bfloat16), cotangent[...])
-    out[:width] = gate_part.astype(jnp.bfloat16)
-    out[width : 2 * width] = up_part.astype(jnp.bfloat16)
-    for i in range(width // units):
-        start = 2 * width + i * units
-        out[start : start + units] = down_part[:, i * units : (i + 1) * units].astype(
-            jnp.bfloat16
-        )
+    down_part = contract_first(hidden.astype(jnp.bfloat16), cotangent[...]).astype(jnp.bfloat16)
+    starts, size = unit_rows(width, units)
+    out[0, :width] = gate_part.astype(jnp.bfloat16)
+    out[1, :width] = up_part.astype(jnp.bfloat16)
+    for i in range(2 * len(starts)):
+        half, start = i // len(starts), starts[i % len(starts)]
+        out[half, start : start + units] = down_part[:, i * units : (i + 1) * units]
     share_rows = parts[0].shape[2]
-    second_gain = jnp.zeros((16, width), jnp.float32)
+    second = jnp.zeros((16, width), jnp.float32)
     for part in parts[2:4]:
         for a in range(2):
             for r in range(part.shape[1]):
-                second_gain = second_gain + part[a, r, share_rows:, :].astype(jnp.float32)
-    second_gain = (second_gain[:8] + second_gain[8:]).astype(jnp.bfloat16)
-    start = 3 * width
-    for i in range(width // units):
-        out[start + 16 * i : start + 16 * i + 8] = second_gain[:, i * units : (i + 1) * units]
-    start += 16 * (width // units)
-    out[start : start + 8, : first_gain.shape[1]] = first_gain[...].astype(jnp.bfloat16)
+                second = second + part[a, r, share_rows:, :].astype(jnp.float32)
+    second = second[:8] + second[8:]
+    second = pltpu.roll(second, lax.rem(width - me[0] * channels, width), 1)
+    out[0, size - 16 :] = jnp.zeros((16, units), jnp.bfloat16)
+    out[1, size - 16 :] = jnp.zeros((16, units), jnp.bfloat16)
+    lanes = first_gain.shape[1]
+    gains = jnp.concatenate([second[:, :lanes], first_gain[...]], axis=0)
+    out[0, size - 16 :, :lanes] = gains.astype(jnp.bfloat16)
 
 
 def unit_grads(me, normed_parts, cotangent_parts, w_gate, w_up, w_down, first_gain):
     width, hidden = w_gate.shape
     chans = lax.axis_size("chan")
     units = hidden // chans
-    rows = 3 * width + 16 * (width // units) + 16
     parts = [*normed_parts, *cotangent_parts]
     tokens = 2 * sum(math.prod(part.shape[:-1]) for part in normed_parts[:2])
-    return pl.pallas_call(
-        unit_grads_kernel,
+    shape = (2, unit_rows(width, units)[1], units)
+    return pl.pallas_call(
+        functools.partial(unit_grads_kernel, width // chans),
         grid_spec=pltpu.PrefetchScalarGridSpec(
             num_scalar_prefetch=1,
             grid=(1,),
@@ -724,15 +779,48 @@
                 pl.BlockSpec((units, width), lambda k, me: (me[0], 0)),
                 whole(first_gain.shape),
             ],
-            out_specs=whole((rows, units)),
+            out_specs=whole(shape),
             scratch_shapes=[pltpu.VMEM((tokens, width), jnp.bfloat16)] * 2,
         ),
-        out_shape=jax.ShapeDtypeStruct((rows, units), jnp.bfloat16),
+        out_shape=jax.ShapeDtypeStruct(shape, jnp.bfloat16),
         compiler_params=vmem(24),
         name="unit_grads",
     )(me, *parts, in_hbm(w_gate), in_hbm(w_up), in_hbm(w_down), first_gain)
 
 
+def finish_units_kernel(core, mine, other, gate, up, down, gains):
+    width, units = gate.shape
+    starts, size = unit_rows(width, units)
+    for which, (low, high) in enumerate(((mine, other), (other, mine))):
+
+        @pl.when(core[0] == which)
+        def _(low=low, high=high):
+            gate[...] = low[:width].astype(jnp.float32)
+            up[...] = high[:width].astype(jnp.float32)
+            for i in range(2 * len(starts)):
+                source, start = (low, high)[i // len(starts)], starts[i % len(starts)]
+                part = source[start : start + units].astype(jnp.float32)
+                down[:, i * units : (i + 1) * units] = part
+            gains[...] = low[size - 16 :].astype(jnp.float32)
+
+
+def finish_units(core, mine, other, width):
+    units = mine.shape[1]
+    shapes = [(width, units), (width, units), (units, width), (16, units)]
+    return pl.pallas_call(
+        finish_units_kernel,
+        grid_spec=pltpu.PrefetchScalarGridSpec(
+            num_scalar_prefetch=1,
+            grid=(1,),
+            in_specs=[whole(mine.shape), whole(mine.shape)],
+            out_specs=[whole(shape) for shape in shapes],
+        ),
+        out_shape=[jax.ShapeDtypeStruct(shape, jnp.float32) for shape in shapes],
+        compiler_params=vmem(16),
+        name="finish_units",
+    )(core, mine, other)
+
+
 def swap(values, axis, mask):
     count = lax.axis_size(axis)
     return lax.ppermute(values, axis, [(i, i ^ mask) for i in range(count)])
@@ -742,6 +830,10 @@
     return [1 << b for b in range(lax.axis_size(axis).bit_length() - 1)]
 
 
+def entry(values, index, dim):
+    return lax.dynamic_slice_in_dim(values, index, 1, dim, allow_negative_indices=False)
+
+
 def join(mine, other, high, dim):
     return jnp.where(
         high, jnp.concatenate([other, mine], dim), jnp.concatenate([mine, other], dim)
@@ -752,15 +844,14 @@
     return lax.optimization_barrier(values)
 
 
-def gather_round(held, mask):
-    me = lax.axis_index("chan")
-    return join(held[None], swap(held, "chan", mask)[None], (me & mask) != 0, 0)
+def gather_round(held, mask, bits):
+    return join(held[None], swap(held, "chan", mask)[None], bits[mask][0] != 0, 0)
 
 
 class Gather:
-    def __init__(self, values, half):
+    def __init__(self, values, half, bits):
         masks = bits_of("chan")
-        self.half = half
+        self.half, self.bits = half, bits
         self.shape = values.shape
         self.common = masks[2:]
         self.orders = [(masks[1], masks[0]), (masks[0], masks[1])]
@@ -768,13 +859,14 @@
 
     def first(self):
         for mask in self.common:
-            self.held = gather_round(self.held, mask).reshape(-1, *self.shape)
+            self.held = gather_round(self.held, mask, self.bits).reshape(-1, *self.shape)
         return self.held
 
     def second(self):
         self.halves = [self.held[:, : self.half], self.held[:, self.half :]]
         self.halves = [
-            gather_round(h, order[0]) for h, order in zip(self.halves, self.orders, strict=True)
+            gather_round(h, order[0], self.bits)
+            for h, order in zip(self.halves, self.orders, strict=True)
         ]
         return self.halves
 
@@ -792,42 +884,39 @@
     return left.astype(jnp.float32) + right.astype(jnp.float32)
 
 
-def own_entry(values, mask, dim):
-    return add(*exchange(values, mask, dim)).squeeze(dim)
-
-
-def exchange(values, mask, dim):
-    bit = (lax.axis_index("chan") & mask) // mask
-    keep = lax.dynamic_slice_in_dim(values, bit, 1, dim)
-    give = lax.dynamic_slice_in_dim(values, 1 - bit, 1, dim)
+def own_entry(values, mask, dim, bits):
+    return add(*exchange(values, mask, dim, bits)).squeeze(dim)
+
+
+def exchange_rest(kept, came):
+    count = 2 * kept.shape[0]
+    held = jnp.stack([kept, came], axis=1).reshape(count, *kept.shape[1:])
+    for mask in bits_of("chan")[1:]:
+        split = held.reshape(-1, 2, mask, *held.shape[1:])
+        kept, came = split[:, 0], swap(split[:, 1], "chan", mask)
+        held = jnp.stack([kept, came], axis=1).reshape(held.shape)
+    return kept.reshape(count // 2, *held.shape[1:]), came.reshape(count // 2, *held.shape[1:])
+
+
+def exchange(values, mask, dim, bits):
+    keep, give = (entry(values, bit, dim) for bit in bits[mask])
     return keep, swap(give, "chan", mask)
 
 
-def scatter_tokens(keep0, give0, keep1, give1, beside):
+def scatter_tokens(keep0, give0, keep1, give1, beside, bits):
     masks = bits_of("chan")
     got0, got1 = swap(give0, "chan", masks[0]), swap(give1, "chan", masks[1])
     half0 = add(keep0, got0).astype(jnp.bfloat16)
     half1 = add(keep1, got1).astype(jnp.bfloat16)
     half0, half1, *beside = tie(half0, half1, *beside)
-    half0 = own_entry(half0, masks[1], 1)
-    half1 = own_entry(half1, masks[0], 1)
+    half0 = own_entry(half0, masks[1], 1, bits)
+    half1 = own_entry(half1, masks[0], 1, bits)
     held = jnp.concatenate([half0, half1], axis=1)
     for mask in masks[:2:-1]:
         held = held.astype(jnp.bfloat16).reshape(2, -1, *held.shape[1:])
-        held = own_entry(held, mask, 0)
+        held = own_entry(held, mask, 0, bits)
     held = held.astype(jnp.bfloat16)
-    return held, exchange(held, masks[2], 0)[1][0], beside
-
-
-def core_halves(values):
-    core = lax.axis_index("rows") & 1
-    half = values.shape[0] // 2
-    return [lax.dynamic_slice_in_dim(values, which * half, half, 0) for which in (core, 1 - core)]
-
-
-def both_halves(held, dim):
-    other = swap(held, "rows", 1).astype(jnp.float32)
-    return join(held.astype(jnp.float32), other, (lax.axis_index("rows") & 1) != 0, dim)
+    return held, exchange(held, masks[2], 0, bits)[1][0], beside
 
 
 def shards(
@@ -838,7 +927,17 @@
     at = me.reshape(1)
     _, share, width = hidden_in.shape
     channels = width // chans
-    cotangent_gather = Gather(out_grad[0], share // 2)
+    core = lax.axis_index("rows").astype(jnp.int32) & 1
+    other_core = 1 - core
+    bits = [(me >> b) & 1 for b in range(len(bits_of("chan")))]
+    bits = [bit ^ flip for bit in bits for flip in range(2)]
+    scales = lax.dynamic_slice_in_dim(gain_one, me * channels, channels)
+    scales = jnp.pad(scales, (0, 128 - channels), constant_values=1.0)[None, :]
+    hidden_in, scales, at, core, other_core, *bits = tie(
+        hidden_in, scales, at, core, other_core, *bits
+    )
+    bits = dict(zip(bits_of("chan"), zip(bits[::2], bits[1::2], strict=True), strict=True))
+    cotangent_gather = Gather(out_grad[0], share // 2, bits)
     cotangent_gather.first()
     pieces = lax.all_to_all(
         first_norm(at, hidden_in, gain_one, segments, chans),
@@ -851,18 +950,19 @@
     peer_pieces, lags = tie(peer_pieces, lags)
     peer_maps, peer_lags = spectral_maps(peer_pieces, filters, channels, 0, K // 2)
     cotangent_gather.second()
+    lags, *cotangent_gather.halves = tie(lags, *cotangent_gather.halves)
     beside = (peer_maps, *cotangent_gather.third())
-    held, got, (peer_maps, *cotangent_gather.others) = scatter_tokens(*cut, beside)
-    last_bit = ((me >> 2) & 1).reshape(1)
+    held, got, (peer_maps, *cotangent_gather.others) = scatter_tokens(*cut, beside, bits)
+    last_bit = bits[4][0].reshape(1)
     output, normed_two, resid_grad, resid_low = feed_forward(
         last_bit, held, got, hidden_in, gain_two, out_grad, w_gate, w_up, w_down
     )
-    grad_gather = Gather(resid_low, share // 2)
+    grad_gather = Gather(resid_low, share // 2, bits)
     first = grad_gather.first()
     peer_pieces, resid_grad = tie(peer_pieces, resid_grad)
     peer_maps, _ = spectral_maps(peer_pieces, filters, channels, K // 2, K // 2, peer_maps)
     normed_two, grad_gather.held, peer_maps = tie(normed_two, first, peer_maps)
-    normed_gather = Gather(normed_two, share // 2)
+    normed_gather = Gather(normed_two, share // 2, bits)
     normed_gather.first()
     grad_gather.second()
     normed_gather.second()
@@ -871,15 +971,16 @@
     full_grad = place(at, grad_gather.parts())
     peer_grad = swap(full_grad, "rows", 2)
     acc = spectral_back(full_grad, mixing, filters, pieces)
-    back, first_local = lag_back(acc, mixing, full_grad, lags, pieces)
-    came = lax.all_to_all(back, "chan", split_axis=0, concat_axis=0)
+    back, give, first_local = lag_back(at, acc, mixing, full_grad, lags, pieces, scales)
+    came = swap(give, "chan", 1)
     first_local, *normed_parts = tie(first_local, *normed_gather.parts())
     unit_parts = unit_grads(
         at, normed_parts, cotangent_gather.parts(), w_gate, w_up, w_down, first_local
     )
-    unit_parts, full_grad = tie(unit_parts, full_grad)
-    keep, give = core_halves(unit_parts)
-    unit_given = swap(give, "rows", 1)
+    unit_parts, full_grad, back, came = tie(unit_parts, full_grad, back, came)
+    back, came = exchange_rest(back, came)
+    keep = entry(unit_parts, core, 0)[0]
+    unit_given = swap(entry(unit_parts, other_core, 0)[0], "rows", 1)
     own, own_lags = own_mixing_grad(maps, lags, full_grad)
     own_lags, unit_given = tie(own_lags, unit_given)
     unit_half = add(keep, unit_given).astype(jnp.bfloat16)
@@ -889,34 +990,29 @@
     first_part, peer_grad = tie(first_part, peer_grad)
     second_part = mixing_grad(1, peer_maps, peer_lags, peer_grad, own, own_lags)
     second_part, came, unit_other = tie(second_part, came, unit_other)
-    sums = []
-    for part in (first_part, second_part):
-        for mask in [1, *bits_of("rows")[2:]]:
-            part = add(part, swap(part, "rows", mask)).astype(jnp.bfloat16)
-        sums.append(part.astype(jnp.float32))
-    mixing_sum = jnp.concatenate(sums, axis=0).reshape(mixing.shape)
-    input_total = first_norm_back(came, hidden_in, gain_one, resid_grad)
+    input_total = first_norm_back(at, back, came, hidden_in, gain_one, resid_grad)
     unit_half = add(unit_half, unit_other).astype(jnp.bfloat16)
     for mask in bits_of("rows")[2:]:
         unit_half = add(unit_half, swap(unit_half, "rows", mask)).astype(jnp.bfloat16)
-    unit_sum = both_halves(unit_half, 0)
-    units = w_gate.shape[1] // chans
-    columns = range(0, width, units)
-    down_sum = jnp.concatenate([unit_sum[2 * width + i : 2 * width + i + units] for i in columns], 1)
-    gains = [unit_sum[3 * width + 16 * i] for i in range(len(columns))]
-    second_gain = lax.dynamic_slice_in_dim(jnp.concatenate(gains), me * channels, channels)
-    first_gain = unit_sum[3 * width + 16 * len(columns), :channels] / (
-        lax.dynamic_slice_in_dim(gain_one, me * channels, channels)
-    )
+    gate_sum, up_sum, down_sum, gains = finish_units(
+        core.reshape(1), unit_half, swap(unit_half, "rows", 1), width
+    )
+    mixing_sum = None
+    for part, first in ((first_part, 0), (second_part, K)):
+        masks = [1, *bits_of("rows")[2:]]
+        for mask in masks[:-1]:
+            part = add(part, swap(part, "rows", mask)).astype(jnp.bfloat16)
+        got = swap(part, "rows", masks[-1])
+        mixing_sum = finish_mixing(part, got, first, mixing.shape, mixing_sum)
     return (
         output,
         input_total,
         mixing_sum,
-        unit_sum[:width],
-        unit_sum[width : 2 * width],
+        gate_sum,
+        up_sum,
         down_sum,
-        first_gain,
-        second_gain,
+        gains[8, :channels],
+        gains[0, :channels],
     )
 
 

time: 158 us -> 142 us (0.90)
  waiting for transfers between devices: 15.4 us -> 35 us
  other arithmetic: 16.8 us -> 1.77 us
  Pallas kernels: 67.1 us -> 57.5 us
  starting transfers between devices: 51.1 us -> 44.3 us
  local copies, waits for them, and re-layouts: 5.72 us -> 2.34 us
    ppermute x27 -> x30, waiting for transfers between devices: 12.2 us -> 31.2 us  [swap(): return lax.ppermute(values, axis, [(i, i ^ mask) for i in range(count)])]
    all_to_all x1 -> x0, starting transfers between devices: 8.01 us -> none  [shards(): came = lax.all_to_all(back, 'chan', split_axis=0, concat_axis=0)]
    convert_element_type x4 -> x1, other arithmetic: 7.2 us -> 0.13 us  [shards(): unit_half = add(unit_half, unit_other).astype(jnp.bfloat16)]
    pallas_call x6 -> x9, Pallas kernels: 25.2 us -> 21.3 us  [the longest x2 4.96 us: mixing_grad(): pl.pallas_call(functools.partial(mixing_grad_kernel, which), in_specs=[in...]
    reshape x1 -> x0, other arithmetic: 3.75 us -> none  [shards(): mixing_sum = jnp.concatenate(sums, axis=0).reshape(mixing.shape)]
    unnamed x36 -> x20, local copies, waits for them, and re-layouts: 3.2 us -> 0.85 us
    pallas_call x2, Pallas kernels: 9.03 us -> 7.22 us  [spectral_maps(): pl.pallas_call(functools.partial(maps_kernel, start), grid=(count // PER_...]
    ppermute x27 -> x30, starting transfers between devices: 39.3 us -> 40.5 us  [swap(): return lax.ppermute(values, axis, [(i, i ^ mask) for i in range(count)])]
  transfers between devices with their start and end apart: 29 -> 31, of which waited for: 8 -> 12; matrix products, arithmetic and copies ran while one was open for 7% -> 2% of each run, Pallas kernels for 38% -> 35%
where the time goes in v3:
time: 142 us
  Pallas kernels  57.5 us (40%)
  starting transfers between devices  44.3 us (31%)
  waiting for transfers between devices  35 us (25%)
  local copies, waits for them, and re-layouts  2.34 us (2%)
  other arithmetic  1.77 us (1%)
    ppermute x30, starting transfers between devices, swap(): return lax.ppermute(values, axis, [(i, i ^ mask) for i in range(count)])  40.5 us
    ppermute x30, waiting for transfers between devices, swap(): return lax.ppermute(values, axis, [(i, i ^ mask) for i in range(count)])  31.2 us
    pallas_call x1, Pallas kernels, spectral_mixed(): pl.pallas_call(mixed_kernel, grid_spec=pltpu.PrefetchScalarGridSpec(num_s...  11.8 us
    pallas_call x1, Pallas kernels, spectral_back(): pl.pallas_call(spectral_back_kernel, grid=(steps,), in_specs=[whole(filte...  9.95 us
    pallas_call x2, Pallas kernels, spectral_maps(): pl.pallas_call(functools.partial(maps_kernel, start), grid=(count // PER_...  7.22 us
    pallas_call x1, Pallas kernels, feed_forward(): pl.pallas_call(feed_forward_kernel, grid_spec=pltpu.PrefetchScalarGridSpe...  5.3 us
    pallas_call x2, Pallas kernels, mixing_grad(): pl.pallas_call(functools.partial(mixing_grad_kernel, which), in_specs=[in...  4.96 us
    pallas_call x2, Pallas kernels, finish_mixing(): pl.pallas_call(finish_mixing_kernel, grid=(steps,), in_specs=[pl.BlockSpe...  4.41 us
  transfers between devices with their start and end apart: 31, of which 12 were waited for; matrix products, arithmetic and copies ran while one was open for 2% of the time, Pallas kernels for 35%

profile of v3, /device:TPU:0, one launch (start us, length us, event | category | flops | bytes accessed | tf_op | source)
XLA Modules:
  0.0 141.9 jit_solution(1913184740153782168)
XLA Ops:
  0.6 4.1 %collective-permute-start.3 = (bf16[1,128,512]{2,1,0:T(8,128)(2,1)}, bf16[1,128,512]{2,1,0:T(8,128)(2,1)S(1)}, u32[]{:S(2)}, u32[]{:S(2)}) collective-permute-start(bf16[1,128,512]{2,1,0:T(8,128)(2,1)} %cotangent.1), channel_id=1, source_target_pairs={{0,4},{1,5},{2,6},{3,7},{4,0},{5,1},{6,2},{7,3},{8,12},{9,13},{10,... | collective-permute-start | bytes 393224 | tf_op jit(solution)/shard_map/ppermute | solution.py:826
  4.7 0.8 dynamic_slice.24
  5.5 1.8 %first_norm.1 = bf16[8,80,128]{2,1,0:T(8,128)(2,1)} custom-call(s32[1]{0:T(128)} %bitcast.1.me, bf16[1,128,512]{2,1,0:T(8,128)(2,1)} %hidden.1, f32[1,512]{1,0:T(1,128)} %bitcast.63, s32[1,1024]{1,0:T(1,128)} %segments.1), custom_call_target="tpu_custom_call" | custom-call | tf_op jit(solution)/shard_map/first_norm/pallas_call | solution.py:71
  7.3 3.8 %all-to-all-start = ((bf16[8,80,128]{2,1,0:T(8,128)(2,1)}), bf16[8,80,128]{2,1,0:T(8,128)(2,1)S(1)}, u32[]{:S(2)}, u32[]{:S(2)}) async-start(bf16[8,80,128]{2,1,0:T(8,128)(2,1)} %first_norm.1), calls=%async_computation | async-start | bytes 327680 | tf_op jit(solution)/shard_map/all_to_all | solution.py:942
  11.3 1.0 maximum_select_fusion.2
  12.3 1.9 %collective-permute-start.4 = (bf16[2,64,512]{2,1,0:T(8,128)(2,1)S(1)}, bf16[2,64,512]{2,1,0:T(8,128)(2,1)S(1)}, u32[]{:S(2)}, u32[]{:S(2)}) collective-permute-start(bf16[2,64,512]{2,1,0:T(8,128)(2,1)S(1)} %get-tuple-element.151), channel_id=1, source_target_pairs={{0,2},{1,3},{2,0},{3,1},{4,6},{5,7},{6,4},{7,5},{8,10},{9,11},{10,... | collective-permute-start | bytes 393224 | tf_op jit(solution)/shard_map/ppermute | solution.py:826
  14.2 1.5 %collective-permute-start.5 = (bf16[2,64,512]{2,1,0:T(8,128)(2,1)S(1)}, bf16[2,64,512]{2,1,0:T(8,128)(2,1)S(1)}, u32[]{:S(2)}, u32[]{:S(2)}) collective-permute-start(bf16[2,64,512]{2,1,0:T(8,128)(2,1)S(1)} %get-tuple-element.148), channel_id=1, source_target_pairs={{0,1},{1,0},{2,3},{3,2},{4,5},{5,4},{6,7},{7,6},{8,9},{9,8},{10,11... | collective-permute-start | bytes 393224 | tf_op jit(solution)/shard_map/ppermute | solution.py:826
  15.7 3.8 %all-to-all-done.pieces = bf16[8,80,128]{2,1,0:T(8,128)(2,1)S(1)} async-done(((bf16[8,80,128]{2,1,0:T(8,128)(2,1)}), bf16[8,80,128]{2,1,0:T(8,128)(2,1)S(1)}, u32[]{:S(2)}, u32[]{:S(2)}) %all-to-all-start) | async-done | bytes 163872 | tf_op jit(solution)/shard_map/all_to_all | solution.py:942
  19.5 1.5 %collective-permute-start.2 = (bf16[8,80,128]{2,1,0:T(8,128)(2,1)S(1)}, bf16[8,80,128]{2,1,0:T(8,128)(2,1)S(1)}, u32[]{:S(2)}, u32[]{:S(2)}) collective-permute-start(bf16[8,80,128]{2,1,0:T(8,128)(2,1)S(1)} %all-to-all-done.pieces), channel_id=1, source_target_pairs={{0,16},{8,24},{16,0},{24,8},{1,17},{9,25},{17,1},{25,9},{2,18},{10... | collective-permute-start | bytes 491528 | tf_op jit(solution)/shard_map/ppermute | solution.py:826
  21.1 0.8 copy-done.5
  21.9 11.8 %spectral_mixed.1 = (bf16[2,24,64,1024]{3,2,1,0:T(8,128)(2,1)S(1)}, bf16[3,64,1024]{2,1,0:T(8,128)(2,1)S(1)}, bf16[2,2,256,128]{3,2,1,0:T(8,128)(2,1)S(1)}, bf16...) custom-call(s32[1]{0:T(128)} %bitcast.1.me, ...), custom_call_target="tpu_custom_call" | custom-call | tf_op jit(solution)/shard_map/spectral_mixed/pallas_call | solution.py:436
  34.0 1.5 %collective-permute-start = (bf16[2,2,256,128]{3,2,0,1:T(8,128)(2,1)S(1)}, bf16[2,2,256,128]{3,2,0,1:T(8,128)(2,1)S(1)}, u32[]{:S(2)}, u32[]{:S(2)}) collective-permute-start(bf16[2,2,256,128]{3,2,0,1:T(8,128)(2,1)S(1)} %copy.21), channel_id=1, source_target_pairs={{0,1},{1,0},{2,3},{3,2},{4,5},{5,4},{6,7},{7,6},{8,9},{9,8},{10,11... | collective-permute-start | bytes 786440 | tf_op jit(solution)/shard_map/ppermute | solution.py:826
  35.5 3.5 %spectral_maps.2 = (bf16[2,24,64,1024]{3,2,1,0:T(8,128)(2,1)S(1)}, bf16[3,64,1024]{2,1,0:T(8,128)(2,1)S(1)}) custom-call(bf16[24,1024]{1,0:T(8,128)(2,1)S(1)} %copy-done.5, bf16[8,80,128]{2,1,0:T(8,128)(2,1)S(1)} %collective-permute-done.2.pieces), custom_call_target="tpu_custom_call" | custom-call | flops 4831838208 | bytes 4194304 | tf_op jit(solution)/shard_map/spectral_maps/pallas_call | solution.py:406
  39.7 1.9 %collective-permute-start.7 = (bf16[2,2,64,512]{3,2,1,0:T(8,128)(2,1)S(1)}, bf16[2,2,64,512]{3,2,1,0:T(8,128)(2,1)S(1)}, u32[]{:S(2)}, u32[]{:S(2)}) collective-permute-start(bf16[2,2,64,512]{3,2,1,0:T(8,128)(2,1)S(1)} %maximum_select_fusion.4.refs_6_), channel_id=1, source_target_pairs={{0,2},{1,3},{2,0},{3,1},{4,6},{5,7},{6,4},{7,5},{8,10},{9,11},{10,... | collective-permute-start | bytes 786440 | tf_op jit(solution)/shard_map/ppermute | solution.py:826
  41.7 0.7 collective-permute-done
  42.5 3.6 %collective-permute-done.6.refs_5_ = bf16[2,2,64,512]{3,2,1,0:T(8,128)(2,1)S(1)} collective-permute-done((bf16[2,2,64,512]{3,2,1,0:T(8,128)(2,1)S(1)}, bf16[2,2,64,512]{3,2,1,0:T(8,128)(2,1)S(1)}, u32[]{:S(2)}, u32[]{:S(2)}) %collective-permute-start.6) | collective-permute-done | bytes 262176 | tf_op jit(solution)/shard_map/ppermute | solution.py:826
  46.1 2.0 %collective-permute-start.8 = (bf16[2,1,256,128]{3,2,0,1:T(8,128)(2,1)S(1)}, bf16[2,1,256,128]{3,2,0,1:T(8,128)(2,1)S(1)}, u32[]{:S(2)}, u32[]{:S(2)}) collective-permute-start(bf16[2,1,256,128]{3,2,0,1:T(8,128)(2,1)S(1)} %constant_dynamic-slice_fusion.1), channel_id=1, source_target_pairs={{0,2},{1,3},{2,0},{3,1},{4,6},{5,7},{6,4},{7,5},{8,10},{9,11},{10,... | collective-permute-start | bytes 393224 | tf_op jit(solution)/shard_map/ppermute | solution.py:826
  48.3 2.8 %collective-permute-done.8 = bf16[2,1,256,128]{3,2,0,1:T(8,128)(2,1)S(1)} collective-permute-done((bf16[2,1,256,128]{3,2,0,1:T(8,128)(2,1)S(1)}, bf16[2,1,256,128]{3,2,0,1:T(8,128)(2,1)S(1)}, u32[]{:S(2)}, u32[]{:S(2)}) %collective-permute-start.8) | collective-permute-done | bytes 131104 | tf_op jit(solution)/shard_map/ppermute | solution.py:826
  51.2 1.9 %collective-permute-done.9 = bf16[2,1,256,128]{3,2,0,1:T(8,128)(2,1)S(1)} collective-permute-done((bf16[2,1,256,128]{3,2,0,1:T(8,128)(2,1)S(1)}, bf16[2,1,256,128]{3,2,0,1:T(8,128)(2,1)S(1)}, u32[]{:S(2)}, u32[]{:S(2)}) %collective-permute-start.9) | collective-permute-done | bytes 131104 | tf_op jit(solution)/shard_map/ppermute | solution.py:826
  53.2 1.3 collective-permute-start.10
  54.5 5.6 %collective-permute-done.10 = bf16[1,512,128]{2,1,0:T(8,128)(2,1)S(1)} collective-permute-done((bf16[1,512,128]{2,1,0:T(8,128)(2,1)S(1)}, bf16[1,512,128]{2,1,0:T(8,128)(2,1)S(1)}, u32[]{:S(2)}, u32[]{:S(2)}) %collective-permute-start.10) | collective-permute-done | bytes 131104 | tf_op jit(solution)/shard_map/ppermute | solution.py:826
  60.1 5.3 %feed_forward.1 = (bf16[1,128,512]{2,1,0:T(8,128)(2,1)}, bf16[144,512]{1,0:T(8,128)(2,1)S(1)}, f32[128,512]{1,0:T(8,128)S(1)}, bf16[128,512]{1,0:T(8,128)(2,1)S(1)}) custom-call(s32[1]{0:T(128)} %bitcast.2.bit, bf16[2,512,128]{2,1,0:T(8,128)(2,1)S(1)} %pad_maximum_fusion.held, bf16[512,128]{1,0:T(8,128)(2,1)S(1)} %bitcast.60, ...), custom_call_target="tpu_custom_call" | custom-call | tf_op jit(solution)/shard_map/feed_forward/pallas_call | solution.py:597
  65.8 3.7 %spectral_maps.3 = (bf16[2,24,64,1024]{3,2,1,0:T(8,128)(2,1)S(1)}, bf16[3,64,1024]{2,1,0:T(8,128)(2,1)}) custom-call(bf16[24,1024]{1,0:T(8,128)(2,1)S(1)} %copy-done.6, bf16[8,80,128]{2,1,0:T(8,128)(2,1)S(1)} %collective-permute-done.2.pieces, bf16[2,24,64,1024]{3,2,1,0:T(8,128)(2,1)S(1)} %get-tuple-element.99.refs_0_), custom_call_target="tpu_custom_call", output_to_operand_aliasing={{0}: (2, {})} | custom-call | flops 4831838208 | bytes 4194304 | tf_op jit(solution)/shard_map/spectral_maps/pallas_call | solution.py:406
  69.6 2.2 %collective-permute-done.11 = bf16[1,128,512]{2,1,0:T(8,128)(2,1)S(1)} collective-permute-done((bf16[1,128,512]{2,1,0:T(8,128)(2,1)S(1)}, bf16[1,128,512]{2,1,0:T(8,128)(2,1)S(1)}, u32[]{:S(2)}, u32[]{:S(2)}) %collective-permute-start.11) | collective-permute-done | bytes 131104 | tf_op jit(solution)/shard_map/ppermute | solution.py:826
  71.9 1.8 %collective-permute-start.14 = (bf16[2,64,512]{2,1,0:T(8,128)(2,1)S(1)}, bf16[2,64,512]{2,1,0:T(8,128)(2,1)S(1)}, u32[]{:S(2)}, u32[]{:S(2)}) collective-permute-start(bf16[2,64,512]{2,1,0:T(8,128)(2,1)S(1)} %get-tuple-element.144), channel_id=1, source_target_pairs={{0,1},{1,0},{2,3},{3,2},{4,5},{5,4},{6,7},{7,6},{8,9},{9,8},{10,11... | collective-permute-start | bytes 393224 | tf_op jit(solution)/shard_map/ppermute | solution.py:826
  73.7 1.2 collective-permute-start.12
  74.8 3.6 %collective-permute-start.16 = (bf16[1,144,512]{2,1,0:T(8,128)(2,1)S(1)}, bf16[1,144,512]{2,1,0:T(8,128)(2,1)S(1)}, u32[]{:S(2)}, u32[]{:S(2)}) collective-permute-start(bf16[1,144,512]{2,1,0:T(8,128)(2,1)S(1)} %bitcast.56), channel_id=1, source_target_pairs={{0,4},{1,5},{2,6},{3,7},{4,0},{5,1},{6,2},{7,3},{8,12},{9,13},{10,... | collective-permute-start | bytes 442376 | tf_op jit(solution)/shard_map/ppermute | solution.py:826
  78.4 0.8 collective-permute-start.15
  79.3 2.8 %collective-permute-start.13 = (bf16[2,2,64,512]{3,2,1,0:T(8,128)(2,1)S(1)}, bf16[2,2,64,512]{3,2,1,0:T(8,128)(2,1)S(1)}, u32[]{:S(2)}, u32[]{:S(2)}) collective-permute-start(bf16[2,2,64,512]{3,2,1,0:T(8,128)(2,1)S(1)} %maximum_select_fusion.6.part0), channel_id=1, source_target_pairs={{0,1},{1,0},{2,3},{3,2},{4,5},{5,4},{6,7},{7,6},{8,9},{9,8},{10,11... | collective-permute-start | bytes 786440 | tf_op jit(solution)/shard_map/ppermute | solution.py:826
  82.2 2.4 %collective-permute-start.17 = (bf16[2,64,512]{2,1,0:T(8,128)(2,1)S(1)}, bf16[2,64,512]{2,1,0:T(8,128)(2,1)S(1)}, u32[]{:S(2)}, u32[]{:S(2)}) collective-permute-start(bf16[2,64,512]{2,1,0:T(8,128)(2,1)S(1)} %get-tuple-element.142), channel_id=1, source_target_pairs={{0,2},{1,3},{2,0},{3,1},{4,6},{5,7},{6,4},{7,5},{8,10},{9,11},{10,... | collective-permute-start | bytes 393224 | tf_op jit(solution)/shard_map/ppermute | solution.py:826
  84.6 5.9 %collective-permute-done.19 = bf16[2,80,512]{2,1,0:T(8,128)(2,1)S(1)} collective-permute-done((bf16[2,80,512]{2,1,0:T(8,128)(2,1)S(1)}, bf16[2,80,512]{2,1,0:T(8,128)(2,1)S(1)}, u32[]{:S(2)}, u32[]{:S(2)}) %collective-permute-start.19) | collective-permute-done | bytes 163872 | tf_op jit(solution)/shard_map/ppermute | solution.py:826
  90.6 0.7 collective-permute-start.20
  91.3 1.6 %collective-permute-start.24 = (bf16[1024,512]{1,0:T(8,128)(2,1)S(1)}, bf16[1024,512]{1,0:T(8,128)(2,1)S(1)}, u32[]{:S(2)}, u32[]{:S(2)}) collective-permute-start(bf16[1024,512]{1,0:T(8,128)(2,1)S(1)} %place.1.grads), channel_id=1, source_target_pairs={{0,16},{8,24},{16,0},{24,8},{1,17},{9,25},{17,1},{25,9},{2,18},{10... | collective-permute-start | bytes 3145736 | tf_op jit(solution)/shard_map/ppermute | solution.py:826
  92.9 2.0 %collective-permute-start.18 = (bf16[2,2,64,512]{3,2,1,0:T(8,128)(2,1)S(1)}, bf16[2,2,64,512]{3,2,1,0:T(8,128)(2,1)S(1)}, u32[]{:S(2)}, u32[]{:S(2)}) collective-permute-start(bf16[2,2,64,512]{3,2,1,0:T(8,128)(2,1)S(1)} %maximum_select_fusion.8.refs_0_), channel_id=1, source_target_pairs={{0,1},{1,0},{2,3},{3,2},{4,5},{5,4},{6,7},{7,6},{8,9},{9,8},{10,11... | collective-permute-start | bytes 786440 | tf_op jit(solution)/shard_map/ppermute | solution.py:826
  94.9 9.9 %spectral_back.1.acc = f32[128,1024]{1,0:T(8,128)S(1)} custom-call(bf16[24,1024]{1,0:T(8,128)(2,1)S(1)} %copy-done.6, bf16[51,64,512]{2,1,0:T(8,128)(2,1)} %lag_mixing.3, bf16[51,64,512]{2,1,0:T(8,128)(2,1)} %lag_mixing.3, bf16[8,80,128]{2,1,0:T(8,128)(2,1)S(1)} %all-to-all-done.pieces, bf16[1024,512]{1,0:T(8,128)(2,1)S(1)} %place.1.grads), custom_call_target="tpu_custom_call" | custom-call | tf_op jit(solution)/shard_map/spectral_back/pallas_call | solution.py:469
  104.9 1.9 %lag_back.1 = (bf16[4,64,128]{2,1,0:T(8,128)(2,1)S(1)}, bf16[4,64,128]{2,1,0:T(8,128)(2,1)S(1)}, f32[8,128]{1,0:T(8,128)S(1)}) custom-call(s32[1]{0:T(128)} %bitcast.1.me, f32[128,1024]{1,0:T(8,128)S(1)} %spectral_back.1.acc, bf16[51,64,512]{2,1,0:T(8,128)(2,1)} %lag_mixing.3, bf16[1024,512]{1,0:T(8,128)(2,1)S(1)} %place.1.grads, ...), custom_call_target="tpu_custom_call" | custom-call | tf_op jit(solution)/shard_map/lag_back/pallas_call | solution.py:494
  107.0 3.6 %unit_grads.1 = bf16[2,784,256]{2,1,0:T(8,128)(2,1)S(1)} custom-call(s32[1]{0:T(128)} %bitcast.1.me, bf16[2,2,64,512]{3,2,1,0:T(8,128)(2,1)S(1)} %maximum_select_fusion.8.refs_0_, bf16[2,2,64,512]{3,2,1,0:T(8,128)(2,1)S(1)} %collective-permute-done.18.refs_1_, bf16[2,2,80,512]{3,2,1,0:T(8,128)(2,1)S(1)} %maximum_select_fusion.refs_2_, ...), custom_call_target="tpu_custom_call" | custom-call | tf_op jit(solution)/shard_map/unit_grads/pallas_call | solution.py:770
  111.3 2.0 %collective-permute-start.22 = (bf16[2,2,64,128]{3,2,1,0:T(8,128)(2,1)S(1)}, bf16[2,2,64,128]{3,2,1,0:T(8,128)(2,1)S(1)}, u32[]{:S(2)}, u32[]{:S(2)}) collective-permute-start(bf16[2,2,64,128]{3,2,1,0:T(8,128)(2,1)S(1)} %bitcast.74), channel_id=1, source_target_pairs={{0,2},{1,3},{2,0},{3,1},{4,6},{5,7},{6,4},{7,5},{8,10},{9,11},{10,... | collective-permute-start | bytes 196616 | tf_op jit(solution)/shard_map/ppermute | solution.py:826
  113.3 4.3 %own_mixing_grad.1 = (bf16[2,24,64,512]{3,2,1,0:T(8,128)(2,1)S(1)}, bf16[3,64,512]{2,1,0:T(8,128)(2,1)S(1)}) custom-call(bf16[2,24,64,1024]{3,2,1,0:T(8,128)(2,1)S(1)} %get-tuple-element.121.maps, bf16[3,64,1024]{2,1,0:T(8,128)(2,1)S(1)} %get-tuple-element.102.inputs.lags, bf16[1024,512]{1,0:T(8,128)(2,1)S(1)} %place.1.grads), custom_call_target="tpu_custom_call" | custom-call | tf_op jit(solution)/shard_map/own_mixing_grad/pallas_call | solution.py:653
  118.4 3.1 %collective-permute-start.25 = (bf16[1,4,64,128]{3,2,1,0:T(8,128)(2,1)S(1)}, bf16[1,4,64,128]{3,2,1,0:T(8,128)(2,1)S(1)}, u32[]{:S(2)}, u32[]{:S(2)}) collective-permute-start(bf16[1,4,64,128]{3,2,1,0:T(8,128)(2,1)S(1)} %get-tuple-element.152), channel_id=1, source_target_pairs={{0,4},{1,5},{2,6},{3,7},{4,0},{5,1},{6,2},{7,3},{8,12},{9,13},{10,... | collective-permute-start | bytes 196616 | tf_op jit(solution)/shard_map/ppermute | solution.py:826
  121.5 2.3 %mixing_grad.2.part = bf16[1536,512]{1,0:T(8,128)(2,1)S(1)} custom-call(bf16[2,24,64,1024]{3,2,1,0:T(8,128)(2,1)S(1)} %get-tuple-element.117.maps, bf16[3,64,1024]{2,1,0:T(8,128)(2,1)S(1)} %get-tuple-element.118.lags, bf16[1024,512]{1,0:T(8,128)(2,1)S(1)} %collective-permute-done.24.grads, bf16[2,24,64,512]{3,2,1,0:T(8,128)(2,1)S(1)} %get-tuple-element.127.own, ...), custom_call_target="tpu_custom_call" | custom-call | tf_op jit(solution)/shard_map/mixing_grad/pallas_call | solution.py:686
  123.8 2.7 %mixing_grad.3.part = bf16[1728,512]{1,0:T(8,128)(2,1)S(1)} custom-call(bf16[2,24,64,1024]{3,2,1,0:T(8,128)(2,1)S(1)} %get-tuple-element.117.maps, bf16[3,64,1024]{2,1,0:T(8,128)(2,1)S(1)} %get-tuple-element.118.lags, bf16[1024,512]{1,0:T(8,128)(2,1)S(1)} %collective-permute-done.24.grads, bf16[2,24,64,512]{3,2,1,0:T(8,128)(2,1)S(1)} %get-tuple-element.127.own, ...), custom_call_target="tpu_custom_call" | custom-call | tf_op jit(solution)/shard_map/mixing_grad/pallas_call | solution.py:686
  126.5 2.8 %collective-permute-done.26 = bf16[784,256]{1,0:T(8,128)(2,1)S(1)} collective-permute-done((bf16[784,256]{1,0:T(8,128)(2,1)S(1)}, bf16[784,256]{1,0:T(8,128)(2,1)S(1)}, u32[]{:S(2)}, u32[]{:S(2)}) %collective-permute-start.26) | collective-permute-done | bytes 401440 | tf_op jit(solution)/shard_map/ppermute | solution.py:826
  130.0 0.9 first_norm_back.1
  130.9 4.9 %collective-permute-done.29.other = bf16[784,256]{1,0:T(8,128)(2,1)S(1)} collective-permute-done((bf16[784,256]{1,0:T(8,128)(2,1)S(1)}, bf16[784,256]{1,0:T(8,128)(2,1)S(1)}, u32[]{:S(2)}, u32[]{:S(2)}) %collective-permute-start.29) | collective-permute-done | bytes 401440 | tf_op jit(solution)/shard_map/ppermute | solution.py:826
  135.8 1.2 finish_units.1
  137.5 2.1 %finish_mixing.2.refs_0_ = f32[51,64,512]{2,1,0:T(8,128)} custom-call(bf16[1536,512]{1,0:T(8,128)(2,1)S(1)} %mixing_grad.2.part, bf16[1536,512]{1,0:T(8,128)(2,1)S(1)} %collective-permute-done.28.got), custom_call_target="tpu_custom_call" | custom-call | tf_op jit(solution)/shard_map/finish_mixing/pallas_call | solution.py:707
  139.7 2.3 %finish_mixing.3 = f32[51,64,512]{2,1,0:T(8,128)} custom-call(bf16[1728,512]{1,0:T(8,128)(2,1)S(1)} %mixing_grad.3.part, bf16[1728,512]{1,0:T(8,128)(2,1)S(1)} %collective-permute-done.27.got, f32[51,64,512]{2,1,0:T(8,128)} %finish_mixing.2.refs_0_), custom_call_target="tpu_custom_call", output_to_operand_aliasing={{}: (2, {})} | custom-call | tf_op jit(solution)/shard_map/finish_mixing/pallas_call | solution.py:707
  (82 shorter events, 5.4 us)
Async XLA Ops:
  0.6 10.6 %collective-permute-start.3 = (bf16[1,128,512]{2,1,0:T(8,128)(2,1)}, bf16[1,128,512]{2,1,0:T(8,128)(2,1)S(1)}, u32[]{:S(2)}, u32[]{:S(2)}) collective-permute-start(bf16[1,128,512]{2,1,0:T(8,128)(2,1)} %cotangent.1), channel_id=1, source_target_pairs={{0,4},{1,5},{2,6},{3,7},{4,0},{5,1},{6,2},{7,3},{8,12},{9,13},{10,... | collective-permute-start | bytes 393224 | tf_op jit(solution)/shard_map/ppermute | solution.py:826
  7.3 12.2 %all-to-all-start = ((bf16[8,80,128]{2,1,0:T(8,128)(2,1)}), bf16[8,80,128]{2,1,0:T(8,128)(2,1)S(1)}, u32[]{:S(2)}, u32[]{:S(2)}) async-start(bf16[8,80,128]{2,1,0:T(8,128)(2,1)} %first_norm.1), calls=%async_computation | async-start | bytes 327680 | tf_op jit(solution)/shard_map/all_to_all | solution.py:942
  12.3 8.7 %collective-permute-start.4 = (bf16[2,64,512]{2,1,0:T(8,128)(2,1)S(1)}, bf16[2,64,512]{2,1,0:T(8,128)(2,1)S(1)}, u32[]{:S(2)}, u32[]{:S(2)}) collective-permute-start(bf16[2,64,512]{2,1,0:T(8,128)(2,1)S(1)} %get-tuple-element.151), channel_id=1, source_target_pairs={{0,2},{1,3},{2,0},{3,1},{4,6},{5,7},{6,4},{7,5},{8,10},{9,11},{10,... | collective-permute-start | bytes 393224 | tf_op jit(solution)/shard_map/ppermute | solution.py:826
  14.2 6.9 %collective-permute-start.5 = (bf16[2,64,512]{2,1,0:T(8,128)(2,1)S(1)}, bf16[2,64,512]{2,1,0:T(8,128)(2,1)S(1)}, u32[]{:S(2)}, u32[]{:S(2)}) collective-permute-start(bf16[2,64,512]{2,1,0:T(8,128)(2,1)S(1)} %get-tuple-element.148), channel_id=1, source_target_pairs={{0,1},{1,0},{2,3},{3,2},{4,5},{5,4},{6,7},{7,6},{8,9},{9,8},{10,11... | collective-permute-start | bytes 393224 | tf_op jit(solution)/shard_map/ppermute | solution.py:826
  19.5 16.0 %collective-permute-start.2 = (bf16[8,80,128]{2,1,0:T(8,128)(2,1)S(1)}, bf16[8,80,128]{2,1,0:T(8,128)(2,1)S(1)}, u32[]{:S(2)}, u32[]{:S(2)}) collective-permute-start(bf16[8,80,128]{2,1,0:T(8,128)(2,1)S(1)} %all-to-all-done.pieces), channel_id=1, source_target_pairs={{0,16},{8,24},{16,0},{24,8},{1,17},{9,25},{17,1},{25,9},{2,18},{10... | collective-permute-start | bytes 491528 | tf_op jit(solution)/shard_map/ppermute | solution.py:826
  21.1 0.8 copy-start.5
  33.8 7.8 %collective-permute-start.1 = (bf16[2,2,256,128]{3,2,0,1:T(8,128)(2,1)S(1)}, bf16[2,2,256,128]{3,2,0,1:T(8,128)(2,1)S(1)}, u32[]{:S(2)}, u32[]{:S(2)}) collective-permute-start(bf16[2,2,256,128]{3,2,0,1:T(8,128)(2,1)S(1)} %copy.23), channel_id=1, source_target_pairs={{0,2},{1,3},{2,0},{3,1},{4,6},{5,7},{6,4},{7,5},{8,10},{9,11},{10,... | collective-permute-start | bytes 786440 | tf_op jit(solution)/shard_map/ppermute | solution.py:826
  34.0 8.4 %collective-permute-start = (bf16[2,2,256,128]{3,2,0,1:T(8,128)(2,1)S(1)}, bf16[2,2,256,128]{3,2,0,1:T(8,128)(2,1)S(1)}, u32[]{:S(2)}, u32[]{:S(2)}) collective-permute-start(bf16[2,2,256,128]{3,2,0,1:T(8,128)(2,1)S(1)} %copy.21), channel_id=1, source_target_pairs={{0,1},{1,0},{2,3},{3,2},{4,5},{5,4},{6,7},{7,6},{8,9},{9,8},{10,11... | collective-permute-start | bytes 786440 | tf_op jit(solution)/shard_map/ppermute | solution.py:826
  35.5 24.5 %copy-start.1 = (bf16[512,2048]{1,0:T(8,128)(2,1)S(1)}, bf16[512,2048]{1,0:T(8,128)(2,1)}, u32[]{:S(2)}) copy-start(bf16[512,2048]{1,0:T(8,128)(2,1)} %refs_9_.1) | copy-start | bytes 6291460
  35.5 24.5 %copy-start.2 = (bf16[2048,512]{1,0:T(8,128)(2,1)S(1)}, bf16[2048,512]{1,0:T(8,128)(2,1)}, u32[]{:S(2)}) copy-start(bf16[2048,512]{1,0:T(8,128)(2,1)} %refs_10_.1) | copy-start | bytes 6291460
  39.0 21.1 %copy-start = (bf16[512,2048]{1,0:T(8,128)(2,1)S(1)}, bf16[512,2048]{1,0:T(8,128)(2,1)}, u32[]{:S(2)}) copy-start(bf16[512,2048]{1,0:T(8,128)(2,1)} %refs_8_.1) | copy-start | bytes 6291460
  39.0 21.1 %copy-start.3 = (bf16[1,128,512]{2,1,0:T(8,128)(2,1)S(1)}, bf16[1,128,512]{2,1,0:T(8,128)(2,1)}, u32[]{:S(2)}) copy-start(bf16[1,128,512]{2,1,0:T(8,128)(2,1)} %hidden.1) | copy-start | bytes 393220
  39.0 21.1 %copy-start.4 = (bf16[1,128,512]{2,1,0:T(8,128)(2,1)S(1)}, bf16[1,128,512]{2,1,0:T(8,128)(2,1)}, u32[]{:S(2)}) copy-start(bf16[1,128,512]{2,1,0:T(8,128)(2,1)} %cotangent.1) | copy-start | bytes 393220
  39.0 21.1 %copy-start.8 = (f32[512]{0:T(512)S(1)}, f32[512]{0:T(512)}, u32[]{:S(2)}) copy-start(f32[512]{0:T(512)} %param.15) | copy-start | bytes 6148
  39.0 7.0 %collective-permute-start.6 = (bf16[2,2,64,512]{3,2,1,0:T(8,128)(2,1)S(1)}, bf16[2,2,64,512]{3,2,1,0:T(8,128)(2,1)S(1)}, u32[]{:S(2)}, u32[]{:S(2)}) collective-permute-start(bf16[2,2,64,512]{3,2,1,0:T(8,128)(2,1)S(1)} %maximum_select_fusion.3.refs_4_), channel_id=1, source_target_pairs={{0,1},{1,0},{2,3},{3,2},{4,5},{5,4},{6,7},{7,6},{8,9},{9,8},{10,11... | collective-permute-start | bytes 786440 | tf_op jit(solution)/shard_map/ppermute | solution.py:826
  39.7 6.4 %collective-permute-start.7 = (bf16[2,2,64,512]{3,2,1,0:T(8,128)(2,1)S(1)}, bf16[2,2,64,512]{3,2,1,0:T(8,128)(2,1)S(1)}, u32[]{:S(2)}, u32[]{:S(2)}) collective-permute-start(bf16[2,2,64,512]{3,2,1,0:T(8,128)(2,1)S(1)} %maximum_select_fusion.4.refs_6_), channel_id=1, source_target_pairs={{0,2},{1,3},{2,0},{3,1},{4,6},{5,7},{6,4},{7,5},{8,10},{9,11},{10,... | collective-permute-start | bytes 786440 | tf_op jit(solution)/shard_map/ppermute | solution.py:826
  46.1 5.0 %collective-permute-start.8 = (bf16[2,1,256,128]{3,2,0,1:T(8,128)(2,1)S(1)}, bf16[2,1,256,128]{3,2,0,1:T(8,128)(2,1)S(1)}, u32[]{:S(2)}, u32[]{:S(2)}) collective-permute-start(bf16[2,1,256,128]{3,2,0,1:T(8,128)(2,1)S(1)} %constant_dynamic-slice_fusion.1), channel_id=1, source_target_pairs={{0,2},{1,3},{2,0},{3,1},{4,6},{5,7},{6,4},{7,5},{8,10},{9,11},{10,... | collective-permute-start | bytes 393224 | tf_op jit(solution)/shard_map/ppermute | solution.py:826
  48.1 5.0 %collective-permute-start.9 = (bf16[2,1,256,128]{3,2,0,1:T(8,128)(2,1)S(1)}, bf16[2,1,256,128]{3,2,0,1:T(8,128)(2,1)S(1)}, u32[]{:S(2)}, u32[]{:S(2)}) collective-permute-start(bf16[2,1,256,128]{3,2,0,1:T(8,128)(2,1)S(1)} %constant_dynamic-slice_fusion), channel_id=1, source_target_pairs={{0,1},{1,0},{2,3},{3,2},{4,5},{5,4},{6,7},{7,6},{8,9},{9,8},{10,11... | collective-permute-start | bytes 393224 | tf_op jit(solution)/shard_map/ppermute | solution.py:826
  53.2 6.9 %collective-permute-start.10 = (bf16[1,512,128]{2,1,0:T(8,128)(2,1)S(1)}, bf16[1,512,128]{2,1,0:T(8,128)(2,1)S(1)}, u32[]{:S(2)}, u32[]{:S(2)}) collective-permute-start(bf16[1,512,128]{2,1,0:T(8,128)(2,1)S(1)} %fusion.3), channel_id=1, source_target_pairs={{0,4},{1,5},{2,6},{3,7},{4,0},{5,1},{6,2},{7,3},{8,12},{9,13},{10,... | collective-permute-start | bytes 393224 | tf_op jit(solution)/shard_map/ppermute | solution.py:826
  60.1 5.7 %copy-start.6 = (bf16[24,1024]{1,0:T(8,128)(2,1)S(1)}, bf16[24,1024]{1,0:T(8,128)(2,1)}, u32[]{:S(2)}) copy-start(bf16[24,1024]{1,0:T(8,128)(2,1)} %filters.7) | copy-start | bytes 147460
  65.4 6.4 %collective-permute-start.11 = (bf16[1,128,512]{2,1,0:T(8,128)(2,1)S(1)}, bf16[1,128,512]{2,1,0:T(8,128)(2,1)S(1)}, u32[]{:S(2)}, u32[]{:S(2)}) collective-permute-start(bf16[1,128,512]{2,1,0:T(8,128)(2,1)S(1)} %bitcast.58), channel_id=1, source_target_pairs={{0,4},{1,5},{2,6},{3,7},{4,0},{5,1},{6,2},{7,3},{8,12},{9,13},{10,... | collective-permute-start | bytes 393224 | tf_op jit(solution)/shard_map/ppermute | solution.py:826
  71.9 6.6 %collective-permute-start.14 = (bf16[2,64,512]{2,1,0:T(8,128)(2,1)S(1)}, bf16[2,64,512]{2,1,0:T(8,128)(2,1)S(1)}, u32[]{:S(2)}, u32[]{:S(2)}) collective-permute-start(bf16[2,64,512]{2,1,0:T(8,128)(2,1)S(1)} %get-tuple-element.144), channel_id=1, source_target_pairs={{0,1},{1,0},{2,3},{3,2},{4,5},{5,4},{6,7},{7,6},{8,9},{9,8},{10,11... | collective-permute-start | bytes 393224 | tf_op jit(solution)/shard_map/ppermute | solution.py:826
  73.7 5.6 %collective-permute-start.12 = (bf16[2,64,512]{2,1,0:T(8,128)(2,1)S(1)}, bf16[2,64,512]{2,1,0:T(8,128)(2,1)S(1)}, u32[]{:S(2)}, u32[]{:S(2)}) collective-permute-start(bf16[2,64,512]{2,1,0:T(8,128)(2,1)S(1)} %get-tuple-element.147), channel_id=1, source_target_pairs={{0,2},{1,3},{2,0},{3,1},{4,6},{5,7},{6,4},{7,5},{8,10},{9,11},{10,... | collective-permute-start | bytes 393224 | tf_op jit(solution)/shard_map/ppermute | solution.py:826
  74.8 7.2 %collective-permute-start.16 = (bf16[1,144,512]{2,1,0:T(8,128)(2,1)S(1)}, bf16[1,144,512]{2,1,0:T(8,128)(2,1)S(1)}, u32[]{:S(2)}, u32[]{:S(2)}) collective-permute-start(bf16[1,144,512]{2,1,0:T(8,128)(2,1)S(1)} %bitcast.56), channel_id=1, source_target_pairs={{0,4},{1,5},{2,6},{3,7},{4,0},{5,1},{6,2},{7,3},{8,12},{9,13},{10,... | collective-permute-start | bytes 442376 | tf_op jit(solution)/shard_map/ppermute | solution.py:826
  78.4 12.8 %collective-permute-start.15 = (bf16[2,2,64,512]{3,2,1,0:T(8,128)(2,1)S(1)}, bf16[2,2,64,512]{3,2,1,0:T(8,128)(2,1)S(1)}, u32[]{:S(2)}, u32[]{:S(2)}) collective-permute-start(bf16[2,2,64,512]{3,2,1,0:T(8,128)(2,1)S(1)} %maximum_select_fusion.7.part2), channel_id=1, source_target_pairs={{0,2},{1,3},{2,0},{3,1},{4,6},{5,7},{6,4},{7,5},{8,10},{9,11},{10,... | collective-permute-start | bytes 786440 | tf_op jit(solution)/shard_map/ppermute | solution.py:826
  79.3 11.9 %collective-permute-start.13 = (bf16[2,2,64,512]{3,2,1,0:T(8,128)(2,1)S(1)}, bf16[2,2,64,512]{3,2,1,0:T(8,128)(2,1)S(1)}, u32[]{:S(2)}, u32[]{:S(2)}) collective-permute-start(bf16[2,2,64,512]{3,2,1,0:T(8,128)(2,1)S(1)} %maximum_select_fusion.6.part0), channel_id=1, source_target_pairs={{0,1},{1,0},{2,3},{3,2},{4,5},{5,4},{6,7},{7,6},{8,9},{9,8},{10,11... | collective-permute-start | bytes 786440 | tf_op jit(solution)/shard_map/ppermute | solution.py:826
  82.1 8.4 %collective-permute-start.19 = (bf16[2,80,512]{2,1,0:T(8,128)(2,1)S(1)}, bf16[2,80,512]{2,1,0:T(8,128)(2,1)S(1)}, u32[]{:S(2)}, u32[]{:S(2)}) collective-permute-start(bf16[2,80,512]{2,1,0:T(8,128)(2,1)S(1)} %get-tuple-element.140), channel_id=1, source_target_pairs={{0,1},{1,0},{2,3},{3,2},{4,5},{5,4},{6,7},{7,6},{8,9},{9,8},{10,11... | collective-permute-start | bytes 491528 | tf_op jit(solution)/shard_map/ppermute | solution.py:826
  82.2 10.7 %collective-permute-start.17 = (bf16[2,64,512]{2,1,0:T(8,128)(2,1)S(1)}, bf16[2,64,512]{2,1,0:T(8,128)(2,1)S(1)}, u32[]{:S(2)}, u32[]{:S(2)}) collective-permute-start(bf16[2,64,512]{2,1,0:T(8,128)(2,1)S(1)} %get-tuple-element.142), channel_id=1, source_target_pairs={{0,2},{1,3},{2,0},{3,1},{4,6},{5,7},{6,4},{7,5},{8,10},{9,11},{10,... | collective-permute-start | bytes 393224 | tf_op jit(solution)/shard_map/ppermute | solution.py:826
  90.6 16.4 %collective-permute-start.20 = (bf16[2,2,80,512]{3,2,1,0:T(8,128)(2,1)S(1)}, bf16[2,2,80,512]{3,2,1,0:T(8,128)(2,1)S(1)}, u32[]{:S(2)}, u32[]{:S(2)}) collective-permute-start(bf16[2,2,80,512]{3,2,1,0:T(8,128)(2,1)S(1)} %maximum_select_fusion.refs_2_), channel_id=1, source_target_pairs={{0,2},{1,3},{2,0},{3,1},{4,6},{5,7},{6,4},{7,5},{8,10},{9,11},{10,... | collective-permute-start | bytes 983048 | tf_op jit(solution)/shard_map/ppermute | solution.py:826
  91.3 26.4 %collective-permute-start.24 = (bf16[1024,512]{1,0:T(8,128)(2,1)S(1)}, bf16[1024,512]{1,0:T(8,128)(2,1)S(1)}, u32[]{:S(2)}, u32[]{:S(2)}) collective-permute-start(bf16[1024,512]{1,0:T(8,128)(2,1)S(1)} %place.1.grads), channel_id=1, source_target_pairs={{0,16},{8,24},{16,0},{24,8},{1,17},{9,25},{17,1},{25,9},{2,18},{10... | collective-permute-start | bytes 3145736 | tf_op jit(solution)/shard_map/ppermute | solution.py:826
  92.9 14.0 %collective-permute-start.18 = (bf16[2,2,64,512]{3,2,1,0:T(8,128)(2,1)S(1)}, bf16[2,2,64,512]{3,2,1,0:T(8,128)(2,1)S(1)}, u32[]{:S(2)}, u32[]{:S(2)}) collective-permute-start(bf16[2,2,64,512]{3,2,1,0:T(8,128)(2,1)S(1)} %maximum_select_fusion.8.refs_0_), channel_id=1, source_target_pairs={{0,1},{1,0},{2,3},{3,2},{4,5},{5,4},{6,7},{7,6},{8,9},{9,8},{10,11... | collective-permute-start | bytes 786440 | tf_op jit(solution)/shard_map/ppermute | solution.py:826
  106.8 4.3 %collective-permute-start.21 = (bf16[4,64,128]{2,1,0:T(8,128)(2,1)S(1)}, bf16[4,64,128]{2,1,0:T(8,128)(2,1)S(1)}, u32[]{:S(2)}, u32[]{:S(2)}) collective-permute-start(bf16[4,64,128]{2,1,0:T(8,128)(2,1)S(1)} %get-tuple-element.114), channel_id=1, source_target_pairs={{0,1},{1,0},{2,3},{3,2},{4,5},{5,4},{6,7},{7,6},{8,9},{9,8},{10,11... | collective-permute-start | bytes 196616 | tf_op jit(solution)/shard_map/ppermute | solution.py:826
  111.2 6.4 %collective-permute-start.23 = (bf16[784,256]{1,0:T(8,128)(2,1)S(1)}, bf16[784,256]{1,0:T(8,128)(2,1)S(1)}, u32[]{:S(2)}, u32[]{:S(2)}) collective-permute-start(bf16[784,256]{1,0:T(8,128)(2,1)S(1)} %dynamic-slice_bitcast_fusion), channel_id=1, source_target_pairs={{0,8},{8,0},{16,24},{24,16},{1,9},{9,1},{17,25},{25,17},{2,10},{10... | collective-permute-start | bytes 1204232 | tf_op jit(solution)/shard_map/ppermute | solution.py:826
  111.3 7.0 %collective-permute-start.22 = (bf16[2,2,64,128]{3,2,1,0:T(8,128)(2,1)S(1)}, bf16[2,2,64,128]{3,2,1,0:T(8,128)(2,1)S(1)}, u32[]{:S(2)}, u32[]{:S(2)}) collective-permute-start(bf16[2,2,64,128]{3,2,1,0:T(8,128)(2,1)S(1)} %bitcast.74), channel_id=1, source_target_pairs={{0,2},{1,3},{2,0},{3,1},{4,6},{5,7},{6,4},{7,5},{8,10},{9,11},{10,... | collective-permute-start | bytes 196616 | tf_op jit(solution)/shard_map/ppermute | solution.py:826
  117.8 11.5 %collective-permute-start.26 = (bf16[784,256]{1,0:T(8,128)(2,1)S(1)}, bf16[784,256]{1,0:T(8,128)(2,1)S(1)}, u32[]{:S(2)}, u32[]{:S(2)}) collective-permute-start(bf16[784,256]{1,0:T(8,128)(2,1)S(1)} %fusion), channel_id=1, source_target_pairs={{0,16},{8,24},{16,0},{24,8},{1,17},{9,25},{17,1},{25,9},{2,18},{10... | collective-permute-start | bytes 1204232 | tf_op jit(solution)/shard_map/ppermute | solution.py:826
  118.4 8.1 %collective-permute-start.25 = (bf16[1,4,64,128]{3,2,1,0:T(8,128)(2,1)S(1)}, bf16[1,4,64,128]{3,2,1,0:T(8,128)(2,1)S(1)}, u32[]{:S(2)}, u32[]{:S(2)}) collective-permute-start(bf16[1,4,64,128]{3,2,1,0:T(8,128)(2,1)S(1)} %get-tuple-element.152), channel_id=1, source_target_pairs={{0,4},{1,5},{2,6},{3,7},{4,0},{5,1},{6,2},{7,3},{8,12},{9,13},{10,... | collective-permute-start | bytes 196616 | tf_op jit(solution)/shard_map/ppermute | solution.py:826
  123.8 6.2 %copy-start.7 = (f32[512]{0:T(512)S(1)}, f32[512]{0:T(512)}, u32[]{:S(2)}) copy-start(f32[512]{0:T(512)} %param.13) | copy-start | bytes 6148
  129.2 10.4 %collective-permute-start.27 = (bf16[1728,512]{1,0:T(8,128)(2,1)S(1)}, bf16[1728,512]{1,0:T(8,128)(2,1)S(1)}, u32[]{:S(2)}, u32[]{:S(2)}) collective-permute-start(bf16[1728,512]{1,0:T(8,128)(2,1)S(1)} %mixing_grad.3.part), channel_id=1, source_target_pairs={{0,8},{8,0},{16,24},{24,16},{1,9},{9,1},{17,25},{25,17},{2,10},{10... | collective-permute-start | bytes 5308424 | tf_op jit(solution)/shard_map/ppermute | solution.py:826
  129.2 8.3 %collective-permute-start.28 = (bf16[1536,512]{1,0:T(8,128)(2,1)S(1)}, bf16[1536,512]{1,0:T(8,128)(2,1)S(1)}, u32[]{:S(2)}, u32[]{:S(2)}) collective-permute-start(bf16[1536,512]{1,0:T(8,128)(2,1)S(1)} %mixing_grad.2.part), channel_id=1, source_target_pairs={{0,8},{8,0},{16,24},{24,16},{1,9},{9,1},{17,25},{25,17},{2,10},{10... | collective-permute-start | bytes 4718600 | tf_op jit(solution)/shard_map/ppermute | solution.py:826
  129.9 5.9 %collective-permute-start.29 = (bf16[784,256]{1,0:T(8,128)(2,1)S(1)}, bf16[784,256]{1,0:T(8,128)(2,1)S(1)}, u32[]{:S(2)}, u32[]{:S(2)}) collective-permute-start(bf16[784,256]{1,0:T(8,128)(2,1)S(1)} %add_convert_fusion.mine), channel_id=1, source_target_pairs={{0,8},{8,0},{16,24},{24,16},{1,9},{9,1},{17,25},{25,17},{2,10},{10... | collective-permute-start | bytes 1204232 | tf_op jit(solution)/shard_map/ppermute | solution.py:826

commit v4 on v3

--- a/solution.py
+++ b/solution.py
@@ -12,7 +12,7 @@
 AR = 3
 TILE = 256
 HALF = 128
-PER_STEP = 4
+PER_STEP = 8
 
 eps_norm = 1e-05
 
@@ -104,13 +104,7 @@
         grid_spec=pltpu.PrefetchScalarGridSpec(
             num_scalar_prefetch=1,
             grid=(1,),
-            in_specs=[
-                whole(kept.shape),
-                whole(came.shape),
-                whole(hidden_in.shape),
-                whole((1, width)),
-                whole(grad.shape),
-            ],
+            in_specs=[in_vmem()] * 5,
             out_specs=whole(hidden_in.shape),
         ),
         out_shape=jax.ShapeDtypeStruct(hidden_in.shape, jnp.float32),
@@ -194,7 +188,7 @@
     width = taps.shape[1]
     pairs = tile_pairs(length)
     parity = parity_lanes(channels, TILE)
-    for k in range(PER_STEP):
+    for k in range(slabs.shape[0]):
         slab = slabs.at[k]
         build_slab(taps[pl.ds(first + k, 1), :], slab, width)
         for tb in range(length // TILE):
@@ -210,22 +204,15 @@
 
 def maps_kernel(start, filters, pieces, *refs):
     maps, lags, taps, slabs, masks, doubled = refs[-6:]
-    step = pl.program_id(0)
-
-    @pl.when(step == 0)
-    def _():
-        start_maps(filters, pieces, lags, taps, masks, doubled)
-
-    step_maps(start + step * PER_STEP, maps, taps, slabs, masks, doubled)
+    start_maps(filters, pieces, lags, taps, masks, doubled)
+    step_maps(start, maps, taps, slabs, masks, doubled)
 
 
 def mixed_kernel(
     me,
     filters,
     pieces,
-    plus_mixing,
-    minus_mixing,
-    lag_mixing,
+    mixing_given,
     maps,
     lags,
     keep0,
@@ -237,29 +224,40 @@
     masks,
     doubled,
     acc,
+    mixing,
+    arrived,
 ):
-    _, channels, model_width = plus_mixing.shape
+    _, _, model_width = mixing.shape
     count, _, share = pieces.shape
-    length = lags.shape[2]
+    filter_count, length = maps.shape[1], lags.shape[2]
     step = pl.program_id(0)
+
+    copy = pltpu.make_async_copy(mixing_given, mixing, arrived)
 
     @pl.when(step == 0)
     def _():
+        copy.start()
         start_maps(filters, pieces, lags, taps, masks, doubled)
         acc[...] = jnp.zeros_like(acc)
 
     step_maps(step * PER_STEP, maps, taps, slabs, masks, doubled)
+
+    @pl.when(step == 0)
+    def _():
+        copy.wait()
+
     def part(weights, values):
         return contract_first(weights.reshape(-1, model_width), values.reshape(-1, length))
 
-    own = pl.ds(step * PER_STEP, PER_STEP)
-    total = part(plus_mixing[...], maps[0, own]) + part(minus_mixing[...], maps[1, own])
+    plus = pl.ds(step * PER_STEP, PER_STEP)
+    minus = pl.ds(filter_count + step * PER_STEP, PER_STEP)
+    total = part(mixing[plus], maps[0, plus]) + part(mixing[minus], maps[1, plus])
     for i in range(count):
         acc[i] += total[:, i * share : (i + 1) * share]
 
     @pl.when(step == pl.num_programs(0) - 1)
     def _():
-        last = part(lag_mixing[...], lags[...])
+        last = part(mixing[2 * filter_count :], lags[...])
         for i in range(count):
             acc[i] += last[:, i * share : (i + 1) * share]
         half = model_width // 2
@@ -298,8 +296,8 @@
         grid_spec=pltpu.PrefetchScalarGridSpec(
             num_scalar_prefetch=1,
             grid=(1,),
-            in_specs=[whole(part.shape) for part in parts],
-            out_specs=whole(shape),
+            in_specs=[in_vmem()] * 4,
+            out_specs=in_vmem(),
         ),
         out_shape=pltpu.VMEM(shape, jnp.bfloat16),
         compiler_params=vmem(8),
@@ -307,10 +305,9 @@
     )(me, *parts)
 
 
-def spectral_back_kernel(
-    filters, plus_mixing, minus_mixing, pieces, grads, acc, taps, slabs, masks, both
-):
-    _, channels, model_width = plus_mixing.shape
+def spectral_back_kernel(filters, mixing, pieces, grads, acc, taps, slabs, masks, both):
+    _, channels, model_width = mixing.shape
+    count = filters.shape[0]
     length, width = acc.shape[1], taps.shape[1]
     reach = length // 2
     pairs = tile_pairs(length)
@@ -327,9 +324,13 @@
         taps[...] = product(filters[:, :width], flip)
 
     sign = parity_lanes(rows, length, jnp.bfloat16)
-    plus = contract_last(plus_mixing[...].reshape(rows, model_width), grads[...])
+    plus = contract_last(
+        mixing[pl.ds(step * PER_STEP, PER_STEP)].reshape(rows, model_width), grads[...]
+    )
     both[:, :channels, :] = plus.astype(jnp.bfloat16).reshape(PER_STEP, channels, length)
-    minus = contract_last(minus_mixing[...].reshape(rows, model_width), grads[...])
+    minus = contract_last(
+        mixing[pl.ds(count + step * PER_STEP, PER_STEP)].reshape(rows, model_width), grads[...]
+    )
     both[:, channels:, :] = (minus.astype(jnp.bfloat16) * sign).reshape(
         PER_STEP, channels, length
     )
@@ -350,12 +351,12 @@
         acc[:, block(sb)] = total
 
 
-def lag_back_kernel(me, acc, lag_mixing, grads, inputs, pieces, scales, kept, given, gain):
-    _, channels, model_width = lag_mixing.shape
+def lag_back_kernel(me, acc, mixing, grads, inputs, pieces, scales, kept, given, gain):
+    _, channels, model_width = mixing.shape
     length = acc.shape[1]
     half, _, share = kept.shape
     ids = segment_row(pieces)
-    lag_grad = contract_last(lag_mixing[...].reshape(AR * channels, model_width), grads[...])
+    lag_grad = contract_last(mixing[2 * K :].reshape(AR * channels, model_width), grads[...])
     total = acc[:channels] + parity_lanes(channels, length) * acc[channels:]
     for j in range(AR):
         term = lag_grad[j * channels : (j + 1) * channels]
@@ -381,21 +382,24 @@
     row = lax.broadcasted_iota(jnp.int32, by_lane.shape, 0)
     lane = lax.broadcasted_iota(jnp.int32, by_lane.shape, 1)
     total = jnp.sum(jnp.where(row == lane, by_lane, 0.0), axis=0, keepdims=True)
-    gain[...] = jnp.broadcast_to(total / scales[...], gain.shape)
-
-
-def toeplitz_scratch(length, count):
+    width = scales.shape[1]
+    turned = jnp.broadcast_to(scales[...], (8, width))
+    turned = pltpu.roll(turned, lax.rem(width - me[0] * channels, width), 1)
+    gain[...] = jnp.broadcast_to(total, gain.shape) / turned[:, :128]
+
+
+def toeplitz_scratch(length, count, slabs):
     width = slab_width(length)
     return [
         pltpu.VMEM((count, width), jnp.float32),
-        pltpu.VMEM((PER_STEP, TILE, width), jnp.bfloat16),
+        pltpu.VMEM((slabs, TILE, width), jnp.bfloat16),
         pltpu.VMEM((len(tile_pairs(length)), TILE, TILE), jnp.bfloat16),
     ]
 
 
-def maps_scratch(channels, length, count):
+def maps_scratch(channels, length, count, slabs):
     return [
-        *toeplitz_scratch(length, count),
+        *toeplitz_scratch(length, count, slabs),
         pltpu.VMEM((2 * channels, length), jnp.bfloat16),
     ]
 
@@ -405,20 +409,15 @@
     given = [] if into is None else [into]
     return pl.pallas_call(
         functools.partial(maps_kernel, start),
-        grid=(count // PER_STEP,),
-        in_specs=[
-            whole(filters.shape),
-            whole(pieces.shape),
-            *[in_vmem() for _ in given],
-        ],
-        out_specs=[in_vmem(), whole((AR, channels, length))],
+        in_specs=[in_vmem(), in_vmem(), *[in_vmem() for _ in given]],
+        out_specs=[in_vmem()] * 2,
         out_shape=[
             pltpu.VMEM((2, K, channels, length), jnp.bfloat16),
-            jax.ShapeDtypeStruct((AR, channels, length), jnp.bfloat16),
+            pltpu.VMEM((AR, channels, length), jnp.bfloat16),
         ],
-        scratch_shapes=maps_scratch(channels, length, filters.shape[0]),
+        scratch_shapes=maps_scratch(channels, length, filters.shape[0], count),
         input_output_aliases={2: 0} if given else {},
-        compiler_params=vmem(16),
+        compiler_params=vmem(20),
         cost_estimate=pl.CostEstimate(
             flops=6 * channels * count * length * length, transcendentals=0, bytes_accessed=4 << 20
         ),
@@ -430,90 +429,72 @@
     owners, _, share = pieces.shape
     channels, model_width = mixing.shape[1:]
     count, length = filters.shape
-    steps = count // PER_STEP
     cut = (owners // 4, 2, model_width // 2, share)
-    mix_block = (PER_STEP, channels, model_width)
     return pl.pallas_call(
         mixed_kernel,
         grid_spec=pltpu.PrefetchScalarGridSpec(
             num_scalar_prefetch=1,
-            grid=(steps,),
+            grid=(count // PER_STEP,),
             in_specs=[
                 whole(filters.shape),
-                whole(pieces.shape),
-                pl.BlockSpec(mix_block, lambda k, _: (k, 0, 0)),
-                pl.BlockSpec(mix_block, lambda k, _: (k + steps, 0, 0)),
-                pl.BlockSpec((AR, channels, model_width), lambda k, _: (2 * count // AR, 0, 0)),
+                in_vmem(),
+                pl.BlockSpec(memory_space=pltpu.HBM),
             ],
-            out_specs=[in_vmem(), whole((AR, channels, length)), *[whole(cut)] * 4],
+            out_specs=[in_vmem()] * 6,
             scratch_shapes=[
-                *maps_scratch(channels, length, count),
+                *maps_scratch(channels, length, count, PER_STEP),
                 pltpu.VMEM((owners, model_width, share), jnp.float32),
+                pltpu.VMEM(mixing.shape, jnp.bfloat16),
+                pltpu.SemaphoreType.DMA,
             ],
         ),
         out_shape=[
             pltpu.VMEM((2, count, channels, length), jnp.bfloat16),
-            jax.ShapeDtypeStruct((AR, channels, length), jnp.bfloat16),
-            *[jax.ShapeDtypeStruct(cut, jnp.bfloat16)] * 4,
+            pltpu.VMEM((AR, channels, length), jnp.bfloat16),
+            *[pltpu.VMEM(cut, jnp.bfloat16)] * 4,
         ],
-        compiler_params=vmem(24),
+        compiler_params=vmem(20),
+        cost_estimate=pl.CostEstimate(
+            flops=10 * channels * count * length * length, transcendentals=0, bytes_accessed=4 << 20
+        ),
         name="spectral_mixed",
-    )(me, filters, pieces, *[in_hbm(mixing)] * 3)
+    )(me, in_hbm(filters), pieces, in_hbm(mixing))
 
 
 def spectral_back(grads, mixing, filters, pieces):
-    channels, model_width = mixing.shape[1:]
+    channels = mixing.shape[1]
     count, length = filters.shape
-    steps = count // PER_STEP
-    mix_block = (PER_STEP, channels, model_width)
     return pl.pallas_call(
         spectral_back_kernel,
-        grid=(steps,),
-        in_specs=[
-            whole(filters.shape),
-            pl.BlockSpec(mix_block, lambda k: (k, 0, 0)),
-            pl.BlockSpec(mix_block, lambda k: (k + steps, 0, 0)),
-            whole(pieces.shape),
-            whole(grads.shape),
-        ],
-        out_specs=whole((2 * channels, length)),
+        grid=(count // PER_STEP,),
+        in_specs=[in_vmem()] * 4,
+        out_specs=in_vmem(),
         scratch_shapes=[
-            *toeplitz_scratch(length, count),
+            *toeplitz_scratch(length, count, PER_STEP),
             pltpu.VMEM((PER_STEP, 2 * channels, length), jnp.bfloat16),
         ],
-        out_shape=jax.ShapeDtypeStruct((2 * channels, length), jnp.float32),
-        compiler_params=vmem(24),
+        out_shape=pltpu.VMEM((2 * channels, length), jnp.float32),
+        compiler_params=vmem(20),
         name="spectral_back",
-    )(filters, *[in_hbm(mixing)] * 2, pieces, grads)
-
-
-def lag_back(me, acc, mixing, grads, lags, pieces, scales):
-    channels, model_width = mixing.shape[1:]
+    )(filters, mixing, pieces, grads)
+
+
+def lag_back(me, acc, mixing, grads, lags, pieces, gain):
+    channels = mixing.shape[1]
     owners, _, share = pieces.shape
-    sent = (owners // 2, channels, share)
+    sent = pltpu.VMEM((owners // 2, channels, share), jnp.bfloat16)
     return pl.pallas_call(
         lag_back_kernel,
         grid_spec=pltpu.PrefetchScalarGridSpec(
             num_scalar_prefetch=1,
             grid=(1,),
-            in_specs=[
-                whole(acc.shape),
-                pl.BlockSpec((AR, channels, model_width), lambda k, _: (2 * K // AR, 0, 0)),
-                whole(grads.shape),
-                pl.BlockSpec((1, *lags.shape[1:]), lambda k, _: (0, 0, 0)),
-                whole(pieces.shape),
-                whole(scales.shape),
-            ],
-            out_specs=[whole(sent), whole(sent), whole((8, 128))],
+            in_specs=[in_vmem()] * 6,
+            out_specs=[in_vmem()] * 3,
         ),
-        out_shape=[
-            jax.ShapeDtypeStruct(sent, jnp.bfloat16),
-            jax.ShapeDtypeStruct(sent, jnp.bfloat16),
-            jax.ShapeDtypeStruct((8, 128), jnp.float32),
-        ],
-        compiler_params=vmem(16),
+        out_shape=[sent, sent, pltpu.VMEM((8, 128), jnp.float32)],
+        compiler_params=vmem(12),
         name="lag_back",
-    )(me, acc, in_hbm(mixing), grads, lags, pieces, scales)
+    )(me, acc, mixing, grads, lags, pieces, gain[None, :])
 
 
 def gelu_parts(gate_value, upper_value, hidden_grad):
@@ -773,16 +754,16 @@
             num_scalar_prefetch=1,
             grid=(1,),
             in_specs=[
-                *[whole(part.shape) for part in parts],
+                *[in_vmem() for _ in parts],
                 pl.BlockSpec((width, units), lambda k, me: (0, me[0])),
                 pl.BlockSpec((width, units), lambda k, me: (0, me[0])),
                 pl.BlockSpec((units, width), lambda k, me: (me[0], 0)),
-                whole(first_gain.shape),
+                in_vmem(),
             ],
-            out_specs=whole(shape),
+            out_specs=in_vmem(),
             scratch_shapes=[pltpu.VMEM((tokens, width), jnp.bfloat16)] * 2,
         ),
-        out_shape=jax.ShapeDtypeStruct(shape, jnp.bfloat16),
+        out_shape=pltpu.VMEM(shape, jnp.bfloat16),
         compiler_params=vmem(24),
         name="unit_grads",
     )(me, *parts, in_hbm(w_gate), in_hbm(w_up), in_hbm(w_down), first_gain)
@@ -812,7 +793,7 @@
         grid_spec=pltpu.PrefetchScalarGridSpec(
             num_scalar_prefetch=1,
             grid=(1,),
-            in_specs=[whole(mine.shape), whole(mine.shape)],
+            in_specs=[in_vmem()] * 2,
             out_specs=[whole(shape) for shape in shapes],
         ),
         out_shape=[jax.ShapeDtypeStruct(shape, jnp.float32) for shape in shapes],
@@ -844,8 +825,9 @@
     return lax.optimization_barrier(values)
 
 
-def gather_round(held, mask, bits):
-    return join(held[None], swap(held, "chan", mask)[None], bits[mask][0] != 0, 0)
+def gather_round(held, mask, bits, came=None):
+    came = swap(held, "chan", mask) if came is None else came
+    return join(held[None], came[None], bits[mask][2], 0)
 
 
 class Gather:
@@ -857,9 +839,10 @@
         self.orders = [(masks[1], masks[0]), (masks[0], masks[1])]
         self.held = values[None]
 
-    def first(self):
+    def first(self, came=None):
         for mask in self.common:
-            self.held = gather_round(self.held, mask, self.bits).reshape(-1, *self.shape)
+            self.held = gather_round(self.held, mask, self.bits, came).reshape(-1, *self.shape)
+            came = None
         return self.held
 
     def second(self):
@@ -899,24 +882,23 @@
 
 
 def exchange(values, mask, dim, bits):
-    keep, give = (entry(values, bit, dim) for bit in bits[mask])
+    keep, give = (entry(values, bit, dim) for bit in bits[mask][:2])
     return keep, swap(give, "chan", mask)
 
 
-def scatter_tokens(keep0, give0, keep1, give1, beside, bits):
+def scatter_tokens(keep0, give0, keep1, give1, bits, beside):
     masks = bits_of("chan")
     got0, got1 = swap(give0, "chan", masks[0]), swap(give1, "chan", masks[1])
     half0 = add(keep0, got0).astype(jnp.bfloat16)
     half1 = add(keep1, got1).astype(jnp.bfloat16)
-    half0, half1, *beside = tie(half0, half1, *beside)
+    half0, half1 = beside(half0, half1)
     half0 = own_entry(half0, masks[1], 1, bits)
     half1 = own_entry(half1, masks[0], 1, bits)
     held = jnp.concatenate([half0, half1], axis=1)
     for mask in masks[:2:-1]:
         held = held.astype(jnp.bfloat16).reshape(2, -1, *held.shape[1:])
         held = own_entry(held, mask, 0, bits)
-    held = held.astype(jnp.bfloat16)
-    return held, exchange(held, masks[2], 0, bits)[1][0], beside
+    return held.astype(jnp.bfloat16)
 
 
 def shards(
@@ -930,60 +912,66 @@
     core = lax.axis_index("rows").astype(jnp.int32) & 1
     other_core = 1 - core
     bits = [(me >> b) & 1 for b in range(len(bits_of("chan")))]
-    bits = [bit ^ flip for bit in bits for flip in range(2)]
-    scales = lax.dynamic_slice_in_dim(gain_one, me * channels, channels)
-    scales = jnp.pad(scales, (0, 128 - channels), constant_values=1.0)[None, :]
-    hidden_in, scales, at, core, other_core, *bits = tie(
-        hidden_in, scales, at, core, other_core, *bits
-    )
-    bits = dict(zip(bits_of("chan"), zip(bits[::2], bits[1::2], strict=True), strict=True))
-    cotangent_gather = Gather(out_grad[0], share // 2, bits)
-    cotangent_gather.first()
+    bits = [value for bit in bits for value in (bit, bit ^ 1, bit != 0)]
+    hidden_in, at, core, other_core, *bits = tie(hidden_in, at, core, other_core, *bits)
+    bits = {mask: bits[3 * i : 3 * i + 3] for i, mask in enumerate(bits_of("chan"))}
     pieces = lax.all_to_all(
         first_norm(at, hidden_in, gain_one, segments, chans),
         "chan",
         split_axis=0,
         concat_axis=0,
     )
+    pieces, cotangent = tie(pieces, out_grad)
+    cotangent_gather = Gather(cotangent[0], share // 2, bits)
+    came = swap(cotangent_gather.held, "chan", 4)
+    maps, lags, *cut = spectral_mixed(at, pieces, filters, mixing)
+    pieces, lags, came = tie(pieces, lags, came)
+    cotangent_gather.first(came)
     peer_pieces = swap(pieces, "rows", 2)
-    maps, lags, *cut = spectral_mixed(at, pieces, filters, mixing)
-    peer_pieces, lags = tie(peer_pieces, lags)
+
+    def beside(*values):
+        *values, cotangent_gather.held = tie(*values, cotangent_gather.held)
+        cotangent_gather.second()
+        return values
+
+    held = scatter_tokens(*cut, bits, beside)
+    held, peer_pieces, *cotangent_gather.halves = tie(
+        held, peer_pieces, *cotangent_gather.halves
+    )
+    got = exchange(held, 4, 0, bits)[1][0]
     peer_maps, peer_lags = spectral_maps(peer_pieces, filters, channels, 0, K // 2)
-    cotangent_gather.second()
-    lags, *cotangent_gather.halves = tie(lags, *cotangent_gather.halves)
-    beside = (peer_maps, *cotangent_gather.third())
-    held, got, (peer_maps, *cotangent_gather.others) = scatter_tokens(*cut, beside, bits)
-    last_bit = bits[4][0].reshape(1)
+    held, got, peer_maps = tie(held, got, peer_maps)
+    cotangent_gather.third()
     output, normed_two, resid_grad, resid_low = feed_forward(
-        last_bit, held, got, hidden_in, gain_two, out_grad, w_gate, w_up, w_down
+        bits[4][0].reshape(1), held, got, hidden_in, gain_two, out_grad, w_gate, w_up, w_down
     )
     grad_gather = Gather(resid_low, share // 2, bits)
-    first = grad_gather.first()
+    first, *cotangent_gather.others = tie(grad_gather.first(), *cotangent_gather.others)
     peer_pieces, resid_grad = tie(peer_pieces, resid_grad)
     peer_maps, _ = spectral_maps(peer_pieces, filters, channels, K // 2, K // 2, peer_maps)
-    normed_two, grad_gather.held, peer_maps = tie(normed_two, first, peer_maps)
+    grad_gather.held, peer_maps = tie(first, peer_maps)
+    grad_gather.second()
+    normed_two, *grad_gather.halves = tie(normed_two, *grad_gather.halves)
+    grad_gather.third()
     normed_gather = Gather(normed_two, share // 2, bits)
     normed_gather.first()
-    grad_gather.second()
-    normed_gather.second()
-    grad_gather.third()
-    normed_gather.third()
     full_grad = place(at, grad_gather.parts())
     peer_grad = swap(full_grad, "rows", 2)
+    normed_gather.second()
     acc = spectral_back(full_grad, mixing, filters, pieces)
-    back, give, first_local = lag_back(at, acc, mixing, full_grad, lags, pieces, scales)
+    acc, *normed_gather.halves = tie(acc, *normed_gather.halves)
+    normed_gather.third()
+    back, give, first_local = lag_back(at, acc, mixing, full_grad, lags, pieces, gain_one)
     came = swap(give, "chan", 1)
-    first_local, *normed_parts = tie(first_local, *normed_gather.parts())
+    first_local, full_grad = tie(first_local, full_grad)
+    own, own_lags = own_mixing_grad(maps, lags, full_grad)
+    own_lags, back, came, *normed_parts = tie(own_lags, back, came, *normed_gather.parts())
     unit_parts = unit_grads(
         at, normed_parts, cotangent_gather.parts(), w_gate, w_up, w_down, first_local
     )
-    unit_parts, full_grad, back, came = tie(unit_parts, full_grad, back, came)
     back, came = exchange_rest(back, came)
-    keep = entry(unit_parts, core, 0)[0]
     unit_given = swap(entry(unit_parts, other_core, 0)[0], "rows", 1)
-    own, own_lags = own_mixing_grad(maps, lags, full_grad)
-    own_lags, unit_given = tie(own_lags, unit_given)
-    unit_half = add(keep, unit_given).astype(jnp.bfloat16)
+    unit_half = add(entry(unit_parts, core, 0)[0], unit_given).astype(jnp.bfloat16)
     unit_half, peer_grad = tie(unit_half, peer_grad)
     unit_other = swap(unit_half, "rows", 2)
     first_part = mixing_grad(0, peer_maps, peer_lags, peer_grad, own, own_lags)
@@ -994,9 +982,7 @@
     unit_half = add(unit_half, unit_other).astype(jnp.bfloat16)
     for mask in bits_of("rows")[2:]:
         unit_half = add(unit_half, swap(unit_half, "rows", mask)).astype(jnp.bfloat16)
-    gate_sum, up_sum, down_sum, gains = finish_units(
-        core.reshape(1), unit_half, swap(unit_half, "rows", 1), width
-    )
+    unit_other = swap(unit_half, "rows", 1)
     mixing_sum = None
     for part, first in ((first_part, 0), (second_part, K)):
         masks = [1, *bits_of("rows")[2:]]
@@ -1004,6 +990,11 @@
             part = add(part, swap(part, "rows", mask)).astype(jnp.bfloat16)
         got = swap(part, "rows", masks[-1])
         mixing_sum = finish_mixing(part, got, first, mixing.shape, mixing_sum)
+        if not first:
+            mixing_sum, unit_half = tie(mixing_sum, unit_half)
+    gate_sum, up_sum, down_sum, gains = finish_units(
+        core.reshape(1), unit_half, unit_other, width
+    )
     return (
         output,
         input_total,

time: 142 us -> 128 us (0.901)
  blocking collectives: 0 us -> 14.6 us
  starting transfers between devices: 44.3 us -> 32.2 us
  waiting for transfers between devices: 35 us -> 25.5 us
  Pallas kernels: 57.5 us -> 52.6 us
  local copies, waits for them, and re-layouts: 2.34 us -> 0.82 us
    all_to_all x0 -> x1, blocking collectives: none -> 14.6 us  [shards(): lax.all_to_all(first_norm(at, hidden_in, gain_one, segments, chans), 'cha...]
    ppermute x30, starting transfers between devices: 40.5 us -> 32.2 us  [swap(): return lax.ppermute(values, axis, [(i, i ^ mask) for i in range(count)])]
    ppermute x30, waiting for transfers between devices: 31.2 us -> 25.5 us  [swap(): return lax.ppermute(values, axis, [(i, i ^ mask) for i in range(count)])]
    all_to_all x1 -> x0, waiting for transfers between devices: 3.84 us -> none  [shards(): lax.all_to_all(first_norm(at, hidden_in, gain_one, segments, chans), 'cha...]
    all_to_all x1 -> x0, starting transfers between devices: 3.78 us -> none  [shards(): lax.all_to_all(first_norm(at, hidden_in, gain_one, segments, chans), 'cha...]
    pallas_call x3, Pallas kernels: 17.2 us -> 14.6 us  [the longest x1 8.31 us: spectral_back(): pl.pallas_call(spectral_back_kernel, grid=(count // PER_STEP,), in_specs=...]
  transfers between devices with their start and end apart: 31 -> 30, of which waited for: 12 -> 13; matrix products, arithmetic and copies ran while one was open for 2% -> 1% of each run, Pallas kernels for 35% -> 30%
where the time goes in v4:
time: 128 us
  Pallas kernels  52.6 us (41%)
  starting transfers between devices  32.2 us (25%)
  waiting for transfers between devices  25.5 us (20%)
  blocking collectives  14.6 us (11%)
    ppermute x30, starting transfers between devices, swap(): return lax.ppermute(values, axis, [(i, i ^ mask) for i in range(count)])  32.2 us
    ppermute x30, waiting for transfers between devices, swap(): return lax.ppermute(values, axis, [(i, i ^ mask) for i in range(count)])  25.5 us
    all_to_all x1, blocking collectives, shards(): lax.all_to_all(first_norm(at, hidden_in, gain_one, segments, chans), 'cha...  14.6 us
    pallas_call x1, Pallas kernels, spectral_mixed(): pl.pallas_call(mixed_kernel, grid_spec=pltpu.PrefetchScalarGridSpec(num_s...  11.2 us
    pallas_call x1, Pallas kernels, spectral_back(): pl.pallas_call(spectral_back_kernel, grid=(count // PER_STEP,), in_specs=...  8.31 us
    pallas_call x2, Pallas kernels, spectral_maps(): pl.pallas_call(functools.partial(maps_kernel, start), in_specs=[in_vmem()...  6.29 us
    pallas_call x1, Pallas kernels, feed_forward(): pl.pallas_call(feed_forward_kernel, grid_spec=pltpu.PrefetchScalarGridSpe...  5.29 us
    pallas_call x2, Pallas kernels, mixing_grad(): pl.pallas_call(functools.partial(mixing_grad_kernel, which), in_specs=[in...  4.96 us
  transfers between devices with their start and end apart: 30, of which 13 were waited for; matrix products, arithmetic and copies ran while one was open for 1% of the time, Pallas kernels for 30%

profile of v4, /device:TPU:0, one launch (start us, length us, event | category | flops | bytes accessed | tf_op | source)
XLA Modules:
  0.0 127.6 jit_solution(6051533072304168338)
XLA Ops:
  0.6 1.1 first_norm.1
  1.8 14.6 %all_to_all.5.pieces = bf16[8,80,128]{2,1,0:T(8,128)(2,1)S(1)} all-to-all(bf16[8,80,128]{2,1,0:T(8,128)(2,1)S(1)} %first_norm.1), channel_id=1, replica_groups=mesh['rows'=4,'chan'=8] {'chan'}, dimensions={0} | all-to-all | bytes 327680 | tf_op jit(solution)/shard_map/all_to_all | solution.py:918
  16.4 11.2 %spectral_mixed.1 = (bf16[2,24,64,1024]{3,2,1,0:T(8,128)(2,1)S(1)}, bf16[3,64,1024]{2,1,0:T(8,128)(2,1)S(1)}, bf16[2,2,256,128]{3,2,1,0:T(8,128)(2,1)S(1)}, bf16...) custom-call(s32[1]{0:T(128)} %bitcast.me, ...), custom_call_target="tpu_custom_call" | custom-call | flops 16106127360 | bytes 4194304 | tf_op jit(solution)/shard_map/spectral_mixed/pallas_call | solution.py:433
  28.0 1.2 collective-permute-start.2
  29.2 1.4 %collective-permute-start = (bf16[2,2,256,128]{3,2,0,1:T(8,128)(2,1)S(1)}, bf16[2,2,256,128]{3,2,0,1:T(8,128)(2,1)S(1)}, u32[]{:S(2)}, u32[]{:S(2)}) collective-permute-start(bf16[2,2,256,128]{3,2,0,1:T(8,128)(2,1)S(1)} %copy.21), channel_id=1, source_target_pairs={{0,1},{1,0},{2,3},{3,2},{4,5},{5,4},{6,7},{7,6},{8,9},{9,8},{10,11... | collective-permute-start | bytes 786440 | tf_op jit(solution)/shard_map/ppermute | solution.py:807
  30.5 4.5 %collective-permute-done.2 = bf16[1,128,512]{2,1,0:T(8,128)(2,1)S(1)} collective-permute-done((bf16[1,128,512]{2,1,0:T(8,128)(2,1)S(1)}, bf16[1,128,512]{2,1,0:T(8,128)(2,1)S(1)}, u32[]{:S(2)}, u32[]{:S(2)}) %collective-permute-start.2) | collective-permute-done | bytes 131104 | tf_op jit(solution)/shard_map/ppermute | solution.py:807
  35.0 1.5 %collective-permute-start.5 = (bf16[8,80,128]{2,1,0:T(8,128)(2,1)S(1)}, bf16[8,80,128]{2,1,0:T(8,128)(2,1)S(1)}, u32[]{:S(2)}, u32[]{:S(2)}) collective-permute-start(bf16[8,80,128]{2,1,0:T(8,128)(2,1)S(1)} %all_to_all.5.pieces), channel_id=1, source_target_pairs={{0,16},{8,24},{16,0},{24,8},{1,17},{9,25},{17,1},{25,9},{2,18},{10... | collective-permute-start | bytes 491528 | tf_op jit(solution)/shard_map/ppermute | solution.py:807
  36.6 0.6 collective-permute-done.1
  37.4 2.2 %collective-permute-start.3 = (bf16[2,1,256,128]{3,2,0,1:T(8,128)(2,1)S(1)}, bf16[2,1,256,128]{3,2,0,1:T(8,128)(2,1)S(1)}, u32[]{:S(2)}, u32[]{:S(2)}) collective-permute-start(bf16[2,1,256,128]{3,2,0,1:T(8,128)(2,1)S(1)} %constant_dynamic-slice_fusion.2), channel_id=1, source_target_pairs={{0,2},{1,3},{2,0},{3,1},{4,6},{5,7},{6,4},{7,5},{8,10},{9,11},{10,... | collective-permute-start | bytes 393224 | tf_op jit(solution)/shard_map/ppermute | solution.py:807
  39.6 1.6 %collective-permute-start.7 = (bf16[2,64,512]{2,1,0:T(8,128)(2,1)S(1)}, bf16[2,64,512]{2,1,0:T(8,128)(2,1)S(1)}, u32[]{:S(2)}, u32[]{:S(2)}) collective-permute-start(bf16[2,64,512]{2,1,0:T(8,128)(2,1)S(1)} %get-tuple-element.178), channel_id=1, source_target_pairs={{0,1},{1,0},{2,3},{3,2},{4,5},{5,4},{6,7},{7,6},{8,9},{9,8},{10,11... | collective-permute-start | bytes 393224 | tf_op jit(solution)/shard_map/ppermute | solution.py:807
  41.2 0.6 collective-permute-start.4
  41.8 1.6 %collective-permute-done.3 = bf16[2,1,256,128]{3,2,0,1:T(8,128)(2,1)S(1)} collective-permute-done((bf16[2,1,256,128]{3,2,0,1:T(8,128)(2,1)S(1)}, bf16[2,1,256,128]{3,2,0,1:T(8,128)(2,1)S(1)}, u32[]{:S(2)}, u32[]{:S(2)}) %collective-permute-start.3) | collective-permute-done | bytes 131104 | tf_op jit(solution)/shard_map/ppermute | solution.py:807
  43.4 2.8 %collective-permute-done.4 = bf16[2,1,256,128]{3,2,0,1:T(8,128)(2,1)S(1)} collective-permute-done((bf16[2,1,256,128]{3,2,0,1:T(8,128)(2,1)S(1)}, bf16[2,1,256,128]{3,2,0,1:T(8,128)(2,1)S(1)}, u32[]{:S(2)}, u32[]{:S(2)}) %collective-permute-start.4) | collective-permute-done | bytes 131104 | tf_op jit(solution)/shard_map/ppermute | solution.py:807
  46.5 2.3 %collective-permute-start.8 = (bf16[1,512,128]{2,1,0:T(8,128)(2,1)S(1)}, bf16[1,512,128]{2,1,0:T(8,128)(2,1)S(1)}, u32[]{:S(2)}, u32[]{:S(2)}) collective-permute-start(bf16[1,512,128]{2,1,0:T(8,128)(2,1)S(1)} %constant_dynamic-slice_fusion), channel_id=1, source_target_pairs={{0,4},{1,5},{2,6},{3,7},{4,0},{5,1},{6,2},{7,3},{8,12},{9,13},{10,... | collective-permute-start | bytes 393224 | tf_op jit(solution)/shard_map/ppermute | solution.py:807
  48.8 2.8 %spectral_maps.2 = (bf16[2,24,64,1024]{3,2,1,0:T(8,128)(2,1)S(1)}, bf16[3,64,1024]{2,1,0:T(8,128)(2,1)S(1)}) custom-call(bf16[24,1024]{1,0:T(8,128)(2,1)S(1)} %copy-done.6, bf16[8,80,128]{2,1,0:T(8,128)(2,1)S(1)} %collective-permute-done.5.pieces), custom_call_target="tpu_custom_call" | custom-call | flops 4831838208 | bytes 4194304 | tf_op jit(solution)/shard_map/spectral_maps/pallas_call | solution.py:410
  51.6 1.0 collective-permute-start.10
  53.0 5.3 %feed_forward.1 = (bf16[1,128,512]{2,1,0:T(8,128)(2,1)}, bf16[144,512]{1,0:T(8,128)(2,1)S(1)}, f32[128,512]{1,0:T(8,128)S(1)}, bf16[128,512]{1,0:T(8,128)(2,1)S(1)}) custom-call(s32[1]{0:T(128)} %bitcast.1.bit, bf16[2,512,128]{2,1,0:T(8,128)(2,1)S(1)} %pad_maximum_fusion.held, bf16[512,128]{1,0:T(8,128)(2,1)S(1)} %bitcast.58, ...), custom_call_target="tpu_custom_call" | custom-call | tf_op jit(solution)/shard_map/feed_forward/pallas_call | solution.py:578
  58.3 3.1 %collective-permute-start.9 = (bf16[1,128,512]{2,1,0:T(8,128)(2,1)S(1)}, bf16[1,128,512]{2,1,0:T(8,128)(2,1)S(1)}, u32[]{:S(2)}, u32[]{:S(2)}) collective-permute-start(bf16[1,128,512]{2,1,0:T(8,128)(2,1)S(1)} %bitcast.56), channel_id=1, source_target_pairs={{0,4},{1,5},{2,6},{3,7},{4,0},{5,1},{6,2},{7,3},{8,12},{9,13},{10,... | collective-permute-start | bytes 393224 | tf_op jit(solution)/shard_map/ppermute | solution.py:807
  61.4 3.5 %spectral_maps.3 = (bf16[2,24,64,1024]{3,2,1,0:T(8,128)(2,1)S(1)}, bf16[3,64,1024]{2,1,0:T(8,128)(2,1)}) custom-call(bf16[24,1024]{1,0:T(8,128)(2,1)S(1)} %copy-done.6, bf16[8,80,128]{2,1,0:T(8,128)(2,1)S(1)} %collective-permute-done.5.pieces, bf16[2,24,64,1024]{3,2,1,0:T(8,128)(2,1)S(1)} %get-tuple-element.127.refs_0_), custom_call_target="tpu_custom_call", output_to_operand_aliasing={{0}: (2, {})} | custom-call | flops 4831838208 | bytes 4194304 | tf_op jit(solution)/shard_map/spectral_maps/pallas_call | solution.py:410
  65.0 3.0 %collective-permute-start.13 = (bf16[2,64,512]{2,1,0:T(8,128)(2,1)S(1)}, bf16[2,64,512]{2,1,0:T(8,128)(2,1)S(1)}, u32[]{:S(2)}, u32[]{:S(2)}) collective-permute-start(bf16[2,64,512]{2,1,0:T(8,128)(2,1)S(1)} %get-tuple-element.174), channel_id=1, source_target_pairs={{0,1},{1,0},{2,3},{3,2},{4,5},{5,4},{6,7},{7,6},{8,9},{9,8},{10,11... | collective-permute-start | bytes 393224 | tf_op jit(solution)/shard_map/ppermute | solution.py:807
  68.0 3.8 %collective-permute-done.13 = bf16[2,64,512]{2,1,0:T(8,128)(2,1)S(1)} collective-permute-done((bf16[2,64,512]{2,1,0:T(8,128)(2,1)S(1)}, bf16[2,64,512]{2,1,0:T(8,128)(2,1)S(1)}, u32[]{:S(2)}, u32[]{:S(2)}) %collective-permute-start.13) | collective-permute-done | bytes 131104 | tf_op jit(solution)/shard_map/ppermute | solution.py:807
  71.8 2.9 %collective-permute-done.12 = bf16[2,64,512]{2,1,0:T(8,128)(2,1)S(1)} collective-permute-done((bf16[2,64,512]{2,1,0:T(8,128)(2,1)S(1)}, bf16[2,64,512]{2,1,0:T(8,128)(2,1)S(1)}, u32[]{:S(2)}, u32[]{:S(2)}) %collective-permute-start.12) | collective-permute-done | bytes 131104 | tf_op jit(solution)/shard_map/ppermute | solution.py:807
  74.8 0.7 collective-permute-start.16
  75.5 1.5 %collective-permute-start.14 = (bf16[2,2,64,512]{3,2,1,0:T(8,128)(2,1)S(1)}, bf16[2,2,64,512]{3,2,1,0:T(8,128)(2,1)S(1)}, u32[]{:S(2)}, u32[]{:S(2)}) collective-permute-start(bf16[2,2,64,512]{3,2,1,0:T(8,128)(2,1)S(1)} %maximum_select_fusion.6.part0), channel_id=1, source_target_pairs={{0,1},{1,0},{2,3},{3,2},{4,5},{5,4},{6,7},{7,6},{8,9},{9,8},{10,11... | collective-permute-start | bytes 786440 | tf_op jit(solution)/shard_map/ppermute | solution.py:807
  77.3 4.3 %collective-permute-done.16 = bf16[1,144,512]{2,1,0:T(8,128)(2,1)S(1)} collective-permute-done((bf16[1,144,512]{2,1,0:T(8,128)(2,1)S(1)}, bf16[1,144,512]{2,1,0:T(8,128)(2,1)S(1)}, u32[]{:S(2)}, u32[]{:S(2)}) %collective-permute-start.16) | collective-permute-done | bytes 147488 | tf_op jit(solution)/shard_map/ppermute | solution.py:807
  81.8 1.5 %collective-permute-start.18 = (bf16[2,80,512]{2,1,0:T(8,128)(2,1)S(1)}, bf16[2,80,512]{2,1,0:T(8,128)(2,1)S(1)}, u32[]{:S(2)}, u32[]{:S(2)}) collective-permute-start(bf16[2,80,512]{2,1,0:T(8,128)(2,1)S(1)} %get-tuple-element.170), channel_id=1, source_target_pairs={{0,1},{1,0},{2,3},{3,2},{4,5},{5,4},{6,7},{7,6},{8,9},{9,8},{10,11... | collective-permute-start | bytes 491528 | tf_op jit(solution)/shard_map/ppermute | solution.py:807
  83.3 1.0 collective-permute-done.15.part3
  84.4 8.3 %spectral_back.1.acc = f32[128,1024]{1,0:T(8,128)S(1)} custom-call(bf16[24,1024]{1,0:T(8,128)(2,1)S(1)} %copy-done.6, bf16[51,64,512]{2,1,0:T(8,128)(2,1)S(1)} %copy-done, bf16[8,80,128]{2,1,0:T(8,128)(2,1)S(1)} %all_to_all.5.pieces, bf16[1024,512]{1,0:T(8,128)(2,1)S(1)} %place.1.grads), custom_call_target="tpu_custom_call" | custom-call | tf_op jit(solution)/shard_map/spectral_back/pallas_call | solution.py:467
  92.8 1.0 collective-permute-start.21
  93.9 1.3 collective-permute-start.24
  95.1 0.7 collective-permute-start.20
  95.8 0.8 lag_back.1
  96.6 1.4 %collective-permute-start.19 = (bf16[4,64,128]{2,1,0:T(8,128)(2,1)S(1)}, bf16[4,64,128]{2,1,0:T(8,128)(2,1)S(1)}, u32[]{:S(2)}, u32[]{:S(2)}) collective-permute-start(bf16[4,64,128]{2,1,0:T(8,128)(2,1)S(1)} %get-tuple-element.138), channel_id=1, source_target_pairs={{0,1},{1,0},{2,3},{3,2},{4,5},{5,4},{6,7},{7,6},{8,9},{9,8},{10,11... | collective-permute-start | bytes 196616 | tf_op jit(solution)/shard_map/ppermute | solution.py:807
  98.0 4.3 %own_mixing_grad.1 = (bf16[2,24,64,512]{3,2,1,0:T(8,128)(2,1)S(1)}, bf16[3,64,512]{2,1,0:T(8,128)(2,1)S(1)}) custom-call(bf16[2,24,64,1024]{3,2,1,0:T(8,128)(2,1)S(1)} %get-tuple-element.118.maps, bf16[3,64,1024]{2,1,0:T(8,128)(2,1)S(1)} %get-tuple-element.119.inputs.lags, bf16[1024,512]{1,0:T(8,128)(2,1)S(1)} %place.1.grads), custom_call_target="tpu_custom_call" | custom-call | tf_op jit(solution)/shard_map/own_mixing_grad/pallas_call | solution.py:634
  102.3 3.6 %unit_grads.1 = bf16[2,784,256]{2,1,0:T(8,128)(2,1)S(1)} custom-call(s32[1]{0:T(128)} %bitcast.me, bf16[2,2,64,512]{3,2,1,0:T(8,128)(2,1)S(1)} %maximum_select_fusion.8.refs_0_, bf16[2,2,64,512]{3,2,1,0:T(8,128)(2,1)S(1)} %collective-permute-done.20.refs_1_, bf16[2,2,80,512]{3,2,1,0:T(8,128)(2,1)S(1)} %maximum_select_fusion.refs_2_, ...), custom_call_target="tpu_custom_call" | custom-call | tf_op jit(solution)/shard_map/unit_grads/pallas_call | solution.py:751
  106.1 1.2 collective-permute-start.22
  107.9 2.2 %collective-permute-done.24.grads = bf16[1024,512]{1,0:T(8,128)(2,1)S(1)} collective-permute-done((bf16[1024,512]{1,0:T(8,128)(2,1)S(1)}, bf16[1024,512]{1,0:T(8,128)(2,1)S(1)}, u32[]{:S(2)}, u32[]{:S(2)}) %collective-permute-start.24) | collective-permute-done | bytes 1048608 | tf_op jit(solution)/shard_map/ppermute | solution.py:807
  110.1 0.9 collective-permute-start.26
  111.1 2.4 %collective-permute-start.25 = (bf16[1,4,64,128]{3,2,1,0:T(8,128)(2,1)S(1)}, bf16[1,4,64,128]{3,2,1,0:T(8,128)(2,1)S(1)}, u32[]{:S(2)}, u32[]{:S(2)}) collective-permute-start(bf16[1,4,64,128]{3,2,1,0:T(8,128)(2,1)S(1)} %get-tuple-element.182), channel_id=1, source_target_pairs={{0,4},{1,5},{2,6},{3,7},{4,0},{5,1},{6,2},{7,3},{8,12},{9,13},{10,... | collective-permute-start | bytes 196616 | tf_op jit(solution)/shard_map/ppermute | solution.py:807
  113.5 2.3 %mixing_grad.2.part = bf16[1536,512]{1,0:T(8,128)(2,1)S(1)} custom-call(bf16[2,24,64,1024]{3,2,1,0:T(8,128)(2,1)S(1)} %get-tuple-element.143.maps, bf16[3,64,1024]{2,1,0:T(8,128)(2,1)S(1)} %get-tuple-element.144.lags, bf16[1024,512]{1,0:T(8,128)(2,1)S(1)} %collective-permute-done.24.grads, bf16[2,24,64,512]{3,2,1,0:T(8,128)(2,1)S(1)} %get-tuple-element.155.own, ...), custom_call_target="tpu_custom_call" | custom-call | tf_op jit(solution)/shard_map/mixing_grad/pallas_call | solution.py:667
  115.9 2.7 %mixing_grad.3.part = bf16[1728,512]{1,0:T(8,128)(2,1)S(1)} custom-call(bf16[2,24,64,1024]{3,2,1,0:T(8,128)(2,1)S(1)} %get-tuple-element.143.maps, bf16[3,64,1024]{2,1,0:T(8,128)(2,1)S(1)} %get-tuple-element.144.lags, bf16[1024,512]{1,0:T(8,128)(2,1)S(1)} %collective-permute-done.24.grads, bf16[2,24,64,512]{3,2,1,0:T(8,128)(2,1)S(1)} %get-tuple-element.155.own, ...), custom_call_target="tpu_custom_call" | custom-call | tf_op jit(solution)/shard_map/mixing_grad/pallas_call | solution.py:667
  118.6 0.7 collective-permute-done.26
  119.4 0.6 collective-permute-start.29
  120.0 0.9 first_norm_back.1
  120.9 2.1 %finish_mixing.2.refs_0_ = f32[51,64,512]{2,1,0:T(8,128)} custom-call(bf16[1536,512]{1,0:T(8,128)(2,1)S(1)} %mixing_grad.2.part, bf16[1536,512]{1,0:T(8,128)(2,1)S(1)} %collective-permute-done.28.got), custom_call_target="tpu_custom_call" | custom-call | tf_op jit(solution)/shard_map/finish_mixing/pallas_call | solution.py:688
  123.1 0.5 collective-permute-done.29.other
  123.6 1.2 finish_units.1
  125.4 2.3 %finish_mixing.3 = f32[51,64,512]{2,1,0:T(8,128)} custom-call(bf16[1728,512]{1,0:T(8,128)(2,1)S(1)} %mixing_grad.3.part, bf16[1728,512]{1,0:T(8,128)(2,1)S(1)} %collective-permute-done.27.got, f32[51,64,512]{2,1,0:T(8,128)} %finish_mixing.2.refs_0_), custom_call_target="tpu_custom_call", output_to_operand_aliasing={{}: (2, {})} | custom-call | tf_op jit(solution)/shard_map/finish_mixing/pallas_call | solution.py:688
  (79 shorter events, 3.5 us)
Async XLA Ops:
  16.4 11.6 %copy-start.5 = (bf16[1,128,512]{2,1,0:T(8,128)(2,1)S(1)}, bf16[1,128,512]{2,1,0:T(8,128)(2,1)}, u32[]{:S(2)}) copy-start(bf16[1,128,512]{2,1,0:T(8,128)(2,1)} %cotangent.1) | copy-start | bytes 393220
  27.7 9.5 %collective-permute-start.1 = (bf16[2,2,256,128]{3,2,0,1:T(8,128)(2,1)S(1)}, bf16[2,2,256,128]{3,2,0,1:T(8,128)(2,1)S(1)}, u32[]{:S(2)}, u32[]{:S(2)}) collective-permute-start(bf16[2,2,256,128]{3,2,0,1:T(8,128)(2,1)S(1)} %copy.23), channel_id=1, source_target_pairs={{0,2},{1,3},{2,0},{3,1},{4,6},{5,7},{6,4},{7,5},{8,10},{9,11},{10,... | collective-permute-start | bytes 786440 | tf_op jit(solution)/shard_map/ppermute | solution.py:807
  28.0 7.1 %collective-permute-start.2 = (bf16[1,128,512]{2,1,0:T(8,128)(2,1)S(1)}, bf16[1,128,512]{2,1,0:T(8,128)(2,1)S(1)}, u32[]{:S(2)}, u32[]{:S(2)}) collective-permute-start(bf16[1,128,512]{2,1,0:T(8,128)(2,1)S(1)} %copy-done.5), channel_id=1, source_target_pairs={{0,4},{1,5},{2,6},{3,7},{4,0},{5,1},{6,2},{7,3},{8,12},{9,13},{10,... | collective-permute-start | bytes 393224 | tf_op jit(solution)/shard_map/ppermute | solution.py:807
  29.2 19.6 %copy-start.6 = (bf16[24,1024]{1,0:T(8,128)(2,1)S(1)}, bf16[24,1024]{1,0:T(8,128)(2,1)}, u32[]{:S(2)}) copy-start(bf16[24,1024]{1,0:T(8,128)(2,1)} %filters.7) | copy-start | bytes 147460
  29.2 8.1 %collective-permute-start = (bf16[2,2,256,128]{3,2,0,1:T(8,128)(2,1)S(1)}, bf16[2,2,256,128]{3,2,0,1:T(8,128)(2,1)S(1)}, u32[]{:S(2)}, u32[]{:S(2)}) collective-permute-start(bf16[2,2,256,128]{3,2,0,1:T(8,128)(2,1)S(1)} %copy.21), channel_id=1, source_target_pairs={{0,1},{1,0},{2,3},{3,2},{4,5},{5,4},{6,7},{7,6},{8,9},{9,8},{10,11... | collective-permute-start | bytes 786440 | tf_op jit(solution)/shard_map/ppermute | solution.py:807
  35.0 11.4 %collective-permute-start.5 = (bf16[8,80,128]{2,1,0:T(8,128)(2,1)S(1)}, bf16[8,80,128]{2,1,0:T(8,128)(2,1)S(1)}, u32[]{:S(2)}, u32[]{:S(2)}) collective-permute-start(bf16[8,80,128]{2,1,0:T(8,128)(2,1)S(1)} %all_to_all.5.pieces), channel_id=1, source_target_pairs={{0,16},{8,24},{16,0},{24,8},{1,17},{9,25},{17,1},{25,9},{2,18},{10... | collective-permute-start | bytes 491528 | tf_op jit(solution)/shard_map/ppermute | solution.py:807
  37.4 6.0 %collective-permute-start.3 = (bf16[2,1,256,128]{3,2,0,1:T(8,128)(2,1)S(1)}, bf16[2,1,256,128]{3,2,0,1:T(8,128)(2,1)S(1)}, u32[]{:S(2)}, u32[]{:S(2)}) collective-permute-start(bf16[2,1,256,128]{3,2,0,1:T(8,128)(2,1)S(1)} %constant_dynamic-slice_fusion.2), channel_id=1, source_target_pairs={{0,2},{1,3},{2,0},{3,1},{4,6},{5,7},{6,4},{7,5},{8,10},{9,11},{10,... | collective-permute-start | bytes 393224 | tf_op jit(solution)/shard_map/ppermute | solution.py:807
  39.6 6.7 %collective-permute-start.7 = (bf16[2,64,512]{2,1,0:T(8,128)(2,1)S(1)}, bf16[2,64,512]{2,1,0:T(8,128)(2,1)S(1)}, u32[]{:S(2)}, u32[]{:S(2)}) collective-permute-start(bf16[2,64,512]{2,1,0:T(8,128)(2,1)S(1)} %get-tuple-element.178), channel_id=1, source_target_pairs={{0,1},{1,0},{2,3},{3,2},{4,5},{5,4},{6,7},{7,6},{8,9},{9,8},{10,11... | collective-permute-start | bytes 393224 | tf_op jit(solution)/shard_map/ppermute | solution.py:807
  41.2 5.2 %collective-permute-start.6 = (bf16[2,64,512]{2,1,0:T(8,128)(2,1)S(1)}, bf16[2,64,512]{2,1,0:T(8,128)(2,1)S(1)}, u32[]{:S(2)}, u32[]{:S(2)}) collective-permute-start(bf16[2,64,512]{2,1,0:T(8,128)(2,1)S(1)} %get-tuple-element.181), channel_id=1, source_target_pairs={{0,2},{1,3},{2,0},{3,1},{4,6},{5,7},{6,4},{7,5},{8,10},{9,11},{10,... | collective-permute-start | bytes 393224 | tf_op jit(solution)/shard_map/ppermute | solution.py:807
  41.2 5.0 %collective-permute-start.4 = (bf16[2,1,256,128]{3,2,0,1:T(8,128)(2,1)S(1)}, bf16[2,1,256,128]{3,2,0,1:T(8,128)(2,1)S(1)}, u32[]{:S(2)}, u32[]{:S(2)}) collective-permute-start(bf16[2,1,256,128]{3,2,0,1:T(8,128)(2,1)S(1)} %constant_dynamic-slice_fusion.1), channel_id=1, source_target_pairs={{0,1},{1,0},{2,3},{3,2},{4,5},{5,4},{6,7},{7,6},{8,9},{9,8},{10,11... | collective-permute-start | bytes 393224 | tf_op jit(solution)/shard_map/ppermute | solution.py:807
  46.4 6.6 %copy-start.1 = (bf16[512,2048]{1,0:T(8,128)(2,1)S(1)}, bf16[512,2048]{1,0:T(8,128)(2,1)}, u32[]{:S(2)}) copy-start(bf16[512,2048]{1,0:T(8,128)(2,1)} %refs_8_.1) | copy-start | bytes 6291460
  46.4 6.6 %copy-start.2 = (bf16[512,2048]{1,0:T(8,128)(2,1)S(1)}, bf16[512,2048]{1,0:T(8,128)(2,1)}, u32[]{:S(2)}) copy-start(bf16[512,2048]{1,0:T(8,128)(2,1)} %refs_9_.1) | copy-start | bytes 6291460
  46.5 6.5 %copy-start.3 = (bf16[2048,512]{1,0:T(8,128)(2,1)S(1)}, bf16[2048,512]{1,0:T(8,128)(2,1)}, u32[]{:S(2)}) copy-start(bf16[2048,512]{1,0:T(8,128)(2,1)} %refs_10_.1) | copy-start | bytes 6291460
  46.5 6.5 %copy-start.4 = (bf16[1,128,512]{2,1,0:T(8,128)(2,1)S(1)}, bf16[1,128,512]{2,1,0:T(8,128)(2,1)}, u32[]{:S(2)}) copy-start(bf16[1,128,512]{2,1,0:T(8,128)(2,1)} %hidden.1) | copy-start | bytes 393220
  46.5 6.5 %copy-start.8 = (f32[512]{0:T(512)S(1)}, f32[512]{0:T(512)}, u32[]{:S(2)}) copy-start(f32[512]{0:T(512)} %param.15) | copy-start | bytes 6148
  46.5 6.5 %collective-permute-start.8 = (bf16[1,512,128]{2,1,0:T(8,128)(2,1)S(1)}, bf16[1,512,128]{2,1,0:T(8,128)(2,1)S(1)}, u32[]{:S(2)}, u32[]{:S(2)}) collective-permute-start(bf16[1,512,128]{2,1,0:T(8,128)(2,1)S(1)} %constant_dynamic-slice_fusion), channel_id=1, source_target_pairs={{0,4},{1,5},{2,6},{3,7},{4,0},{5,1},{6,2},{7,3},{8,12},{9,13},{10,... | collective-permute-start | bytes 393224 | tf_op jit(solution)/shard_map/ppermute | solution.py:807
  51.6 13.4 %collective-permute-start.10 = (bf16[2,2,64,512]{3,2,1,0:T(8,128)(2,1)S(1)}, bf16[2,2,64,512]{3,2,1,0:T(8,128)(2,1)S(1)}, u32[]{:S(2)}, u32[]{:S(2)}) collective-permute-start(bf16[2,2,64,512]{3,2,1,0:T(8,128)(2,1)S(1)} %maximum_select_fusion.3.refs_4_), channel_id=1, source_target_pairs={{0,1},{1,0},{2,3},{3,2},{4,5},{5,4},{6,7},{7,6},{8,9},{9,8},{10,11... | collective-permute-start | bytes 786440 | tf_op jit(solution)/shard_map/ppermute | solution.py:807
  52.6 12.4 %collective-permute-start.11 = (bf16[2,2,64,512]{3,2,1,0:T(8,128)(2,1)S(1)}, bf16[2,2,64,512]{3,2,1,0:T(8,128)(2,1)S(1)}, u32[]{:S(2)}, u32[]{:S(2)}) collective-permute-start(bf16[2,2,64,512]{3,2,1,0:T(8,128)(2,1)S(1)} %maximum_select_fusion.4.refs_6_), channel_id=1, source_target_pairs={{0,2},{1,3},{2,0},{3,1},{4,6},{5,7},{6,4},{7,5},{8,10},{9,11},{10,... | collective-permute-start | bytes 786440 | tf_op jit(solution)/shard_map/ppermute | solution.py:807
  58.3 6.6 %collective-permute-start.9 = (bf16[1,128,512]{2,1,0:T(8,128)(2,1)S(1)}, bf16[1,128,512]{2,1,0:T(8,128)(2,1)S(1)}, u32[]{:S(2)}, u32[]{:S(2)}) collective-permute-start(bf16[1,128,512]{2,1,0:T(8,128)(2,1)S(1)} %bitcast.56), channel_id=1, source_target_pairs={{0,4},{1,5},{2,6},{3,7},{4,0},{5,1},{6,2},{7,3},{8,12},{9,13},{10,... | collective-permute-start | bytes 393224 | tf_op jit(solution)/shard_map/ppermute | solution.py:807
  64.9 19.5 %copy-start = (bf16[51,64,512]{2,1,0:T(8,128)(2,1)S(1)}, bf16[51,64,512]{2,1,0:T(8,128)(2,1)}, u32[]{:S(2)}) copy-start(bf16[51,64,512]{2,1,0:T(8,128)(2,1)} %mixing.3) | copy-start | bytes 10027012
  65.0 6.8 %collective-permute-start.13 = (bf16[2,64,512]{2,1,0:T(8,128)(2,1)S(1)}, bf16[2,64,512]{2,1,0:T(8,128)(2,1)S(1)}, u32[]{:S(2)}, u32[]{:S(2)}) collective-permute-start(bf16[2,64,512]{2,1,0:T(8,128)(2,1)S(1)} %get-tuple-element.174), channel_id=1, source_target_pairs={{0,1},{1,0},{2,3},{3,2},{4,5},{5,4},{6,7},{7,6},{8,9},{9,8},{10,11... | collective-permute-start | bytes 393224 | tf_op jit(solution)/shard_map/ppermute | solution.py:807
  68.0 6.7 %collective-permute-start.12 = (bf16[2,64,512]{2,1,0:T(8,128)(2,1)S(1)}, bf16[2,64,512]{2,1,0:T(8,128)(2,1)S(1)}, u32[]{:S(2)}, u32[]{:S(2)}) collective-permute-start(bf16[2,64,512]{2,1,0:T(8,128)(2,1)S(1)} %get-tuple-element.177), channel_id=1, source_target_pairs={{0,2},{1,3},{2,0},{3,1},{4,6},{5,7},{6,4},{7,5},{8,10},{9,11},{10,... | collective-permute-start | bytes 393224 | tf_op jit(solution)/shard_map/ppermute | solution.py:807
  74.8 6.8 %collective-permute-start.16 = (bf16[1,144,512]{2,1,0:T(8,128)(2,1)S(1)}, bf16[1,144,512]{2,1,0:T(8,128)(2,1)S(1)}, u32[]{:S(2)}, u32[]{:S(2)}) collective-permute-start(bf16[1,144,512]{2,1,0:T(8,128)(2,1)S(1)} %bitcast.54), channel_id=1, source_target_pairs={{0,4},{1,5},{2,6},{3,7},{4,0},{5,1},{6,2},{7,3},{8,12},{9,13},{10,... | collective-permute-start | bytes 442376 | tf_op jit(solution)/shard_map/ppermute | solution.py:807
  75.5 7.8 %collective-permute-start.14 = (bf16[2,2,64,512]{3,2,1,0:T(8,128)(2,1)S(1)}, bf16[2,2,64,512]{3,2,1,0:T(8,128)(2,1)S(1)}, u32[]{:S(2)}, u32[]{:S(2)}) collective-permute-start(bf16[2,2,64,512]{3,2,1,0:T(8,128)(2,1)S(1)} %maximum_select_fusion.6.part0), channel_id=1, source_target_pairs={{0,1},{1,0},{2,3},{3,2},{4,5},{5,4},{6,7},{7,6},{8,9},{9,8},{10,11... | collective-permute-start | bytes 786440 | tf_op jit(solution)/shard_map/ppermute | solution.py:807
  76.9 7.3 %collective-permute-start.15 = (bf16[2,2,64,512]{3,2,1,0:T(8,128)(2,1)S(1)}, bf16[2,2,64,512]{3,2,1,0:T(8,128)(2,1)S(1)}, u32[]{:S(2)}, u32[]{:S(2)}) collective-permute-start(bf16[2,2,64,512]{3,2,1,0:T(8,128)(2,1)S(1)} %maximum_select_fusion.7.part2), channel_id=1, source_target_pairs={{0,2},{1,3},{2,0},{3,1},{4,6},{5,7},{6,4},{7,5},{8,10},{9,11},{10,... | collective-permute-start | bytes 786440 | tf_op jit(solution)/shard_map/ppermute | solution.py:807
  81.6 11.1 %collective-permute-start.17 = (bf16[2,64,512]{2,1,0:T(8,128)(2,1)S(1)}, bf16[2,64,512]{2,1,0:T(8,128)(2,1)S(1)}, u32[]{:S(2)}, u32[]{:S(2)}) collective-permute-start(bf16[2,64,512]{2,1,0:T(8,128)(2,1)S(1)} %get-tuple-element.172), channel_id=1, source_target_pairs={{0,2},{1,3},{2,0},{3,1},{4,6},{5,7},{6,4},{7,5},{8,10},{9,11},{10,... | collective-permute-start | bytes 393224 | tf_op jit(solution)/shard_map/ppermute | solution.py:807
  81.8 11.0 %collective-permute-start.18 = (bf16[2,80,512]{2,1,0:T(8,128)(2,1)S(1)}, bf16[2,80,512]{2,1,0:T(8,128)(2,1)S(1)}, u32[]{:S(2)}, u32[]{:S(2)}) collective-permute-start(bf16[2,80,512]{2,1,0:T(8,128)(2,1)S(1)} %get-tuple-element.170), channel_id=1, source_target_pairs={{0,1},{1,0},{2,3},{3,2},{4,5},{5,4},{6,7},{7,6},{8,9},{9,8},{10,11... | collective-permute-start | bytes 491528 | tf_op jit(solution)/shard_map/ppermute | solution.py:807
  84.4 11.4 %copy-start.7 = (f32[512]{0:T(512)S(1)}, f32[512]{0:T(512)}, u32[]{:S(2)}) copy-start(f32[512]{0:T(512)} %param.13) | copy-start | bytes 6148
  92.8 9.5 %collective-permute-start.21 = (bf16[2,2,80,512]{3,2,1,0:T(8,128)(2,1)S(1)}, bf16[2,2,80,512]{3,2,1,0:T(8,128)(2,1)S(1)}, u32[]{:S(2)}, u32[]{:S(2)}) collective-permute-start(bf16[2,2,80,512]{3,2,1,0:T(8,128)(2,1)S(1)} %maximum_select_fusion.refs_2_), channel_id=1, source_target_pairs={{0,2},{1,3},{2,0},{3,1},{4,6},{5,7},{6,4},{7,5},{8,10},{9,11},{10,... | collective-permute-start | bytes 983048 | tf_op jit(solution)/shard_map/ppermute | solution.py:807
  93.9 16.3 %collective-permute-start.24 = (bf16[1024,512]{1,0:T(8,128)(2,1)S(1)}, bf16[1024,512]{1,0:T(8,128)(2,1)S(1)}, u32[]{:S(2)}, u32[]{:S(2)}) collective-permute-start(bf16[1024,512]{1,0:T(8,128)(2,1)S(1)} %place.1.grads), channel_id=1, source_target_pairs={{0,16},{8,24},{16,0},{24,8},{1,17},{9,25},{17,1},{25,9},{2,18},{10... | collective-permute-start | bytes 3145736 | tf_op jit(solution)/shard_map/ppermute | solution.py:807
  95.1 7.2 %collective-permute-start.20 = (bf16[2,2,64,512]{3,2,1,0:T(8,128)(2,1)S(1)}, bf16[2,2,64,512]{3,2,1,0:T(8,128)(2,1)S(1)}, u32[]{:S(2)}, u32[]{:S(2)}) collective-permute-start(bf16[2,2,64,512]{3,2,1,0:T(8,128)(2,1)S(1)} %maximum_select_fusion.8.refs_0_), channel_id=1, source_target_pairs={{0,1},{1,0},{2,3},{3,2},{4,5},{5,4},{6,7},{7,6},{8,9},{9,8},{10,11... | collective-permute-start | bytes 786440 | tf_op jit(solution)/shard_map/ppermute | solution.py:807
  96.6 5.7 %collective-permute-start.19 = (bf16[4,64,128]{2,1,0:T(8,128)(2,1)S(1)}, bf16[4,64,128]{2,1,0:T(8,128)(2,1)S(1)}, u32[]{:S(2)}, u32[]{:S(2)}) collective-permute-start(bf16[4,64,128]{2,1,0:T(8,128)(2,1)S(1)} %get-tuple-element.138), channel_id=1, source_target_pairs={{0,1},{1,0},{2,3},{3,2},{4,5},{5,4},{6,7},{7,6},{8,9},{9,8},{10,11... | collective-permute-start | bytes 196616 | tf_op jit(solution)/shard_map/ppermute | solution.py:807
  106.0 1.8 %collective-permute-start.23 = (bf16[784,256]{1,0:T(8,128)(2,1)S(1)}, bf16[784,256]{1,0:T(8,128)(2,1)S(1)}, u32[]{:S(2)}, u32[]{:S(2)}) collective-permute-start(bf16[784,256]{1,0:T(8,128)(2,1)S(1)} %dynamic-slice_bitcast_fusion), channel_id=1, source_target_pairs={{0,8},{8,0},{16,24},{24,16},{1,9},{9,1},{17,25},{25,17},{2,10},{10... | collective-permute-start | bytes 1204232 | tf_op jit(solution)/shard_map/ppermute | solution.py:807
  106.1 5.0 %collective-permute-start.22 = (bf16[2,2,64,128]{3,2,1,0:T(8,128)(2,1)S(1)}, bf16[2,2,64,128]{3,2,1,0:T(8,128)(2,1)S(1)}, u32[]{:S(2)}, u32[]{:S(2)}) collective-permute-start(bf16[2,2,64,128]{3,2,1,0:T(8,128)(2,1)S(1)} %bitcast.73), channel_id=1, source_target_pairs={{0,2},{1,3},{2,0},{3,1},{4,6},{5,7},{6,4},{7,5},{8,10},{9,11},{10,... | collective-permute-start | bytes 196616 | tf_op jit(solution)/shard_map/ppermute | solution.py:807
  110.1 9.2 %collective-permute-start.26 = (bf16[784,256]{1,0:T(8,128)(2,1)S(1)}, bf16[784,256]{1,0:T(8,128)(2,1)S(1)}, u32[]{:S(2)}, u32[]{:S(2)}) collective-permute-start(bf16[784,256]{1,0:T(8,128)(2,1)S(1)} %fusion), channel_id=1, source_target_pairs={{0,16},{8,24},{16,0},{24,8},{1,17},{9,25},{17,1},{25,9},{2,18},{10... | collective-permute-start | bytes 1204232 | tf_op jit(solution)/shard_map/ppermute | solution.py:807
  111.1 7.5 %collective-permute-start.25 = (bf16[1,4,64,128]{3,2,1,0:T(8,128)(2,1)S(1)}, bf16[1,4,64,128]{3,2,1,0:T(8,128)(2,1)S(1)}, u32[]{:S(2)}, u32[]{:S(2)}) collective-permute-start(bf16[1,4,64,128]{3,2,1,0:T(8,128)(2,1)S(1)} %get-tuple-element.182), channel_id=1, source_target_pairs={{0,4},{1,5},{2,6},{3,7},{4,0},{5,1},{6,2},{7,3},{8,12},{9,13},{10,... | collective-permute-start | bytes 196616 | tf_op jit(solution)/shard_map/ppermute | solution.py:807
  115.8 5.1 %collective-permute-start.28 = (bf16[1536,512]{1,0:T(8,128)(2,1)S(1)}, bf16[1536,512]{1,0:T(8,128)(2,1)S(1)}, u32[]{:S(2)}, u32[]{:S(2)}) collective-permute-start(bf16[1536,512]{1,0:T(8,128)(2,1)S(1)} %mixing_grad.2.part), channel_id=1, source_target_pairs={{0,8},{8,0},{16,24},{24,16},{1,9},{9,1},{17,25},{25,17},{2,10},{10... | collective-permute-start | bytes 4718600 | tf_op jit(solution)/shard_map/ppermute | solution.py:807
  119.3 6.0 %collective-permute-start.27 = (bf16[1728,512]{1,0:T(8,128)(2,1)S(1)}, bf16[1728,512]{1,0:T(8,128)(2,1)S(1)}, u32[]{:S(2)}, u32[]{:S(2)}) collective-permute-start(bf16[1728,512]{1,0:T(8,128)(2,1)S(1)} %mixing_grad.3.part), channel_id=1, source_target_pairs={{0,8},{8,0},{16,24},{24,16},{1,9},{9,1},{17,25},{25,17},{2,10},{10... | collective-permute-start | bytes 5308424 | tf_op jit(solution)/shard_map/ppermute | solution.py:807
  119.4 4.2 %collective-permute-start.29 = (bf16[784,256]{1,0:T(8,128)(2,1)S(1)}, bf16[784,256]{1,0:T(8,128)(2,1)S(1)}, u32[]{:S(2)}, u32[]{:S(2)}) collective-permute-start(bf16[784,256]{1,0:T(8,128)(2,1)S(1)} %add_convert_fusion.mine), channel_id=1, source_target_pairs={{0,8},{8,0},{16,24},{24,16},{1,9},{9,1},{17,25},{25,17},{2,10},{10... | collective-permute-start | bytes 1204232 | tf_op jit(solution)/shard_map/ppermute | solution.py:807

commit v5 on v4

--- a/solution.py
+++ b/solution.py
@@ -12,7 +12,8 @@
 AR = 3
 TILE = 256
 HALF = 128
-PER_STEP = 8
+PER_STEP = 12
+FEED_STEPS = 4
 
 eps_norm = 1e-05
 
@@ -183,7 +184,7 @@
         lags[j] = (pltpu.roll(inputs, j, 1) * lag_keep(ids, j)).astype(jnp.bfloat16)
 
 
-def step_maps(first, maps, taps, slabs, masks, doubled):
+def step_maps(first, place, maps, taps, slabs, masks, doubled):
     channels, length = maps.shape[2:]
     width = taps.shape[1]
     pairs = tile_pairs(length)
@@ -198,14 +199,13 @@
             both = product(
                 doubled[:, low * TILE : (tb + 1) * TILE], jnp.concatenate(tiles, axis=0)
             )
-            maps[0, first + k, :, block(tb)] = both[:channels].astype(jnp.bfloat16)
-            maps[1, first + k, :, block(tb)] = (both[channels:] * parity).astype(jnp.bfloat16)
-
-
-def maps_kernel(start, filters, pieces, *refs):
-    maps, lags, taps, slabs, masks, doubled = refs[-6:]
+            maps[0, place + k, :, block(tb)] = both[:channels].astype(jnp.bfloat16)
+            maps[1, place + k, :, block(tb)] = (both[channels:] * parity).astype(jnp.bfloat16)
+
+
+def maps_kernel(start, filters, pieces, maps, lags, taps, slabs, masks, doubled):
     start_maps(filters, pieces, lags, taps, masks, doubled)
-    step_maps(start, maps, taps, slabs, masks, doubled)
+    step_maps(start, 0, maps, taps, slabs, masks, doubled)
 
 
 def mixed_kernel(
@@ -240,7 +240,7 @@
         start_maps(filters, pieces, lags, taps, masks, doubled)
         acc[...] = jnp.zeros_like(acc)
 
-    step_maps(step * PER_STEP, maps, taps, slabs, masks, doubled)
+    step_maps(step * PER_STEP, step * PER_STEP, maps, taps, slabs, masks, doubled)
 
     @pl.when(step == 0)
     def _():
@@ -270,26 +270,28 @@
 
 
 def place_tokens(me, parts, out):
-    rows = parts[0].shape[2]
-    for half, pair in enumerate((parts[:2], parts[2:])):
-        for other, part in enumerate(pair):
-            low, near = me & 1, (me >> 1) & 1
-            for a in range(2):
-                for r in range(part.shape[1]):
-                    if half == 0:
-                        owner = r * 4 + a * 2 + (low ^ other)
-                    else:
-                        owner = r * 4 + (near ^ other) * 2 + a
-                    start = pl.multiple_of((owner * 2 + half) * rows, rows)
-                    out[pl.ds(start, rows), :] = part[a, r, :rows, :]
-
-
-def place_kernel(me, part0, part1, part2, part3, out):
-    place_tokens(me[0], (part0, part1, part2, part3), out)
+    low, near = me & 1, (me >> 1) & 1
+    halves = len(parts) // 2
+    rest = parts[0].shape[1]
+    rows = out.shape[0] // (4 * rest * halves)
+    for index, part in enumerate(parts):
+        half, other = index // 2, index % 2
+        for a in range(2):
+            for r in range(rest):
+                if half == 0:
+                    owner = r * 4 + a * 2 + (low ^ other)
+                else:
+                    owner = r * 4 + (near ^ other) * 2 + a
+                start = pl.multiple_of((owner * halves + half) * rows, rows)
+                out[pl.ds(start, rows), :] = part[a, r, :rows, :]
+
+
+def place_kernel(me, *refs):
+    place_tokens(me[0], refs[:-1], refs[-1])
 
 
 def place(me, parts):
-    count = 2 * sum(math.prod(part.shape[:-1]) for part in parts[:2])
+    count = sum(math.prod(part.shape[:-1]) for part in parts)
     shape = (count, parts[0].shape[-1])
     return pl.pallas_call(
         place_kernel,
@@ -305,46 +307,39 @@
     )(me, *parts)
 
 
-def spectral_back_kernel(filters, mixing, pieces, grads, acc, taps, slabs, masks, both):
+def spectral_back_kernel(start, filters, mixing, pieces, grads, *refs):
+    *before, acc, taps, slabs, masks, both = refs
     _, channels, model_width = mixing.shape
     count = filters.shape[0]
     length, width = acc.shape[1], taps.shape[1]
     reach = length // 2
     pairs = tile_pairs(length)
-    rows = PER_STEP * channels
-    step = pl.program_id(0)
-
-    @pl.when(step == 0)
-    def _():
-        build_masks(segment_row(pieces), masks, length, True)
-        acc[...] = jnp.zeros_like(acc)
-        source = lax.broadcasted_iota(jnp.int32, (width, width), 0)
-        target = lax.broadcasted_iota(jnp.int32, (width, width), 1)
-        flip = jnp.where(source + target == reach, 1.0, 0.0).astype(jnp.bfloat16)
-        taps[...] = product(filters[:, :width], flip)
-
+    some = slabs.shape[0]
+    rows = some * channels
+    build_masks(segment_row(pieces), masks, length, True)
+    source = lax.broadcasted_iota(jnp.int32, (width, width), 0)
+    target = lax.broadcasted_iota(jnp.int32, (width, width), 1)
+    flip = jnp.where(source + target == reach, 1.0, 0.0).astype(jnp.bfloat16)
+    taps[...] = product(filters[:, :width], flip)
     sign = parity_lanes(rows, length, jnp.bfloat16)
-    plus = contract_last(
-        mixing[pl.ds(step * PER_STEP, PER_STEP)].reshape(rows, model_width), grads[...]
-    )
-    both[:, :channels, :] = plus.astype(jnp.bfloat16).reshape(PER_STEP, channels, length)
-    minus = contract_last(
-        mixing[pl.ds(count + step * PER_STEP, PER_STEP)].reshape(rows, model_width), grads[...]
-    )
-    both[:, channels:, :] = (minus.astype(jnp.bfloat16) * sign).reshape(
-        PER_STEP, channels, length
-    )
-    for k in range(PER_STEP):
-        build_slab(taps[pl.ds(step * PER_STEP + k, 1), :], slabs.at[k], width)
+
+    def by_map(first):
+        weights = mixing[first : first + some].reshape(rows, model_width)
+        return contract_last(weights, grads[...]).astype(jnp.bfloat16)
+
+    both[:, :channels, :] = by_map(start).reshape(some, channels, length)
+    both[:, channels:, :] = (by_map(count + start) * sign).reshape(some, channels, length)
+    for k in range(some):
+        build_slab(taps[start + k : start + k + 1, :], slabs.at[k], width)
     for sb in range(length // TILE):
         chosen = [(i, tb) for i, (tb, s) in enumerate(pairs) if s == sb]
         last = chosen[-1][1]
-        total = acc[:, block(sb)]
-        for k in range(PER_STEP):
+        total = before[0][:, block(sb)] if before else jnp.zeros((2 * channels, TILE), jnp.float32)
+        for k in range(some):
             tiles = []
             for i, tb in chosen:
-                start = reach - (tb - sb) * TILE
-                tiles.append(slabs[k, :, start : start + TILE] * masks[i])
+                place = reach - (tb - sb) * TILE
+                tiles.append(slabs[k, :, place : place + TILE] * masks[i])
             total = total + product(
                 both[k, :, sb * TILE : (last + 1) * TILE], jnp.concatenate(tiles, axis=0)
             )
@@ -404,25 +399,23 @@
     ]
 
 
-def spectral_maps(pieces, filters, channels, start, count, into=None):
+def spectral_maps(pieces, filters, channels, start, count):
     length = filters.shape[1]
-    given = [] if into is None else [into]
     return pl.pallas_call(
         functools.partial(maps_kernel, start),
-        in_specs=[in_vmem(), in_vmem(), *[in_vmem() for _ in given]],
+        in_specs=[in_vmem()] * 2,
         out_specs=[in_vmem()] * 2,
         out_shape=[
-            pltpu.VMEM((2, K, channels, length), jnp.bfloat16),
+            pltpu.VMEM((2, count, channels, length), jnp.bfloat16),
             pltpu.VMEM((AR, channels, length), jnp.bfloat16),
         ],
         scratch_shapes=maps_scratch(channels, length, filters.shape[0], count),
-        input_output_aliases={2: 0} if given else {},
-        compiler_params=vmem(20),
+        compiler_params=vmem(12 + length // 128),
         cost_estimate=pl.CostEstimate(
             flops=6 * channels * count * length * length, transcendentals=0, bytes_accessed=4 << 20
         ),
         name="spectral_maps",
-    )(filters, pieces, *given)
+    )(filters, pieces)
 
 
 def spectral_mixed(me, pieces, filters, mixing):
@@ -453,30 +446,26 @@
             pltpu.VMEM((AR, channels, length), jnp.bfloat16),
             *[pltpu.VMEM(cut, jnp.bfloat16)] * 4,
         ],
-        compiler_params=vmem(20),
-        cost_estimate=pl.CostEstimate(
-            flops=10 * channels * count * length * length, transcendentals=0, bytes_accessed=4 << 20
-        ),
+        compiler_params=vmem(12 + length // 128),
         name="spectral_mixed",
     )(me, in_hbm(filters), pieces, in_hbm(mixing))
 
 
-def spectral_back(grads, mixing, filters, pieces):
+def spectral_back(grads, mixing, filters, pieces, start, some, *before):
     channels = mixing.shape[1]
     count, length = filters.shape
     return pl.pallas_call(
-        spectral_back_kernel,
-        grid=(count // PER_STEP,),
-        in_specs=[in_vmem()] * 4,
+        functools.partial(spectral_back_kernel, start),
+        in_specs=[in_vmem() for _ in range(4 + len(before))],
         out_specs=in_vmem(),
         scratch_shapes=[
-            *toeplitz_scratch(length, count, PER_STEP),
-            pltpu.VMEM((PER_STEP, 2 * channels, length), jnp.bfloat16),
+            *toeplitz_scratch(length, count, some),
+            pltpu.VMEM((some, 2 * channels, length), jnp.bfloat16),
         ],
         out_shape=pltpu.VMEM((2 * channels, length), jnp.float32),
-        compiler_params=vmem(20),
+        compiler_params=vmem(12 + length // 128),
         name="spectral_back",
-    )(filters, mixing, pieces, grads)
+    )(filters, mixing, pieces, grads, *before)
 
 
 def lag_back(me, acc, mixing, grads, lags, pieces, gain):
@@ -512,100 +501,54 @@
 
 
 def feed_forward_kernel(
-    bit,
-    held,
-    got,
-    hidden_in,
-    gain,
-    cotangent,
-    gate,
-    up,
-    down,
-    output,
-    normed_out,
-    grad,
-    grad_low,
-    normed,
-    resid,
-    acc,
-    normed_grad,
+    bit, held, got, hidden_in, gain, cotangent, gate, up, down, output, normed_out, grad, grad_low
 ):
-    step = pl.program_id(0)
-    share = resid.shape[0]
-
-    @pl.when(step == 0)
-    def _():
-        mixed = held[bit[0]].astype(jnp.float32) + got[...].astype(jnp.float32)
-        resid[...] = hidden_in[0].astype(jnp.float32) + mixed.T
-        normed[...] = rms_scale(resid[...], gain[...]).astype(jnp.bfloat16)
-        acc[...] = jnp.zeros_like(acc)
-        normed_grad[...] = jnp.zeros_like(normed_grad)
-
-    gate_value = product(normed[...], gate[...])
-    upper_value = product(normed[...], up[...])
-    hidden_grad = contract_last(cotangent[0], down[...])
-    hidden, gate_back, upper_back = gelu_parts(gate_value, upper_value, hidden_grad)
-    acc[...] += product(hidden.astype(jnp.bfloat16), down[...])
-    normed_grad[...] += contract_last(gate_back.astype(jnp.bfloat16), gate[...]) + contract_last(
-        upper_back.astype(jnp.bfloat16), up[...]
-    )
-
-    @pl.when(step == pl.num_programs(0) - 1)
-    def _():
-        value, back = resid[...], normed_grad[...]
-        output[0] = (value + acc[...]).astype(jnp.bfloat16)
-        scale = lax.rsqrt(jnp.mean(value * value, axis=-1, keepdims=True) + eps_norm)
-        weighed = back * gain[...]
-        along = jnp.mean(weighed * value, axis=-1, keepdims=True)
-        total = cotangent[0].astype(jnp.float32) + scale * (
-            weighed - value * (scale * scale * along)
-        )
-        grad[...] = total
-        grad_low[...] = total.astype(jnp.bfloat16)
-        gains = jnp.sum(back * value * scale, axis=0, keepdims=True)
-        high = jnp.broadcast_to(gains, (16, gains.shape[1])).astype(jnp.bfloat16)
-        low = (gains - high.astype(jnp.float32)).astype(jnp.bfloat16)
-        row = lax.broadcasted_iota(jnp.int32, low.shape, 0)
-        normed_out[:share, :] = normed[...]
-        normed_out[share:, :] = jnp.where(row < 8, high, low)
+    share, width = grad.shape
+    mixed = held[bit[0]].astype(jnp.float32) + got[...].astype(jnp.float32)
+    resid = hidden_in[0].astype(jnp.float32) + mixed.T
+    scale = lax.rsqrt(jnp.mean(resid * resid, axis=-1, keepdims=True) + eps_norm)
+    normed = (resid * scale * gain[...]).astype(jnp.bfloat16)
+    value, back = resid, jnp.zeros_like(resid)
+    units = gate.shape[1] // FEED_STEPS
+    for step in range(FEED_STEPS):
+        own = slice(step * units, (step + 1) * units)
+        gate_value = product(normed, gate[:, own])
+        upper_value = product(normed, up[:, own])
+        hidden_grad = contract_last(cotangent[0], down[own, :])
+        hidden, gate_back, upper_back = gelu_parts(gate_value, upper_value, hidden_grad)
+        value = value + product(hidden.astype(jnp.bfloat16), down[own, :])
+        back = back + contract_last(gate_back.astype(jnp.bfloat16), gate[:, own])
+        back = back + contract_last(upper_back.astype(jnp.bfloat16), up[:, own])
+    output[0] = value.astype(jnp.bfloat16)
+    weighed = back * gain[...]
+    along = jnp.mean(weighed * resid, axis=-1, keepdims=True)
+    total = scale * (weighed - resid * (scale * scale * along))
+    total = cotangent[0].astype(jnp.float32) + total
+    grad[...] = total
+    grad_low[...] = total.astype(jnp.bfloat16)
+    gains = jnp.sum(back * resid * scale, axis=0, keepdims=True)
+    high = jnp.broadcast_to(gains, (16, width)).astype(jnp.bfloat16)
+    low = (gains - high.astype(jnp.float32)).astype(jnp.bfloat16)
+    row = lax.broadcasted_iota(jnp.int32, low.shape, 0)
+    normed_out[:share, :] = normed
+    normed_out[share:, :] = jnp.where(row < 8, high, low)
 
 
 def feed_forward(bit, held, got, hidden_in, gain, cotangent, w_gate, w_up, w_down):
     _, share, width = hidden_in.shape
-    steps = 4
-    units = w_gate.shape[1] // steps
-    tokens = (share, width)
     return pl.pallas_call(
         feed_forward_kernel,
         grid_spec=pltpu.PrefetchScalarGridSpec(
             num_scalar_prefetch=1,
-            grid=(steps,),
-            in_specs=[
-                whole(held.shape),
-                whole(got.shape),
-                whole(hidden_in.shape),
-                whole((1, width)),
-                whole(cotangent.shape),
-                pl.BlockSpec((width, units), lambda k, _: (0, k)),
-                pl.BlockSpec((width, units), lambda k, _: (0, k)),
-                pl.BlockSpec((units, width), lambda k, _: (k, 0)),
-            ],
-            out_specs=[
-                whole(hidden_in.shape),
-                whole((share + 16, width)),
-                whole(tokens),
-                whole(tokens),
-            ],
-            scratch_shapes=[
-                pltpu.VMEM(tokens, jnp.bfloat16),
-                *[pltpu.VMEM(tokens, jnp.float32)] * 3,
-            ],
+            grid=(1,),
+            in_specs=[in_vmem()] * 8,
+            out_specs=[whole(hidden_in.shape), *[in_vmem()] * 3],
         ),
         out_shape=[
             jax.ShapeDtypeStruct(hidden_in.shape, jnp.bfloat16),
-            jax.ShapeDtypeStruct((share + 16, width), jnp.bfloat16),
-            jax.ShapeDtypeStruct(tokens, jnp.float32),
-            jax.ShapeDtypeStruct(tokens, jnp.bfloat16),
+            pltpu.VMEM((share + 16, width), jnp.bfloat16),
+            pltpu.VMEM((share, width), jnp.float32),
+            pltpu.VMEM((share, width), jnp.bfloat16),
         ],
         compiler_params=vmem(16),
         name="feed_forward",
@@ -644,39 +587,46 @@
     )(maps, lags, grads)
 
 
-def mixing_grad_kernel(which, maps, lags, grads, own, own_lags, out):
+def mixing_grad_kernel(which, maps0, maps1, lags, grads, own, own_lags, out):
     def total(values, mine):
         values = product(values.reshape(-1, values.shape[-1]), grads[...])
         return (values + mine.reshape(values.shape).astype(jnp.float32)).astype(out.dtype)
 
-    count, channels = maps.shape[1:3]
-
-    def chunk(index, _):
-        part = pl.ds(index * CHUNK, CHUNK)
-        start = pl.multiple_of(index * CHUNK * channels, CHUNK * channels)
-        out[pl.ds(start, CHUNK * channels), :] = total(maps[which, part], own[which, part])
-
-    lax.fori_loop(0, count // CHUNK, chunk, None)
+    channels = lags.shape[1]
+    done = 0
+    for maps in (maps0, maps1):
+
+        def chunk(index, _, maps=maps, done=done):
+            part, place = (pl.ds(start + index * CHUNK, CHUNK) for start in (0, done))
+            rows = CHUNK * channels
+            start = pl.multiple_of(done * channels + index * rows, rows)
+            out[pl.ds(start, rows), :] = total(maps[which, part], own[which, place])
+
+        lax.fori_loop(0, maps.shape[1] // CHUNK, chunk, None)
+        done += maps.shape[1]
     if which:
-        out[count * channels :, :] = total(lags[...], own_lags[...])
+        out[done * channels :, :] = total(lags[...], own_lags[...])
 
 
 def mixing_grad(which, maps, lags, grads, own, own_lags):
-    _, count, channels, _ = maps.shape
+    channels = lags.shape[1]
+    count = own.shape[1]
     shape = ((count + which * AR) * channels, grads.shape[1])
     return pl.pallas_call(
         functools.partial(mixing_grad_kernel, which),
-        in_specs=[in_vmem()] * 5,
+        in_specs=[in_vmem()] * 6,
         out_specs=in_vmem(),
         out_shape=pltpu.VMEM(shape, jnp.bfloat16),
         compiler_params=vmem(16),
         name="mixing_grad",
-    )(maps, lags, grads, own, own_lags)
+    )(*maps, lags, grads, own, own_lags)
 
 
 def finish_mixing_kernel(part, got, *refs):
     out = refs[-1]
-    out[...] = (part[...].astype(jnp.float32) + got[...].astype(jnp.float32)).reshape(out.shape)
+    rows = out.shape[0] * out.shape[1]
+    own = pl.ds(pl.multiple_of(pl.program_id(0) * rows, rows), rows)
+    out[...] = (part[own, :].astype(jnp.float32) + got[own, :].astype(jnp.float32)).reshape(out.shape)
 
 
 def finish_mixing(part, got, first, total, into=None):
@@ -688,11 +638,7 @@
     return pl.pallas_call(
         finish_mixing_kernel,
         grid=(steps,),
-        in_specs=[
-            pl.BlockSpec((size * channels, total[2]), lambda k: (k, 0)),
-            pl.BlockSpec((size * channels, total[2]), lambda k: (k, 0)),
-            *[pl.BlockSpec(memory_space=pl.ANY) for _ in given],
-        ],
+        in_specs=[in_vmem(), in_vmem(), *[pl.BlockSpec(memory_space=pl.ANY) for _ in given]],
         out_specs=pl.BlockSpec(
             tuple(map(pl.Element, (size, *total[1:]))), lambda k: (first + k * size, 0, 0)
         ),
@@ -712,10 +658,11 @@
     *parts, gate, up, down, first_gain, out, normed, cotangent = refs
     place_tokens(me[0], parts[:4], normed)
     place_tokens(me[0], parts[4:], cotangent)
-    width, units = gate.shape
-    hidden_grad = contract_last(cotangent[...], down[...])
-    gate_value = product(normed[...], gate[...])
-    upper_value = product(normed[...], up[...])
+    width, units = gate.shape[0], out.shape[2]
+    mine = pl.ds(pl.multiple_of(me[0] * units, units), units)
+    hidden_grad = contract_last(cotangent[...], down[mine, :])
+    gate_value = product(normed[...], gate[:, mine])
+    upper_value = product(normed[...], up[:, mine])
     hidden, gate_back, upper_back = gelu_parts(gate_value, upper_value, hidden_grad)
     gate_part = contract_first(normed[...], gate_back.astype(jnp.bfloat16))
     up_part = contract_first(normed[...], upper_back.astype(jnp.bfloat16))
@@ -726,12 +673,11 @@
     for i in range(2 * len(starts)):
         half, start = i // len(starts), starts[i % len(starts)]
         out[half, start : start + units] = down_part[:, i * units : (i + 1) * units]
-    share_rows = parts[0].shape[2]
     second = jnp.zeros((16, width), jnp.float32)
     for part in parts[2:4]:
         for a in range(2):
             for r in range(part.shape[1]):
-                second = second + part[a, r, share_rows:, :].astype(jnp.float32)
+                second = second + part[a, r, -16:, :].astype(jnp.float32)
     second = second[:8] + second[8:]
     second = pltpu.roll(second, lax.rem(width - me[0] * channels, width), 1)
     out[0, size - 16 :] = jnp.zeros((16, units), jnp.bfloat16)
@@ -746,7 +692,7 @@
     chans = lax.axis_size("chan")
     units = hidden // chans
     parts = [*normed_parts, *cotangent_parts]
-    tokens = 2 * sum(math.prod(part.shape[:-1]) for part in normed_parts[:2])
+    tokens = sum(math.prod(part.shape[:-1]) for part in cotangent_parts)
     shape = (2, unit_rows(width, units)[1], units)
     return pl.pallas_call(
         functools.partial(unit_grads_kernel, width // chans),
@@ -755,10 +701,7 @@
             grid=(1,),
             in_specs=[
                 *[in_vmem() for _ in parts],
-                pl.BlockSpec((width, units), lambda k, me: (0, me[0])),
-                pl.BlockSpec((width, units), lambda k, me: (0, me[0])),
-                pl.BlockSpec((units, width), lambda k, me: (me[0], 0)),
-                in_vmem(),
+                *[in_vmem()] * 4,
             ],
             out_specs=in_vmem(),
             scratch_shapes=[pltpu.VMEM((tokens, width), jnp.bfloat16)] * 2,
@@ -766,7 +709,7 @@
         out_shape=pltpu.VMEM(shape, jnp.bfloat16),
         compiler_params=vmem(24),
         name="unit_grads",
-    )(me, *parts, in_hbm(w_gate), in_hbm(w_up), in_hbm(w_down), first_gain)
+    )(me, *parts, w_gate, w_up, w_down, first_gain)
 
 
 def finish_units_kernel(core, mine, other, gate, up, down, gains):
@@ -831,12 +774,12 @@
 
 
 class Gather:
-    def __init__(self, values, half, bits):
+    def __init__(self, values, halves, bits):
         masks = bits_of("chan")
-        self.half, self.bits = half, bits
+        self.bits = bits
         self.shape = values.shape
         self.common = masks[2:]
-        self.orders = [(masks[1], masks[0]), (masks[0], masks[1])]
+        self.orders = [(masks[1], masks[0]), (masks[0], masks[1])][:halves]
         self.held = values[None]
 
     def first(self, came=None):
@@ -846,7 +789,10 @@
         return self.held
 
     def second(self):
-        self.halves = [self.held[:, : self.half], self.held[:, self.half :]]
+        self.halves = [self.held]
+        if len(self.orders) == 2:
+            half = self.shape[0] // 32 * 16
+            self.halves = [self.held[:, :half], self.held[:, half:]]
         self.halves = [
             gather_round(h, order[0], self.bits)
             for h, order in zip(self.halves, self.orders, strict=True)
@@ -860,7 +806,7 @@
         return self.others
 
     def parts(self):
-        return (self.halves[0], self.others[0], self.halves[1], self.others[1])
+        return [part for pair in zip(self.halves, self.others, strict=True) for part in pair]
 
 
 def add(left, right):
@@ -922,7 +868,7 @@
         concat_axis=0,
     )
     pieces, cotangent = tie(pieces, out_grad)
-    cotangent_gather = Gather(cotangent[0], share // 2, bits)
+    cotangent_gather = Gather(cotangent[0], 2, bits)
     came = swap(cotangent_gather.held, "chan", 4)
     maps, lags, *cut = spectral_mixed(at, pieces, filters, mixing)
     pieces, lags, came = tie(pieces, lags, came)
@@ -939,40 +885,42 @@
         held, peer_pieces, *cotangent_gather.halves
     )
     got = exchange(held, 4, 0, bits)[1][0]
-    peer_maps, peer_lags = spectral_maps(peer_pieces, filters, channels, 0, K // 2)
-    held, got, peer_maps = tie(held, got, peer_maps)
+    first_maps, peer_lags = spectral_maps(peer_pieces, filters, channels, 0, K // 2)
+    held, got, first_maps = tie(held, got, first_maps)
     cotangent_gather.third()
     output, normed_two, resid_grad, resid_low = feed_forward(
         bits[4][0].reshape(1), held, got, hidden_in, gain_two, out_grad, w_gate, w_up, w_down
     )
-    grad_gather = Gather(resid_low, share // 2, bits)
+    grad_gather = Gather(resid_low, 2, bits)
     first, *cotangent_gather.others = tie(grad_gather.first(), *cotangent_gather.others)
     peer_pieces, resid_grad = tie(peer_pieces, resid_grad)
-    peer_maps, _ = spectral_maps(peer_pieces, filters, channels, K // 2, K // 2, peer_maps)
-    grad_gather.held, peer_maps = tie(first, peer_maps)
+    second_maps, _ = spectral_maps(peer_pieces, filters, channels, K // 2, K // 2)
+    grad_gather.held, second_maps = tie(first, second_maps)
+    peer_maps = (first_maps, second_maps)
     grad_gather.second()
     normed_two, *grad_gather.halves = tie(normed_two, *grad_gather.halves)
     grad_gather.third()
-    normed_gather = Gather(normed_two, share // 2, bits)
+    normed_gather = Gather(normed_two, 2, bits)
     normed_gather.first()
     full_grad = place(at, grad_gather.parts())
     peer_grad = swap(full_grad, "rows", 2)
     normed_gather.second()
-    acc = spectral_back(full_grad, mixing, filters, pieces)
+    acc = spectral_back(full_grad, mixing, filters, pieces, 0, K // 2)
     acc, *normed_gather.halves = tie(acc, *normed_gather.halves)
     normed_gather.third()
+    acc = spectral_back(full_grad, mixing, filters, pieces, K // 2, K // 2, acc)
     back, give, first_local = lag_back(at, acc, mixing, full_grad, lags, pieces, gain_one)
     came = swap(give, "chan", 1)
-    first_local, full_grad = tie(first_local, full_grad)
-    own, own_lags = own_mixing_grad(maps, lags, full_grad)
-    own_lags, back, came, *normed_parts = tie(own_lags, back, came, *normed_gather.parts())
+    first_local, *normed_parts = tie(first_local, *normed_gather.parts())
     unit_parts = unit_grads(
         at, normed_parts, cotangent_gather.parts(), w_gate, w_up, w_down, first_local
     )
+    unit_parts, full_grad, back, came = tie(unit_parts, full_grad, back, came)
+    own, own_lags = own_mixing_grad(maps, lags, full_grad)
     back, came = exchange_rest(back, came)
     unit_given = swap(entry(unit_parts, other_core, 0)[0], "rows", 1)
     unit_half = add(entry(unit_parts, core, 0)[0], unit_given).astype(jnp.bfloat16)
-    unit_half, peer_grad = tie(unit_half, peer_grad)
+    own_lags, unit_half, peer_grad = tie(own_lags, unit_half, peer_grad)
     unit_other = swap(unit_half, "rows", 2)
     first_part = mixing_grad(0, peer_maps, peer_lags, peer_grad, own, own_lags)
     first_part, peer_grad = tie(first_part, peer_grad)

time: 128 us -> 126 us (0.984)
  waiting for transfers between devices: 25.5 us -> 29.2 us
  Pallas kernels: 52.6 us -> 49.4 us
  starting transfers between devices: 32.2 us -> 29.8 us
    ppermute x30, waiting for transfers between devices: 25.5 us -> 29.2 us  [swap(): return lax.ppermute(values, axis, [(i, i ^ mask) for i in range(count)])]
    ppermute x30, starting transfers between devices: 32.2 us -> 29.8 us  [swap(): return lax.ppermute(values, axis, [(i, i ^ mask) for i in range(count)])]
    pallas_call x1, Pallas kernels: 5.29 us -> 3.83 us  [feed_forward(): pl.pallas_call(feed_forward_kernel, grid_spec=pltpu.PrefetchScalarGridSpe...]
    pallas_call x3 -> x4, Pallas kernels: 12.7 us -> 12.2 us  [the longest x2 7.83 us: spectral_back(): pl.pallas_call(functools.partial(spectral_back_kernel, start), in_specs=[...]
  transfers between devices with their start and end apart: 30 -> 30, of which waited for: 13 -> 11; matrix products, arithmetic and copies ran while one was open for 1% -> 1% of each run, Pallas kernels for 30% -> 28%
where the time goes in v5:
time: 126 us
  Pallas kernels  49.4 us (39%)
  starting transfers between devices  29.8 us (24%)
  waiting for transfers between devices  29.2 us (23%)
  blocking collectives  14.6 us (12%)
    ppermute x30, starting transfers between devices, swap(): return lax.ppermute(values, axis, [(i, i ^ mask) for i in range(count)])  29.8 us
    ppermute x30, waiting for transfers between devices, swap(): return lax.ppermute(values, axis, [(i, i ^ mask) for i in range(count)])  29.2 us
    all_to_all x1, blocking collectives, shards(): lax.all_to_all(first_norm(at, hidden_in, gain_one, segments, chans), 'cha...  14.6 us
    pallas_call x1, Pallas kernels, spectral_mixed(): pl.pallas_call(mixed_kernel, grid_spec=pltpu.PrefetchScalarGridSpec(num_s...  10.9 us
    pallas_call x2, Pallas kernels, spectral_back(): pl.pallas_call(functools.partial(spectral_back_kernel, start), in_specs=[...  7.83 us
    pallas_call x2, Pallas kernels, spectral_maps(): pl.pallas_call(functools.partial(maps_kernel, start), in_specs=[in_vmem()...  6.29 us
    pallas_call x2, Pallas kernels, mixing_grad(): pl.pallas_call(functools.partial(mixing_grad_kernel, which), in_specs=[in...  4.96 us
    pallas_call x1, Pallas kernels, own_mixing_grad(): pl.pallas_call(own_mixing_grad_kernel, in_specs=[in_vmem()] * 3, out_spec...  4.47 us
  transfers between devices with their start and end apart: 30, of which 11 were waited for; matrix products, arithmetic and copies ran while one was open for 1% of the time, Pallas kernels for 28%

profile of v5, /device:TPU:0, one launch (start us, length us, event | category | flops | bytes accessed | tf_op | source)
XLA Modules:
  0.0 125.7 jit_solution(14138631269279308690)
XLA Ops:
  0.7 1.1 first_norm.1
  1.8 14.6 %all_to_all.5.pieces = bf16[8,80,128]{2,1,0:T(8,128)(2,1)S(1)} all-to-all(bf16[8,80,128]{2,1,0:T(8,128)(2,1)S(1)} %first_norm.1), channel_id=1, replica_groups=mesh['rows'=4,'chan'=8] {'chan'}, dimensions={0} | all-to-all | bytes 327680 | tf_op jit(solution)/shard_map/all_to_all | solution.py:864
  16.4 10.9 %spectral_mixed.1 = (bf16[2,24,64,1024]{3,2,1,0:T(8,128)(2,1)S(1)}, bf16[3,64,1024]{2,1,0:T(8,128)(2,1)S(1)}, bf16[2,2,256,128]{3,2,1,0:T(8,128)(2,1)S(1)}, bf16...) custom-call(s32[1]{0:T(128)} %bitcast.me, ...), custom_call_target="tpu_custom_call" | custom-call | tf_op jit(solution)/shard_map/spectral_mixed/pallas_call | solution.py:426
  27.6 1.1 collective-permute-start.2
  28.8 1.4 %collective-permute-start = (bf16[2,2,256,128]{3,2,0,1:T(8,128)(2,1)S(1)}, bf16[2,2,256,128]{3,2,0,1:T(8,128)(2,1)S(1)}, u32[]{:S(2)}, u32[]{:S(2)}) collective-permute-start(bf16[2,2,256,128]{3,2,0,1:T(8,128)(2,1)S(1)} %copy.20), channel_id=1, source_target_pairs={{0,1},{1,0},{2,3},{3,2},{4,5},{5,4},{6,7},{7,6},{8,9},{9,8},{10,11... | collective-permute-start | bytes 786440 | tf_op jit(solution)/shard_map/ppermute | solution.py:750
  30.2 4.5 %collective-permute-done.2 = bf16[1,128,512]{2,1,0:T(8,128)(2,1)S(1)} collective-permute-done((bf16[1,128,512]{2,1,0:T(8,128)(2,1)S(1)}, bf16[1,128,512]{2,1,0:T(8,128)(2,1)S(1)}, u32[]{:S(2)}, u32[]{:S(2)}) %collective-permute-start.2) | collective-permute-done | bytes 131104 | tf_op jit(solution)/shard_map/ppermute | solution.py:750
  34.7 1.5 %collective-permute-start.5 = (bf16[8,80,128]{2,1,0:T(8,128)(2,1)S(1)}, bf16[8,80,128]{2,1,0:T(8,128)(2,1)S(1)}, u32[]{:S(2)}, u32[]{:S(2)}) collective-permute-start(bf16[8,80,128]{2,1,0:T(8,128)(2,1)S(1)} %all_to_all.5.pieces), channel_id=1, source_target_pairs={{0,16},{8,24},{16,0},{24,8},{1,17},{9,25},{17,1},{25,9},{2,18},{10... | collective-permute-start | bytes 491528 | tf_op jit(solution)/shard_map/ppermute | solution.py:750
  36.2 0.6 collective-permute-done.1
  37.0 2.2 %collective-permute-start.3 = (bf16[2,1,256,128]{3,2,0,1:T(8,128)(2,1)S(1)}, bf16[2,1,256,128]{3,2,0,1:T(8,128)(2,1)S(1)}, u32[]{:S(2)}, u32[]{:S(2)}) collective-permute-start(bf16[2,1,256,128]{3,2,0,1:T(8,128)(2,1)S(1)} %constant_dynamic-slice_fusion.2), channel_id=1, source_target_pairs={{0,2},{1,3},{2,0},{3,1},{4,6},{5,7},{6,4},{7,5},{8,10},{9,11},{10,... | collective-permute-start | bytes 393224 | tf_op jit(solution)/shard_map/ppermute | solution.py:750
  39.3 1.6 %collective-permute-start.7 = (bf16[2,64,512]{2,1,0:T(8,128)(2,1)S(1)}, bf16[2,64,512]{2,1,0:T(8,128)(2,1)S(1)}, u32[]{:S(2)}, u32[]{:S(2)}) collective-permute-start(bf16[2,64,512]{2,1,0:T(8,128)(2,1)S(1)} %get-tuple-element.180), channel_id=1, source_target_pairs={{0,1},{1,0},{2,3},{3,2},{4,5},{5,4},{6,7},{7,6},{8,9},{9,8},{10,11... | collective-permute-start | bytes 393224 | tf_op jit(solution)/shard_map/ppermute | solution.py:750
  40.9 0.6 collective-permute-start.4
  41.5 1.6 %collective-permute-done.3 = bf16[2,1,256,128]{3,2,0,1:T(8,128)(2,1)S(1)} collective-permute-done((bf16[2,1,256,128]{3,2,0,1:T(8,128)(2,1)S(1)}, bf16[2,1,256,128]{3,2,0,1:T(8,128)(2,1)S(1)}, u32[]{:S(2)}, u32[]{:S(2)}) %collective-permute-start.3) | collective-permute-done | bytes 131104 | tf_op jit(solution)/shard_map/ppermute | solution.py:750
  43.1 2.8 %collective-permute-done.4 = bf16[2,1,256,128]{3,2,0,1:T(8,128)(2,1)S(1)} collective-permute-done((bf16[2,1,256,128]{3,2,0,1:T(8,128)(2,1)S(1)}, bf16[2,1,256,128]{3,2,0,1:T(8,128)(2,1)S(1)}, u32[]{:S(2)}, u32[]{:S(2)}) %collective-permute-start.4) | collective-permute-done | bytes 131104 | tf_op jit(solution)/shard_map/ppermute | solution.py:750
  46.1 2.3 %collective-permute-start.8 = (bf16[1,512,128]{2,1,0:T(8,128)(2,1)S(1)}, bf16[1,512,128]{2,1,0:T(8,128)(2,1)S(1)}, u32[]{:S(2)}, u32[]{:S(2)}) collective-permute-start(bf16[1,512,128]{2,1,0:T(8,128)(2,1)S(1)} %constant_dynamic-slice_fusion), channel_id=1, source_target_pairs={{0,4},{1,5},{2,6},{3,7},{4,0},{5,1},{6,2},{7,3},{8,12},{9,13},{10,... | collective-permute-start | bytes 393224 | tf_op jit(solution)/shard_map/ppermute | solution.py:750
  48.5 2.8 %spectral_maps.2 = (bf16[2,12,64,1024]{3,2,1,0:T(8,128)(2,1)S(1)}, bf16[3,64,1024]{2,1,0:T(8,128)(2,1)S(1)}) custom-call(bf16[24,1024]{1,0:T(8,128)(2,1)S(1)} %copy-done.6, bf16[8,80,128]{2,1,0:T(8,128)(2,1)S(1)} %collective-permute-done.5.pieces), custom_call_target="tpu_custom_call" | custom-call | flops 4831838208 | bytes 4194304 | tf_op jit(solution)/shard_map/spectral_maps/pallas_call | solution.py:404
  51.3 1.0 collective-permute-start.10
  52.3 0.4 collective-permute-start.11
  52.7 3.8 %feed_forward.1 = (bf16[1,128,512]{2,1,0:T(8,128)(2,1)}, bf16[144,512]{1,0:T(8,128)(2,1)S(1)}, f32[128,512]{1,0:T(8,128)S(1)}, bf16[128,512]{1,0:T(8,128)(2,1)S(1)}) custom-call(s32[1]{0:T(128)} %bitcast.1.bit, bf16[2,512,128]{2,1,0:T(8,128)(2,1)S(1)} %pad_maximum_fusion.held, bf16[512,128]{1,0:T(8,128)(2,1)S(1)} %bitcast.58, ...), custom_call_target="tpu_custom_call" | custom-call | tf_op jit(solution)/shard_map/feed_forward/pallas_call | solution.py:539
  56.5 3.0 %collective-permute-start.9 = (bf16[1,128,512]{2,1,0:T(8,128)(2,1)S(1)}, bf16[1,128,512]{2,1,0:T(8,128)(2,1)S(1)}, u32[]{:S(2)}, u32[]{:S(2)}) collective-permute-start(bf16[1,128,512]{2,1,0:T(8,128)(2,1)S(1)} %bitcast.56), channel_id=1, source_target_pairs={{0,4},{1,5},{2,6},{3,7},{4,0},{5,1},{6,2},{7,3},{8,12},{9,13},{10,... | collective-permute-start | bytes 393224 | tf_op jit(solution)/shard_map/ppermute | solution.py:750
  59.5 3.5 %spectral_maps.3 = (bf16[2,12,64,1024]{3,2,1,0:T(8,128)(2,1)S(1)}, bf16[3,64,1024]{2,1,0:T(8,128)(2,1)}) custom-call(bf16[24,1024]{1,0:T(8,128)(2,1)S(1)} %copy-done.6, bf16[8,80,128]{2,1,0:T(8,128)(2,1)S(1)} %collective-permute-done.5.pieces), custom_call_target="tpu_custom_call" | custom-call | flops 4831838208 | bytes 4194304 | tf_op jit(solution)/shard_map/spectral_maps/pallas_call | solution.py:404
  63.1 3.1 %collective-permute-start.13 = (bf16[2,64,512]{2,1,0:T(8,128)(2,1)S(1)}, bf16[2,64,512]{2,1,0:T(8,128)(2,1)S(1)}, u32[]{:S(2)}, u32[]{:S(2)}) collective-permute-start(bf16[2,64,512]{2,1,0:T(8,128)(2,1)S(1)} %get-tuple-element.176), channel_id=1, source_target_pairs={{0,1},{1,0},{2,3},{3,2},{4,5},{5,4},{6,7},{7,6},{8,9},{9,8},{10,11... | collective-permute-start | bytes 393224 | tf_op jit(solution)/shard_map/ppermute | solution.py:750
  66.2 3.8 %collective-permute-done.13 = bf16[2,64,512]{2,1,0:T(8,128)(2,1)S(1)} collective-permute-done((bf16[2,64,512]{2,1,0:T(8,128)(2,1)S(1)}, bf16[2,64,512]{2,1,0:T(8,128)(2,1)S(1)}, u32[]{:S(2)}, u32[]{:S(2)}) %collective-permute-start.13) | collective-permute-done | bytes 131104 | tf_op jit(solution)/shard_map/ppermute | solution.py:750
  70.1 3.0 %collective-permute-done.12 = bf16[2,64,512]{2,1,0:T(8,128)(2,1)S(1)} collective-permute-done((bf16[2,64,512]{2,1,0:T(8,128)(2,1)S(1)}, bf16[2,64,512]{2,1,0:T(8,128)(2,1)S(1)}, u32[]{:S(2)}, u32[]{:S(2)}) %collective-permute-start.12) | collective-permute-done | bytes 131104 | tf_op jit(solution)/shard_map/ppermute | solution.py:750
  73.2 1.8 %collective-permute-start.14 = (bf16[2,2,64,512]{3,2,1,0:T(8,128)(2,1)S(1)}, bf16[2,2,64,512]{3,2,1,0:T(8,128)(2,1)S(1)}, u32[]{:S(2)}, u32[]{:S(2)}) collective-permute-start(bf16[2,2,64,512]{3,2,1,0:T(8,128)(2,1)S(1)} %maximum_select_fusion.6.refs_0_), channel_id=1, source_target_pairs={{0,1},{1,0},{2,3},{3,2},{4,5},{5,4},{6,7},{7,6},{8,9},{9,8},{10,11... | collective-permute-start | bytes 786440 | tf_op jit(solution)/shard_map/ppermute | solution.py:750
  75.0 4.9 %collective-permute-done.16 = bf16[1,144,512]{2,1,0:T(8,128)(2,1)S(1)} collective-permute-done((bf16[1,144,512]{2,1,0:T(8,128)(2,1)S(1)}, bf16[1,144,512]{2,1,0:T(8,128)(2,1)S(1)}, u32[]{:S(2)}, u32[]{:S(2)}) %collective-permute-start.16) | collective-permute-done | bytes 147488 | tf_op jit(solution)/shard_map/ppermute | solution.py:750
  80.1 1.7 %collective-permute-start.18 = (bf16[2,80,512]{2,1,0:T(8,128)(2,1)S(1)}, bf16[2,80,512]{2,1,0:T(8,128)(2,1)S(1)}, u32[]{:S(2)}, u32[]{:S(2)}) collective-permute-start(bf16[2,80,512]{2,1,0:T(8,128)(2,1)S(1)} %get-tuple-element.172), channel_id=1, source_target_pairs={{0,1},{1,0},{2,3},{3,2},{4,5},{5,4},{6,7},{7,6},{8,9},{9,8},{10,11... | collective-permute-start | bytes 491528 | tf_op jit(solution)/shard_map/ppermute | solution.py:750
  81.7 2.8 %collective-permute-done.15.refs_3_ = bf16[2,2,64,512]{3,2,1,0:T(8,128)(2,1)S(1)} collective-permute-done((bf16[2,2,64,512]{3,2,1,0:T(8,128)(2,1)S(1)}, bf16[2,2,64,512]{3,2,1,0:T(8,128)(2,1)S(1)}, u32[]{:S(2)}, u32[]{:S(2)}) %collective-permute-start.15) | collective-permute-done | bytes 262176 | tf_op jit(solution)/shard_map/ppermute | solution.py:750
  84.7 4.0 %spectral_back.2.refs_0_ = f32[128,1024]{1,0:T(8,128)S(1)} custom-call(bf16[24,1024]{1,0:T(8,128)(2,1)S(1)} %copy-done.6, bf16[51,64,512]{2,1,0:T(8,128)(2,1)S(1)} %copy-done, bf16[8,80,128]{2,1,0:T(8,128)(2,1)S(1)} %all_to_all.5.pieces, bf16[1024,512]{1,0:T(8,128)(2,1)S(1)} %place.1.grads), custom_call_target="tpu_custom_call" | custom-call | tf_op jit(solution)/shard_map/spectral_back/pallas_call | solution.py:457
  88.9 1.9 %collective-permute-start.24 = (bf16[1024,512]{1,0:T(8,128)(2,1)S(1)}, bf16[1024,512]{1,0:T(8,128)(2,1)S(1)}, u32[]{:S(2)}, u32[]{:S(2)}) collective-permute-start(bf16[1024,512]{1,0:T(8,128)(2,1)S(1)} %place.1.grads), channel_id=1, source_target_pairs={{0,16},{8,24},{16,0},{24,8},{1,17},{9,25},{17,1},{25,9},{2,18},{10... | collective-permute-start | bytes 3145736 | tf_op jit(solution)/shard_map/ppermute | solution.py:750
  90.8 1.0 collective-permute-start.19
  91.8 3.8 %spectral_back.3.acc = f32[128,1024]{1,0:T(8,128)S(1)} custom-call(bf16[24,1024]{1,0:T(8,128)(2,1)S(1)} %copy-done.6, bf16[51,64,512]{2,1,0:T(8,128)(2,1)S(1)} %copy-done, bf16[8,80,128]{2,1,0:T(8,128)(2,1)S(1)} %all_to_all.5.pieces, bf16[1024,512]{1,0:T(8,128)(2,1)S(1)} %place.1.grads, f32[128,1024]{1,0:T(8,128)S(1)} %spectral_back.2.refs_0_), custom_call_target="tpu_custom_call" | custom-call | tf_op jit(solution)/shard_map/spectral_back/pallas_call | solution.py:457
  95.6 0.8 lag_back.1
  96.4 1.1 collective-permute-start.21
  97.5 2.5 %unit_grads.1 = bf16[2,784,256]{2,1,0:T(8,128)(2,1)S(1)} custom-call(s32[1]{0:T(128)} %bitcast.me, bf16[2,2,64,512]{3,2,1,0:T(8,128)(2,1)S(1)} %maximum_select_fusion.8.refs_0_, bf16[2,2,64,512]{3,2,1,0:T(8,128)(2,1)S(1)} %collective-permute-done.19.refs_1_, bf16[2,2,80,512]{3,2,1,0:T(8,128)(2,1)S(1)} %maximum_select_fusion.refs_2_, ...), custom_call_target="tpu_custom_call" | custom-call | tf_op jit(solution)/shard_map/unit_grads/pallas_call | solution.py:697
  100.0 0.7 collective-permute-done.21
  101.0 4.5 %own_mixing_grad.1 = (bf16[2,24,64,512]{3,2,1,0:T(8,128)(2,1)S(1)}, bf16[3,64,512]{2,1,0:T(8,128)(2,1)S(1)}) custom-call(bf16[2,24,64,1024]{3,2,1,0:T(8,128)(2,1)S(1)} %get-tuple-element.150.maps, bf16[3,64,1024]{2,1,0:T(8,128)(2,1)S(1)} %get-tuple-element.132.inputs.lags, bf16[1024,512]{1,0:T(8,128)(2,1)S(1)} %place.1.grads), custom_call_target="tpu_custom_call" | custom-call | tf_op jit(solution)/shard_map/own_mixing_grad/pallas_call | solution.py:577
  105.7 1.2 collective-permute-start.26
  106.9 1.5 %collective-permute-start.25 = (bf16[1,4,64,128]{3,2,1,0:T(8,128)(2,1)S(1)}, bf16[1,4,64,128]{3,2,1,0:T(8,128)(2,1)S(1)}, u32[]{:S(2)}, u32[]{:S(2)}) collective-permute-start(bf16[1,4,64,128]{3,2,1,0:T(8,128)(2,1)S(1)} %get-tuple-element.184), channel_id=1, source_target_pairs={{0,4},{1,5},{2,6},{3,7},{4,0},{5,1},{6,2},{7,3},{8,12},{9,13},{10,... | collective-permute-start | bytes 196616 | tf_op jit(solution)/shard_map/ppermute | solution.py:750
  108.5 2.3 %mixing_grad.2.part = bf16[1536,512]{1,0:T(8,128)(2,1)S(1)} custom-call(bf16[2,12,64,1024]{3,2,1,0:T(8,128)(2,1)S(1)} %get-tuple-element.147.maps0, bf16[2,12,64,1024]{3,2,1,0:T(8,128)(2,1)S(1)} %get-tuple-element.148.maps1, bf16[3,64,1024]{2,1,0:T(8,128)(2,1)S(1)} %get-tuple-element.149.lags, bf16[1024,512]{1,0:T(8,128)(2,1)S(1)} %collective-permute-done.24.grads, ...), custom_call_target="tpu_custom_call" | custom-call | tf_op jit(solution)/shard_map/mixing_grad/pallas_call | solution.py:615
  110.8 2.7 %mixing_grad.3.part = bf16[1728,512]{1,0:T(8,128)(2,1)S(1)} custom-call(bf16[2,12,64,1024]{3,2,1,0:T(8,128)(2,1)S(1)} %get-tuple-element.147.maps0, bf16[2,12,64,1024]{3,2,1,0:T(8,128)(2,1)S(1)} %get-tuple-element.148.maps1, bf16[3,64,1024]{2,1,0:T(8,128)(2,1)S(1)} %get-tuple-element.149.lags, bf16[1024,512]{1,0:T(8,128)(2,1)S(1)} %collective-permute-done.24.grads, ...), custom_call_target="tpu_custom_call" | custom-call | tf_op jit(solution)/shard_map/mixing_grad/pallas_call | solution.py:615
  113.5 3.9 %collective-permute-done.26 = bf16[784,256]{1,0:T(8,128)(2,1)S(1)} collective-permute-done((bf16[784,256]{1,0:T(8,128)(2,1)S(1)}, bf16[784,256]{1,0:T(8,128)(2,1)S(1)}, u32[]{:S(2)}, u32[]{:S(2)}) %collective-permute-start.26) | collective-permute-done | bytes 401440 | tf_op jit(solution)/shard_map/ppermute | solution.py:750
  117.5 0.6 collective-permute-start.29
  118.1 0.9 first_norm_back.1
  119.0 2.1 %finish_mixing.2.refs_0_ = f32[51,64,512]{2,1,0:T(8,128)} custom-call(bf16[1536,512]{1,0:T(8,128)(2,1)S(1)} %mixing_grad.2.part, bf16[1536,512]{1,0:T(8,128)(2,1)S(1)} %collective-permute-done.28.got), custom_call_target="tpu_custom_call" | custom-call | tf_op jit(solution)/shard_map/finish_mixing/pallas_call | solution.py:638
  121.2 0.5 collective-permute-done.29.other
  121.7 1.2 finish_units.1
  122.9 0.5 slice_bitcast_fusion.2
  123.4 2.3 %finish_mixing.3 = f32[51,64,512]{2,1,0:T(8,128)} custom-call(bf16[1728,512]{1,0:T(8,128)(2,1)S(1)} %mixing_grad.3.part, bf16[1728,512]{1,0:T(8,128)(2,1)S(1)} %collective-permute-done.27.got, f32[51,64,512]{2,1,0:T(8,128)} %finish_mixing.2.refs_0_), custom_call_target="tpu_custom_call", output_to_operand_aliasing={{}: (2, {})} | custom-call | tf_op jit(solution)/shard_map/finish_mixing/pallas_call | solution.py:638
  (80 shorter events, 2.1 us)
Async XLA Ops:
  0.6 27.0 %copy-start.5 = (bf16[1,128,512]{2,1,0:T(8,128)(2,1)S(1)}, bf16[1,128,512]{2,1,0:T(8,128)(2,1)}, u32[]{:S(2)}) copy-start(bf16[1,128,512]{2,1,0:T(8,128)(2,1)} %cotangent.1) | copy-start | bytes 393220
  27.3 9.5 %collective-permute-start.1 = (bf16[2,2,256,128]{3,2,0,1:T(8,128)(2,1)S(1)}, bf16[2,2,256,128]{3,2,0,1:T(8,128)(2,1)S(1)}, u32[]{:S(2)}, u32[]{:S(2)}) collective-permute-start(bf16[2,2,256,128]{3,2,0,1:T(8,128)(2,1)S(1)} %copy.22), channel_id=1, source_target_pairs={{0,2},{1,3},{2,0},{3,1},{4,6},{5,7},{6,4},{7,5},{8,10},{9,11},{10,... | collective-permute-start | bytes 786440 | tf_op jit(solution)/shard_map/ppermute | solution.py:750
  27.6 7.1 %collective-permute-start.2 = (bf16[1,128,512]{2,1,0:T(8,128)(2,1)S(1)}, bf16[1,128,512]{2,1,0:T(8,128)(2,1)S(1)}, u32[]{:S(2)}, u32[]{:S(2)}) collective-permute-start(bf16[1,128,512]{2,1,0:T(8,128)(2,1)S(1)} %copy-done.5), channel_id=1, source_target_pairs={{0,4},{1,5},{2,6},{3,7},{4,0},{5,1},{6,2},{7,3},{8,12},{9,13},{10,... | collective-permute-start | bytes 393224 | tf_op jit(solution)/shard_map/ppermute | solution.py:750
  28.8 19.6 %copy-start.6 = (bf16[24,1024]{1,0:T(8,128)(2,1)S(1)}, bf16[24,1024]{1,0:T(8,128)(2,1)}, u32[]{:S(2)}) copy-start(bf16[24,1024]{1,0:T(8,128)(2,1)} %filters.9) | copy-start | bytes 147460
  28.8 8.1 %collective-permute-start = (bf16[2,2,256,128]{3,2,0,1:T(8,128)(2,1)S(1)}, bf16[2,2,256,128]{3,2,0,1:T(8,128)(2,1)S(1)}, u32[]{:S(2)}, u32[]{:S(2)}) collective-permute-start(bf16[2,2,256,128]{3,2,0,1:T(8,128)(2,1)S(1)} %copy.20), channel_id=1, source_target_pairs={{0,1},{1,0},{2,3},{3,2},{4,5},{5,4},{6,7},{7,6},{8,9},{9,8},{10,11... | collective-permute-start | bytes 786440 | tf_op jit(solution)/shard_map/ppermute | solution.py:750
  34.7 11.4 %collective-permute-start.5 = (bf16[8,80,128]{2,1,0:T(8,128)(2,1)S(1)}, bf16[8,80,128]{2,1,0:T(8,128)(2,1)S(1)}, u32[]{:S(2)}, u32[]{:S(2)}) collective-permute-start(bf16[8,80,128]{2,1,0:T(8,128)(2,1)S(1)} %all_to_all.5.pieces), channel_id=1, source_target_pairs={{0,16},{8,24},{16,0},{24,8},{1,17},{9,25},{17,1},{25,9},{2,18},{10... | collective-permute-start | bytes 491528 | tf_op jit(solution)/shard_map/ppermute | solution.py:750
  37.0 6.0 %collective-permute-start.3 = (bf16[2,1,256,128]{3,2,0,1:T(8,128)(2,1)S(1)}, bf16[2,1,256,128]{3,2,0,1:T(8,128)(2,1)S(1)}, u32[]{:S(2)}, u32[]{:S(2)}) collective-permute-start(bf16[2,1,256,128]{3,2,0,1:T(8,128)(2,1)S(1)} %constant_dynamic-slice_fusion.2), channel_id=1, source_target_pairs={{0,2},{1,3},{2,0},{3,1},{4,6},{5,7},{6,4},{7,5},{8,10},{9,11},{10,... | collective-permute-start | bytes 393224 | tf_op jit(solution)/shard_map/ppermute | solution.py:750
  39.3 6.7 %collective-permute-start.7 = (bf16[2,64,512]{2,1,0:T(8,128)(2,1)S(1)}, bf16[2,64,512]{2,1,0:T(8,128)(2,1)S(1)}, u32[]{:S(2)}, u32[]{:S(2)}) collective-permute-start(bf16[2,64,512]{2,1,0:T(8,128)(2,1)S(1)} %get-tuple-element.180), channel_id=1, source_target_pairs={{0,1},{1,0},{2,3},{3,2},{4,5},{5,4},{6,7},{7,6},{8,9},{9,8},{10,11... | collective-permute-start | bytes 393224 | tf_op jit(solution)/shard_map/ppermute | solution.py:750
  40.8 5.2 %collective-permute-start.6 = (bf16[2,64,512]{2,1,0:T(8,128)(2,1)S(1)}, bf16[2,64,512]{2,1,0:T(8,128)(2,1)S(1)}, u32[]{:S(2)}, u32[]{:S(2)}) collective-permute-start(bf16[2,64,512]{2,1,0:T(8,128)(2,1)S(1)} %get-tuple-element.183), channel_id=1, source_target_pairs={{0,2},{1,3},{2,0},{3,1},{4,6},{5,7},{6,4},{7,5},{8,10},{9,11},{10,... | collective-permute-start | bytes 393224 | tf_op jit(solution)/shard_map/ppermute | solution.py:750
  40.9 5.0 %collective-permute-start.4 = (bf16[2,1,256,128]{3,2,0,1:T(8,128)(2,1)S(1)}, bf16[2,1,256,128]{3,2,0,1:T(8,128)(2,1)S(1)}, u32[]{:S(2)}, u32[]{:S(2)}) collective-permute-start(bf16[2,1,256,128]{3,2,0,1:T(8,128)(2,1)S(1)} %constant_dynamic-slice_fusion.1), channel_id=1, source_target_pairs={{0,1},{1,0},{2,3},{3,2},{4,5},{5,4},{6,7},{7,6},{8,9},{9,8},{10,11... | collective-permute-start | bytes 393224 | tf_op jit(solution)/shard_map/ppermute | solution.py:750
  46.1 6.6 %copy-start.1 = (bf16[512,2048]{1,0:T(8,128)(2,1)S(1)}, bf16[512,2048]{1,0:T(8,128)(2,1)}, u32[]{:S(2)}) copy-start(bf16[512,2048]{1,0:T(8,128)(2,1)} %refs_8_.1) | copy-start | bytes 6291460
  46.1 6.6 %copy-start.2 = (bf16[512,2048]{1,0:T(8,128)(2,1)S(1)}, bf16[512,2048]{1,0:T(8,128)(2,1)}, u32[]{:S(2)}) copy-start(bf16[512,2048]{1,0:T(8,128)(2,1)} %refs_9_.1) | copy-start | bytes 6291460
  46.1 6.6 %copy-start.3 = (bf16[2048,512]{1,0:T(8,128)(2,1)S(1)}, bf16[2048,512]{1,0:T(8,128)(2,1)}, u32[]{:S(2)}) copy-start(bf16[2048,512]{1,0:T(8,128)(2,1)} %refs_10_.1) | copy-start | bytes 6291460
  46.1 6.6 %copy-start.4 = (bf16[1,128,512]{2,1,0:T(8,128)(2,1)S(1)}, bf16[1,128,512]{2,1,0:T(8,128)(2,1)}, u32[]{:S(2)}) copy-start(bf16[1,128,512]{2,1,0:T(8,128)(2,1)} %hidden.1) | copy-start | bytes 393220
  46.1 6.6 %copy-start.8 = (f32[512]{0:T(512)S(1)}, f32[512]{0:T(512)}, u32[]{:S(2)}) copy-start(f32[512]{0:T(512)} %param.15) | copy-start | bytes 6148
  46.1 6.5 %collective-permute-start.8 = (bf16[1,512,128]{2,1,0:T(8,128)(2,1)S(1)}, bf16[1,512,128]{2,1,0:T(8,128)(2,1)S(1)}, u32[]{:S(2)}, u32[]{:S(2)}) collective-permute-start(bf16[1,512,128]{2,1,0:T(8,128)(2,1)S(1)} %constant_dynamic-slice_fusion), channel_id=1, source_target_pairs={{0,4},{1,5},{2,6},{3,7},{4,0},{5,1},{6,2},{7,3},{8,12},{9,13},{10,... | collective-permute-start | bytes 393224 | tf_op jit(solution)/shard_map/ppermute | solution.py:750
  51.3 11.8 %collective-permute-start.10 = (bf16[2,2,64,512]{3,2,1,0:T(8,128)(2,1)S(1)}, bf16[2,2,64,512]{3,2,1,0:T(8,128)(2,1)S(1)}, u32[]{:S(2)}, u32[]{:S(2)}) collective-permute-start(bf16[2,2,64,512]{3,2,1,0:T(8,128)(2,1)S(1)} %maximum_select_fusion.3.refs_4_), channel_id=1, source_target_pairs={{0,1},{1,0},{2,3},{3,2},{4,5},{5,4},{6,7},{7,6},{8,9},{9,8},{10,11... | collective-permute-start | bytes 786440 | tf_op jit(solution)/shard_map/ppermute | solution.py:750
  52.3 10.8 %collective-permute-start.11 = (bf16[2,2,64,512]{3,2,1,0:T(8,128)(2,1)S(1)}, bf16[2,2,64,512]{3,2,1,0:T(8,128)(2,1)S(1)}, u32[]{:S(2)}, u32[]{:S(2)}) collective-permute-start(bf16[2,2,64,512]{3,2,1,0:T(8,128)(2,1)S(1)} %maximum_select_fusion.4.refs_6_), channel_id=1, source_target_pairs={{0,2},{1,3},{2,0},{3,1},{4,6},{5,7},{6,4},{7,5},{8,10},{9,11},{10,... | collective-permute-start | bytes 786440 | tf_op jit(solution)/shard_map/ppermute | solution.py:750
  56.5 6.5 %collective-permute-start.9 = (bf16[1,128,512]{2,1,0:T(8,128)(2,1)S(1)}, bf16[1,128,512]{2,1,0:T(8,128)(2,1)S(1)}, u32[]{:S(2)}, u32[]{:S(2)}) collective-permute-start(bf16[1,128,512]{2,1,0:T(8,128)(2,1)S(1)} %bitcast.56), channel_id=1, source_target_pairs={{0,4},{1,5},{2,6},{3,7},{4,0},{5,1},{6,2},{7,3},{8,12},{9,13},{10,... | collective-permute-start | bytes 393224 | tf_op jit(solution)/shard_map/ppermute | solution.py:750
  63.0 21.6 %copy-start = (bf16[51,64,512]{2,1,0:T(8,128)(2,1)S(1)}, bf16[51,64,512]{2,1,0:T(8,128)(2,1)}, u32[]{:S(2)}) copy-start(bf16[51,64,512]{2,1,0:T(8,128)(2,1)} %mixing.5) | copy-start | bytes 10027012
  63.1 6.9 %collective-permute-start.13 = (bf16[2,64,512]{2,1,0:T(8,128)(2,1)S(1)}, bf16[2,64,512]{2,1,0:T(8,128)(2,1)S(1)}, u32[]{:S(2)}, u32[]{:S(2)}) collective-permute-start(bf16[2,64,512]{2,1,0:T(8,128)(2,1)S(1)} %get-tuple-element.176), channel_id=1, source_target_pairs={{0,1},{1,0},{2,3},{3,2},{4,5},{5,4},{6,7},{7,6},{8,9},{9,8},{10,11... | collective-permute-start | bytes 393224 | tf_op jit(solution)/shard_map/ppermute | solution.py:750
  66.2 6.9 %collective-permute-start.12 = (bf16[2,64,512]{2,1,0:T(8,128)(2,1)S(1)}, bf16[2,64,512]{2,1,0:T(8,128)(2,1)S(1)}, u32[]{:S(2)}, u32[]{:S(2)}) collective-permute-start(bf16[2,64,512]{2,1,0:T(8,128)(2,1)S(1)} %get-tuple-element.179), channel_id=1, source_target_pairs={{0,2},{1,3},{2,0},{3,1},{4,6},{5,7},{6,4},{7,5},{8,10},{9,11},{10,... | collective-permute-start | bytes 393224 | tf_op jit(solution)/shard_map/ppermute | solution.py:750
  73.1 6.8 %collective-permute-start.16 = (bf16[1,144,512]{2,1,0:T(8,128)(2,1)S(1)}, bf16[1,144,512]{2,1,0:T(8,128)(2,1)S(1)}, u32[]{:S(2)}, u32[]{:S(2)}) collective-permute-start(bf16[1,144,512]{2,1,0:T(8,128)(2,1)S(1)} %bitcast.54), channel_id=1, source_target_pairs={{0,4},{1,5},{2,6},{3,7},{4,0},{5,1},{6,2},{7,3},{8,12},{9,13},{10,... | collective-permute-start | bytes 442376 | tf_op jit(solution)/shard_map/ppermute | solution.py:750
  73.2 8.5 %collective-permute-start.14 = (bf16[2,2,64,512]{3,2,1,0:T(8,128)(2,1)S(1)}, bf16[2,2,64,512]{3,2,1,0:T(8,128)(2,1)S(1)}, u32[]{:S(2)}, u32[]{:S(2)}) collective-permute-start(bf16[2,2,64,512]{3,2,1,0:T(8,128)(2,1)S(1)} %maximum_select_fusion.6.refs_0_), channel_id=1, source_target_pairs={{0,1},{1,0},{2,3},{3,2},{4,5},{5,4},{6,7},{7,6},{8,9},{9,8},{10,11... | collective-permute-start | bytes 786440 | tf_op jit(solution)/shard_map/ppermute | solution.py:750
  75.0 9.6 %collective-permute-start.15 = (bf16[2,2,64,512]{3,2,1,0:T(8,128)(2,1)S(1)}, bf16[2,2,64,512]{3,2,1,0:T(8,128)(2,1)S(1)}, u32[]{:S(2)}, u32[]{:S(2)}) collective-permute-start(bf16[2,2,64,512]{3,2,1,0:T(8,128)(2,1)S(1)} %maximum_select_fusion.7.refs_2_), channel_id=1, source_target_pairs={{0,2},{1,3},{2,0},{3,1},{4,6},{5,7},{6,4},{7,5},{8,10},{9,11},{10,... | collective-permute-start | bytes 786440 | tf_op jit(solution)/shard_map/ppermute | solution.py:750
  79.9 8.8 %collective-permute-start.17 = (bf16[2,64,512]{2,1,0:T(8,128)(2,1)S(1)}, bf16[2,64,512]{2,1,0:T(8,128)(2,1)S(1)}, u32[]{:S(2)}, u32[]{:S(2)}) collective-permute-start(bf16[2,64,512]{2,1,0:T(8,128)(2,1)S(1)} %get-tuple-element.174), channel_id=1, source_target_pairs={{0,2},{1,3},{2,0},{3,1},{4,6},{5,7},{6,4},{7,5},{8,10},{9,11},{10,... | collective-permute-start | bytes 393224 | tf_op jit(solution)/shard_map/ppermute | solution.py:750
  80.1 8.7 %collective-permute-start.18 = (bf16[2,80,512]{2,1,0:T(8,128)(2,1)S(1)}, bf16[2,80,512]{2,1,0:T(8,128)(2,1)S(1)}, u32[]{:S(2)}, u32[]{:S(2)}) collective-permute-start(bf16[2,80,512]{2,1,0:T(8,128)(2,1)S(1)} %get-tuple-element.172), channel_id=1, source_target_pairs={{0,1},{1,0},{2,3},{3,2},{4,5},{5,4},{6,7},{7,6},{8,9},{9,8},{10,11... | collective-permute-start | bytes 491528 | tf_op jit(solution)/shard_map/ppermute | solution.py:750
  88.8 6.8 %copy-start.7 = (f32[512]{0:T(512)S(1)}, f32[512]{0:T(512)}, u32[]{:S(2)}) copy-start(f32[512]{0:T(512)} %param.13) | copy-start | bytes 6148
  88.8 8.7 %collective-permute-start.20 = (bf16[2,2,80,512]{3,2,1,0:T(8,128)(2,1)S(1)}, bf16[2,2,80,512]{3,2,1,0:T(8,128)(2,1)S(1)}, u32[]{:S(2)}, u32[]{:S(2)}) collective-permute-start(bf16[2,2,80,512]{3,2,1,0:T(8,128)(2,1)S(1)} %maximum_select_fusion.refs_2_), channel_id=1, source_target_pairs={{0,2},{1,3},{2,0},{3,1},{4,6},{5,7},{6,4},{7,5},{8,10},{9,11},{10,... | collective-permute-start | bytes 983048 | tf_op jit(solution)/shard_map/ppermute | solution.py:750
  88.9 16.8 %collective-permute-start.24 = (bf16[1024,512]{1,0:T(8,128)(2,1)S(1)}, bf16[1024,512]{1,0:T(8,128)(2,1)S(1)}, u32[]{:S(2)}, u32[]{:S(2)}) collective-permute-start(bf16[1024,512]{1,0:T(8,128)(2,1)S(1)} %place.1.grads), channel_id=1, source_target_pairs={{0,16},{8,24},{16,0},{24,8},{1,17},{9,25},{17,1},{25,9},{2,18},{10... | collective-permute-start | bytes 3145736 | tf_op jit(solution)/shard_map/ppermute | solution.py:750
  90.8 6.7 %collective-permute-start.19 = (bf16[2,2,64,512]{3,2,1,0:T(8,128)(2,1)S(1)}, bf16[2,2,64,512]{3,2,1,0:T(8,128)(2,1)S(1)}, u32[]{:S(2)}, u32[]{:S(2)}) collective-permute-start(bf16[2,2,64,512]{3,2,1,0:T(8,128)(2,1)S(1)} %maximum_select_fusion.8.refs_0_), channel_id=1, source_target_pairs={{0,1},{1,0},{2,3},{3,2},{4,5},{5,4},{6,7},{7,6},{8,9},{9,8},{10,11... | collective-permute-start | bytes 786440 | tf_op jit(solution)/shard_map/ppermute | solution.py:750
  96.4 4.3 %collective-permute-start.21 = (bf16[4,64,128]{2,1,0:T(8,128)(2,1)S(1)}, bf16[4,64,128]{2,1,0:T(8,128)(2,1)S(1)}, u32[]{:S(2)}, u32[]{:S(2)}) collective-permute-start(bf16[4,64,128]{2,1,0:T(8,128)(2,1)S(1)} %get-tuple-element.144), channel_id=1, source_target_pairs={{0,1},{1,0},{2,3},{3,2},{4,5},{5,4},{6,7},{7,6},{8,9},{9,8},{10,11... | collective-permute-start | bytes 196616 | tf_op jit(solution)/shard_map/ppermute | solution.py:750
  100.8 4.7 %collective-permute-start.23 = (bf16[784,256]{1,0:T(8,128)(2,1)S(1)}, bf16[784,256]{1,0:T(8,128)(2,1)S(1)}, u32[]{:S(2)}, u32[]{:S(2)}) collective-permute-start(bf16[784,256]{1,0:T(8,128)(2,1)S(1)} %dynamic-slice_bitcast_fusion), channel_id=1, source_target_pairs={{0,8},{8,0},{16,24},{24,16},{1,9},{9,1},{17,25},{25,17},{2,10},{10... | collective-permute-start | bytes 1204232 | tf_op jit(solution)/shard_map/ppermute | solution.py:750
  100.9 6.0 %collective-permute-start.22 = (bf16[2,2,64,128]{3,2,1,0:T(8,128)(2,1)S(1)}, bf16[2,2,64,128]{3,2,1,0:T(8,128)(2,1)S(1)}, u32[]{:S(2)}, u32[]{:S(2)}) collective-permute-start(bf16[2,2,64,128]{3,2,1,0:T(8,128)(2,1)S(1)} %bitcast.73), channel_id=1, source_target_pairs={{0,2},{1,3},{2,0},{3,1},{4,6},{5,7},{6,4},{7,5},{8,10},{9,11},{10,... | collective-permute-start | bytes 196616 | tf_op jit(solution)/shard_map/ppermute | solution.py:750
  105.7 11.7 %collective-permute-start.26 = (bf16[784,256]{1,0:T(8,128)(2,1)S(1)}, bf16[784,256]{1,0:T(8,128)(2,1)S(1)}, u32[]{:S(2)}, u32[]{:S(2)}) collective-permute-start(bf16[784,256]{1,0:T(8,128)(2,1)S(1)} %fusion), channel_id=1, source_target_pairs={{0,16},{8,24},{16,0},{24,8},{1,17},{9,25},{17,1},{25,9},{2,18},{10... | collective-permute-start | bytes 1204232 | tf_op jit(solution)/shard_map/ppermute | solution.py:750
  106.9 6.6 %collective-permute-start.25 = (bf16[1,4,64,128]{3,2,1,0:T(8,128)(2,1)S(1)}, bf16[1,4,64,128]{3,2,1,0:T(8,128)(2,1)S(1)}, u32[]{:S(2)}, u32[]{:S(2)}) collective-permute-start(bf16[1,4,64,128]{3,2,1,0:T(8,128)(2,1)S(1)} %get-tuple-element.184), channel_id=1, source_target_pairs={{0,4},{1,5},{2,6},{3,7},{4,0},{5,1},{6,2},{7,3},{8,12},{9,13},{10,... | collective-permute-start | bytes 196616 | tf_op jit(solution)/shard_map/ppermute | solution.py:750
  110.7 8.3 %collective-permute-start.28 = (bf16[1536,512]{1,0:T(8,128)(2,1)S(1)}, bf16[1536,512]{1,0:T(8,128)(2,1)S(1)}, u32[]{:S(2)}, u32[]{:S(2)}) collective-permute-start(bf16[1536,512]{1,0:T(8,128)(2,1)S(1)} %mixing_grad.2.part), channel_id=1, source_target_pairs={{0,8},{8,0},{16,24},{24,16},{1,9},{9,1},{17,25},{25,17},{2,10},{10... | collective-permute-start | bytes 4718600 | tf_op jit(solution)/shard_map/ppermute | solution.py:750
  117.4 6.0 %collective-permute-start.27 = (bf16[1728,512]{1,0:T(8,128)(2,1)S(1)}, bf16[1728,512]{1,0:T(8,128)(2,1)S(1)}, u32[]{:S(2)}, u32[]{:S(2)}) collective-permute-start(bf16[1728,512]{1,0:T(8,128)(2,1)S(1)} %mixing_grad.3.part), channel_id=1, source_target_pairs={{0,8},{8,0},{16,24},{24,16},{1,9},{9,1},{17,25},{25,17},{2,10},{10... | collective-permute-start | bytes 5308424 | tf_op jit(solution)/shard_map/ppermute | solution.py:750
  117.5 4.1 %collective-permute-start.29 = (bf16[784,256]{1,0:T(8,128)(2,1)S(1)}, bf16[784,256]{1,0:T(8,128)(2,1)S(1)}, u32[]{:S(2)}, u32[]{:S(2)}) collective-permute-start(bf16[784,256]{1,0:T(8,128)(2,1)S(1)} %add_convert_fusion.mine), channel_id=1, source_target_pairs={{0,8},{8,0},{16,24},{24,16},{1,9},{9,1},{17,25},{25,17},{2,10},{10... | collective-permute-start | bytes 1204232 | tf_op jit(solution)/shard_map/ppermute | solution.py:750

commit v6 on v5

--- a/solution.py
+++ b/solution.py
@@ -13,7 +13,7 @@
 TILE = 256
 HALF = 128
 PER_STEP = 12
-FEED_STEPS = 4
+FEED_STEPS = 2
 
 eps_norm = 1e-05
 
@@ -555,7 +555,7 @@
     )(bit, held, got, hidden_in, gain[None, :], cotangent, w_gate, w_up, w_down)
 
 
-CHUNK = 6
+CHUNK = 12
 
 
 def own_mixing_grad_kernel(maps, lags, grads, out, lag_out):

time: 126 us -> 126 us (level)
  Pallas kernels: 49.4 us -> 47.7 us
  transfers between devices with their start and end apart: 30 -> 30, of which waited for: 11 -> 12; matrix products, arithmetic and copies ran while one was open for 1% -> 1% of each run, Pallas kernels for 28% -> 27%
where the time goes in v6:
time: 126 us; the launch traced here: 125 us
  Pallas kernels  47.7 us (38%)
  waiting for transfers between devices  30.2 us (24%)
  starting transfers between devices  30 us (24%)
  blocking collectives  14.6 us (12%)
    ppermute x30, waiting for transfers between devices, swap(): return lax.ppermute(values, axis, [(i, i ^ mask) for i in range(count)])  30.2 us
    ppermute x30, starting transfers between devices, swap(): return lax.ppermute(values, axis, [(i, i ^ mask) for i in range(count)])  30 us
    all_to_all x1, blocking collectives, shards(): lax.all_to_all(first_norm(at, hidden_in, gain_one, segments, chans), 'cha...  14.6 us
    pallas_call x1, Pallas kernels, spectral_mixed(): pl.pallas_call(mixed_kernel, grid_spec=pltpu.PrefetchScalarGridSpec(num_s...  10.9 us
    pallas_call x2, Pallas kernels, spectral_back(): pl.pallas_call(functools.partial(spectral_back_kernel, start), in_specs=[...  7.83 us
    pallas_call x2, Pallas kernels, spectral_maps(): pl.pallas_call(functools.partial(maps_kernel, start), in_specs=[in_vmem()...  6.29 us
    pallas_call x2, Pallas kernels, finish_mixing(): pl.pallas_call(finish_mixing_kernel, grid=(steps,), in_specs=[in_vmem(),...  4.41 us
    pallas_call x1, Pallas kernels, own_mixing_grad(): pl.pallas_call(own_mixing_grad_kernel, in_specs=[in_vmem()] * 3, out_spec...  4.13 us
  transfers between devices with their start and end apart: 30, of which 12 were waited for; matrix products, arithmetic and copies ran while one was open for 1% of the time, Pallas kernels for 27%

profile of v6, /device:TPU:0, one launch (start us, length us, event | category | flops | bytes accessed | tf_op | source)
XLA Modules:
  0.0 125.3 jit_solution(11892914928405147720)
XLA Ops:
  0.7 1.1 first_norm.1
  1.8 14.6 %all_to_all.5.pieces = bf16[8,80,128]{2,1,0:T(8,128)(2,1)S(1)} all-to-all(bf16[8,80,128]{2,1,0:T(8,128)(2,1)S(1)} %first_norm.1), channel_id=1, replica_groups=mesh['rows'=4,'chan'=8] {'chan'}, dimensions={0} | all-to-all | bytes 327680 | tf_op jit(solution)/shard_map/all_to_all | solution.py:864
  16.4 10.9 %spectral_mixed.1 = (bf16[2,24,64,1024]{3,2,1,0:T(8,128)(2,1)S(1)}, bf16[3,64,1024]{2,1,0:T(8,128)(2,1)S(1)}, bf16[2,2,256,128]{3,2,1,0:T(8,128)(2,1)S(1)}, bf16...) custom-call(s32[1]{0:T(128)} %bitcast.me, ...), custom_call_target="tpu_custom_call" | custom-call | tf_op jit(solution)/shard_map/spectral_mixed/pallas_call | solution.py:426
  27.6 1.1 collective-permute-start.2
  28.8 1.4 %collective-permute-start = (bf16[2,2,256,128]{3,2,0,1:T(8,128)(2,1)S(1)}, bf16[2,2,256,128]{3,2,0,1:T(8,128)(2,1)S(1)}, u32[]{:S(2)}, u32[]{:S(2)}) collective-permute-start(bf16[2,2,256,128]{3,2,0,1:T(8,128)(2,1)S(1)} %copy.20), channel_id=1, source_target_pairs={{0,1},{1,0},{2,3},{3,2},{4,5},{5,4},{6,7},{7,6},{8,9},{9,8},{10,11... | collective-permute-start | bytes 786440 | tf_op jit(solution)/shard_map/ppermute | solution.py:750
  30.2 4.5 %collective-permute-done.2 = bf16[1,128,512]{2,1,0:T(8,128)(2,1)S(1)} collective-permute-done((bf16[1,128,512]{2,1,0:T(8,128)(2,1)S(1)}, bf16[1,128,512]{2,1,0:T(8,128)(2,1)S(1)}, u32[]{:S(2)}, u32[]{:S(2)}) %collective-permute-start.2) | collective-permute-done | bytes 131104 | tf_op jit(solution)/shard_map/ppermute | solution.py:750
  34.7 1.5 %collective-permute-start.5 = (bf16[8,80,128]{2,1,0:T(8,128)(2,1)S(1)}, bf16[8,80,128]{2,1,0:T(8,128)(2,1)S(1)}, u32[]{:S(2)}, u32[]{:S(2)}) collective-permute-start(bf16[8,80,128]{2,1,0:T(8,128)(2,1)S(1)} %all_to_all.5.pieces), channel_id=1, source_target_pairs={{0,16},{8,24},{16,0},{24,8},{1,17},{9,25},{17,1},{25,9},{2,18},{10... | collective-permute-start | bytes 491528 | tf_op jit(solution)/shard_map/ppermute | solution.py:750
  36.2 0.6 collective-permute-done.1
  37.0 2.2 %collective-permute-start.3 = (bf16[2,1,256,128]{3,2,0,1:T(8,128)(2,1)S(1)}, bf16[2,1,256,128]{3,2,0,1:T(8,128)(2,1)S(1)}, u32[]{:S(2)}, u32[]{:S(2)}) collective-permute-start(bf16[2,1,256,128]{3,2,0,1:T(8,128)(2,1)S(1)} %constant_dynamic-slice_fusion.2), channel_id=1, source_target_pairs={{0,2},{1,3},{2,0},{3,1},{4,6},{5,7},{6,4},{7,5},{8,10},{9,11},{10,... | collective-permute-start | bytes 393224 | tf_op jit(solution)/shard_map/ppermute | solution.py:750
  39.3 1.6 %collective-permute-start.7 = (bf16[2,64,512]{2,1,0:T(8,128)(2,1)S(1)}, bf16[2,64,512]{2,1,0:T(8,128)(2,1)S(1)}, u32[]{:S(2)}, u32[]{:S(2)}) collective-permute-start(bf16[2,64,512]{2,1,0:T(8,128)(2,1)S(1)} %get-tuple-element.180), channel_id=1, source_target_pairs={{0,1},{1,0},{2,3},{3,2},{4,5},{5,4},{6,7},{7,6},{8,9},{9,8},{10,11... | collective-permute-start | bytes 393224 | tf_op jit(solution)/shard_map/ppermute | solution.py:750
  40.9 0.6 collective-permute-start.4
  41.5 1.6 %collective-permute-done.3 = bf16[2,1,256,128]{3,2,0,1:T(8,128)(2,1)S(1)} collective-permute-done((bf16[2,1,256,128]{3,2,0,1:T(8,128)(2,1)S(1)}, bf16[2,1,256,128]{3,2,0,1:T(8,128)(2,1)S(1)}, u32[]{:S(2)}, u32[]{:S(2)}) %collective-permute-start.3) | collective-permute-done | bytes 131104 | tf_op jit(solution)/shard_map/ppermute | solution.py:750
  43.1 2.8 %collective-permute-done.4 = bf16[2,1,256,128]{3,2,0,1:T(8,128)(2,1)S(1)} collective-permute-done((bf16[2,1,256,128]{3,2,0,1:T(8,128)(2,1)S(1)}, bf16[2,1,256,128]{3,2,0,1:T(8,128)(2,1)S(1)}, u32[]{:S(2)}, u32[]{:S(2)}) %collective-permute-start.4) | collective-permute-done | bytes 131104 | tf_op jit(solution)/shard_map/ppermute | solution.py:750
  46.1 2.3 %collective-permute-start.8 = (bf16[1,512,128]{2,1,0:T(8,128)(2,1)S(1)}, bf16[1,512,128]{2,1,0:T(8,128)(2,1)S(1)}, u32[]{:S(2)}, u32[]{:S(2)}) collective-permute-start(bf16[1,512,128]{2,1,0:T(8,128)(2,1)S(1)} %constant_dynamic-slice_fusion), channel_id=1, source_target_pairs={{0,4},{1,5},{2,6},{3,7},{4,0},{5,1},{6,2},{7,3},{8,12},{9,13},{10,... | collective-permute-start | bytes 393224 | tf_op jit(solution)/shard_map/ppermute | solution.py:750
  48.5 2.8 %spectral_maps.2 = (bf16[2,12,64,1024]{3,2,1,0:T(8,128)(2,1)S(1)}, bf16[3,64,1024]{2,1,0:T(8,128)(2,1)S(1)}) custom-call(bf16[24,1024]{1,0:T(8,128)(2,1)S(1)} %copy-done.6, bf16[8,80,128]{2,1,0:T(8,128)(2,1)S(1)} %collective-permute-done.5.pieces), custom_call_target="tpu_custom_call" | custom-call | flops 4831838208 | bytes 4194304 | tf_op jit(solution)/shard_map/spectral_maps/pallas_call | solution.py:404
  51.3 1.0 collective-permute-start.10
  52.7 3.7 %feed_forward.1 = (bf16[1,128,512]{2,1,0:T(8,128)(2,1)}, bf16[144,512]{1,0:T(8,128)(2,1)S(1)}, f32[128,512]{1,0:T(8,128)S(1)}, bf16[128,512]{1,0:T(8,128)(2,1)S(1)}) custom-call(s32[1]{0:T(128)} %bitcast.1.bit, bf16[2,512,128]{2,1,0:T(8,128)(2,1)S(1)} %pad_maximum_fusion.held, bf16[512,128]{1,0:T(8,128)(2,1)S(1)} %bitcast.58, ...), custom_call_target="tpu_custom_call" | custom-call | tf_op jit(solution)/shard_map/feed_forward/pallas_call | solution.py:539
  56.4 3.1 %collective-permute-start.9 = (bf16[1,128,512]{2,1,0:T(8,128)(2,1)S(1)}, bf16[1,128,512]{2,1,0:T(8,128)(2,1)S(1)}, u32[]{:S(2)}, u32[]{:S(2)}) collective-permute-start(bf16[1,128,512]{2,1,0:T(8,128)(2,1)S(1)} %bitcast.56), channel_id=1, source_target_pairs={{0,4},{1,5},{2,6},{3,7},{4,0},{5,1},{6,2},{7,3},{8,12},{9,13},{10,... | collective-permute-start | bytes 393224 | tf_op jit(solution)/shard_map/ppermute | solution.py:750
  59.5 3.5 %spectral_maps.3 = (bf16[2,12,64,1024]{3,2,1,0:T(8,128)(2,1)S(1)}, bf16[3,64,1024]{2,1,0:T(8,128)(2,1)}) custom-call(bf16[24,1024]{1,0:T(8,128)(2,1)S(1)} %copy-done.6, bf16[8,80,128]{2,1,0:T(8,128)(2,1)S(1)} %collective-permute-done.5.pieces), custom_call_target="tpu_custom_call" | custom-call | flops 4831838208 | bytes 4194304 | tf_op jit(solution)/shard_map/spectral_maps/pallas_call | solution.py:404
  63.1 3.1 %collective-permute-start.13 = (bf16[2,64,512]{2,1,0:T(8,128)(2,1)S(1)}, bf16[2,64,512]{2,1,0:T(8,128)(2,1)S(1)}, u32[]{:S(2)}, u32[]{:S(2)}) collective-permute-start(bf16[2,64,512]{2,1,0:T(8,128)(2,1)S(1)} %get-tuple-element.176), channel_id=1, source_target_pairs={{0,1},{1,0},{2,3},{3,2},{4,5},{5,4},{6,7},{7,6},{8,9},{9,8},{10,11... | collective-permute-start | bytes 393224 | tf_op jit(solution)/shard_map/ppermute | solution.py:750
  66.2 3.8 %collective-permute-done.13 = bf16[2,64,512]{2,1,0:T(8,128)(2,1)S(1)} collective-permute-done((bf16[2,64,512]{2,1,0:T(8,128)(2,1)S(1)}, bf16[2,64,512]{2,1,0:T(8,128)(2,1)S(1)}, u32[]{:S(2)}, u32[]{:S(2)}) %collective-permute-start.13) | collective-permute-done | bytes 131104 | tf_op jit(solution)/shard_map/ppermute | solution.py:750
  70.0 3.1 %collective-permute-done.12 = bf16[2,64,512]{2,1,0:T(8,128)(2,1)S(1)} collective-permute-done((bf16[2,64,512]{2,1,0:T(8,128)(2,1)S(1)}, bf16[2,64,512]{2,1,0:T(8,128)(2,1)S(1)}, u32[]{:S(2)}, u32[]{:S(2)}) %collective-permute-start.12) | collective-permute-done | bytes 131104 | tf_op jit(solution)/shard_map/ppermute | solution.py:750
  73.2 1.8 %collective-permute-start.14 = (bf16[2,2,64,512]{3,2,1,0:T(8,128)(2,1)S(1)}, bf16[2,2,64,512]{3,2,1,0:T(8,128)(2,1)S(1)}, u32[]{:S(2)}, u32[]{:S(2)}) collective-permute-start(bf16[2,2,64,512]{3,2,1,0:T(8,128)(2,1)S(1)} %maximum_select_fusion.6.refs_0_), channel_id=1, source_target_pairs={{0,1},{1,0},{2,3},{3,2},{4,5},{5,4},{6,7},{7,6},{8,9},{9,8},{10,11... | collective-permute-start | bytes 786440 | tf_op jit(solution)/shard_map/ppermute | solution.py:750
  75.0 4.9 %collective-permute-done.16 = bf16[1,144,512]{2,1,0:T(8,128)(2,1)S(1)} collective-permute-done((bf16[1,144,512]{2,1,0:T(8,128)(2,1)S(1)}, bf16[1,144,512]{2,1,0:T(8,128)(2,1)S(1)}, u32[]{:S(2)}, u32[]{:S(2)}) %collective-permute-start.16) | collective-permute-done | bytes 147488 | tf_op jit(solution)/shard_map/ppermute | solution.py:750
  80.1 1.6 %collective-permute-start.18 = (bf16[2,80,512]{2,1,0:T(8,128)(2,1)S(1)}, bf16[2,80,512]{2,1,0:T(8,128)(2,1)S(1)}, u32[]{:S(2)}, u32[]{:S(2)}) collective-permute-start(bf16[2,80,512]{2,1,0:T(8,128)(2,1)S(1)} %get-tuple-element.172), channel_id=1, source_target_pairs={{0,1},{1,0},{2,3},{3,2},{4,5},{5,4},{6,7},{7,6},{8,9},{9,8},{10,11... | collective-permute-start | bytes 491528 | tf_op jit(solution)/shard_map/ppermute | solution.py:750
  81.7 2.8 %collective-permute-done.15.refs_3_ = bf16[2,2,64,512]{3,2,1,0:T(8,128)(2,1)S(1)} collective-permute-done((bf16[2,2,64,512]{3,2,1,0:T(8,128)(2,1)S(1)}, bf16[2,2,64,512]{3,2,1,0:T(8,128)(2,1)S(1)}, u32[]{:S(2)}, u32[]{:S(2)}) %collective-permute-start.15) | collective-permute-done | bytes 262176 | tf_op jit(solution)/shard_map/ppermute | solution.py:750
  84.6 4.0 %spectral_back.2.refs_0_ = f32[128,1024]{1,0:T(8,128)S(1)} custom-call(bf16[24,1024]{1,0:T(8,128)(2,1)S(1)} %copy-done.6, bf16[51,64,512]{2,1,0:T(8,128)(2,1)S(1)} %copy-done, bf16[8,80,128]{2,1,0:T(8,128)(2,1)S(1)} %all_to_all.5.pieces, bf16[1024,512]{1,0:T(8,128)(2,1)S(1)} %place.1.grads), custom_call_target="tpu_custom_call" | custom-call | tf_op jit(solution)/shard_map/spectral_back/pallas_call | solution.py:457
  88.9 1.9 %collective-permute-start.24 = (bf16[1024,512]{1,0:T(8,128)(2,1)S(1)}, bf16[1024,512]{1,0:T(8,128)(2,1)S(1)}, u32[]{:S(2)}, u32[]{:S(2)}) collective-permute-start(bf16[1024,512]{1,0:T(8,128)(2,1)S(1)} %place.1.grads), channel_id=1, source_target_pairs={{0,16},{8,24},{16,0},{24,8},{1,17},{9,25},{17,1},{25,9},{2,18},{10... | collective-permute-start | bytes 3145736 | tf_op jit(solution)/shard_map/ppermute | solution.py:750
  90.7 1.0 collective-permute-start.19
  91.7 3.8 %spectral_back.3.acc = f32[128,1024]{1,0:T(8,128)S(1)} custom-call(bf16[24,1024]{1,0:T(8,128)(2,1)S(1)} %copy-done.6, bf16[51,64,512]{2,1,0:T(8,128)(2,1)S(1)} %copy-done, bf16[8,80,128]{2,1,0:T(8,128)(2,1)S(1)} %all_to_all.5.pieces, bf16[1024,512]{1,0:T(8,128)(2,1)S(1)} %place.1.grads, f32[128,1024]{1,0:T(8,128)S(1)} %spectral_back.2.refs_0_), custom_call_target="tpu_custom_call" | custom-call | tf_op jit(solution)/shard_map/spectral_back/pallas_call | solution.py:457
  95.5 0.8 lag_back.1
  96.3 1.1 collective-permute-start.21
  97.5 2.5 %unit_grads.1 = bf16[2,784,256]{2,1,0:T(8,128)(2,1)S(1)} custom-call(s32[1]{0:T(128)} %bitcast.me, bf16[2,2,64,512]{3,2,1,0:T(8,128)(2,1)S(1)} %maximum_select_fusion.8.refs_0_, bf16[2,2,64,512]{3,2,1,0:T(8,128)(2,1)S(1)} %collective-permute-done.19.refs_1_, bf16[2,2,80,512]{3,2,1,0:T(8,128)(2,1)S(1)} %maximum_select_fusion.refs_2_, ...), custom_call_target="tpu_custom_call" | custom-call | tf_op jit(solution)/shard_map/unit_grads/pallas_call | solution.py:697
  100.0 0.7 collective-permute-done.21
  100.9 4.1 %own_mixing_grad.1 = (bf16[2,24,64,512]{3,2,1,0:T(8,128)(2,1)S(1)}, bf16[3,64,512]{2,1,0:T(8,128)(2,1)S(1)}) custom-call(bf16[2,24,64,1024]{3,2,1,0:T(8,128)(2,1)S(1)} %get-tuple-element.150.maps, bf16[3,64,1024]{2,1,0:T(8,128)(2,1)S(1)} %get-tuple-element.132.inputs.lags, bf16[1024,512]{1,0:T(8,128)(2,1)S(1)} %place.1.grads), custom_call_target="tpu_custom_call" | custom-call | tf_op jit(solution)/shard_map/own_mixing_grad/pallas_call | solution.py:577
  105.2 1.3 %collective-permute-start.26 = (bf16[784,256]{1,0:T(8,128)(2,1)S(1)}, bf16[784,256]{1,0:T(8,128)(2,1)S(1)}, u32[]{:S(2)}, u32[]{:S(2)}) collective-permute-start(bf16[784,256]{1,0:T(8,128)(2,1)S(1)} %fusion), channel_id=1, source_target_pairs={{0,16},{8,24},{16,0},{24,8},{1,17},{9,25},{17,1},{25,9},{2,18},{10... | collective-permute-start | bytes 1204232 | tf_op jit(solution)/shard_map/ppermute | solution.py:750
  106.6 1.6 %collective-permute-start.25 = (bf16[1,4,64,128]{3,2,1,0:T(8,128)(2,1)S(1)}, bf16[1,4,64,128]{3,2,1,0:T(8,128)(2,1)S(1)}, u32[]{:S(2)}, u32[]{:S(2)}) collective-permute-start(bf16[1,4,64,128]{3,2,1,0:T(8,128)(2,1)S(1)} %get-tuple-element.184), channel_id=1, source_target_pairs={{0,4},{1,5},{2,6},{3,7},{4,0},{5,1},{6,2},{7,3},{8,12},{9,13},{10,... | collective-permute-start | bytes 196616 | tf_op jit(solution)/shard_map/ppermute | solution.py:750
  108.2 1.8 %mixing_grad.2.part = bf16[1536,512]{1,0:T(8,128)(2,1)S(1)} custom-call(bf16[2,12,64,1024]{3,2,1,0:T(8,128)(2,1)S(1)} %get-tuple-element.147.maps0, bf16[2,12,64,1024]{3,2,1,0:T(8,128)(2,1)S(1)} %get-tuple-element.148.maps1, bf16[3,64,1024]{2,1,0:T(8,128)(2,1)S(1)} %get-tuple-element.149.lags, bf16[1024,512]{1,0:T(8,128)(2,1)S(1)} %collective-permute-done.24.grads, ...), custom_call_target="tpu_custom_call" | custom-call | tf_op jit(solution)/shard_map/mixing_grad/pallas_call | solution.py:615
  110.0 2.0 %mixing_grad.3.part = bf16[1728,512]{1,0:T(8,128)(2,1)S(1)} custom-call(bf16[2,12,64,1024]{3,2,1,0:T(8,128)(2,1)S(1)} %get-tuple-element.147.maps0, bf16[2,12,64,1024]{3,2,1,0:T(8,128)(2,1)S(1)} %get-tuple-element.148.maps1, bf16[3,64,1024]{2,1,0:T(8,128)(2,1)S(1)} %get-tuple-element.149.lags, bf16[1024,512]{1,0:T(8,128)(2,1)S(1)} %collective-permute-done.24.grads, ...), custom_call_target="tpu_custom_call" | custom-call | tf_op jit(solution)/shard_map/mixing_grad/pallas_call | solution.py:615
  112.1 0.8 collective-permute-done.25
  112.8 4.1 %collective-permute-done.26 = bf16[784,256]{1,0:T(8,128)(2,1)S(1)} collective-permute-done((bf16[784,256]{1,0:T(8,128)(2,1)S(1)}, bf16[784,256]{1,0:T(8,128)(2,1)S(1)}, u32[]{:S(2)}, u32[]{:S(2)}) %collective-permute-start.26) | collective-permute-done | bytes 401440 | tf_op jit(solution)/shard_map/ppermute | solution.py:750
  117.1 0.6 collective-permute-start.29
  117.7 0.9 first_norm_back.1
  118.6 2.1 %finish_mixing.2.refs_0_ = f32[51,64,512]{2,1,0:T(8,128)} custom-call(bf16[1536,512]{1,0:T(8,128)(2,1)S(1)} %mixing_grad.2.part, bf16[1536,512]{1,0:T(8,128)(2,1)S(1)} %collective-permute-done.28.got), custom_call_target="tpu_custom_call" | custom-call | tf_op jit(solution)/shard_map/finish_mixing/pallas_call | solution.py:638
  120.8 0.5 collective-permute-done.29.other
  121.3 1.2 finish_units.1
  122.5 0.5 slice_bitcast_fusion.2
  123.0 2.3 %finish_mixing.3 = f32[51,64,512]{2,1,0:T(8,128)} custom-call(bf16[1728,512]{1,0:T(8,128)(2,1)S(1)} %mixing_grad.3.part, bf16[1728,512]{1,0:T(8,128)(2,1)S(1)} %collective-permute-done.27.got, f32[51,64,512]{2,1,0:T(8,128)} %finish_mixing.2.refs_0_), custom_call_target="tpu_custom_call", output_to_operand_aliasing={{}: (2, {})} | custom-call | tf_op jit(solution)/shard_map/finish_mixing/pallas_call | solution.py:638
  (80 shorter events, 2.5 us)
Async XLA Ops:
  0.6 27.0 %copy-start.5 = (bf16[1,128,512]{2,1,0:T(8,128)(2,1)S(1)}, bf16[1,128,512]{2,1,0:T(8,128)(2,1)}, u32[]{:S(2)}) copy-start(bf16[1,128,512]{2,1,0:T(8,128)(2,1)} %cotangent.1) | copy-start | bytes 393220
  27.3 9.5 %collective-permute-start.1 = (bf16[2,2,256,128]{3,2,0,1:T(8,128)(2,1)S(1)}, bf16[2,2,256,128]{3,2,0,1:T(8,128)(2,1)S(1)}, u32[]{:S(2)}, u32[]{:S(2)}) collective-permute-start(bf16[2,2,256,128]{3,2,0,1:T(8,128)(2,1)S(1)} %copy.22), channel_id=1, source_target_pairs={{0,2},{1,3},{2,0},{3,1},{4,6},{5,7},{6,4},{7,5},{8,10},{9,11},{10,... | collective-permute-start | bytes 786440 | tf_op jit(solution)/shard_map/ppermute | solution.py:750
  27.6 7.1 %collective-permute-start.2 = (bf16[1,128,512]{2,1,0:T(8,128)(2,1)S(1)}, bf16[1,128,512]{2,1,0:T(8,128)(2,1)S(1)}, u32[]{:S(2)}, u32[]{:S(2)}) collective-permute-start(bf16[1,128,512]{2,1,0:T(8,128)(2,1)S(1)} %copy-done.5), channel_id=1, source_target_pairs={{0,4},{1,5},{2,6},{3,7},{4,0},{5,1},{6,2},{7,3},{8,12},{9,13},{10,... | collective-permute-start | bytes 393224 | tf_op jit(solution)/shard_map/ppermute | solution.py:750
  28.8 19.6 %copy-start.6 = (bf16[24,1024]{1,0:T(8,128)(2,1)S(1)}, bf16[24,1024]{1,0:T(8,128)(2,1)}, u32[]{:S(2)}) copy-start(bf16[24,1024]{1,0:T(8,128)(2,1)} %filters.9) | copy-start | bytes 147460
  28.8 8.1 %collective-permute-start = (bf16[2,2,256,128]{3,2,0,1:T(8,128)(2,1)S(1)}, bf16[2,2,256,128]{3,2,0,1:T(8,128)(2,1)S(1)}, u32[]{:S(2)}, u32[]{:S(2)}) collective-permute-start(bf16[2,2,256,128]{3,2,0,1:T(8,128)(2,1)S(1)} %copy.20), channel_id=1, source_target_pairs={{0,1},{1,0},{2,3},{3,2},{4,5},{5,4},{6,7},{7,6},{8,9},{9,8},{10,11... | collective-permute-start | bytes 786440 | tf_op jit(solution)/shard_map/ppermute | solution.py:750
  34.7 11.4 %collective-permute-start.5 = (bf16[8,80,128]{2,1,0:T(8,128)(2,1)S(1)}, bf16[8,80,128]{2,1,0:T(8,128)(2,1)S(1)}, u32[]{:S(2)}, u32[]{:S(2)}) collective-permute-start(bf16[8,80,128]{2,1,0:T(8,128)(2,1)S(1)} %all_to_all.5.pieces), channel_id=1, source_target_pairs={{0,16},{8,24},{16,0},{24,8},{1,17},{9,25},{17,1},{25,9},{2,18},{10... | collective-permute-start | bytes 491528 | tf_op jit(solution)/shard_map/ppermute | solution.py:750
  37.0 6.0 %collective-permute-start.3 = (bf16[2,1,256,128]{3,2,0,1:T(8,128)(2,1)S(1)}, bf16[2,1,256,128]{3,2,0,1:T(8,128)(2,1)S(1)}, u32[]{:S(2)}, u32[]{:S(2)}) collective-permute-start(bf16[2,1,256,128]{3,2,0,1:T(8,128)(2,1)S(1)} %constant_dynamic-slice_fusion.2), channel_id=1, source_target_pairs={{0,2},{1,3},{2,0},{3,1},{4,6},{5,7},{6,4},{7,5},{8,10},{9,11},{10,... | collective-permute-start | bytes 393224 | tf_op jit(solution)/shard_map/ppermute | solution.py:750
  39.3 6.7 %collective-permute-start.7 = (bf16[2,64,512]{2,1,0:T(8,128)(2,1)S(1)}, bf16[2,64,512]{2,1,0:T(8,128)(2,1)S(1)}, u32[]{:S(2)}, u32[]{:S(2)}) collective-permute-start(bf16[2,64,512]{2,1,0:T(8,128)(2,1)S(1)} %get-tuple-element.180), channel_id=1, source_target_pairs={{0,1},{1,0},{2,3},{3,2},{4,5},{5,4},{6,7},{7,6},{8,9},{9,8},{10,11... | collective-permute-start | bytes 393224 | tf_op jit(solution)/shard_map/ppermute | solution.py:750
  40.8 5.2 %collective-permute-start.6 = (bf16[2,64,512]{2,1,0:T(8,128)(2,1)S(1)}, bf16[2,64,512]{2,1,0:T(8,128)(2,1)S(1)}, u32[]{:S(2)}, u32[]{:S(2)}) collective-permute-start(bf16[2,64,512]{2,1,0:T(8,128)(2,1)S(1)} %get-tuple-element.183), channel_id=1, source_target_pairs={{0,2},{1,3},{2,0},{3,1},{4,6},{5,7},{6,4},{7,5},{8,10},{9,11},{10,... | collective-permute-start | bytes 393224 | tf_op jit(solution)/shard_map/ppermute | solution.py:750
  40.9 5.0 %collective-permute-start.4 = (bf16[2,1,256,128]{3,2,0,1:T(8,128)(2,1)S(1)}, bf16[2,1,256,128]{3,2,0,1:T(8,128)(2,1)S(1)}, u32[]{:S(2)}, u32[]{:S(2)}) collective-permute-start(bf16[2,1,256,128]{3,2,0,1:T(8,128)(2,1)S(1)} %constant_dynamic-slice_fusion.1), channel_id=1, source_target_pairs={{0,1},{1,0},{2,3},{3,2},{4,5},{5,4},{6,7},{7,6},{8,9},{9,8},{10,11... | collective-permute-start | bytes 393224 | tf_op jit(solution)/shard_map/ppermute | solution.py:750
  46.1 6.6 %copy-start.1 = (bf16[512,2048]{1,0:T(8,128)(2,1)S(1)}, bf16[512,2048]{1,0:T(8,128)(2,1)}, u32[]{:S(2)}) copy-start(bf16[512,2048]{1,0:T(8,128)(2,1)} %refs_8_.1) | copy-start | bytes 6291460
  46.1 6.6 %copy-start.2 = (bf16[512,2048]{1,0:T(8,128)(2,1)S(1)}, bf16[512,2048]{1,0:T(8,128)(2,1)}, u32[]{:S(2)}) copy-start(bf16[512,2048]{1,0:T(8,128)(2,1)} %refs_9_.1) | copy-start | bytes 6291460
  46.1 6.6 %copy-start.3 = (bf16[2048,512]{1,0:T(8,128)(2,1)S(1)}, bf16[2048,512]{1,0:T(8,128)(2,1)}, u32[]{:S(2)}) copy-start(bf16[2048,512]{1,0:T(8,128)(2,1)} %refs_10_.1) | copy-start | bytes 6291460
  46.1 6.6 %copy-start.4 = (bf16[1,128,512]{2,1,0:T(8,128)(2,1)S(1)}, bf16[1,128,512]{2,1,0:T(8,128)(2,1)}, u32[]{:S(2)}) copy-start(bf16[1,128,512]{2,1,0:T(8,128)(2,1)} %hidden.1) | copy-start | bytes 393220
  46.1 6.6 %copy-start.8 = (f32[512]{0:T(512)S(1)}, f32[512]{0:T(512)}, u32[]{:S(2)}) copy-start(f32[512]{0:T(512)} %param.15) | copy-start | bytes 6148
  46.1 6.5 %collective-permute-start.8 = (bf16[1,512,128]{2,1,0:T(8,128)(2,1)S(1)}, bf16[1,512,128]{2,1,0:T(8,128)(2,1)S(1)}, u32[]{:S(2)}, u32[]{:S(2)}) collective-permute-start(bf16[1,512,128]{2,1,0:T(8,128)(2,1)S(1)} %constant_dynamic-slice_fusion), channel_id=1, source_target_pairs={{0,4},{1,5},{2,6},{3,7},{4,0},{5,1},{6,2},{7,3},{8,12},{9,13},{10,... | collective-permute-start | bytes 393224 | tf_op jit(solution)/shard_map/ppermute | solution.py:750
  51.3 11.8 %collective-permute-start.10 = (bf16[2,2,64,512]{3,2,1,0:T(8,128)(2,1)S(1)}, bf16[2,2,64,512]{3,2,1,0:T(8,128)(2,1)S(1)}, u32[]{:S(2)}, u32[]{:S(2)}) collective-permute-start(bf16[2,2,64,512]{3,2,1,0:T(8,128)(2,1)S(1)} %maximum_select_fusion.3.refs_4_), channel_id=1, source_target_pairs={{0,1},{1,0},{2,3},{3,2},{4,5},{5,4},{6,7},{7,6},{8,9},{9,8},{10,11... | collective-permute-start | bytes 786440 | tf_op jit(solution)/shard_map/ppermute | solution.py:750
  52.3 10.8 %collective-permute-start.11 = (bf16[2,2,64,512]{3,2,1,0:T(8,128)(2,1)S(1)}, bf16[2,2,64,512]{3,2,1,0:T(8,128)(2,1)S(1)}, u32[]{:S(2)}, u32[]{:S(2)}) collective-permute-start(bf16[2,2,64,512]{3,2,1,0:T(8,128)(2,1)S(1)} %maximum_select_fusion.4.refs_6_), channel_id=1, source_target_pairs={{0,2},{1,3},{2,0},{3,1},{4,6},{5,7},{6,4},{7,5},{8,10},{9,11},{10,... | collective-permute-start | bytes 786440 | tf_op jit(solution)/shard_map/ppermute | solution.py:750
  56.4 6.6 %collective-permute-start.9 = (bf16[1,128,512]{2,1,0:T(8,128)(2,1)S(1)}, bf16[1,128,512]{2,1,0:T(8,128)(2,1)S(1)}, u32[]{:S(2)}, u32[]{:S(2)}) collective-permute-start(bf16[1,128,512]{2,1,0:T(8,128)(2,1)S(1)} %bitcast.56), channel_id=1, source_target_pairs={{0,4},{1,5},{2,6},{3,7},{4,0},{5,1},{6,2},{7,3},{8,12},{9,13},{10,... | collective-permute-start | bytes 393224 | tf_op jit(solution)/shard_map/ppermute | solution.py:750
  63.0 21.6 %copy-start = (bf16[51,64,512]{2,1,0:T(8,128)(2,1)S(1)}, bf16[51,64,512]{2,1,0:T(8,128)(2,1)}, u32[]{:S(2)}) copy-start(bf16[51,64,512]{2,1,0:T(8,128)(2,1)} %mixing.5) | copy-start | bytes 10027012
  63.1 6.9 %collective-permute-start.13 = (bf16[2,64,512]{2,1,0:T(8,128)(2,1)S(1)}, bf16[2,64,512]{2,1,0:T(8,128)(2,1)S(1)}, u32[]{:S(2)}, u32[]{:S(2)}) collective-permute-start(bf16[2,64,512]{2,1,0:T(8,128)(2,1)S(1)} %get-tuple-element.176), channel_id=1, source_target_pairs={{0,1},{1,0},{2,3},{3,2},{4,5},{5,4},{6,7},{7,6},{8,9},{9,8},{10,11... | collective-permute-start | bytes 393224 | tf_op jit(solution)/shard_map/ppermute | solution.py:750
  66.2 6.9 %collective-permute-start.12 = (bf16[2,64,512]{2,1,0:T(8,128)(2,1)S(1)}, bf16[2,64,512]{2,1,0:T(8,128)(2,1)S(1)}, u32[]{:S(2)}, u32[]{:S(2)}) collective-permute-start(bf16[2,64,512]{2,1,0:T(8,128)(2,1)S(1)} %get-tuple-element.179), channel_id=1, source_target_pairs={{0,2},{1,3},{2,0},{3,1},{4,6},{5,7},{6,4},{7,5},{8,10},{9,11},{10,... | collective-permute-start | bytes 393224 | tf_op jit(solution)/shard_map/ppermute | solution.py:750
  73.1 6.8 %collective-permute-start.16 = (bf16[1,144,512]{2,1,0:T(8,128)(2,1)S(1)}, bf16[1,144,512]{2,1,0:T(8,128)(2,1)S(1)}, u32[]{:S(2)}, u32[]{:S(2)}) collective-permute-start(bf16[1,144,512]{2,1,0:T(8,128)(2,1)S(1)} %bitcast.54), channel_id=1, source_target_pairs={{0,4},{1,5},{2,6},{3,7},{4,0},{5,1},{6,2},{7,3},{8,12},{9,13},{10,... | collective-permute-start | bytes 442376 | tf_op jit(solution)/shard_map/ppermute | solution.py:750
  73.2 8.5 %collective-permute-start.14 = (bf16[2,2,64,512]{3,2,1,0:T(8,128)(2,1)S(1)}, bf16[2,2,64,512]{3,2,1,0:T(8,128)(2,1)S(1)}, u32[]{:S(2)}, u32[]{:S(2)}) collective-permute-start(bf16[2,2,64,512]{3,2,1,0:T(8,128)(2,1)S(1)} %maximum_select_fusion.6.refs_0_), channel_id=1, source_target_pairs={{0,1},{1,0},{2,3},{3,2},{4,5},{5,4},{6,7},{7,6},{8,9},{9,8},{10,11... | collective-permute-start | bytes 786440 | tf_op jit(solution)/shard_map/ppermute | solution.py:750
  75.0 9.6 %collective-permute-start.15 = (bf16[2,2,64,512]{3,2,1,0:T(8,128)(2,1)S(1)}, bf16[2,2,64,512]{3,2,1,0:T(8,128)(2,1)S(1)}, u32[]{:S(2)}, u32[]{:S(2)}) collective-permute-start(bf16[2,2,64,512]{3,2,1,0:T(8,128)(2,1)S(1)} %maximum_select_fusion.7.refs_2_), channel_id=1, source_target_pairs={{0,2},{1,3},{2,0},{3,1},{4,6},{5,7},{6,4},{7,5},{8,10},{9,11},{10,... | collective-permute-start | bytes 786440 | tf_op jit(solution)/shard_map/ppermute | solution.py:750
  79.9 8.7 %collective-permute-start.17 = (bf16[2,64,512]{2,1,0:T(8,128)(2,1)S(1)}, bf16[2,64,512]{2,1,0:T(8,128)(2,1)S(1)}, u32[]{:S(2)}, u32[]{:S(2)}) collective-permute-start(bf16[2,64,512]{2,1,0:T(8,128)(2,1)S(1)} %get-tuple-element.174), channel_id=1, source_target_pairs={{0,2},{1,3},{2,0},{3,1},{4,6},{5,7},{6,4},{7,5},{8,10},{9,11},{10,... | collective-permute-start | bytes 393224 | tf_op jit(solution)/shard_map/ppermute | solution.py:750
  80.1 8.7 %collective-permute-start.18 = (bf16[2,80,512]{2,1,0:T(8,128)(2,1)S(1)}, bf16[2,80,512]{2,1,0:T(8,128)(2,1)S(1)}, u32[]{:S(2)}, u32[]{:S(2)}) collective-permute-start(bf16[2,80,512]{2,1,0:T(8,128)(2,1)S(1)} %get-tuple-element.172), channel_id=1, source_target_pairs={{0,1},{1,0},{2,3},{3,2},{4,5},{5,4},{6,7},{7,6},{8,9},{9,8},{10,11... | collective-permute-start | bytes 491528 | tf_op jit(solution)/shard_map/ppermute | solution.py:750
  88.7 6.8 %copy-start.7 = (f32[512]{0:T(512)S(1)}, f32[512]{0:T(512)}, u32[]{:S(2)}) copy-start(f32[512]{0:T(512)} %param.13) | copy-start | bytes 6148
  88.8 8.7 %collective-permute-start.20 = (bf16[2,2,80,512]{3,2,1,0:T(8,128)(2,1)S(1)}, bf16[2,2,80,512]{3,2,1,0:T(8,128)(2,1)S(1)}, u32[]{:S(2)}, u32[]{:S(2)}) collective-permute-start(bf16[2,2,80,512]{3,2,1,0:T(8,128)(2,1)S(1)} %maximum_select_fusion.refs_2_), channel_id=1, source_target_pairs={{0,2},{1,3},{2,0},{3,1},{4,6},{5,7},{6,4},{7,5},{8,10},{9,11},{10,... | collective-permute-start | bytes 983048 | tf_op jit(solution)/shard_map/ppermute | solution.py:750
  88.9 16.4 %collective-permute-start.24 = (bf16[1024,512]{1,0:T(8,128)(2,1)S(1)}, bf16[1024,512]{1,0:T(8,128)(2,1)S(1)}, u32[]{:S(2)}, u32[]{:S(2)}) collective-permute-start(bf16[1024,512]{1,0:T(8,128)(2,1)S(1)} %place.1.grads), channel_id=1, source_target_pairs={{0,16},{8,24},{16,0},{24,8},{1,17},{9,25},{17,1},{25,9},{2,18},{10... | collective-permute-start | bytes 3145736 | tf_op jit(solution)/shard_map/ppermute | solution.py:750
  90.7 6.7 %collective-permute-start.19 = (bf16[2,2,64,512]{3,2,1,0:T(8,128)(2,1)S(1)}, bf16[2,2,64,512]{3,2,1,0:T(8,128)(2,1)S(1)}, u32[]{:S(2)}, u32[]{:S(2)}) collective-permute-start(bf16[2,2,64,512]{3,2,1,0:T(8,128)(2,1)S(1)} %maximum_select_fusion.8.refs_0_), channel_id=1, source_target_pairs={{0,1},{1,0},{2,3},{3,2},{4,5},{5,4},{6,7},{7,6},{8,9},{9,8},{10,11... | collective-permute-start | bytes 786440 | tf_op jit(solution)/shard_map/ppermute | solution.py:750
  96.3 4.3 %collective-permute-start.21 = (bf16[4,64,128]{2,1,0:T(8,128)(2,1)S(1)}, bf16[4,64,128]{2,1,0:T(8,128)(2,1)S(1)}, u32[]{:S(2)}, u32[]{:S(2)}) collective-permute-start(bf16[4,64,128]{2,1,0:T(8,128)(2,1)S(1)} %get-tuple-element.144), channel_id=1, source_target_pairs={{0,1},{1,0},{2,3},{3,2},{4,5},{5,4},{6,7},{7,6},{8,9},{9,8},{10,11... | collective-permute-start | bytes 196616 | tf_op jit(solution)/shard_map/ppermute | solution.py:750
  100.7 4.4 %collective-permute-start.23 = (bf16[784,256]{1,0:T(8,128)(2,1)S(1)}, bf16[784,256]{1,0:T(8,128)(2,1)S(1)}, u32[]{:S(2)}, u32[]{:S(2)}) collective-permute-start(bf16[784,256]{1,0:T(8,128)(2,1)S(1)} %dynamic-slice_bitcast_fusion), channel_id=1, source_target_pairs={{0,8},{8,0},{16,24},{24,16},{1,9},{9,1},{17,25},{25,17},{2,10},{10... | collective-permute-start | bytes 1204232 | tf_op jit(solution)/shard_map/ppermute | solution.py:750
  100.8 5.7 %collective-permute-start.22 = (bf16[2,2,64,128]{3,2,1,0:T(8,128)(2,1)S(1)}, bf16[2,2,64,128]{3,2,1,0:T(8,128)(2,1)S(1)}, u32[]{:S(2)}, u32[]{:S(2)}) collective-permute-start(bf16[2,2,64,128]{3,2,1,0:T(8,128)(2,1)S(1)} %bitcast.73), channel_id=1, source_target_pairs={{0,2},{1,3},{2,0},{3,1},{4,6},{5,7},{6,4},{7,5},{8,10},{9,11},{10,... | collective-permute-start | bytes 196616 | tf_op jit(solution)/shard_map/ppermute | solution.py:750
  105.2 11.7 %collective-permute-start.26 = (bf16[784,256]{1,0:T(8,128)(2,1)S(1)}, bf16[784,256]{1,0:T(8,128)(2,1)S(1)}, u32[]{:S(2)}, u32[]{:S(2)}) collective-permute-start(bf16[784,256]{1,0:T(8,128)(2,1)S(1)} %fusion), channel_id=1, source_target_pairs={{0,16},{8,24},{16,0},{24,8},{1,17},{9,25},{17,1},{25,9},{2,18},{10... | collective-permute-start | bytes 1204232 | tf_op jit(solution)/shard_map/ppermute | solution.py:750
  106.6 6.3 %collective-permute-start.25 = (bf16[1,4,64,128]{3,2,1,0:T(8,128)(2,1)S(1)}, bf16[1,4,64,128]{3,2,1,0:T(8,128)(2,1)S(1)}, u32[]{:S(2)}, u32[]{:S(2)}) collective-permute-start(bf16[1,4,64,128]{3,2,1,0:T(8,128)(2,1)S(1)} %get-tuple-element.184), channel_id=1, source_target_pairs={{0,4},{1,5},{2,6},{3,7},{4,0},{5,1},{6,2},{7,3},{8,12},{9,13},{10,... | collective-permute-start | bytes 196616 | tf_op jit(solution)/shard_map/ppermute | solution.py:750
  110.0 8.7 %collective-permute-start.28 = (bf16[1536,512]{1,0:T(8,128)(2,1)S(1)}, bf16[1536,512]{1,0:T(8,128)(2,1)S(1)}, u32[]{:S(2)}, u32[]{:S(2)}) collective-permute-start(bf16[1536,512]{1,0:T(8,128)(2,1)S(1)} %mixing_grad.2.part), channel_id=1, source_target_pairs={{0,8},{8,0},{16,24},{24,16},{1,9},{9,1},{17,25},{25,17},{2,10},{10... | collective-permute-start | bytes 4718600 | tf_op jit(solution)/shard_map/ppermute | solution.py:750
  117.0 6.0 %collective-permute-start.27 = (bf16[1728,512]{1,0:T(8,128)(2,1)S(1)}, bf16[1728,512]{1,0:T(8,128)(2,1)S(1)}, u32[]{:S(2)}, u32[]{:S(2)}) collective-permute-start(bf16[1728,512]{1,0:T(8,128)(2,1)S(1)} %mixing_grad.3.part), channel_id=1, source_target_pairs={{0,8},{8,0},{16,24},{24,16},{1,9},{9,1},{17,25},{25,17},{2,10},{10... | collective-permute-start | bytes 5308424 | tf_op jit(solution)/shard_map/ppermute | solution.py:750
  117.1 4.1 %collective-permute-start.29 = (bf16[784,256]{1,0:T(8,128)(2,1)S(1)}, bf16[784,256]{1,0:T(8,128)(2,1)S(1)}, u32[]{:S(2)}, u32[]{:S(2)}) collective-permute-start(bf16[784,256]{1,0:T(8,128)(2,1)S(1)} %add_convert_fusion.mine), channel_id=1, source_target_pairs={{0,8},{8,0},{16,24},{24,16},{1,9},{9,1},{17,25},{25,17},{2,10},{10... | collective-permute-start | bytes 1204232 | tf_op jit(solution)/shard_map/ppermute | solution.py:750
